TPU v7x, 32 devices: a whole 2x2x4 slice. The times are simulated.
32 devices in a mesh: seq: 8 (over y, x, core), head: 4 (over z).
Axes of the slice: x: 2, y: 2, z: 4, core: 2. Of those that a mesh axis runs over, the one named last changes fastest.
Arguments:
- attn_q: bfloat16 [8192, 5120], P('seq', 'head'), may hold values from -6 to 6
- attn_k: bfloat16 [8192, 5120], P('seq', 'head'), may hold values from -6 to 6
- attn_v: bfloat16 [8192, 5120], P('seq', 'head'), may hold values from -6 to 6
- fast_q: bfloat16 [8192, 5120], P('seq', 'head'), may hold values from -6 to 6
- fast_k: bfloat16 [8192, 5120], P('seq', 'head'), may hold values from -6 to 6
- fast_v: bfloat16 [8192, 5120], P('seq', 'head'), may hold values from -6 to 6
- rates: float32 [8192, 8], P('seq', 'head'), may hold values from 0.00022097086 to 0.0022097088
- fast_gate: float32 [8, 640, 640], P('head'), may hold values from -0.25 to 0.25
- fast_up: float32 [8, 640, 640], P('head'), may hold values from -0.25 to 0.25
- fast_down: float32 [8, 640, 640], P('head'), may hold values from -0.25 to 0.25
Outputs:
- mixed: bfloat16 [8192, 5120], P('seq', 'head')
All inputs are finite; a program needn't handle non-finite values.
Results may differ from a plain program's by a relative error of at most 0.012.
Values may be sent and summed in bfloat16 or wider, within the bound.
No kernel may reach another device: no remote copies, remote signals or barrier semaphores. Data moves between devices by JAX's collectives and lax.ppermute only.
A program may use at most 192 MiB of HBM per device.

v0:
```python
import functools
import math

import jax
import jax.numpy as jnp
from jax import lax
from jax.experimental import pallas as pl
from jax.experimental.pallas import tpu as pltpu
from jax.sharding import PartitionSpec as P


HD = 128
EPS = 1e-06
NN = (((1,), (0,)), ((), ()))
NT = (((1,), (1,)), ((), ()))
TN = (((0,), (0,)), ((), ()))


def mm(a, b, dims=NN):
    return lax.dot_general(a, b, dims, preferred_element_type=jnp.float32)


def attn_kernel(position_ref, *refs, bq, jobs, sources, log_stride):
    queries = refs[: len(jobs)]
    keys = refs[len(jobs) : len(jobs) + sources]
    values = refs[len(jobs) + sources : len(jobs) + 2 * sources]
    rest = list(refs[len(jobs) + 2 * sources :])
    outs = []
    for _, sums in jobs:
        outs.append((rest.pop(0), rest.pop(0) if sums == 1 else None))
    bufs = (rest.pop(0), rest.pop(0))
    logs = [rest.pop(0) if sums else None for _, sums in jobs]
    group = pl.program_id(0)
    heads = queries[0].shape[1] // HD
    c = math.log2(math.e) / math.sqrt(HD)
    ri = lax.broadcasted_iota(jnp.int32, (bq, bq), 0)
    ci = lax.broadcasted_iota(jnp.int32, (bq, bq), 1)
    absent = position_ref[0] == 0
    units = [(h, j, t) for h in range(heads) for j in range(len(jobs)) for t in range(len(jobs[j][0]))]

    def scores(i):
        h, j, t = units[i]
        hs = slice(h * HD, (h + 1) * HD)
        buf = bufs[i % 2]
        q = queries[j][t * bq : (t + 1) * bq, hs]
        tops = []
        at = 0
        for source, lo, hi, edge in jobs[j][0][t]:
            s = mm(q, keys[source][lo:hi, hs], NT)
            n = hi - lo
            if edge == 1:
                kept = jnp.where(ci >= ri, s[:, :bq], -jnp.inf)
                s = jnp.concatenate([kept, s[:, bq:]], axis=1) if n > bq else kept
            elif edge == -1:
                kept = jnp.where(ci <= ri, s[:, n - bq :], -jnp.inf)
                s = jnp.concatenate([s[:, : n - bq], kept], axis=1) if n > bq else kept
            buf[:, at : at + n] = s
            tops.append(jnp.max(s, axis=1, keepdims=True))
            at += n
        if len(tops) == 1:
            return [tops[0] * c]
        m = jnp.maximum(tops[1], jnp.where(absent, -jnp.inf, tops[0])) * c
        return [jnp.where(absent, 1e30, m), m]

    def finish(i, ms):
        h, j, t = units[i]
        plan, sums = jobs[j]
        hs = slice(h * HD, (h + 1) * HD)
        buf = bufs[i % 2]
        out = total = None
        at = 0
        for (source, lo, hi, _), m in zip(plan[t], ms):
            p = jnp.exp2(buf[:, at : at + hi - lo] * c - m)
            part = jnp.sum(p, axis=1, keepdims=True)
            o = mm(p.astype(jnp.bfloat16), values[source][lo:hi, hs])
            total = part if total is None else total + part
            out = o if out is None else out + o
            at += hi - lo
        rows = slice(t * bq, (t + 1) * bq)
        out = (out / total).astype(jnp.bfloat16)
        head = group * heads + h
        if sums == 2:
            outs[j][0][rows, pl.ds(pl.multiple_of(head * HD, HD), HD)] = out
        else:
            outs[j][0][rows, hs] = out
        if sums:
            lane = lax.broadcasted_iota(jnp.int32, (bq, HD), 1)
            log = ms[-1] + jnp.log(total) * math.log2(math.e)
            logs[j][rows, :] = jnp.where(lane == head, log, logs[j][rows, :])

    if any(sums for _, sums in jobs):

        @pl.when(group == 0)
        def _():
            for log in logs:
                if log is not None:
                    log[...] = jnp.zeros(log.shape, log.dtype)

    ms = scores(0)
    for i in range(len(units)):
        nxt = scores(i + 1) if i + 1 < len(units) else None
        finish(i, ms)
        ms = nxt
    if any(sums for _, sums in jobs):

        @pl.when(group == pl.num_programs(0) - 1)
        def _():
            for (_, sums), (out, log_out), log in zip(jobs, outs, logs):
                if sums == 1:
                    log_out[...] = log[...]
                if sums == 2:
                    x = log[...]
                    a = x.astype(jnp.bfloat16).astype(jnp.float32)
                    b = (x - a).astype(jnp.bfloat16).astype(jnp.float32)
                    x = a + pltpu.roll(b, log_stride, 1) + pltpu.roll(x - a - b, 2 * log_stride, 1)
                    out[:, out.shape[1] - HD :] = x.astype(jnp.bfloat16)


def log_stride_of(cols):
    return 16 * pl.cdiv(cols // HD, 16)


def attention(position, jobs, sources, bq, width):
    cols = jobs[0][0].shape[1]
    w = width * HD
    ranges = [r for _, _, plan, _ in jobs for tile in plan for r in tile]
    span = max(sum(hi - lo for _, lo, hi, _ in tile) for _, _, plan, _ in jobs for tile in plan)
    pairs = bq * sum(hi - lo for _, lo, hi, _ in ranges) * cols // HD
    block = lambda n, at: pl.BlockSpec((n, w), lambda g, f: (at, g))
    whole = lambda *shape: pl.BlockSpec(shape, lambda g, f: (0, 0))
    outs, out_specs, logs = [], [], []
    for _, _, plan, sums in jobs:
        rows = len(plan) * bq
        if sums == 2:
            outs.append(jax.ShapeDtypeStruct((rows, cols + HD), jnp.bfloat16))
            out_specs.append(whole(rows, cols + HD))
        else:
            outs.append(jax.ShapeDtypeStruct((rows, cols), jnp.bfloat16))
            out_specs.append(block(rows, 0))
        if sums == 1:
            outs.append(jax.ShapeDtypeStruct((rows, HD), jnp.float32))
            out_specs.append(whole(rows, HD))
        if sums:
            logs.append(pltpu.VMEM((rows, HD), jnp.float32))
    specs = [block(len(plan) * bq, at) for _, at, plan, _ in jobs]
    specs += [block(n, at) for _, at, _, _, n in sources] + [block(n, at) for _, _, _, at, n in sources]
    kernel = functools.partial(
        attn_kernel,
        bq=bq,
        jobs=[(plan, sums) for _, _, plan, sums in jobs],
        sources=len(sources),
        log_stride=log_stride_of(cols),
    )
    return pl.pallas_call(
        kernel,
        grid_spec=pltpu.PrefetchScalarGridSpec(
            num_scalar_prefetch=1,
            grid=(cols // w,),
            in_specs=specs,
            out_specs=out_specs,
            scratch_shapes=[pltpu.VMEM((bq, span), jnp.float32)] * 2 + logs,
        ),
        out_shape=outs,
        cost_estimate=pl.CostEstimate(
            flops=4 * pairs * HD, bytes_accessed=8 * bq * cols * len(ranges), transcendentals=pairs
        ),
    )(position, *[job[0] for job in jobs], *[x[0] for x in sources], *[x[2] for x in sources])


def grad_kernel(s_ref, x_ref, v_ref, r_ref, w1_ref, w3_ref, w2_ref, *refs, head, tm, tn, split):
    w13, w2, gu, hid, og = refs[-5:]
    F = w1_ref.shape[2]
    rows = x_ref.shape[0]
    w13[:, :F] = w1_ref[0].astype(jnp.bfloat16)
    w13[:, F:] = w3_ref[0].astype(jnp.bfloat16)
    w2[...] = w2_ref[0].astype(jnp.bfloat16)
    pick = lax.broadcasted_iota(jnp.int32, r_ref.shape, 0) == head(s_ref)
    rate = jnp.sum(jnp.where(pick, r_ref[...], 0.0), axis=0, keepdims=True)
    rate = jnp.transpose(jnp.broadcast_to(rate, (8, rows)))[:, :1]
    og[...] = (-rate * v_ref[...].astype(jnp.float32)).astype(jnp.bfloat16)
    n = rows // tm

    def products(i):
        r = slice(i * tm, (i + 1) * tm)
        return mm(x_ref[r, :], w13[...]), mm(og[r, :], w2[...], NT)

    def finish(i, pre, hg):
        r = slice(i * tm, (i + 1) * tm)
        pg, pu = pre[:, :F], pre[:, F:]
        sg = jax.nn.sigmoid(pg)
        act = pg * sg
        gu[r, :F] = (hg * pu * (sg * (1.0 + pg * (1.0 - sg)))).astype(jnp.bfloat16)
        gu[r, F:] = (hg * act).astype(jnp.bfloat16)
        hid[r, :] = (act * pu).astype(jnp.bfloat16)

    cur = products(0)
    for i in range(n):
        nxt = products(i + 1) if i + 1 < n else None
        finish(i, *cur)
        cur = nxt
    x = x_ref[...]
    hd = hid[...]
    quarter = 3 * F // 4
    x1, y1 = (s_ref[0] >> 1) & 1, (s_ref[0] >> 2) & 1

    def put(lo, grad):
        if not split:
            refs[0][lo : lo + grad.shape[0], :] = grad.astype(refs[0].dtype)
            return
        grad = grad + refs[0][lo : lo + grad.shape[0], :].astype(jnp.float32)
        at = 0
        while at < grad.shape[0]:
            block, row = divmod(lo + at, quarter)
            n = min(grad.shape[0] - at, quarter - row)
            coordinate = x1 if block < 2 else y1
            slot = jnp.where(coordinate == block % 2, 0, 1)
            refs[1 + block // 2][slot, row : row + n, :] = grad[at : at + n].astype(jnp.bfloat16)
            at += n

    for j in range(2 * F // tn):
        put(j * tn, mm(gu[:, j * tn : (j + 1) * tn], x, TN))
    for j in range(F // HD):
        put(2 * F + j * HD, mm(og[:, j * HD : (j + 1) * HD], hd, TN))
    if split:
        for o in range(2):
            refs[3 + 2 * o][...] = refs[1 + o][0]
            refs[4 + 2 * o][...] = refs[1 + o][1]


def gradients(position, head, fk, fv, rates_t, w1, w3, w2, received=None):
    rows = fk.shape[0]
    F = w1.shape[1]
    tm = min(256, rows)
    tn = 256 if 2 * F % 256 == 0 else HD
    col = pl.BlockSpec((rows, F), lambda i, s: (0, head(s)))
    weight = pl.BlockSpec((1, F, F), lambda i, s: (head(s), 0, 0))
    whole = lambda *shape: pl.BlockSpec(shape, lambda i, s: (0,) * len(shape))
    bf = jnp.bfloat16
    args = [position, fk, fv, rates_t, w1, w3, w2]
    specs = [col, col, whole(*rates_t.shape), weight, weight, weight]
    scratch = [
        pltpu.VMEM((F, 2 * F), bf),
        pltpu.VMEM((F, F), bf),
        pltpu.VMEM((rows, 2 * F), bf),
        pltpu.VMEM((rows, F), bf),
        pltpu.VMEM((rows, F), bf),
    ]
    if received is None:
        shapes = [(3 * F, F)]
    else:
        shapes = [(3 * F // 4, F)] * 4
        args.append(received)
        specs.append(whole(3 * F, F))
        scratch = [pltpu.VMEM((2, 3 * F // 4, F), bf)] * 2 + scratch
    kernel = functools.partial(grad_kernel, head=head, tm=tm, tn=tn, split=received is not None)

    def body(*refs):
        if received is None:
            return kernel(*refs)
        ins, outs, halves, rest = refs[:8], refs[8:12], refs[12:14], refs[14:]
        return kernel(*ins, *halves, *outs, *rest)

    return pl.pallas_call(
        body,
        grid_spec=pltpu.PrefetchScalarGridSpec(
            num_scalar_prefetch=1,
            grid=(1,),
            in_specs=specs,
            out_specs=[whole(*shape) for shape in shapes],
            scratch_shapes=scratch,
        ),
        out_shape=[jax.ShapeDtypeStruct(shape, bf) for shape in shapes],
        cost_estimate=pl.CostEstimate(
            flops=12 * rows * F * F, bytes_accessed=rows * F * 4 + F * F * 18, transcendentals=rows * F
        ),
        name="grads",
    )(*args)


def turn_kernel(s_ref, w1, w3, w2, o_ref, *scratch, units):
    F = w1.shape[2]
    all_ref = scratch[0] if scratch else o_ref
    all_ref[:F, :] = w1[0].T
    all_ref[F : 2 * F, :] = w3[0].T
    all_ref[2 * F :, :] = w2[0].T
    if scratch:
        n = o_ref.shape[0] // len(units)
        for i, unit in enumerate(units):
            start = pl.multiple_of(unit(s_ref) * n, 8)
            o_ref[i * n : (i + 1) * n, :] = all_ref[pl.ds(start, n), :]


def turned(position, head, w1, w3, w2, size=None, units=()):
    F = w1.shape[1]
    weight = pl.BlockSpec((1, F, F), lambda i, s: (head(s), 0, 0))
    shape = (size * len(units), F) if units else (3 * F, F)
    return pl.pallas_call(
        functools.partial(turn_kernel, units=units),
        grid_spec=pltpu.PrefetchScalarGridSpec(
            num_scalar_prefetch=1,
            grid=(1,),
            in_specs=[weight] * 3,
            out_specs=pl.BlockSpec(shape, lambda i, s: (0, 0)),
            scratch_shapes=[pltpu.VMEM((3 * F, F), jnp.float32)] if units else [],
        ),
        out_shape=jax.ShapeDtypeStruct(shape, jnp.float32),
        cost_estimate=pl.CostEstimate(flops=3 * F * F, bytes_accessed=24 * F * F, transcendentals=0),
        name="turned",
    )(position, w1, w3, w2)


def renormed(old, grad):
    new = old - grad
    old_sq = jnp.sum(old * old, axis=-1, keepdims=True)
    new_sq = jnp.sum(new * new, axis=-1, keepdims=True)
    return (new * (jnp.sqrt(old_sq) / jnp.sqrt(new_sq + EPS))).astype(jnp.bfloat16)


def renorm_kernel(s_ref, old_ref, *refs):
    out = refs[-1]
    n = out.shape[0] // 2
    for i in range(2):
        a, b, c = (ref[...].astype(jnp.float32) for ref in refs[3 * i : 3 * i + 3])
        out[i * n : (i + 1) * n, :] = renormed(old_ref[i * n : (i + 1) * n, :], a + b + c)


def renorm_units(position, old, upper, lower):
    unit, F = upper[2][0].shape
    flat = upper + lower
    spec = lambda at: pl.BlockSpec((unit, F), lambda i, s: (at(s), 0))
    whole = pl.BlockSpec((2 * unit, F), lambda i, s: (0, 0))
    return pl.pallas_call(
        renorm_kernel,
        grid_spec=pltpu.PrefetchScalarGridSpec(
            num_scalar_prefetch=1,
            grid=(1,),
            in_specs=[whole] + [spec(at) for _, at in flat],
            out_specs=whole,
        ),
        out_shape=jax.ShapeDtypeStruct((2 * unit, F), jnp.bfloat16),
        cost_estimate=pl.CostEstimate(flops=20 * unit * F, bytes_accessed=24 * unit * F, transcendentals=0),
        name="renorm",
    )(position, old, *[array for array, _ in flat])


def apply_kernel(s_ref, q_ref, high_ref, own_ref, far_ref, own_log, far_log, *rest, head, tm, places, unit, pieces, stride):
    n_ref, a_ref, o_ref = rest[-2], rest[-1], rest[-3]
    F = n_ref.shape[1]
    step = pl.program_id(0)

    @pl.when(step == 0)
    def _():
        slot = 0
        for ref in rest[:pieces]:
            for r in range(ref.shape[0] // unit):
                to = pl.multiple_of(places[slot](s_ref) * unit, min(unit, 16))
                n_ref[pl.ds(to, unit), :] = ref[r * unit : (r + 1) * unit, :]
                slot += 1
        lane = lax.broadcasted_iota(jnp.int32, own_log.shape, 1)
        for j in range(F // HD):
            cs = slice(j * HD, (j + 1) * HD)
            at = head(s_ref) * (F // HD) + j
            pick = lambda ref, of: jnp.sum(
                jnp.where(of, ref[...].astype(jnp.float32), 0.0), axis=1, keepdims=True
            )
            own = pick(own_log, lane == at)
            far = pick(far_log, (lane == at) | (lane == at + stride) | (lane == at + 2 * stride))
            far = jnp.where(s_ref[0] == 0, -jnp.inf, far)
            top = jnp.maximum(own, far)
            own, far = jnp.exp2(own - top), jnp.exp2(far - top)
            share = own / (own + far)
            a, b = own_ref[:, cs].astype(jnp.float32), far_ref[:, cs].astype(jnp.float32)
            a_ref[:, cs] = a * share + b * (1.0 - share)

    @pl.when(step == 1)
    def _():
        a_ref[...] = high_ref[...].astype(jnp.float32)

    n = q_ref.shape[0] // tm

    def first(i):
        return mm(q_ref[i * tm : (i + 1) * tm, :], n_ref[: 2 * F, :], NT)

    def second(i, h):
        g = h[:, :F]
        hid = (g * jax.nn.sigmoid(g) * h[:, F:]).astype(jnp.bfloat16)
        r = slice(i * tm, (i + 1) * tm)
        o_ref[r, :] = (a_ref[r, :] + mm(hid, n_ref[2 * F :, :], NT)).astype(o_ref.dtype)

    cur = first(0)
    for i in range(n):
        nxt = first(i + 1) if i + 1 < n else None
        second(i, cur)
        cur = nxt


def apply_head(position, head, fq, pieces, places, unit, attended, into=None):
    rows, cols = fq.shape
    F = pieces[0].shape[1]
    half = rows // 2
    col = pl.BlockSpec((half, F), lambda i, s: (i, head(s)))
    part = pl.BlockSpec((half, F), lambda i, s: (0, head(s)))
    whole = lambda a: pl.BlockSpec(a.shape, lambda i, s: (0, 0))
    high, own, far, own_log = attended
    far_log = pl.BlockSpec((half, HD), lambda i, s: (0, cols // HD))
    args = [position, fq, high, own, far, own_log, far, *pieces]
    specs = [col, part, part, part, whole(own_log), far_log] + [whole(p) for p in pieces]
    aliases = {}
    if into is not None:
        aliases = {len(args): 0}
        args.append(into)
        specs.append(pl.BlockSpec(memory_space=pl.ANY))
    kernel = functools.partial(
        apply_kernel, head=head, tm=min(256, half), places=places, unit=unit, pieces=len(pieces), stride=log_stride_of(cols)
    )
    return pl.pallas_call(
        kernel,
        grid_spec=pltpu.PrefetchScalarGridSpec(
            num_scalar_prefetch=1,
            grid=(2,),
            in_specs=specs,
            out_specs=col,
            scratch_shapes=[pltpu.VMEM((3 * F, F), jnp.bfloat16), pltpu.VMEM((half, F), jnp.float32)],
        ),
        out_shape=jax.ShapeDtypeStruct((rows, cols), jnp.bfloat16),
        input_output_aliases=aliases,
        cost_estimate=pl.CostEstimate(
            flops=6 * rows * F * F, bytes_accessed=rows * F * 6 + F * F * 6, transcendentals=rows * F
        ),
        name="apply",
    )(*args)


def exchange(block, bit):
    size = lax.axis_size("seq")
    return lax.ppermute(block, "seq", [(i, i ^ (1 << bit)) for i in range(size)])


def shifted(block, by):
    size = lax.axis_size("seq")
    return lax.ppermute(block, "seq", [(i, i + by) for i in range(size) if 0 <= i + by < size])


def synced(total, old, bits, position):
    offset = 0
    for bit in bits:
        half = total.shape[0] // 2
        mine = (position >> bit) & 1
        away = lax.dynamic_slice_in_dim(total, (1 - mine) * half, half, 0).astype(jnp.bfloat16)
        kept = lax.dynamic_slice_in_dim(total, mine * half, half, 0)
        total = kept + exchange(away, bit).astype(jnp.float32)
        offset = offset + mine * half
    part = renormed(lax.dynamic_slice_in_dim(old, offset, total.shape[0], 0), total)
    for bit in reversed(bits):
        mine = (position >> bit) & 1
        other = exchange(part, bit)
        part = jnp.concatenate(
            [jnp.where(mine == 0, part, other), jnp.where(mine == 0, other, part)], axis=0
        )
    return part


def synced_square(position, quarters, old):
    x, y = (position[0] >> 1) & 1, (position[0] >> 2) & 1
    keep_x, send_x, keep_y, send_y = quarters
    unit = keep_x.shape[0] // 2
    top0, bottom0 = exchange(send_x, 1), exchange(send_y, 2)

    def fold(a, b, at):
        a, b = (lax.dynamic_slice_in_dim(v, at * unit, unit, 0).astype(jnp.float32) for v in (a, b))
        return (a + b).astype(jnp.bfloat16)

    top1 = exchange(fold(keep_x, top0, 1 - y), 2)
    bottom1 = exchange(fold(keep_y, bottom0, 1 - x), 1)
    zero = lambda s: 0
    part = renorm_units(
        position,
        old,
        [(keep_x, at_y), (top0, at_y), (top1, zero)],
        [(keep_y, at_x), (bottom0, at_x), (bottom1, zero)],
    )
    over_x, over_y = exchange(part, 1), exchange(part, 2)
    top2, bottom2 = exchange(over_y[:unit], 1), exchange(over_x[unit:], 2)
    return [part, over_x, over_y, top2, bottom2], unit


def at_x(s):
    return (s[0] >> 1) & 1


def at_y(s):
    return (s[0] >> 2) & 1


def place(flip_x, flip_y):
    x = lambda s: at_x(s) ^ flip_x
    y = lambda s: at_y(s) ^ flip_y
    return [lambda s: 2 * x(s) + y(s), lambda s: 4 + 2 * y(s) + x(s)]


def shards(attn_q, attn_k, attn_v, fast_q, fast_k, fast_v, rates, fast_gate, fast_up, fast_down):
    position = lax.axis_index("seq").astype(jnp.int32).reshape(1)
    count = lax.axis_size("seq")
    heads = fast_gate.shape[0]
    rows = attn_q.shape[0]
    half = rows // 2
    width = 2 if attn_q.shape[1] // HD % 2 == 0 else 1
    prev = shifted(jnp.concatenate([attn_k[half:], attn_v[half:]], axis=0), 1)
    guests = shifted(attn_q[:half], -1)
    rates_t = rates.T
    weights = (fast_gate, fast_up, fast_down)

    def grads(head, received=None):
        return gradients(position, head, fast_k, fast_v, rates_t, *weights, received)

    if heads == 2 and count == 8:
        near, far = (lambda s: s[0] & 1), (lambda s: 1 - (s[0] & 1))
        received = exchange(grads(far)[0], 0)
        old = turned(position, near, *weights, size=3 * fast_gate.shape[1] // 8, units=tuple(place(0, 0)))
        quarters = grads(near, received)
        pieces, unit = synced_square(position, quarters, old)
        other = [exchange(p, 0) for p in pieces]
        places = place(0, 0) + place(1, 0) + place(0, 1)
        places += [place(1, 1)[0], place(1, 1)[1]]
        news = [(near, pieces, places, unit), (far, other, places, unit)]
    else:
        news = []
        bits = list(range(count.bit_length() - 1))
        for h in range(heads):
            head = lambda s, h=h: h
            old = turned(position, head, *weights)
            new = synced(grads(head)[0].astype(jnp.float32), old, bits, position[0])
            news.append((head, [new], [lambda s: 0], new.shape[0]))
    bq = min(256, half)
    tiles = half // bq
    late = [
        [(0, t * bq, half, 1), (1, 0, half + (t + 1) * bq, -1)] for t in range(tiles)
    ]
    early = [[(0, 0, (t + 1) * bq, -1)] for t in range(tiles)]
    guest = [[(0, t * bq, rows, 1)] for t in range(tiles)]
    here = (attn_k, 0, attn_v, 0, rows)
    returned, own_out, own_log = attention(position, [(guests, 0, guest, 2), (attn_q, 0, early, 1)], [here], bq, width)
    far_out = shifted(returned, 1)
    (high,) = attention(position, [(attn_q, 1, late, 0)], [(prev, 0, prev, 1, half), here], bq, width)
    attended = (high, own_out, far_out, own_log)
    mixed = None
    for head, pieces, places, unit in news:
        mixed = apply_head(position, head, fast_q, pieces, places, unit, attended, mixed)
    return mixed


def solution(mesh):
    placed = (P("seq", "head"),) * 7 + (P("head", None, None),) * 3
    return jax.shard_map(shards, mesh=mesh, in_specs=placed, out_specs=P("seq", "head"), check_vma=False)
```

profile of v0, /device:TPU:0, one launch (start us, length us, event | category | flops | bytes accessed | tf_op | source)
XLA Modules:
  0.0 154.6 jit_solution(4700651031857263401)
XLA Ops:
  0.0 11.6 %grads.2 = bf16[1920,640]{1,0:T(8,128)(2,1)} custom-call(s32[1]{0:T(128)} %bitcast.position_ref.s_ref.refs_0_, bf16[1024,1280]{1,0:T(8,128)(2,1)} %refs_1_.5, bf16[1024,1280]{1,0:T(8,128)(2,1)} %refs_2_.7, f32[2,1024]{1,0:T(2,128)} %bitcast.2, f32[2,640,640]{2,1,0:T(8,128)} %refs_4_.5, f32[2,640,640]{2,1,0:T(8,128)} %refs_5_.3, f32[2,640,640]{2,1,0:T(8,128)} %refs_6_.3), custom_call_target="tpu_custom_call" | custom-call | flops 5033164800 | bytes 9994240 | tf_op jit(solution)/shard_map/grads/pallas_call | solution.py:263
  12.1 1.1 slice.17
  13.3 1.5 collective-permute-start.1
  15.0 1.7 %pad_maximum_fusion = bf16[1024,1280]{1,0:T(8,128)(2,1)} fusion(bf16[512,1280]{1,0:T(8,128)(2,1)S(1)} %slice-done, bf16[512,1280]{1,0:T(8,128)(2,1)S(1)} %slice-done.1), kind=kLoop, calls=%fused_computation | loop fusion | flops 5242880 | bytes 5242880 | tf_op jit(solution)/shard_map/concatenate | solution.py:508
  16.7 4.4 %collective-permute-start = (bf16[1024,1280]{1,0:T(8,128)(2,1)}, bf16[1024,1280]{1,0:T(8,128)(2,1)}, u32[]{:S(2)}, u32[]{:S(2)}) collective-permute-start(bf16[1024,1280]{1,0:T(8,128)(2,1)} %pad_maximum_fusion), channel_id=1, source_target_pairs={{0,4},{4,8},{8,12},{12,16},{16,20},{20,24},{24,28},{1,5},{5,9},{9,... | collective-permute-start | bytes 7864328 | tf_op jit(solution)/shard_map/ppermute | solution.py:441
  21.1 12.5 %grads.3 = (bf16[480,640]{1,0:T(8,128)(2,1)}, bf16[480,640]{1,0:T(8,128)(2,1)}, bf16[480,640]{1,0:T(8,128)(2,1)}, bf16[480,640]{1,0:T(8,128)(2,1)}) custom-call(s32[1]{0:T(128)} %bitcast.position_ref.s_ref.refs_0_, bf16[1024,1280]{1,0:T(8,128)(2,1)} %refs_1_.5, bf16[1024,1280]{1,0:T(8,128)(2,1)} %refs_2_.7, f32[2,1024]{1,0:T(2,128)} %bitcast.3, ...), custom_call_target="tpu_custom_call" | custom-call | flops 5033164800 | bytes 9994240 | tf_op jit(solution)/shard_map/grads/pallas_call | solution.py:263
  33.5 1.2 collective-permute-start.4
  34.7 2.6 %collective-permute-start.6 = (bf16[480,640]{1,0:T(8,128)(2,1)}, bf16[480,640]{1,0:T(8,128)(2,1)}, u32[]{:S(2)}, u32[]{:S(2)}) collective-permute-start(bf16[480,640]{1,0:T(8,128)(2,1)} %get-tuple-element.18), channel_id=1, source_target_pairs={{0,16},{4,20},{8,24},{12,28},{16,0},{20,4},{24,8},{28,12},{1,17},{... | collective-permute-start | bytes 1843208 | tf_op jit(solution)/shard_map/ppermute | solution.py:436
  37.4 13.8 %shard_map.101 = (bf16[512,1408]{1,0:T(8,128)(2,1)}, bf16[512,1280]{1,0:T(8,128)(2,1)}, f32[512,128]{1,0:T(8,128)}) custom-call(s32[1]{0:T(128)} %bitcast.position_ref.s_ref.refs_0_, bf16[512,1280]{1,0:T(8,128)(2,1)} %collective-permute-done.1.refs_0_, bf16[1024,1280]{1,0:T(8,128)(2,1)} %refs_1_.3, bf16[1024,1280]{1,0:T(8,128)(2,1)} %refs_2_.5, ...), custom_call_target="tpu_custom_call" | custom-call | flops 3355443200 | bytes 10485760 | tf_op jit(solution)/shard_map/pallas_call | solution.py:154
  51.1 6.8 %collective-permute-start.2 = (bf16[512,1408]{1,0:T(8,128)(2,1)}, bf16[512,1408]{1,0:T(8,128)(2,1)S(1)}, u32[]{:S(2)}, u32[]{:S(2)}) collective-permute-start(bf16[512,1408]{1,0:T(8,128)(2,1)} %get-tuple-element.13), channel_id=1, source_target_pairs={{0,4},{4,8},{8,12},{12,16},{16,20},{20,24},{24,28},{1,5},{5,9},{9,... | collective-permute-start | bytes 4325384 | tf_op jit(solution)/shard_map/ppermute | solution.py:441
  57.9 0.9 add_convert_fusion.1
  58.9 3.4 %collective-permute-start.5 = (bf16[240,640]{1,0:T(8,128)(2,1)}, bf16[240,640]{1,0:T(8,128)(2,1)S(1)}, u32[]{:S(2)}, u32[]{:S(2)}) collective-permute-start(bf16[240,640]{1,0:T(8,128)(2,1)} %add_convert_fusion.1), channel_id=1, source_target_pairs={{0,16},{4,20},{8,24},{12,28},{16,0},{20,4},{24,8},{28,12},{1,17},{... | collective-permute-start | bytes 921608 | tf_op jit(solution)/shard_map/ppermute | solution.py:436
  62.2 10.3 %collective-permute-done.6.refs_4_ = bf16[480,640]{1,0:T(8,128)(2,1)} collective-permute-done((bf16[480,640]{1,0:T(8,128)(2,1)}, bf16[480,640]{1,0:T(8,128)(2,1)}, u32[]{:S(2)}, u32[]{:S(2)}) %collective-permute-start.6) | collective-permute-done | bytes 614432 | tf_op jit(solution)/shard_map/ppermute | solution.py:436
  72.6 1.8 %add_convert_fusion = bf16[240,640]{1,0:T(8,128)(2,1)} fusion(bf16[480,640]{1,0:T(8,128)(2,1)} %collective-permute-done.6.refs_4_, s32[]{:T(128)S(6)} %select_n.9, bf16[480,640]{1,0:T(8,128)(2,1)S(1)} %copy-done.3), kind=kLoop, calls=%fused_computation.1 | loop fusion | flops 614400 | bytes 921604 | tf_op jit(solution)/shard_map/convert_element_type | solution.py:471
  74.3 5.1 %turned.1.old_ref = f32[480,640]{1,0:T(8,128)} custom-call(s32[1]{0:T(128)} %bitcast.position_ref.s_ref.refs_0_, f32[2,640,640]{2,1,0:T(8,128)} %refs_4_.5, f32[2,640,640]{2,1,0:T(8,128)} %refs_5_.3, f32[2,640,640]{2,1,0:T(8,128)} %refs_6_.3), custom_call_target="tpu_custom_call" | custom-call | flops 1228800 | bytes 9830400 | tf_op jit(solution)/shard_map/turned/pallas_call | solution.py:297
  79.4 3.6 %collective-permute-done.5.refs_2_ = bf16[240,640]{1,0:T(8,128)(2,1)S(1)} collective-permute-done((bf16[240,640]{1,0:T(8,128)(2,1)}, bf16[240,640]{1,0:T(8,128)(2,1)S(1)}, u32[]{:S(2)}, u32[]{:S(2)}) %collective-permute-start.5) | collective-permute-done | bytes 307232 | tf_op jit(solution)/shard_map/ppermute | solution.py:436
  83.0 1.7 %collective-permute-done.7.refs_5_ = bf16[240,640]{1,0:T(8,128)(2,1)S(1)} collective-permute-done((bf16[240,640]{1,0:T(8,128)(2,1)}, bf16[240,640]{1,0:T(8,128)(2,1)S(1)}, u32[]{:S(2)}, u32[]{:S(2)}) %collective-permute-start.7) | collective-permute-done | bytes 307232 | tf_op jit(solution)/shard_map/ppermute | solution.py:436
  84.7 0.7 copy-done.9
  85.4 3.2 %renorm.1.rest_0_ = bf16[480,640]{1,0:T(8,128)(2,1)} custom-call(s32[1]{0:T(128)} %bitcast.position_ref.s_ref.refs_0_, f32[480,640]{1,0:T(8,128)} %turned.1.old_ref, bf16[480,640]{1,0:T(8,128)(2,1)} %get-tuple-element.15.refs_0_, bf16[480,640]{1,0:T(8,128)(2,1)} %copy-done.4, bf16[240,640]{1,0:T(8,128)(2,1)} %copy-done.8, ...), custom_call_target="tpu_custom_call" | custom-call | flops 3072000 | bytes 3686400 | tf_op jit(solution)/shard_map/renorm/pallas_call | solution.py:332
  88.6 1.9 %collective-permute-start.11 = (bf16[480,640]{1,0:T(8,128)(2,1)}, bf16[480,640]{1,0:T(8,128)(2,1)S(1)}, u32[]{:S(2)}, u32[]{:S(2)}) collective-permute-start(bf16[480,640]{1,0:T(8,128)(2,1)} %renorm.1.rest_0_), channel_id=1, source_target_pairs={{0,16},{4,20},{8,24},{12,28},{16,0},{20,4},{24,8},{28,12},{1,17},{... | collective-permute-start | bytes 1843208 | tf_op jit(solution)/shard_map/ppermute | solution.py:436
  90.6 0.5 collective-permute-start.9
  91.1 10.1 %collective-permute-done.11.rest_2_ = bf16[480,640]{1,0:T(8,128)(2,1)S(1)} collective-permute-done((bf16[480,640]{1,0:T(8,128)(2,1)}, bf16[480,640]{1,0:T(8,128)(2,1)S(1)}, u32[]{:S(2)}, u32[]{:S(2)}) %collective-permute-start.11) | collective-permute-done | bytes 614432 | tf_op jit(solution)/shard_map/ppermute | solution.py:436
  101.3 2.4 %collective-permute-done.9.rest_1_ = bf16[480,640]{1,0:T(8,128)(2,1)S(1)} collective-permute-done((bf16[480,640]{1,0:T(8,128)(2,1)}, bf16[480,640]{1,0:T(8,128)(2,1)S(1)}, u32[]{:S(2)}, u32[]{:S(2)}) %collective-permute-start.9) | collective-permute-done | bytes 614432 | tf_op jit(solution)/shard_map/ppermute | solution.py:436
  103.7 1.2 collective-permute-start.15
  104.9 15.3 %collective-permute-start.8 = (bf16[480,640]{1,0:T(8,128)(2,1)}, bf16[480,640]{1,0:T(8,128)(2,1)S(1)}, u32[]{:S(2)}, u32[]{:S(2)}) collective-permute-start(bf16[480,640]{1,0:T(8,128)(2,1)} %renorm.1.rest_0_), channel_id=1, source_target_pairs={{0,4},{4,0},{8,12},{12,8},{16,20},{20,16},{24,28},{28,24},{1,5},{5... | collective-permute-start | bytes 1843208 | tf_op jit(solution)/shard_map/ppermute | solution.py:436
  120.2 0.5 collective-permute-start.12
  120.7 2.2 %collective-permute-start.14 = (bf16[240,640]{1,0:T(8,128)(2,1)}, bf16[240,640]{1,0:T(8,128)(2,1)}, u32[]{:S(2)}, u32[]{:S(2)}) collective-permute-start(bf16[240,640]{1,0:T(8,128)(2,1)} %collective-permute-done.13.rest_3_), channel_id=1, source_target_pairs={{0,4},{4,0},{8,12},{12,8},{16,20},{20,16},{24,28},{28,24},{1,5},{5... | collective-permute-start | bytes 921608 | tf_op jit(solution)/shard_map/ppermute | solution.py:436
  123.0 1.6 %collective-permute-start.16 = (bf16[240,640]{1,0:T(8,128)(2,1)}, bf16[240,640]{1,0:T(8,128)(2,1)}, u32[]{:S(2)}, u32[]{:S(2)}) collective-permute-start(bf16[240,640]{1,0:T(8,128)(2,1)} %collective-permute-done.15.rest_4_), channel_id=1, source_target_pairs={{0,4},{4,0},{8,12},{12,8},{16,20},{20,16},{24,28},{28,24},{1,5},{5... | collective-permute-start | bytes 921608 | tf_op jit(solution)/shard_map/ppermute | solution.py:436
  124.5 12.4 %shard_map.100.high_ref = bf16[512,1280]{1,0:T(8,128)(2,1)} custom-call(s32[1]{0:T(128)} %bitcast.position_ref.s_ref.refs_0_, bf16[1024,1280]{1,0:T(8,128)(2,1)} %refs_1_.3, bf16[1024,1280]{1,0:T(8,128)(2,1)} %collective-permute-done.refs_1_.refs_3_, bf16[1024,1280]{1,0:T(8,128)(2,1)} %refs_2_.5, bf16[1024,1280]{1,0:T(8,128)(2,1)} %collective-permute-done.refs_1_.refs_3_, ...), custom_call_target="tpu_custom_call" | custom-call | flops 3355443200 | bytes 10485760 | tf_op jit(solution)/shard_map/pallas_call | solution.py:154
  136.9 8.4 %apply.2.rest_5_ = bf16[1024,1280]{1,0:T(8,128)(2,1)} custom-call(s32[1]{0:T(128)} %bitcast.position_ref.s_ref.refs_0_, bf16[1024,1280]{1,0:T(8,128)(2,1)} %q_ref.3, bf16[512,1280]{1,0:T(8,128)(2,1)} %shard_map.100.high_ref, bf16[512,1280]{1,0:T(8,128)(2,1)} %get-tuple-element.12.own_ref, bf16[512,1408]{1,0:T(8,128)(2,1)} %copy-done, ...), custom_call_target="tpu_custom_call" | custom-call | flops 2516582400 | bytes 6389760 | tf_op jit(solution)/shard_map/apply/pallas_call | solution.py:416
  145.4 0.8 copy-done.7
  146.2 8.4 %apply.3 = bf16[1024,1280]{1,0:T(8,128)(2,1)} custom-call(s32[1]{0:T(128)} %bitcast.position_ref.s_ref.refs_0_, bf16[1024,1280]{1,0:T(8,128)(2,1)} %q_ref.3, bf16[512,1280]{1,0:T(8,128)(2,1)} %shard_map.100.high_ref, bf16[512,1280]{1,0:T(8,128)(2,1)} %get-tuple-element.12.own_ref, bf16[512,1408]{1,0:T(8,128)(2,1)} %copy-done, ...), custom_call_target="tpu_custom_call", output_to_operand_aliasing={{}: (12, {})} | custom-call | flops 2516582400 | bytes 6389760 | tf_op jit(solution)/shard_map/apply/pallas_call | solution.py:416
  (40 shorter events, 0.8 us)
Async XLA Ops:
  0.0 12.1 %copy-start.1 = (bf16[1024,1280]{1,0:T(8,128)(2,1)S(1)}, bf16[1024,1280]{1,0:T(8,128)(2,1)}, u32[]{:S(2)}) copy-start(bf16[1024,1280]{1,0:T(8,128)(2,1)} %refs_1_.3) | copy-start | bytes 7864324
  11.7 9.4 %collective-permute-start.3 = (bf16[1920,640]{1,0:T(8,128)(2,1)}, bf16[1920,640]{1,0:T(8,128)(2,1)}, u32[]{:S(2)}, u32[]{:S(2)}) collective-permute-start(bf16[1920,640]{1,0:T(8,128)(2,1)} %grads.2), channel_id=1, source_target_pairs={{0,4},{4,0},{8,12},{12,8},{16,20},{20,16},{24,28},{28,24},{1,5},{5... | collective-permute-start | bytes 7372808 | tf_op jit(solution)/shard_map/ppermute | solution.py:436
  13.3 1.6 %slice-start = ((bf16[1024,1280]{1,0:T(8,128)(2,1)}), bf16[512,1280]{1,0:T(8,128)(2,1)S(1)}, s32[]{:S(2)}) async-start(bf16[1024,1280]{1,0:T(8,128)(2,1)} %refs_3_.1), calls=%async_computation | async-start | bytes 2621440 | tf_op jit(solution)/shard_map/slice | solution.py:508
  13.3 1.7 %slice-start.1 = ((bf16[1024,1280]{1,0:T(8,128)(2,1)}), bf16[512,1280]{1,0:T(8,128)(2,1)S(1)}, s32[]{:S(2)}) async-start(bf16[1024,1280]{1,0:T(8,128)(2,1)} %refs_2_.5), calls=%async_computation.1 | async-start | bytes 2621440 | tf_op jit(solution)/shard_map/slice | solution.py:508
  13.3 24.1 %collective-permute-start.1 = (bf16[512,1280]{1,0:T(8,128)(2,1)}, bf16[512,1280]{1,0:T(8,128)(2,1)}, u32[]{:S(2)}, u32[]{:S(2)}) collective-permute-start(bf16[512,1280]{1,0:T(8,128)(2,1)} %slice.17), channel_id=1, source_target_pairs={{4,0},{8,4},{12,8},{16,12},{20,16},{24,20},{28,24},{5,1},{9,5},{13... | collective-permute-start | bytes 3932168 | tf_op jit(solution)/shard_map/ppermute | solution.py:441
  16.7 103.5 %collective-permute-start = (bf16[1024,1280]{1,0:T(8,128)(2,1)}, bf16[1024,1280]{1,0:T(8,128)(2,1)}, u32[]{:S(2)}, u32[]{:S(2)}) collective-permute-start(bf16[1024,1280]{1,0:T(8,128)(2,1)} %pad_maximum_fusion), channel_id=1, source_target_pairs={{0,4},{4,8},{8,12},{12,16},{16,20},{20,24},{24,28},{1,5},{5,9},{9,... | collective-permute-start | bytes 7864328 | tf_op jit(solution)/shard_map/ppermute | solution.py:441
  33.5 24.4 %collective-permute-start.4 = (bf16[480,640]{1,0:T(8,128)(2,1)}, bf16[480,640]{1,0:T(8,128)(2,1)S(1)}, u32[]{:S(2)}, u32[]{:S(2)}) collective-permute-start(bf16[480,640]{1,0:T(8,128)(2,1)} %get-tuple-element.16), channel_id=1, source_target_pairs={{0,8},{4,12},{8,0},{12,4},{16,24},{20,28},{24,16},{28,20},{1,9},{5... | collective-permute-start | bytes 1843208 | tf_op jit(solution)/shard_map/ppermute | solution.py:436
  34.7 23.2 %copy-start.2 = (bf16[480,640]{1,0:T(8,128)(2,1)S(1)}, bf16[480,640]{1,0:T(8,128)(2,1)}, u32[]{:S(2)}) copy-start(bf16[480,640]{1,0:T(8,128)(2,1)} %get-tuple-element.15.refs_0_) | copy-start | bytes 1843204
  34.7 37.8 %copy-start.3 = (bf16[480,640]{1,0:T(8,128)(2,1)S(1)}, bf16[480,640]{1,0:T(8,128)(2,1)}, u32[]{:S(2)}) copy-start(bf16[480,640]{1,0:T(8,128)(2,1)} %get-tuple-element.17.refs_3_) | copy-start | bytes 1843204
  34.7 37.8 %collective-permute-start.6 = (bf16[480,640]{1,0:T(8,128)(2,1)}, bf16[480,640]{1,0:T(8,128)(2,1)}, u32[]{:S(2)}, u32[]{:S(2)}) collective-permute-start(bf16[480,640]{1,0:T(8,128)(2,1)} %get-tuple-element.18), channel_id=1, source_target_pairs={{0,16},{4,20},{8,24},{12,28},{16,0},{20,4},{24,8},{28,12},{1,17},{... | collective-permute-start | bytes 1843208 | tf_op jit(solution)/shard_map/ppermute | solution.py:436
  51.1 69.1 %collective-permute-start.2 = (bf16[512,1408]{1,0:T(8,128)(2,1)}, bf16[512,1408]{1,0:T(8,128)(2,1)S(1)}, u32[]{:S(2)}, u32[]{:S(2)}) collective-permute-start(bf16[512,1408]{1,0:T(8,128)(2,1)} %get-tuple-element.13), channel_id=1, source_target_pairs={{0,4},{4,8},{8,12},{12,16},{16,20},{20,24},{24,28},{1,5},{5,9},{9,... | collective-permute-start | bytes 4325384 | tf_op jit(solution)/shard_map/ppermute | solution.py:441
  57.9 21.4 %copy-start.4 = (bf16[480,640]{1,0:T(8,128)(2,1)}, bf16[480,640]{1,0:T(8,128)(2,1)S(1)}, u32[]{:S(2)}) copy-start(bf16[480,640]{1,0:T(8,128)(2,1)S(1)} %collective-permute-done.4.refs_1_) | copy-start | bytes 1843204
  58.9 24.1 %collective-permute-start.5 = (bf16[240,640]{1,0:T(8,128)(2,1)}, bf16[240,640]{1,0:T(8,128)(2,1)S(1)}, u32[]{:S(2)}, u32[]{:S(2)}) collective-permute-start(bf16[240,640]{1,0:T(8,128)(2,1)} %add_convert_fusion.1), channel_id=1, source_target_pairs={{0,16},{4,20},{8,24},{12,28},{16,0},{20,4},{24,8},{28,12},{1,17},{... | collective-permute-start | bytes 921608 | tf_op jit(solution)/shard_map/ppermute | solution.py:436
  74.3 10.4 %collective-permute-start.7 = (bf16[240,640]{1,0:T(8,128)(2,1)}, bf16[240,640]{1,0:T(8,128)(2,1)S(1)}, u32[]{:S(2)}, u32[]{:S(2)}) collective-permute-start(bf16[240,640]{1,0:T(8,128)(2,1)} %add_convert_fusion), channel_id=1, source_target_pairs={{0,8},{4,12},{8,0},{12,4},{16,24},{20,28},{24,16},{28,20},{1,9},{5... | collective-permute-start | bytes 921608 | tf_op jit(solution)/shard_map/ppermute | solution.py:436
  83.0 1.7 %copy-start.8 = (bf16[240,640]{1,0:T(8,128)(2,1)}, bf16[240,640]{1,0:T(8,128)(2,1)S(1)}, u32[]{:S(2)}) copy-start(bf16[240,640]{1,0:T(8,128)(2,1)S(1)} %collective-permute-done.5.refs_2_) | copy-start | bytes 921604
  84.7 0.7 copy-start.9
  88.6 12.6 %collective-permute-start.11 = (bf16[480,640]{1,0:T(8,128)(2,1)}, bf16[480,640]{1,0:T(8,128)(2,1)S(1)}, u32[]{:S(2)}, u32[]{:S(2)}) collective-permute-start(bf16[480,640]{1,0:T(8,128)(2,1)} %renorm.1.rest_0_), channel_id=1, source_target_pairs={{0,16},{4,20},{8,24},{12,28},{16,0},{20,4},{24,8},{28,12},{1,17},{... | collective-permute-start | bytes 1843208 | tf_op jit(solution)/shard_map/ppermute | solution.py:436
  90.6 13.1 %collective-permute-start.9 = (bf16[480,640]{1,0:T(8,128)(2,1)}, bf16[480,640]{1,0:T(8,128)(2,1)S(1)}, u32[]{:S(2)}, u32[]{:S(2)}) collective-permute-start(bf16[480,640]{1,0:T(8,128)(2,1)} %renorm.1.rest_0_), channel_id=1, source_target_pairs={{0,8},{4,12},{8,0},{12,4},{16,24},{20,28},{24,16},{28,20},{1,9},{5... | collective-permute-start | bytes 1843208 | tf_op jit(solution)/shard_map/ppermute | solution.py:436
  101.2 35.8 %copy-start.5 = (bf16[480,640]{1,0:T(8,128)(2,1)}, bf16[480,640]{1,0:T(8,128)(2,1)S(1)}, u32[]{:S(2)}) copy-start(bf16[480,640]{1,0:T(8,128)(2,1)S(1)} %collective-permute-done.11.rest_2_) | copy-start | bytes 1843204
  101.2 19.5 %collective-permute-start.13 = (bf16[240,640]{1,0:T(8,128)(2,1)S(1)}, bf16[240,640]{1,0:T(8,128)(2,1)}, u32[]{:S(2)}, u32[]{:S(2)}) collective-permute-start(bf16[240,640]{1,0:T(8,128)(2,1)S(1)} %slice.20), channel_id=1, source_target_pairs={{0,8},{4,12},{8,0},{12,4},{16,24},{20,28},{24,16},{28,20},{1,9},{5... | collective-permute-start | bytes 921608 | tf_op jit(solution)/shard_map/ppermute | solution.py:436
  103.7 33.2 %copy-start.6 = (bf16[480,640]{1,0:T(8,128)(2,1)}, bf16[480,640]{1,0:T(8,128)(2,1)S(1)}, u32[]{:S(2)}) copy-start(bf16[480,640]{1,0:T(8,128)(2,1)S(1)} %collective-permute-done.9.rest_1_) | copy-start | bytes 1843204
  103.7 19.2 %collective-permute-start.15 = (bf16[240,640]{1,0:T(8,128)(2,1)S(1)}, bf16[240,640]{1,0:T(8,128)(2,1)}, u32[]{:S(2)}, u32[]{:S(2)}) collective-permute-start(bf16[240,640]{1,0:T(8,128)(2,1)S(1)} %slice.21), channel_id=1, source_target_pairs={{0,16},{4,20},{8,24},{12,28},{16,0},{20,4},{24,8},{28,12},{1,17},{... | collective-permute-start | bytes 921608 | tf_op jit(solution)/shard_map/ppermute | solution.py:436
  104.9 40.5 %collective-permute-start.8 = (bf16[480,640]{1,0:T(8,128)(2,1)}, bf16[480,640]{1,0:T(8,128)(2,1)S(1)}, u32[]{:S(2)}, u32[]{:S(2)}) collective-permute-start(bf16[480,640]{1,0:T(8,128)(2,1)} %renorm.1.rest_0_), channel_id=1, source_target_pairs={{0,4},{4,0},{8,12},{12,8},{16,20},{20,16},{24,28},{28,24},{1,5},{5... | collective-permute-start | bytes 1843208 | tf_op jit(solution)/shard_map/ppermute | solution.py:436
  120.2 25.2 %collective-permute-start.10 = (bf16[480,640]{1,0:T(8,128)(2,1)S(1)}, bf16[480,640]{1,0:T(8,128)(2,1)}, u32[]{:S(2)}, u32[]{:S(2)}) collective-permute-start(bf16[480,640]{1,0:T(8,128)(2,1)S(1)} %collective-permute-done.9.rest_1_), channel_id=1, source_target_pairs={{0,4},{4,0},{8,12},{12,8},{16,20},{20,16},{24,28},{28,24},{1,5},{5... | collective-permute-start | bytes 1843208 | tf_op jit(solution)/shard_map/ppermute | solution.py:436
  120.2 16.7 %copy-start = (bf16[512,1408]{1,0:T(8,128)(2,1)}, bf16[512,1408]{1,0:T(8,128)(2,1)S(1)}, u32[]{:S(2)}) copy-start(bf16[512,1408]{1,0:T(8,128)(2,1)S(1)} %collective-permute-done.2.far_ref.far_log) | copy-start | bytes 4325380
  120.2 25.2 %collective-permute-start.12 = (bf16[480,640]{1,0:T(8,128)(2,1)S(1)}, bf16[480,640]{1,0:T(8,128)(2,1)}, u32[]{:S(2)}, u32[]{:S(2)}) collective-permute-start(bf16[480,640]{1,0:T(8,128)(2,1)S(1)} %collective-permute-done.11.rest_2_), channel_id=1, source_target_pairs={{0,4},{4,0},{8,12},{12,8},{16,20},{20,16},{24,28},{28,24},{1,5},{5... | collective-permute-start | bytes 1843208 | tf_op jit(solution)/shard_map/ppermute | solution.py:436
  120.7 24.7 %collective-permute-start.14 = (bf16[240,640]{1,0:T(8,128)(2,1)}, bf16[240,640]{1,0:T(8,128)(2,1)}, u32[]{:S(2)}, u32[]{:S(2)}) collective-permute-start(bf16[240,640]{1,0:T(8,128)(2,1)} %collective-permute-done.13.rest_3_), channel_id=1, source_target_pairs={{0,4},{4,0},{8,12},{12,8},{16,20},{20,16},{24,28},{28,24},{1,5},{5... | collective-permute-start | bytes 921608 | tf_op jit(solution)/shard_map/ppermute | solution.py:436
  123.0 22.4 %collective-permute-start.16 = (bf16[240,640]{1,0:T(8,128)(2,1)}, bf16[240,640]{1,0:T(8,128)(2,1)}, u32[]{:S(2)}, u32[]{:S(2)}) collective-permute-start(bf16[240,640]{1,0:T(8,128)(2,1)} %collective-permute-done.15.rest_4_), channel_id=1, source_target_pairs={{0,4},{4,0},{8,12},{12,8},{16,20},{20,16},{24,28},{28,24},{1,5},{5... | collective-permute-start | bytes 921608 | tf_op jit(solution)/shard_map/ppermute | solution.py:436
  145.4 0.8 copy-start.7
where the time goes:
time: 155 us
  Pallas kernels  75.4 us (49%)
  starting transfers between devices  43.7 us (28%)
  waiting for transfers between devices  28.1 us (18%)
  other arithmetic  4.35 us (3%)
  local copies, waits for them, and re-layouts  2.88 us (2%)
    ppermute x14, starting transfers between devices, exchange(): return lax.ppermute(block, 'seq', [(i, i ^ 1 << bit) for i in range(size)])  31 us
    ppermute x14, waiting for transfers between devices, exchange(): return lax.ppermute(block, 'seq', [(i, i ^ 1 << bit) for i in range(size)])  28.1 us
    pallas_call x2, Pallas kernels, attention(): pl.pallas_call(kernel, grid_spec=pltpu.PrefetchScalarGridSpec(num_scalar_...  26.1 us
    pallas_call x2, Pallas kernels, gradients(): pl.pallas_call(body, grid_spec=pltpu.PrefetchScalarGridSpec(num_scalar_pr...  24.1 us
    pallas_call x2, Pallas kernels, apply_head(): pl.pallas_call(kernel, grid_spec=pltpu.PrefetchScalarGridSpec(num_scalar_...  16.9 us
    ppermute x3, starting transfers between devices, shifted(): lax.ppermute(block, 'seq', [(i, i + by) for i in range(size) if 0 <= i +...  12.7 us
    pallas_call x1, Pallas kernels, turned(): pl.pallas_call(functools.partial(turn_kernel, units=units), grid_spec=plt...  5.05 us
    pallas_call x1, Pallas kernels, renorm_units(): pl.pallas_call(renorm_kernel, grid_spec=pltpu.PrefetchScalarGridSpec(num_...  3.21 us
  transfers between devices with their start and end apart: 17, of which 5 were waited for; matrix products, arithmetic and copies ran while one was open for 4% of the time, Pallas kernels for 36%

commit v1 on v0

--- a/solution.py
+++ b/solution.py
@@ -200,7 +200,6 @@
         cur = nxt
     x = x_ref[...]
     hd = hid[...]
-    quarter = 3 * F // 4
     x1, y1 = (s_ref[0] >> 1) & 1, (s_ref[0] >> 2) & 1
 
     def put(lo, grad):
@@ -208,14 +207,13 @@
             refs[0][lo : lo + grad.shape[0], :] = grad.astype(refs[0].dtype)
             return
         grad = grad + refs[0][lo : lo + grad.shape[0], :].astype(jnp.float32)
-        at = 0
-        while at < grad.shape[0]:
-            block, row = divmod(lo + at, quarter)
-            n = min(grad.shape[0] - at, quarter - row)
-            coordinate = x1 if block < 2 else y1
-            slot = jnp.where(coordinate == block % 2, 0, 1)
-            refs[1 + block // 2][slot, row : row + n, :] = grad[at : at + n].astype(jnp.bfloat16)
-            at += n
+        edges = [0, F // 2, F, 2 * F, 3 * F]
+        for block in range(4):
+            a, b = max(lo, edges[block]), min(lo + grad.shape[0], edges[block + 1])
+            if a < b:
+                slot = jnp.where((x1 if block < 2 else y1) == block % 2, 0, 1)
+                rows_at = slice(a - edges[block], b - edges[block])
+                refs[1 + block // 2][slot, rows_at, :] = grad[a - lo : b - lo].astype(jnp.bfloat16)
 
     for j in range(2 * F // tn):
         put(j * tn, mm(gu[:, j * tn : (j + 1) * tn], x, TN))
@@ -248,10 +246,10 @@
     if received is None:
         shapes = [(3 * F, F)]
     else:
-        shapes = [(3 * F // 4, F)] * 4
+        shapes = [(F // 2, F)] * 2 + [(F, F)] * 2
         args.append(received)
         specs.append(whole(3 * F, F))
-        scratch = [pltpu.VMEM((2, 3 * F // 4, F), bf)] * 2 + scratch
+        scratch = [pltpu.VMEM((2, F // 2, F), bf), pltpu.VMEM((2, F, F), bf)] + scratch
     kernel = functools.partial(grad_kernel, head=head, tm=tm, tn=tn, split=received is not None)
 
     def body(*refs):
@@ -277,31 +275,30 @@
     )(*args)
 
 
-def turn_kernel(s_ref, w1, w3, w2, o_ref, *scratch, units):
+def turn_kernel(s_ref, w1, w3, w2, o_ref, *scratch, parts):
     F = w1.shape[2]
     all_ref = scratch[0] if scratch else o_ref
     all_ref[:F, :] = w1[0].T
     all_ref[F : 2 * F, :] = w3[0].T
     all_ref[2 * F :, :] = w2[0].T
-    if scratch:
-        n = o_ref.shape[0] // len(units)
-        for i, unit in enumerate(units):
-            start = pl.multiple_of(unit(s_ref) * n, 8)
-            o_ref[i * n : (i + 1) * n, :] = all_ref[pl.ds(start, n), :]
-
-
-def turned(position, head, w1, w3, w2, size=None, units=()):
+    at = 0
+    for n, start in parts:
+        o_ref[at : at + n, :] = all_ref[pl.ds(pl.multiple_of(start(s_ref), 8), n), :]
+        at += n
+
+
+def turned(position, head, w1, w3, w2, parts=()):
     F = w1.shape[1]
     weight = pl.BlockSpec((1, F, F), lambda i, s: (head(s), 0, 0))
-    shape = (size * len(units), F) if units else (3 * F, F)
+    shape = (sum(n for n, _ in parts), F) if parts else (3 * F, F)
     return pl.pallas_call(
-        functools.partial(turn_kernel, units=units),
+        functools.partial(turn_kernel, parts=parts),
         grid_spec=pltpu.PrefetchScalarGridSpec(
             num_scalar_prefetch=1,
             grid=(1,),
             in_specs=[weight] * 3,
             out_specs=pl.BlockSpec(shape, lambda i, s: (0, 0)),
-            scratch_shapes=[pltpu.VMEM((3 * F, F), jnp.float32)] if units else [],
+            scratch_shapes=[pltpu.VMEM((3 * F, F), jnp.float32)] if parts else [],
         ),
         out_shape=jax.ShapeDtypeStruct(shape, jnp.float32),
         cost_estimate=pl.CostEstimate(flops=3 * F * F, bytes_accessed=24 * F * F, transcendentals=0),
@@ -318,63 +315,89 @@
 
 def renorm_kernel(s_ref, old_ref, *refs):
     out = refs[-1]
-    n = out.shape[0] // 2
+    at = 0
     for i in range(2):
         a, b, c = (ref[...].astype(jnp.float32) for ref in refs[3 * i : 3 * i + 3])
-        out[i * n : (i + 1) * n, :] = renormed(old_ref[i * n : (i + 1) * n, :], a + b + c)
+        rows = slice(at, at + a.shape[0])
+        out[rows, :] = renormed(old_ref[rows, :], a + b + c)
+        at += a.shape[0]
 
 
 def renorm_units(position, old, upper, lower):
-    unit, F = upper[2][0].shape
-    flat = upper + lower
-    spec = lambda at: pl.BlockSpec((unit, F), lambda i, s: (at(s), 0))
-    whole = pl.BlockSpec((2 * unit, F), lambda i, s: (0, 0))
+    rows, F = old.shape
+    specs = [pl.BlockSpec((rows, F), lambda i, s: (0, 0))]
+    for group in (upper, lower):
+        size = group[2][0].shape[0]
+        specs += [pl.BlockSpec((size, F), lambda i, s, at=at: (at(s), 0)) for _, at in group]
     return pl.pallas_call(
         renorm_kernel,
         grid_spec=pltpu.PrefetchScalarGridSpec(
             num_scalar_prefetch=1,
             grid=(1,),
-            in_specs=[whole] + [spec(at) for _, at in flat],
-            out_specs=whole,
-        ),
-        out_shape=jax.ShapeDtypeStruct((2 * unit, F), jnp.bfloat16),
-        cost_estimate=pl.CostEstimate(flops=20 * unit * F, bytes_accessed=24 * unit * F, transcendentals=0),
+            in_specs=specs,
+            out_specs=pl.BlockSpec((rows, F), lambda i, s: (0, 0)),
+        ),
+        out_shape=jax.ShapeDtypeStruct((rows, F), jnp.bfloat16),
+        cost_estimate=pl.CostEstimate(flops=10 * rows * F, bytes_accessed=12 * rows * F, transcendentals=0),
         name="renorm",
-    )(position, old, *[array for array, _ in flat])
-
-
-def apply_kernel(s_ref, q_ref, high_ref, own_ref, far_ref, own_log, far_log, *rest, head, tm, places, unit, pieces, stride):
+    )(position, old, *[array for array, _ in upper + lower])
+
+
+def merge_kernel(s_ref, own_ref, far_ref, own_log, far_log, o_ref, *, stride):
+    lane = lax.broadcasted_iota(jnp.int32, own_log.shape, 1)
+    heads = o_ref.shape[1] // HD
+    for j in range(heads):
+        cs = slice(j * HD, (j + 1) * HD)
+        at = pl.program_id(0) * heads + j
+        pick = lambda ref, of: jnp.sum(
+            jnp.where(of, ref[...].astype(jnp.float32), 0.0), axis=1, keepdims=True
+        )
+        own = pick(own_log, lane == at)
+        far = pick(far_log, (lane == at) | (lane == at + stride) | (lane == at + 2 * stride))
+        far = jnp.where(s_ref[0] == 0, -jnp.inf, far)
+        top = jnp.maximum(own, far)
+        own, far = jnp.exp2(own - top), jnp.exp2(far - top)
+        share = own / (own + far)
+        a, b = own_ref[:, cs].astype(jnp.float32), far_ref[:, cs].astype(jnp.float32)
+        o_ref[:, cs] = (a * share + b * (1.0 - share)).astype(o_ref.dtype)
+
+
+def merged(position, own, far, own_log, width):
+    rows, cols = own.shape
+    w = width * HD
+    col = pl.BlockSpec((rows, w), lambda g, s: (0, g))
+    log = lambda at: pl.BlockSpec((rows, HD), lambda g, s: (0, at))
+    return pl.pallas_call(
+        functools.partial(merge_kernel, stride=log_stride_of(cols)),
+        grid_spec=pltpu.PrefetchScalarGridSpec(
+            num_scalar_prefetch=1,
+            grid=(cols // w,),
+            in_specs=[col, col, log(0), log(cols // HD)],
+            out_specs=col,
+        ),
+        out_shape=jax.ShapeDtypeStruct((rows, cols), jnp.bfloat16),
+        cost_estimate=pl.CostEstimate(
+            flops=8 * rows * cols, bytes_accessed=6 * rows * cols, transcendentals=rows * cols // HD
+        ),
+        name="merge",
+    )(position, own, far, own_log, far)
+
+
+def apply_kernel(s_ref, q_ref, high_ref, low_ref, *rest, tm, parts):
     n_ref, a_ref, o_ref = rest[-2], rest[-1], rest[-3]
     F = n_ref.shape[1]
     step = pl.program_id(0)
 
     @pl.when(step == 0)
     def _():
-        slot = 0
-        for ref in rest[:pieces]:
-            for r in range(ref.shape[0] // unit):
-                to = pl.multiple_of(places[slot](s_ref) * unit, min(unit, 16))
-                n_ref[pl.ds(to, unit), :] = ref[r * unit : (r + 1) * unit, :]
-                slot += 1
-        lane = lax.broadcasted_iota(jnp.int32, own_log.shape, 1)
-        for j in range(F // HD):
-            cs = slice(j * HD, (j + 1) * HD)
-            at = head(s_ref) * (F // HD) + j
-            pick = lambda ref, of: jnp.sum(
-                jnp.where(of, ref[...].astype(jnp.float32), 0.0), axis=1, keepdims=True
-            )
-            own = pick(own_log, lane == at)
-            far = pick(far_log, (lane == at) | (lane == at + stride) | (lane == at + 2 * stride))
-            far = jnp.where(s_ref[0] == 0, -jnp.inf, far)
-            top = jnp.maximum(own, far)
-            own, far = jnp.exp2(own - top), jnp.exp2(far - top)
-            share = own / (own + far)
-            a, b = own_ref[:, cs].astype(jnp.float32), far_ref[:, cs].astype(jnp.float32)
-            a_ref[:, cs] = a * share + b * (1.0 - share)
+        for piece, row, n, start in parts:
+            to = pl.multiple_of(start(s_ref), 16)
+            n_ref[pl.ds(to, n), :] = rest[piece][row : row + n, :]
+        a_ref[...] = low_ref[...]
 
     @pl.when(step == 1)
     def _():
-        a_ref[...] = high_ref[...].astype(jnp.float32)
+        a_ref[...] = high_ref[...]
 
     n = q_ref.shape[0] // tm
 
@@ -385,7 +408,7 @@
         g = h[:, :F]
         hid = (g * jax.nn.sigmoid(g) * h[:, F:]).astype(jnp.bfloat16)
         r = slice(i * tm, (i + 1) * tm)
-        o_ref[r, :] = (a_ref[r, :] + mm(hid, n_ref[2 * F :, :], NT)).astype(o_ref.dtype)
+        o_ref[r, :] = (a_ref[r, :].astype(jnp.float32) + mm(hid, n_ref[2 * F :, :], NT)).astype(o_ref.dtype)
 
     cur = first(0)
     for i in range(n):
@@ -394,33 +417,28 @@
         cur = nxt
 
 
-def apply_head(position, head, fq, pieces, places, unit, attended, into=None):
+def apply_head(position, head, fq, pieces, parts, high, low, into=None):
     rows, cols = fq.shape
     F = pieces[0].shape[1]
     half = rows // 2
     col = pl.BlockSpec((half, F), lambda i, s: (i, head(s)))
     part = pl.BlockSpec((half, F), lambda i, s: (0, head(s)))
     whole = lambda a: pl.BlockSpec(a.shape, lambda i, s: (0, 0))
-    high, own, far, own_log = attended
-    far_log = pl.BlockSpec((half, HD), lambda i, s: (0, cols // HD))
-    args = [position, fq, high, own, far, own_log, far, *pieces]
-    specs = [col, part, part, part, whole(own_log), far_log] + [whole(p) for p in pieces]
+    args = [position, fq, high, low, *pieces]
+    specs = [col, part, part] + [whole(p) for p in pieces]
     aliases = {}
     if into is not None:
         aliases = {len(args): 0}
         args.append(into)
         specs.append(pl.BlockSpec(memory_space=pl.ANY))
-    kernel = functools.partial(
-        apply_kernel, head=head, tm=min(256, half), places=places, unit=unit, pieces=len(pieces), stride=log_stride_of(cols)
-    )
     return pl.pallas_call(
-        kernel,
+        functools.partial(apply_kernel, tm=min(256, half), parts=parts),
         grid_spec=pltpu.PrefetchScalarGridSpec(
             num_scalar_prefetch=1,
             grid=(2,),
             in_specs=specs,
             out_specs=col,
-            scratch_shapes=[pltpu.VMEM((3 * F, F), jnp.bfloat16), pltpu.VMEM((half, F), jnp.float32)],
+            scratch_shapes=[pltpu.VMEM((3 * F, F), jnp.bfloat16), pltpu.VMEM((half, F), jnp.bfloat16)],
         ),
         out_shape=jax.ShapeDtypeStruct((rows, cols), jnp.bfloat16),
         input_output_aliases=aliases,
@@ -460,14 +478,14 @@
     return part
 
 
-def synced_square(position, quarters, old):
+def synced_square(position, blocks, old):
     x, y = (position[0] >> 1) & 1, (position[0] >> 2) & 1
-    keep_x, send_x, keep_y, send_y = quarters
-    unit = keep_x.shape[0] // 2
+    keep_x, send_x, keep_y, send_y = blocks
     top0, bottom0 = exchange(send_x, 1), exchange(send_y, 2)
 
     def fold(a, b, at):
-        a, b = (lax.dynamic_slice_in_dim(v, at * unit, unit, 0).astype(jnp.float32) for v in (a, b))
+        n = a.shape[0] // 2
+        a, b = (lax.dynamic_slice_in_dim(v, at * n, n, 0).astype(jnp.float32) for v in (a, b))
         return (a + b).astype(jnp.bfloat16)
 
     top1 = exchange(fold(keep_x, top0, 1 - y), 2)
@@ -479,9 +497,10 @@
         [(keep_x, at_y), (top0, at_y), (top1, zero)],
         [(keep_y, at_x), (bottom0, at_x), (bottom1, zero)],
     )
+    n = top1.shape[0]
     over_x, over_y = exchange(part, 1), exchange(part, 2)
-    top2, bottom2 = exchange(over_y[:unit], 1), exchange(over_x[unit:], 2)
-    return [part, over_x, over_y, top2, bottom2], unit
+    top2, bottom2 = exchange(over_y[:n], 1), exchange(over_x[n:], 2)
+    return [part, over_x, over_y, top2, bottom2]
 
 
 def at_x(s):
@@ -492,10 +511,10 @@
     return (s[0] >> 2) & 1
 
 
-def place(flip_x, flip_y):
+def place(F, flip_x, flip_y):
     x = lambda s: at_x(s) ^ flip_x
     y = lambda s: at_y(s) ^ flip_y
-    return [lambda s: 2 * x(s) + y(s), lambda s: 4 + 2 * y(s) + x(s)]
+    return lambda s: (2 * x(s) + y(s)) * (F // 4), lambda s: F + (2 * y(s) + x(s)) * (F // 2)
 
 
 def shards(attn_q, attn_k, attn_v, fast_q, fast_k, fast_v, rates, fast_gate, fast_up, fast_down):
@@ -516,13 +535,20 @@
     if heads == 2 and count == 8:
         near, far = (lambda s: s[0] & 1), (lambda s: 1 - (s[0] & 1))
         received = exchange(grads(far)[0], 0)
-        old = turned(position, near, *weights, size=3 * fast_gate.shape[1] // 8, units=tuple(place(0, 0)))
-        quarters = grads(near, received)
-        pieces, unit = synced_square(position, quarters, old)
+        F = fast_gate.shape[1]
+        n, m = F // 4, F // 2
+        upper, lower = place(F, 0, 0)
+        old = turned(position, near, *weights, parts=((n, upper), (m, lower)))
+        blocks = grads(near, received)
+        pieces = synced_square(position, blocks, old)
         other = [exchange(p, 0) for p in pieces]
-        places = place(0, 0) + place(1, 0) + place(0, 1)
-        places += [place(1, 1)[0], place(1, 1)[1]]
-        news = [(near, pieces, places, unit), (far, other, places, unit)]
+        parts = []
+        for piece, (flip_x, flip_y) in enumerate([(0, 0), (1, 0), (0, 1)]):
+            upper, lower = place(F, flip_x, flip_y)
+            parts += [(piece, 0, n, upper), (piece, n, m, lower)]
+        upper, lower = place(F, 1, 1)
+        parts += [(3, 0, n, upper), (4, 0, m, lower)]
+        news = [(near, pieces, parts), (far, other, parts)]
     else:
         news = []
         bits = list(range(count.bit_length() - 1))
@@ -530,7 +556,7 @@
             head = lambda s, h=h: h
             old = turned(position, head, *weights)
             new = synced(grads(head)[0].astype(jnp.float32), old, bits, position[0])
-            news.append((head, [new], [lambda s: 0], new.shape[0]))
+            news.append((head, [new], [(0, 0, new.shape[0], lambda s: 0)]))
     bq = min(256, half)
     tiles = half // bq
     late = [
@@ -542,10 +568,10 @@
     returned, own_out, own_log = attention(position, [(guests, 0, guest, 2), (attn_q, 0, early, 1)], [here], bq, width)
     far_out = shifted(returned, 1)
     (high,) = attention(position, [(attn_q, 1, late, 0)], [(prev, 0, prev, 1, half), here], bq, width)
-    attended = (high, own_out, far_out, own_log)
+    low = merged(position, own_out, far_out, own_log, width)
     mixed = None
-    for head, pieces, places, unit in news:
-        mixed = apply_head(position, head, fast_q, pieces, places, unit, attended, mixed)
+    for head, pieces, parts in news:
+        mixed = apply_head(position, head, fast_q, pieces, parts, high, low, mixed)
     return mixed
 
 

time: 155 us -> 169 us (1.090)
  waiting for transfers between devices: 28.1 us -> 54.1 us
  starting transfers between devices: 43.7 us -> 27.1 us
  Pallas kernels: 75.4 us -> 79 us
    ppermute x14, waiting for transfers between devices: 28.1 us -> 54.1 us  [exchange(): return lax.ppermute(block, 'seq', [(i, i ^ 1 << bit) for i in range(size)])]
    ppermute x14, starting transfers between devices: 31 us -> 15 us  [exchange(): return lax.ppermute(block, 'seq', [(i, i ^ 1 << bit) for i in range(size)])]
    pallas_call x3 -> x4, Pallas kernels: 21.9 us -> 25 us  [the longest x2 14.1 us: apply_head(): pl.pallas_call(functools.partial(apply_kernel, tm=min(256, half), parts=p...]
where the time goes in v1:
time: 169 us
  Pallas kernels  79 us (47%)
  waiting for transfers between devices  54.1 us (32%)
  starting transfers between devices  27.1 us (16%)
  other arithmetic  4.59 us (3%)
  local copies, waits for them, and re-layouts  3.98 us (2%)
    ppermute x14, waiting for transfers between devices, exchange(): return lax.ppermute(block, 'seq', [(i, i ^ 1 << bit) for i in range(size)])  54.1 us
    pallas_call x2, Pallas kernels, attention(): pl.pallas_call(kernel, grid_spec=pltpu.PrefetchScalarGridSpec(num_scalar_...  26.2 us
    pallas_call x2, Pallas kernels, gradients(): pl.pallas_call(body, grid_spec=pltpu.PrefetchScalarGridSpec(num_scalar_pr...  24.5 us
    ppermute x14, starting transfers between devices, exchange(): return lax.ppermute(block, 'seq', [(i, i ^ 1 << bit) for i in range(size)])  15 us
    pallas_call x2, Pallas kernels, apply_head(): pl.pallas_call(functools.partial(apply_kernel, tm=min(256, half), parts=p...  14.1 us
    ppermute x3, starting transfers between devices, shifted(): lax.ppermute(block, 'seq', [(i, i + by) for i in range(size) if 0 <= i +...  12.2 us
    pallas_call x1, Pallas kernels, merged(): pl.pallas_call(functools.partial(merge_kernel, stride=log_stride_of(cols)...  5.76 us
    pallas_call x1, Pallas kernels, turned(): pl.pallas_call(functools.partial(turn_kernel, parts=parts), grid_spec=plt...  5.14 us
  transfers between devices with their start and end apart: 17, of which 5 were waited for; matrix products, arithmetic and copies ran while one was open for 4% of the time, Pallas kernels for 36%

profile of v1, /device:TPU:0, one launch (start us, length us, event | category | flops | bytes accessed | tf_op | source)
XLA Modules:
  0.0 169.0 jit_solution(5226325645147458154)
XLA Ops:
  0.0 11.7 %grads.2 = bf16[1920,640]{1,0:T(8,128)(2,1)} custom-call(s32[1]{0:T(128)} %bitcast.position_ref.s_ref.refs_0_, bf16[1024,1280]{1,0:T(8,128)(2,1)} %refs_1_.5, bf16[1024,1280]{1,0:T(8,128)(2,1)} %refs_2_.7, f32[2,1024]{1,0:T(2,128)} %bitcast.2, f32[2,640,640]{2,1,0:T(8,128)} %refs_4_.5, f32[2,640,640]{2,1,0:T(8,128)} %refs_5_.3, f32[2,640,640]{2,1,0:T(8,128)} %refs_6_.3), custom_call_target="tpu_custom_call" | custom-call | flops 5033164800 | bytes 9994240 | tf_op jit(solution)/shard_map/grads/pallas_call | solution.py:261
  11.7 0.5 collective-permute-start.3
  12.2 1.2 slice.17
  13.4 1.5 collective-permute-start.1
  15.1 1.7 pad_maximum_fusion
  16.8 3.2 %collective-permute-start = (bf16[1024,1280]{1,0:T(8,128)(2,1)}, bf16[1024,1280]{1,0:T(8,128)(2,1)S(1)}, u32[]{:S(2)}, u32[]{:S(2)}) collective-permute-start(bf16[1024,1280]{1,0:T(8,128)(2,1)} %pad_maximum_fusion), channel_id=1, source_target_pairs={{0,4},{4,8},{8,12},{12,16},{16,20},{20,24},{24,28},{1,5},{5,9},{9,... | collective-permute-start | bytes 7864328 | tf_op jit(solution)/shard_map/ppermute | solution.py:459
  20.0 12.8 %grads.3 = (bf16[320,640]{1,0:T(8,128)(2,1)}, bf16[320,640]{1,0:T(8,128)(2,1)}, bf16[640,640]{1,0:T(8,128)(2,1)}, bf16[640,640]{1,0:T(8,128)(2,1)}) custom-call(s32[1]{0:T(128)} %bitcast.position_ref.s_ref.refs_0_, bf16[1024,1280]{1,0:T(8,128)(2,1)} %refs_1_.5, bf16[1024,1280]{1,0:T(8,128)(2,1)} %refs_2_.7, f32[2,1024]{1,0:T(2,128)} %bitcast.3, ...), custom_call_target="tpu_custom_call" | custom-call | flops 5033164800 | bytes 9994240 | tf_op jit(solution)/shard_map/grads/pallas_call | solution.py:261
  32.8 3.4 %collective-permute-start.6 = (bf16[640,640]{1,0:T(8,128)(2,1)}, bf16[640,640]{1,0:T(8,128)(2,1)}, u32[]{:S(2)}, u32[]{:S(2)}) collective-permute-start(bf16[640,640]{1,0:T(8,128)(2,1)} %get-tuple-element.18), channel_id=1, source_target_pairs={{0,16},{4,20},{8,24},{12,28},{16,0},{20,4},{24,8},{28,12},{1,17},{... | collective-permute-start | bytes 2457608 | tf_op jit(solution)/shard_map/ppermute | solution.py:454
  36.2 1.5 collective-permute-start.4
  37.7 13.8 %shard_map.101 = (bf16[512,1408]{1,0:T(8,128)(2,1)}, bf16[512,1280]{1,0:T(8,128)(2,1)}, f32[512,128]{1,0:T(8,128)}) custom-call(s32[1]{0:T(128)} %bitcast.position_ref.s_ref.refs_0_, bf16[512,1280]{1,0:T(8,128)(2,1)} %collective-permute-done.1.refs_0_, bf16[1024,1280]{1,0:T(8,128)(2,1)} %refs_1_.3, bf16[1024,1280]{1,0:T(8,128)(2,1)} %refs_2_.5, ...), custom_call_target="tpu_custom_call" | custom-call | flops 3355443200 | bytes 10485760 | tf_op jit(solution)/shard_map/pallas_call | solution.py:154
  51.5 7.4 %collective-permute-start.2 = (bf16[512,1408]{1,0:T(8,128)(2,1)}, bf16[512,1408]{1,0:T(8,128)(2,1)}, u32[]{:S(2)}, u32[]{:S(2)}) collective-permute-start(bf16[512,1408]{1,0:T(8,128)(2,1)} %get-tuple-element.13), channel_id=1, source_target_pairs={{0,4},{4,8},{8,12},{12,16},{16,20},{20,24},{24,28},{1,5},{5,9},{9,... | collective-permute-start | bytes 4325384 | tf_op jit(solution)/shard_map/ppermute | solution.py:459
  58.8 33.3 %collective-permute-done.6.refs_4_ = bf16[640,640]{1,0:T(8,128)(2,1)} collective-permute-done((bf16[640,640]{1,0:T(8,128)(2,1)}, bf16[640,640]{1,0:T(8,128)(2,1)}, u32[]{:S(2)}, u32[]{:S(2)}) %collective-permute-start.6) | collective-permute-done | bytes 819232 | tf_op jit(solution)/shard_map/ppermute | solution.py:454
  92.2 1.8 %add_convert_fusion = bf16[320,640]{1,0:T(8,128)(2,1)} fusion(bf16[640,640]{1,0:T(8,128)(2,1)} %collective-permute-done.6.refs_4_, s32[]{:T(128)S(6)} %select_n.9, bf16[640,640]{1,0:T(8,128)(2,1)S(1)} %copy-done.2), kind=kLoop, calls=%fused_computation.1 | loop fusion | flops 819200 | bytes 1228804 | tf_op jit(solution)/shard_map/convert_element_type | solution.py:489
  94.0 1.1 add_convert_fusion.1
  95.1 2.5 %collective-permute-start.5 = (bf16[160,640]{1,0:T(8,128)(2,1)S(1)}, bf16[160,640]{1,0:T(8,128)(2,1)S(1)}, u32[]{:S(2)}, u32[]{:S(2)}) collective-permute-start(bf16[160,640]{1,0:T(8,128)(2,1)S(1)} %add_convert_fusion.1), channel_id=1, source_target_pairs={{0,16},{4,20},{8,24},{12,28},{16,0},{20,4},{24,8},{28,12},{1,17},{... | collective-permute-start | bytes 614408 | tf_op jit(solution)/shard_map/ppermute | solution.py:454
  97.7 5.1 %turned.1.old_ref = f32[480,640]{1,0:T(8,128)} custom-call(s32[1]{0:T(128)} %bitcast.position_ref.s_ref.refs_0_, f32[2,640,640]{2,1,0:T(8,128)} %refs_4_.5, f32[2,640,640]{2,1,0:T(8,128)} %refs_5_.3, f32[2,640,640]{2,1,0:T(8,128)} %refs_6_.3), custom_call_target="tpu_custom_call" | custom-call | flops 1228800 | bytes 9830400 | tf_op jit(solution)/shard_map/turned/pallas_call | solution.py:294
  102.9 2.7 %collective-permute-done.7.refs_5_ = bf16[320,640]{1,0:T(8,128)(2,1)S(1)} collective-permute-done((bf16[320,640]{1,0:T(8,128)(2,1)}, bf16[320,640]{1,0:T(8,128)(2,1)S(1)}, u32[]{:S(2)}, u32[]{:S(2)}) %collective-permute-start.7) | collective-permute-done | bytes 409632 | tf_op jit(solution)/shard_map/ppermute | solution.py:454
  105.6 0.7 copy-done.4
  106.3 3.3 %renorm.1.rest_0_ = bf16[480,640]{1,0:T(8,128)(2,1)} custom-call(s32[1]{0:T(128)} %bitcast.position_ref.s_ref.refs_0_, f32[480,640]{1,0:T(8,128)} %turned.1.old_ref, bf16[320,640]{1,0:T(8,128)(2,1)} %get-tuple-element.15.refs_0_, bf16[320,640]{1,0:T(8,128)(2,1)} %collective-permute-done.4.refs_1_, bf16[160,640]{1,0:T(8,128)(2,1)} %copy-done.6, ...), custom_call_target="tpu_custom_call" | custom-call | flops 3072000 | bytes 3686400 | tf_op jit(solution)/shard_map/renorm/pallas_call | solution.py:332
  109.9 2.5 %collective-permute-start.11 = (bf16[480,640]{1,0:T(8,128)(2,1)}, bf16[480,640]{1,0:T(8,128)(2,1)}, u32[]{:S(2)}, u32[]{:S(2)}) collective-permute-start(bf16[480,640]{1,0:T(8,128)(2,1)} %renorm.1.rest_0_), channel_id=1, source_target_pairs={{0,16},{4,20},{8,24},{12,28},{16,0},{20,4},{24,8},{28,12},{1,17},{... | collective-permute-start | bytes 1843208 | tf_op jit(solution)/shard_map/ppermute | solution.py:454
  112.4 12.3 %collective-permute-done.9.rest_1_ = bf16[480,640]{1,0:T(8,128)(2,1)S(1)} collective-permute-done((bf16[480,640]{1,0:T(8,128)(2,1)}, bf16[480,640]{1,0:T(8,128)(2,1)S(1)}, u32[]{:S(2)}, u32[]{:S(2)}) %collective-permute-start.9) | collective-permute-done | bytes 614432 | tf_op jit(solution)/shard_map/ppermute | solution.py:454
  124.8 2.5 %collective-permute-start.15 = (bf16[320,640]{1,0:T(8,128)(2,1)S(1)}, bf16[320,640]{1,0:T(8,128)(2,1)}, u32[]{:S(2)}, u32[]{:S(2)}) collective-permute-start(bf16[320,640]{1,0:T(8,128)(2,1)S(1)} %slice.21), channel_id=1, source_target_pairs={{0,16},{4,20},{8,24},{12,28},{16,0},{20,4},{24,8},{28,12},{1,17},{... | collective-permute-start | bytes 1228808 | tf_op jit(solution)/shard_map/ppermute | solution.py:454
  127.3 0.5 collective-permute-start.10
  127.9 1.2 slice.20
  129.1 0.6 collective-permute-start.13
  129.8 5.7 %collective-permute-done.15.rest_4_ = bf16[320,640]{1,0:T(8,128)(2,1)} collective-permute-done((bf16[320,640]{1,0:T(8,128)(2,1)S(1)}, bf16[320,640]{1,0:T(8,128)(2,1)}, u32[]{:S(2)}, u32[]{:S(2)}) %collective-permute-start.15) | collective-permute-done | bytes 409632 | tf_op jit(solution)/shard_map/ppermute | solution.py:454
  135.4 12.4 %shard_map.100.high_ref = bf16[512,1280]{1,0:T(8,128)(2,1)} custom-call(s32[1]{0:T(128)} %bitcast.position_ref.s_ref.refs_0_, bf16[1024,1280]{1,0:T(8,128)(2,1)} %refs_1_.3, bf16[1024,1280]{1,0:T(8,128)(2,1)} %copy-done, bf16[1024,1280]{1,0:T(8,128)(2,1)} %refs_2_.5, bf16[1024,1280]{1,0:T(8,128)(2,1)} %copy-done, bf16[1024,1280]{1,0:T(8,128)(2,1)} %refs_3_.1), custom_call_target="tpu_custom_call" | custom-call | flops 3355443200 | bytes 10485760 | tf_op jit(solution)/shard_map/pallas_call | solution.py:154
  147.9 5.8 %merge.1.low_ref = bf16[512,1280]{1,0:T(8,128)(2,1)} custom-call(s32[1]{0:T(128)} %bitcast.position_ref.s_ref.refs_0_, bf16[512,1280]{1,0:T(8,128)(2,1)} %get-tuple-element.12.own_ref, bf16[512,1408]{1,0:T(8,128)(2,1)} %collective-permute-done.2.far_ref.far_log, f32[512,128]{1,0:T(8,128)} %get-tuple-element.14.own_log, ...), custom_call_target="tpu_custom_call" | custom-call | flops 5242880 | bytes 3932160 | tf_op jit(solution)/shard_map/merge/pallas_call | solution.py:370
  153.6 0.5 collective-permute-start.14
  154.1 7.1 %apply.2.rest_5_ = bf16[1024,1280]{1,0:T(8,128)(2,1)} custom-call(s32[1]{0:T(128)} %bitcast.position_ref.s_ref.refs_0_, bf16[1024,1280]{1,0:T(8,128)(2,1)} %q_ref.3, bf16[512,1280]{1,0:T(8,128)(2,1)} %shard_map.100.high_ref, bf16[512,1280]{1,0:T(8,128)(2,1)} %merge.1.low_ref, bf16[480,640]{1,0:T(8,128)(2,1)} %renorm.1.rest_0_, bf16[480,640]{1,0:T(8,128)(2,1)} %copy-done.3, ...), custom_call_target="tpu_custom_call" | custom-call | flops 2516582400 | bytes 6389760 | tf_op jit(solution)/shard_map/apply/pallas_call | solution.py:434
  161.2 0.7 copy-done.5
  161.9 7.1 %apply.3 = bf16[1024,1280]{1,0:T(8,128)(2,1)} custom-call(s32[1]{0:T(128)} %bitcast.position_ref.s_ref.refs_0_, bf16[1024,1280]{1,0:T(8,128)(2,1)} %q_ref.3, bf16[512,1280]{1,0:T(8,128)(2,1)} %shard_map.100.high_ref, bf16[512,1280]{1,0:T(8,128)(2,1)} %merge.1.low_ref, ...), custom_call_target="tpu_custom_call", output_to_operand_aliasing={{}: (9, {})} | custom-call | flops 2516582400 | bytes 6389760 | tf_op jit(solution)/shard_map/apply/pallas_call | solution.py:434
  (35 shorter events, 0.7 us)
Async XLA Ops:
  0.0 12.2 %copy-start.1 = (bf16[1024,1280]{1,0:T(8,128)(2,1)S(1)}, bf16[1024,1280]{1,0:T(8,128)(2,1)}, u32[]{:S(2)}) copy-start(bf16[1024,1280]{1,0:T(8,128)(2,1)} %refs_1_.3) | copy-start | bytes 7864324
  11.7 8.3 %collective-permute-start.3 = (bf16[1920,640]{1,0:T(8,128)(2,1)}, bf16[1920,640]{1,0:T(8,128)(2,1)}, u32[]{:S(2)}, u32[]{:S(2)}) collective-permute-start(bf16[1920,640]{1,0:T(8,128)(2,1)} %grads.2), channel_id=1, source_target_pairs={{0,4},{4,0},{8,12},{12,8},{16,20},{20,16},{24,28},{28,24},{1,5},{5... | collective-permute-start | bytes 7372808 | tf_op jit(solution)/shard_map/ppermute | solution.py:454
  13.4 1.6 slice-start
  13.4 1.7 %slice-start.1 = ((bf16[1024,1280]{1,0:T(8,128)(2,1)}), bf16[512,1280]{1,0:T(8,128)(2,1)S(1)}, s32[]{:S(2)}) async-start(bf16[1024,1280]{1,0:T(8,128)(2,1)} %refs_2_.5), calls=%async_computation.1 | async-start | bytes 2621440 | tf_op jit(solution)/shard_map/slice | solution.py:527
  13.4 24.3 %collective-permute-start.1 = (bf16[512,1280]{1,0:T(8,128)(2,1)}, bf16[512,1280]{1,0:T(8,128)(2,1)}, u32[]{:S(2)}, u32[]{:S(2)}) collective-permute-start(bf16[512,1280]{1,0:T(8,128)(2,1)} %slice.17), channel_id=1, source_target_pairs={{4,0},{8,4},{12,8},{16,12},{20,16},{24,20},{28,24},{5,1},{9,5},{13... | collective-permute-start | bytes 3932168 | tf_op jit(solution)/shard_map/ppermute | solution.py:459
  16.8 110.6 %collective-permute-start = (bf16[1024,1280]{1,0:T(8,128)(2,1)}, bf16[1024,1280]{1,0:T(8,128)(2,1)S(1)}, u32[]{:S(2)}, u32[]{:S(2)}) collective-permute-start(bf16[1024,1280]{1,0:T(8,128)(2,1)} %pad_maximum_fusion), channel_id=1, source_target_pairs={{0,4},{4,8},{8,12},{12,16},{16,20},{20,24},{24,28},{1,5},{5,9},{9,... | collective-permute-start | bytes 7864328 | tf_op jit(solution)/shard_map/ppermute | solution.py:459
  32.8 59.4 %collective-permute-start.6 = (bf16[640,640]{1,0:T(8,128)(2,1)}, bf16[640,640]{1,0:T(8,128)(2,1)}, u32[]{:S(2)}, u32[]{:S(2)}) collective-permute-start(bf16[640,640]{1,0:T(8,128)(2,1)} %get-tuple-element.18), channel_id=1, source_target_pairs={{0,16},{4,20},{8,24},{12,28},{16,0},{20,4},{24,8},{28,12},{1,17},{... | collective-permute-start | bytes 2457608 | tf_op jit(solution)/shard_map/ppermute | solution.py:454
  36.2 56.0 %copy-start.2 = (bf16[640,640]{1,0:T(8,128)(2,1)S(1)}, bf16[640,640]{1,0:T(8,128)(2,1)}, u32[]{:S(2)}) copy-start(bf16[640,640]{1,0:T(8,128)(2,1)} %get-tuple-element.17.refs_3_) | copy-start | bytes 2457604
  36.2 57.9 %collective-permute-start.4 = (bf16[320,640]{1,0:T(8,128)(2,1)}, bf16[320,640]{1,0:T(8,128)(2,1)}, u32[]{:S(2)}, u32[]{:S(2)}) collective-permute-start(bf16[320,640]{1,0:T(8,128)(2,1)} %get-tuple-element.16), channel_id=1, source_target_pairs={{0,8},{4,12},{8,0},{12,4},{16,24},{20,28},{24,16},{28,20},{1,9},{5... | collective-permute-start | bytes 1228808 | tf_op jit(solution)/shard_map/ppermute | solution.py:454
  51.5 77.7 %collective-permute-start.2 = (bf16[512,1408]{1,0:T(8,128)(2,1)}, bf16[512,1408]{1,0:T(8,128)(2,1)}, u32[]{:S(2)}, u32[]{:S(2)}) collective-permute-start(bf16[512,1408]{1,0:T(8,128)(2,1)} %get-tuple-element.13), channel_id=1, source_target_pairs={{0,4},{4,8},{8,12},{12,16},{16,20},{20,24},{24,28},{1,5},{5,9},{9,... | collective-permute-start | bytes 4325384 | tf_op jit(solution)/shard_map/ppermute | solution.py:459
  94.0 11.6 %collective-permute-start.7 = (bf16[320,640]{1,0:T(8,128)(2,1)}, bf16[320,640]{1,0:T(8,128)(2,1)S(1)}, u32[]{:S(2)}, u32[]{:S(2)}) collective-permute-start(bf16[320,640]{1,0:T(8,128)(2,1)} %add_convert_fusion), channel_id=1, source_target_pairs={{0,8},{4,12},{8,0},{12,4},{16,24},{20,28},{24,16},{28,20},{1,9},{5... | collective-permute-start | bytes 1228808 | tf_op jit(solution)/shard_map/ppermute | solution.py:454
  95.1 7.8 %collective-permute-start.5 = (bf16[160,640]{1,0:T(8,128)(2,1)S(1)}, bf16[160,640]{1,0:T(8,128)(2,1)S(1)}, u32[]{:S(2)}, u32[]{:S(2)}) collective-permute-start(bf16[160,640]{1,0:T(8,128)(2,1)S(1)} %add_convert_fusion.1), channel_id=1, source_target_pairs={{0,16},{4,20},{8,24},{12,28},{16,0},{20,4},{24,8},{28,12},{1,17},{... | collective-permute-start | bytes 614408 | tf_op jit(solution)/shard_map/ppermute | solution.py:454
  102.9 2.7 %copy-start.6 = (bf16[160,640]{1,0:T(8,128)(2,1)}, bf16[160,640]{1,0:T(8,128)(2,1)S(1)}, u32[]{:S(2)}) copy-start(bf16[160,640]{1,0:T(8,128)(2,1)S(1)} %collective-permute-done.5.refs_2_) | copy-start | bytes 614404
  105.6 0.7 copy-start.4
  109.6 15.1 %collective-permute-start.9 = (bf16[480,640]{1,0:T(8,128)(2,1)}, bf16[480,640]{1,0:T(8,128)(2,1)S(1)}, u32[]{:S(2)}, u32[]{:S(2)}) collective-permute-start(bf16[480,640]{1,0:T(8,128)(2,1)} %renorm.1.rest_0_), channel_id=1, source_target_pairs={{0,8},{4,12},{8,0},{12,4},{16,24},{20,28},{24,16},{28,20},{1,9},{5... | collective-permute-start | bytes 1843208 | tf_op jit(solution)/shard_map/ppermute | solution.py:454
  109.9 17.9 %collective-permute-start.11 = (bf16[480,640]{1,0:T(8,128)(2,1)}, bf16[480,640]{1,0:T(8,128)(2,1)}, u32[]{:S(2)}, u32[]{:S(2)}) collective-permute-start(bf16[480,640]{1,0:T(8,128)(2,1)} %renorm.1.rest_0_), channel_id=1, source_target_pairs={{0,16},{4,20},{8,24},{12,28},{16,0},{20,4},{24,8},{28,12},{1,17},{... | collective-permute-start | bytes 1843208 | tf_op jit(solution)/shard_map/ppermute | solution.py:454
  124.7 23.1 %copy-start.3 = (bf16[480,640]{1,0:T(8,128)(2,1)}, bf16[480,640]{1,0:T(8,128)(2,1)S(1)}, u32[]{:S(2)}) copy-start(bf16[480,640]{1,0:T(8,128)(2,1)S(1)} %collective-permute-done.9.rest_1_) | copy-start | bytes 1843204
  124.8 10.6 %collective-permute-start.15 = (bf16[320,640]{1,0:T(8,128)(2,1)S(1)}, bf16[320,640]{1,0:T(8,128)(2,1)}, u32[]{:S(2)}, u32[]{:S(2)}) collective-permute-start(bf16[320,640]{1,0:T(8,128)(2,1)S(1)} %slice.21), channel_id=1, source_target_pairs={{0,16},{4,20},{8,24},{12,28},{16,0},{20,4},{24,8},{28,12},{1,17},{... | collective-permute-start | bytes 1228808 | tf_op jit(solution)/shard_map/ppermute | solution.py:454
  127.3 33.9 %collective-permute-start.8 = (bf16[480,640]{1,0:T(8,128)(2,1)}, bf16[480,640]{1,0:T(8,128)(2,1)}, u32[]{:S(2)}, u32[]{:S(2)}) collective-permute-start(bf16[480,640]{1,0:T(8,128)(2,1)} %renorm.1.rest_0_), channel_id=1, source_target_pairs={{0,4},{4,0},{8,12},{12,8},{16,20},{20,16},{24,28},{28,24},{1,5},{5... | collective-permute-start | bytes 1843208 | tf_op jit(solution)/shard_map/ppermute | solution.py:454
  127.3 8.1 %copy-start = (bf16[1024,1280]{1,0:T(8,128)(2,1)}, bf16[1024,1280]{1,0:T(8,128)(2,1)S(1)}, u32[]{:S(2)}) copy-start(bf16[1024,1280]{1,0:T(8,128)(2,1)S(1)} %collective-permute-done.refs_1_.refs_3_) | copy-start | bytes 7864324
  127.3 33.9 %collective-permute-start.10 = (bf16[480,640]{1,0:T(8,128)(2,1)S(1)}, bf16[480,640]{1,0:T(8,128)(2,1)}, u32[]{:S(2)}, u32[]{:S(2)}) collective-permute-start(bf16[480,640]{1,0:T(8,128)(2,1)S(1)} %collective-permute-done.9.rest_1_), channel_id=1, source_target_pairs={{0,4},{4,0},{8,12},{12,8},{16,20},{20,16},{24,28},{28,24},{1,5},{5... | collective-permute-start | bytes 1843208 | tf_op jit(solution)/shard_map/ppermute | solution.py:454
  127.8 33.4 %collective-permute-start.12 = (bf16[480,640]{1,0:T(8,128)(2,1)}, bf16[480,640]{1,0:T(8,128)(2,1)}, u32[]{:S(2)}, u32[]{:S(2)}) collective-permute-start(bf16[480,640]{1,0:T(8,128)(2,1)} %collective-permute-done.11.rest_2_), channel_id=1, source_target_pairs={{0,4},{4,0},{8,12},{12,8},{16,20},{20,16},{24,28},{28,24},{1,5},{5... | collective-permute-start | bytes 1843208 | tf_op jit(solution)/shard_map/ppermute | solution.py:454
  129.1 24.5 %collective-permute-start.13 = (bf16[160,640]{1,0:T(8,128)(2,1)S(1)}, bf16[160,640]{1,0:T(8,128)(2,1)}, u32[]{:S(2)}, u32[]{:S(2)}) collective-permute-start(bf16[160,640]{1,0:T(8,128)(2,1)S(1)} %slice.20), channel_id=1, source_target_pairs={{0,8},{4,12},{8,0},{12,4},{16,24},{20,28},{24,16},{28,20},{1,9},{5... | collective-permute-start | bytes 614408 | tf_op jit(solution)/shard_map/ppermute | solution.py:454
  135.4 25.8 %collective-permute-start.16 = (bf16[320,640]{1,0:T(8,128)(2,1)}, bf16[320,640]{1,0:T(8,128)(2,1)}, u32[]{:S(2)}, u32[]{:S(2)}) collective-permute-start(bf16[320,640]{1,0:T(8,128)(2,1)} %collective-permute-done.15.rest_4_), channel_id=1, source_target_pairs={{0,4},{4,0},{8,12},{12,8},{16,20},{20,16},{24,28},{28,24},{1,5},{5... | collective-permute-start | bytes 1228808 | tf_op jit(solution)/shard_map/ppermute | solution.py:454
  153.6 7.6 %collective-permute-start.14 = (bf16[160,640]{1,0:T(8,128)(2,1)}, bf16[160,640]{1,0:T(8,128)(2,1)S(1)}, u32[]{:S(2)}, u32[]{:S(2)}) collective-permute-start(bf16[160,640]{1,0:T(8,128)(2,1)} %collective-permute-done.13.rest_3_), channel_id=1, source_target_pairs={{0,4},{4,0},{8,12},{12,8},{16,20},{20,16},{24,28},{28,24},{1,5},{5... | collective-permute-start | bytes 614408 | tf_op jit(solution)/shard_map/ppermute | solution.py:454
  161.2 0.7 copy-start.5

commit v2 on v1

--- a/solution.py
+++ b/solution.py
@@ -167,6 +167,29 @@
     )(position, *[job[0] for job in jobs], *[x[0] for x in sources], *[x[2] for x in sources])
 
 
+def owned_rows(F):
+    n, m, half = F // 4, F // 8, 3 * F // 2
+    unit = 3 * F // 8
+    segments = []
+    for k in range(4):
+        upper, lower = k * unit, half + (2 * (k % 2) + k // 2) * unit
+        segments += [
+            (k * n, (k + 1) * n, upper),
+            (F + k * n, F + k * n + m, upper + n),
+            (F + k * n + m, F + (k + 1) * n, lower),
+            (2 * F + k * n, 2 * F + (k + 1) * n, lower + m),
+        ]
+    return segments
+
+
+def at_x(s):
+    return (s[0] >> 1) & 1
+
+
+def at_y(s):
+    return (s[0] >> 2) & 1
+
+
 def grad_kernel(s_ref, x_ref, v_ref, r_ref, w1_ref, w3_ref, w2_ref, *refs, head, tm, tn, split):
     w13, w2, gu, hid, og = refs[-5:]
     F = w1_ref.shape[2]
@@ -200,20 +223,22 @@
         cur = nxt
     x = x_ref[...]
     hd = hid[...]
-    x1, y1 = (s_ref[0] >> 1) & 1, (s_ref[0] >> 2) & 1
+    x1, y1 = at_x(s_ref), at_y(s_ref)
+    block_rows = 3 * F // 4
+    segments = owned_rows(F) if split else []
 
     def put(lo, grad):
         if not split:
             refs[0][lo : lo + grad.shape[0], :] = grad.astype(refs[0].dtype)
             return
         grad = grad + refs[0][lo : lo + grad.shape[0], :].astype(jnp.float32)
-        edges = [0, F // 2, F, 2 * F, 3 * F]
-        for block in range(4):
-            a, b = max(lo, edges[block]), min(lo + grad.shape[0], edges[block + 1])
+        for a, b, to in segments:
+            a, b, to = max(lo, a), min(lo + grad.shape[0], b), to + max(lo - a, 0)
             if a < b:
+                block, row = divmod(to, block_rows)
                 slot = jnp.where((x1 if block < 2 else y1) == block % 2, 0, 1)
-                rows_at = slice(a - edges[block], b - edges[block])
-                refs[1 + block // 2][slot, rows_at, :] = grad[a - lo : b - lo].astype(jnp.bfloat16)
+                part = grad[a - lo : b - lo].astype(jnp.bfloat16)
+                refs[1 + block // 2][slot, row : row + b - a, :] = part
 
     for j in range(2 * F // tn):
         put(j * tn, mm(gu[:, j * tn : (j + 1) * tn], x, TN))
@@ -246,10 +271,10 @@
     if received is None:
         shapes = [(3 * F, F)]
     else:
-        shapes = [(F // 2, F)] * 2 + [(F, F)] * 2
+        shapes = [(3 * F // 4, F)] * 4
         args.append(received)
         specs.append(whole(3 * F, F))
-        scratch = [pltpu.VMEM((2, F // 2, F), bf), pltpu.VMEM((2, F, F), bf)] + scratch
+        scratch = [pltpu.VMEM((2, 3 * F // 4, F), bf)] * 2 + scratch
     kernel = functools.partial(grad_kernel, head=head, tm=tm, tn=tn, split=received is not None)
 
     def body(*refs):
@@ -383,33 +408,12 @@
     )(position, own, far, own_log, far)
 
 
-def apply_kernel(s_ref, q_ref, high_ref, low_ref, *rest, tm, parts):
-    n_ref, a_ref, o_ref = rest[-2], rest[-1], rest[-3]
-    F = n_ref.shape[1]
-    step = pl.program_id(0)
-
-    @pl.when(step == 0)
-    def _():
-        for piece, row, n, start in parts:
-            to = pl.multiple_of(start(s_ref), 16)
-            n_ref[pl.ds(to, n), :] = rest[piece][row : row + n, :]
-        a_ref[...] = low_ref[...]
-
-    @pl.when(step == 1)
-    def _():
-        a_ref[...] = high_ref[...]
-
-    n = q_ref.shape[0] // tm
-
-    def first(i):
-        return mm(q_ref[i * tm : (i + 1) * tm, :], n_ref[: 2 * F, :], NT)
-
-    def second(i, h):
-        g = h[:, :F]
-        hid = (g * jax.nn.sigmoid(g) * h[:, F:]).astype(jnp.bfloat16)
-        r = slice(i * tm, (i + 1) * tm)
-        o_ref[r, :] = (a_ref[r, :].astype(jnp.float32) + mm(hid, n_ref[2 * F :, :], NT)).astype(o_ref.dtype)
-
+def gated(h, n):
+    g = h[:, :n]
+    return (g * jax.nn.sigmoid(g) * h[:, n:]).astype(jnp.bfloat16)
+
+
+def staggered(n, first, second):
     cur = first(0)
     for i in range(n):
         nxt = first(i + 1) if i + 1 < n else None
@@ -417,33 +421,146 @@
         cur = nxt
 
 
-def apply_head(position, head, fq, pieces, parts, high, low, into=None):
+def put_quarter(s_ref, ref, rows, values, flip_x, flip_y):
+    n = ref.shape[1] // 4
+    chip = 2 * (at_x(s_ref) ^ flip_x) + (at_y(s_ref) ^ flip_y)
+    for k in range(4):
+
+        @pl.when(chip == k)
+        def _():
+            ref[rows, k * n : (k + 1) * n] = values
+
+
+def hidden_kernel(s_ref, q_ref, own_ref, over_x, over_y, o_ref, w_ref, v_ref, *, tm):
+    F = q_ref.shape[1]
+    n = F // 4
+
+    @pl.when(pl.program_id(0) == 0)
+    def _():
+        for i, ref in enumerate((own_ref, over_x, over_y)):
+            w_ref[i * n : (i + 1) * n, :] = ref[:n, :]
+            w_ref[(3 + i) * n : (4 + i) * n, :] = ref[n : 2 * n, :]
+
+    def first(i):
+        return mm(q_ref[i * tm : (i + 1) * tm, :], w_ref[...], NT)
+
+    def second(i, h):
+        v_ref[i * tm : (i + 1) * tm, : 3 * n] = gated(h, 3 * n)
+
+    staggered(q_ref.shape[0] // tm, first, second)
+    every = slice(0, q_ref.shape[0])
+    for i, flips in enumerate(((0, 0), (1, 0), (0, 1))):
+        put_quarter(s_ref, o_ref, every, v_ref[:, i * n : (i + 1) * n], *flips)
+
+
+def hidden_part(position, head, fq, pieces):
+    rows = fq.shape[0]
+    F = pieces[0].shape[1]
+    half = rows // 2
+    whole = pl.BlockSpec(pieces[0].shape, lambda i, s: (0, 0))
+    bf = jnp.bfloat16
+    return pl.pallas_call(
+        functools.partial(hidden_kernel, tm=min(256, half)),
+        grid_spec=pltpu.PrefetchScalarGridSpec(
+            num_scalar_prefetch=1,
+            grid=(2,),
+            in_specs=[pl.BlockSpec((half, F), lambda i, s: (i, head(s)))] + [whole] * 3,
+            out_specs=pl.BlockSpec((half, F), lambda i, s: (i, 0)),
+            scratch_shapes=[pltpu.VMEM((3 * F // 2, F), bf), pltpu.VMEM((half, F), bf)],
+        ),
+        out_shape=jax.ShapeDtypeStruct((rows, F), bf),
+        cost_estimate=pl.CostEstimate(
+            flops=3 * rows * F * F, bytes_accessed=rows * F * 4 + F * F * 3, transcendentals=rows * F
+        ),
+        name="hidden",
+    )(position, fq, *pieces[:3])
+
+
+def apply_kernel(s_ref, q_ref, high_ref, low_ref, *rest, tm, split):
+    n_ref, w_ref, h_ref, a_ref = rest[-4:]
+    o_ref = rest[-5]
+    F = q_ref.shape[1]
+    n, m = F // 4, F // 8
+    step = pl.program_id(0)
+
+    @pl.when(step == 0)
+    def _():
+        if split:
+            own, over_x, over_y, upper, lower = rest[1:6]
+            for ref, row, flips in (
+                (own, 2 * n, (0, 0)),
+                (over_x, 2 * n, (1, 0)),
+                (over_y, 2 * n, (0, 1)),
+                (lower, m, (1, 1)),
+            ):
+                to = pl.multiple_of(quarter(F, *flips)(s_ref), 16)
+                n_ref[pl.ds(to, n), :] = ref[row : row + n, :]
+            w_ref[: n + m, :] = upper[...]
+            w_ref[n + m :, :] = lower[:m, :]
+        else:
+            w_ref[...] = rest[0][: 2 * F, :]
+            n_ref[...] = rest[0][2 * F :, :]
+        a_ref[...] = low_ref[...]
+
+    @pl.when(step == 1)
+    def _():
+        a_ref[...] = high_ref[...]
+
+    def first(i):
+        return mm(q_ref[i * tm : (i + 1) * tm, :], w_ref[...], NT)
+
+    def second(i, h):
+        r = slice(i * tm, (i + 1) * tm)
+        if split:
+            h_ref[r, :] = rest[0][r, :]
+            put_quarter(s_ref, h_ref, r, gated(h, n), 1, 1)
+            hid = h_ref[r, :]
+        else:
+            hid = gated(h, F)
+        o_ref[r, :] = (a_ref[r, :].astype(jnp.float32) + mm(hid, n_ref[...], NT)).astype(o_ref.dtype)
+
+    staggered(q_ref.shape[0] // tm, first, second)
+
+
+def apply_head(position, head, fq, hidden, pieces, high, low, into=None):
     rows, cols = fq.shape
     F = pieces[0].shape[1]
     half = rows // 2
+    split = hidden is not None
     col = pl.BlockSpec((half, F), lambda i, s: (i, head(s)))
     part = pl.BlockSpec((half, F), lambda i, s: (0, head(s)))
     whole = lambda a: pl.BlockSpec(a.shape, lambda i, s: (0, 0))
-    args = [position, fq, high, low, *pieces]
-    specs = [col, part, part] + [whole(p) for p in pieces]
+    args = [position, fq, high, low]
+    specs = [col, part, part]
+    if split:
+        args.append(hidden)
+        specs.append(pl.BlockSpec((half, F), lambda i, s: (i, 0)))
+    args += pieces
+    specs += [whole(p) for p in pieces]
     aliases = {}
     if into is not None:
         aliases = {len(args): 0}
         args.append(into)
         specs.append(pl.BlockSpec(memory_space=pl.ANY))
+    bf = jnp.bfloat16
     return pl.pallas_call(
-        functools.partial(apply_kernel, tm=min(256, half), parts=parts),
+        functools.partial(apply_kernel, tm=min(256, half), split=split),
         grid_spec=pltpu.PrefetchScalarGridSpec(
             num_scalar_prefetch=1,
             grid=(2,),
             in_specs=specs,
             out_specs=col,
-            scratch_shapes=[pltpu.VMEM((3 * F, F), jnp.bfloat16), pltpu.VMEM((half, F), jnp.bfloat16)],
-        ),
-        out_shape=jax.ShapeDtypeStruct((rows, cols), jnp.bfloat16),
+            scratch_shapes=[
+                pltpu.VMEM((F, F), bf),
+                pltpu.VMEM((F // 2 if split else 2 * F, F), bf),
+                pltpu.VMEM((half, F), bf),
+                pltpu.VMEM((half, F), bf),
+            ],
+        ),
+        out_shape=jax.ShapeDtypeStruct((rows, cols), bf),
         input_output_aliases=aliases,
         cost_estimate=pl.CostEstimate(
-            flops=6 * rows * F * F, bytes_accessed=rows * F * 6 + F * F * 6, transcendentals=rows * F
+            flops=3 * rows * F * F, bytes_accessed=rows * F * 8 + F * F * 6, transcendentals=rows * F
         ),
         name="apply",
     )(*args)
@@ -503,18 +620,8 @@
     return [part, over_x, over_y, top2, bottom2]
 
 
-def at_x(s):
-    return (s[0] >> 1) & 1
-
-
-def at_y(s):
-    return (s[0] >> 2) & 1
-
-
-def place(F, flip_x, flip_y):
-    x = lambda s: at_x(s) ^ flip_x
-    y = lambda s: at_y(s) ^ flip_y
-    return lambda s: (2 * x(s) + y(s)) * (F // 4), lambda s: F + (2 * y(s) + x(s)) * (F // 2)
+def quarter(F, flip_x=0, flip_y=0):
+    return lambda s: (2 * (at_x(s) ^ flip_x) + (at_y(s) ^ flip_y)) * (F // 4)
 
 
 def shards(attn_q, attn_k, attn_v, fast_q, fast_k, fast_v, rates, fast_gate, fast_up, fast_down):
@@ -536,19 +643,15 @@
         near, far = (lambda s: s[0] & 1), (lambda s: 1 - (s[0] & 1))
         received = exchange(grads(far)[0], 0)
         F = fast_gate.shape[1]
-        n, m = F // 4, F // 2
-        upper, lower = place(F, 0, 0)
-        old = turned(position, near, *weights, parts=((n, upper), (m, lower)))
+        mine = quarter(F)
+        starts = [(F // 4, lambda s, at=i * F: at + mine(s)) for i in range(3)]
+        old = turned(position, near, *weights, parts=tuple(starts))
         blocks = grads(near, received)
         pieces = synced_square(position, blocks, old)
         other = [exchange(p, 0) for p in pieces]
-        parts = []
-        for piece, (flip_x, flip_y) in enumerate([(0, 0), (1, 0), (0, 1)]):
-            upper, lower = place(F, flip_x, flip_y)
-            parts += [(piece, 0, n, upper), (piece, n, m, lower)]
-        upper, lower = place(F, 1, 1)
-        parts += [(3, 0, n, upper), (4, 0, m, lower)]
-        news = [(near, pieces, parts), (far, other, parts)]
+        news = []
+        for head, new in ((near, pieces), (far, other)):
+            news.append((head, hidden_part(position, head, fast_q, new), new))
     else:
         news = []
         bits = list(range(count.bit_length() - 1))
@@ -556,7 +659,7 @@
             head = lambda s, h=h: h
             old = turned(position, head, *weights)
             new = synced(grads(head)[0].astype(jnp.float32), old, bits, position[0])
-            news.append((head, [new], [(0, 0, new.shape[0], lambda s: 0)]))
+            news.append((head, None, [new]))
     bq = min(256, half)
     tiles = half // bq
     late = [
@@ -570,8 +673,8 @@
     (high,) = attention(position, [(attn_q, 1, late, 0)], [(prev, 0, prev, 1, half), here], bq, width)
     low = merged(position, own_out, far_out, own_log, width)
     mixed = None
-    for head, pieces, parts in news:
-        mixed = apply_head(position, head, fast_q, pieces, parts, high, low, mixed)
+    for head, hidden, new in news:
+        mixed = apply_head(position, head, fast_q, hidden, new, high, low, mixed)
     return mixed
 
 

time: 169 us -> 168 us (level)
  waiting for transfers between devices: 54.1 us -> 15.7 us
  starting transfers between devices: 27.1 us -> 51.6 us
  Pallas kernels: 79 us -> 90 us
  local copies, waits for them, and re-layouts: 3.98 us -> 5.97 us
    ppermute x14, waiting for transfers between devices: 54.1 us -> 15.7 us  [exchange(): return lax.ppermute(block, 'seq', [(i, i ^ 1 << bit) for i in range(size)])]
    ppermute x14, starting transfers between devices: 15 us -> 39.2 us  [exchange(): return lax.ppermute(block, 'seq', [(i, i ^ 1 << bit) for i in range(size)])]
    pallas_call x2 -> x4, Pallas kernels: 14.1 us -> 25.5 us  [the longest x2 14.3 us: apply_head(): pl.pallas_call(functools.partial(apply_kernel, tm=min(256, half), split=s...]
  transfers between devices with their start and end apart: 17 -> 17, of which waited for: 5 -> 3; matrix products, arithmetic and copies ran while one was open for 4% -> 5% of each run, Pallas kernels for 36% -> 42%
where the time goes in v2:
time: 168 us
  Pallas kernels  90 us (54%)
  starting transfers between devices  51.6 us (31%)
  waiting for transfers between devices  15.7 us (9%)
  local copies, waits for them, and re-layouts  5.97 us (4%)
  other arithmetic  4.57 us (3%)
    ppermute x14, starting transfers between devices, exchange(): return lax.ppermute(block, 'seq', [(i, i ^ 1 << bit) for i in range(size)])  39.2 us
    pallas_call x2, Pallas kernels, attention(): pl.pallas_call(kernel, grid_spec=pltpu.PrefetchScalarGridSpec(num_scalar_...  26.2 us
    pallas_call x2, Pallas kernels, gradients(): pl.pallas_call(body, grid_spec=pltpu.PrefetchScalarGridSpec(num_scalar_pr...  24.2 us
    ppermute x14, waiting for transfers between devices, exchange(): return lax.ppermute(block, 'seq', [(i, i ^ 1 << bit) for i in range(size)])  15.7 us
    pallas_call x2, Pallas kernels, apply_head(): pl.pallas_call(functools.partial(apply_kernel, tm=min(256, half), split=s...  14.3 us
    ppermute x3, starting transfers between devices, shifted(): lax.ppermute(block, 'seq', [(i, i + by) for i in range(size) if 0 <= i +...  12.4 us
    pallas_call x2, Pallas kernels, hidden_part(): pl.pallas_call(functools.partial(hidden_kernel, tm=min(256, half)), grid_...  11.2 us
    pallas_call x1, Pallas kernels, merged(): pl.pallas_call(functools.partial(merge_kernel, stride=log_stride_of(cols)...  5.75 us
  transfers between devices with their start and end apart: 17, of which 3 were waited for; matrix products, arithmetic and copies ran while one was open for 5% of the time, Pallas kernels for 42%

profile of v2, /device:TPU:0, one launch (start us, length us, event | category | flops | bytes accessed | tf_op | source)
XLA Modules:
  0.0 167.8 jit_solution(4910802994843188113)
XLA Ops:
  0.0 11.7 %grads.2 = bf16[1920,640]{1,0:T(8,128)(2,1)} custom-call(s32[1]{0:T(128)} %bitcast.position_ref.s_ref.refs_0_, bf16[1024,1280]{1,0:T(8,128)(2,1)} %refs_1_.5, bf16[1024,1280]{1,0:T(8,128)(2,1)} %refs_2_.7, f32[2,1024]{1,0:T(2,128)} %bitcast.2, f32[2,640,640]{2,1,0:T(8,128)} %refs_4_.5, f32[2,640,640]{2,1,0:T(8,128)} %refs_5_.3, f32[2,640,640]{2,1,0:T(8,128)} %refs_6_.3), custom_call_target="tpu_custom_call" | custom-call | flops 5033164800 | bytes 9994240 | tf_op jit(solution)/shard_map/grads/pallas_call | solution.py:286
  12.2 1.1 slice.17
  13.3 1.5 collective-permute-start.1
  15.0 1.7 pad_maximum_fusion
  16.7 3.2 %collective-permute-start = (bf16[1024,1280]{1,0:T(8,128)(2,1)}, bf16[1024,1280]{1,0:T(8,128)(2,1)S(1)}, u32[]{:S(2)}, u32[]{:S(2)}) collective-permute-start(bf16[1024,1280]{1,0:T(8,128)(2,1)} %pad_maximum_fusion), channel_id=1, source_target_pairs={{0,4},{4,8},{8,12},{12,16},{16,20},{20,24},{24,28},{1,5},{5,9},{9,... | collective-permute-start | bytes 7864328 | tf_op jit(solution)/shard_map/ppermute | solution.py:576
  19.9 12.6 %grads.3 = (bf16[480,640]{1,0:T(8,128)(2,1)}, bf16[480,640]{1,0:T(8,128)(2,1)}, bf16[480,640]{1,0:T(8,128)(2,1)}, bf16[480,640]{1,0:T(8,128)(2,1)}) custom-call(s32[1]{0:T(128)} %bitcast.position_ref.s_ref.refs_0_, bf16[1024,1280]{1,0:T(8,128)(2,1)} %refs_1_.5, bf16[1024,1280]{1,0:T(8,128)(2,1)} %refs_2_.7, f32[2,1024]{1,0:T(2,128)} %bitcast.3, ...), custom_call_target="tpu_custom_call" | custom-call | flops 5033164800 | bytes 9994240 | tf_op jit(solution)/shard_map/grads/pallas_call | solution.py:286
  32.5 2.3 %collective-permute-start.4 = (bf16[480,640]{1,0:T(8,128)(2,1)}, bf16[480,640]{1,0:T(8,128)(2,1)}, u32[]{:S(2)}, u32[]{:S(2)}) collective-permute-start(bf16[480,640]{1,0:T(8,128)(2,1)} %get-tuple-element.16), channel_id=1, source_target_pairs={{0,8},{4,12},{8,0},{12,4},{16,24},{20,28},{24,16},{28,20},{1,9},{5... | collective-permute-start | bytes 1843208 | tf_op jit(solution)/shard_map/ppermute | solution.py:571
  34.8 2.5 %collective-permute-start.6 = (bf16[480,640]{1,0:T(8,128)(2,1)}, bf16[480,640]{1,0:T(8,128)(2,1)}, u32[]{:S(2)}, u32[]{:S(2)}) collective-permute-start(bf16[480,640]{1,0:T(8,128)(2,1)} %get-tuple-element.18), channel_id=1, source_target_pairs={{0,16},{4,20},{8,24},{12,28},{16,0},{20,4},{24,8},{28,12},{1,17},{... | collective-permute-start | bytes 1843208 | tf_op jit(solution)/shard_map/ppermute | solution.py:571
  37.4 13.8 %shard_map.101 = (bf16[512,1408]{1,0:T(8,128)(2,1)}, bf16[512,1280]{1,0:T(8,128)(2,1)}, f32[512,128]{1,0:T(8,128)}) custom-call(s32[1]{0:T(128)} %bitcast.position_ref.s_ref.refs_0_, bf16[512,1280]{1,0:T(8,128)(2,1)} %collective-permute-done.1.refs_0_, bf16[1024,1280]{1,0:T(8,128)(2,1)} %refs_1_.3, bf16[1024,1280]{1,0:T(8,128)(2,1)} %refs_2_.5, ...), custom_call_target="tpu_custom_call" | custom-call | flops 3355443200 | bytes 10485760 | tf_op jit(solution)/shard_map/pallas_call | solution.py:154
  51.1 7.6 %collective-permute-start.2 = (bf16[512,1408]{1,0:T(8,128)(2,1)}, bf16[512,1408]{1,0:T(8,128)(2,1)}, u32[]{:S(2)}, u32[]{:S(2)}) collective-permute-start(bf16[512,1408]{1,0:T(8,128)(2,1)} %get-tuple-element.13), channel_id=1, source_target_pairs={{0,4},{4,8},{8,12},{12,16},{16,20},{20,24},{24,28},{1,5},{5,9},{9,... | collective-permute-start | bytes 4325384 | tf_op jit(solution)/shard_map/ppermute | solution.py:576
  58.7 1.0 add_convert_fusion.1
  59.8 2.4 %collective-permute-start.5 = (bf16[240,640]{1,0:T(8,128)(2,1)S(1)}, bf16[240,640]{1,0:T(8,128)(2,1)S(1)}, u32[]{:S(2)}, u32[]{:S(2)}) collective-permute-start(bf16[240,640]{1,0:T(8,128)(2,1)S(1)} %add_convert_fusion.1), channel_id=1, source_target_pairs={{0,16},{4,20},{8,24},{12,28},{16,0},{20,4},{24,8},{28,12},{1,17},{... | collective-permute-start | bytes 921608 | tf_op jit(solution)/shard_map/ppermute | solution.py:571
  62.2 10.4 %collective-permute-done.6.refs_4_ = bf16[480,640]{1,0:T(8,128)(2,1)} collective-permute-done((bf16[480,640]{1,0:T(8,128)(2,1)}, bf16[480,640]{1,0:T(8,128)(2,1)}, u32[]{:S(2)}, u32[]{:S(2)}) %collective-permute-start.6) | collective-permute-done | bytes 614432 | tf_op jit(solution)/shard_map/ppermute | solution.py:571
  72.6 1.9 %add_convert_fusion = bf16[240,640]{1,0:T(8,128)(2,1)} fusion(bf16[480,640]{1,0:T(8,128)(2,1)} %collective-permute-done.6.refs_4_, s32[]{:T(128)S(6)} %select_n.9, bf16[480,640]{1,0:T(8,128)(2,1)} %get-tuple-element.17.refs_3_), kind=kLoop, calls=%fused_computation.1 | loop fusion | flops 614400 | bytes 921604 | tf_op jit(solution)/shard_map/convert_element_type | solution.py:606
  74.5 5.1 %turned.1.old_ref = f32[480,640]{1,0:T(8,128)} custom-call(s32[1]{0:T(128)} %bitcast.position_ref.s_ref.refs_0_, f32[2,640,640]{2,1,0:T(8,128)} %refs_4_.5, f32[2,640,640]{2,1,0:T(8,128)} %refs_5_.3, f32[2,640,640]{2,1,0:T(8,128)} %refs_6_.3), custom_call_target="tpu_custom_call" | custom-call | flops 1228800 | bytes 9830400 | tf_op jit(solution)/shard_map/turned/pallas_call | solution.py:319
  79.6 3.7 %collective-permute-done.5.refs_2_ = bf16[240,640]{1,0:T(8,128)(2,1)S(1)} collective-permute-done((bf16[240,640]{1,0:T(8,128)(2,1)S(1)}, bf16[240,640]{1,0:T(8,128)(2,1)S(1)}, u32[]{:S(2)}, u32[]{:S(2)}) %collective-permute-start.5) | collective-permute-done | bytes 307232 | tf_op jit(solution)/shard_map/ppermute | solution.py:571
  83.3 1.5 collective-permute-done.7.refs_5_
  85.5 3.2 %renorm.1.own_ref.rest_1_ = bf16[480,640]{1,0:T(8,128)(2,1)} custom-call(s32[1]{0:T(128)} %bitcast.position_ref.s_ref.refs_0_, f32[480,640]{1,0:T(8,128)} %turned.1.old_ref, bf16[480,640]{1,0:T(8,128)(2,1)} %get-tuple-element.15.refs_0_, bf16[480,640]{1,0:T(8,128)(2,1)} %collective-permute-done.4.refs_1_, bf16[240,640]{1,0:T(8,128)(2,1)} %copy-done.5, ...), custom_call_target="tpu_custom_call" | custom-call | flops 3072000 | bytes 3686400 | tf_op jit(solution)/shard_map/renorm/pallas_call | solution.py:357
  88.8 2.5 %collective-permute-start.11 = (bf16[480,640]{1,0:T(8,128)(2,1)}, bf16[480,640]{1,0:T(8,128)(2,1)}, u32[]{:S(2)}, u32[]{:S(2)}) collective-permute-start(bf16[480,640]{1,0:T(8,128)(2,1)} %renorm.1.own_ref.rest_1_), channel_id=1, source_target_pairs={{0,16},{4,20},{8,24},{12,28},{16,0},{20,4},{24,8},{28,12},{1,17},{... | collective-permute-start | bytes 1843208 | tf_op jit(solution)/shard_map/ppermute | solution.py:571
  91.2 18.5 %collective-permute-start.8 = (bf16[480,640]{1,0:T(8,128)(2,1)}, bf16[480,640]{1,0:T(8,128)(2,1)}, u32[]{:S(2)}, u32[]{:S(2)}) collective-permute-start(bf16[480,640]{1,0:T(8,128)(2,1)} %renorm.1.own_ref.rest_1_), channel_id=1, source_target_pairs={{0,4},{4,0},{8,12},{12,8},{16,20},{20,16},{24,28},{28,24},{1,5},{5... | collective-permute-start | bytes 1843208 | tf_op jit(solution)/shard_map/ppermute | solution.py:571
  109.7 5.2 %collective-permute-start.10 = (bf16[480,640]{1,0:T(8,128)(2,1)S(1)}, bf16[480,640]{1,0:T(8,128)(2,1)}, u32[]{:S(2)}, u32[]{:S(2)}) collective-permute-start(bf16[480,640]{1,0:T(8,128)(2,1)S(1)} %collective-permute-done.9.over_x.rest_2_), channel_id=1, source_target_pairs={{0,4},{4,0},{8,12},{12,8},{16,20},{20,16},{24,28},{28,24},{1,5},{5... | collective-permute-start | bytes 1843208 | tf_op jit(solution)/shard_map/ppermute | solution.py:571
  115.0 2.6 %collective-permute-start.12 = (bf16[480,640]{1,0:T(8,128)(2,1)}, bf16[480,640]{1,0:T(8,128)(2,1)}, u32[]{:S(2)}, u32[]{:S(2)}) collective-permute-start(bf16[480,640]{1,0:T(8,128)(2,1)} %collective-permute-done.11.over_y.rest_3_), channel_id=1, source_target_pairs={{0,4},{4,0},{8,12},{12,8},{16,20},{20,16},{24,28},{28,24},{1,5},{5... | collective-permute-start | bytes 1843208 | tf_op jit(solution)/shard_map/ppermute | solution.py:571
  117.6 1.7 %slice.20 = bf16[240,640]{1,0:T(8,128)(2,1)} slice(bf16[480,640]{1,0:T(8,128)(2,1)} %collective-permute-done.11.over_y.rest_3_), slice={[0:240], [0:640]} | slice | bytes 614400 | tf_op jit(solution)/shard_map/slice | solution.py:619
  119.3 0.7 slice.21
  120.4 1.7 %collective-permute-start.15 = (bf16[240,640]{1,0:T(8,128)(2,1)}, bf16[240,640]{1,0:T(8,128)(2,1)}, u32[]{:S(2)}, u32[]{:S(2)}) collective-permute-start(bf16[240,640]{1,0:T(8,128)(2,1)} %slice.21), channel_id=1, source_target_pairs={{0,16},{4,20},{8,24},{12,28},{16,0},{20,4},{24,8},{28,12},{1,17},{... | collective-permute-start | bytes 921608 | tf_op jit(solution)/shard_map/ppermute | solution.py:571
  122.1 12.4 %shard_map.100.high_ref = bf16[512,1280]{1,0:T(8,128)(2,1)} custom-call(s32[1]{0:T(128)} %bitcast.position_ref.s_ref.refs_0_, bf16[1024,1280]{1,0:T(8,128)(2,1)} %refs_1_.3, bf16[1024,1280]{1,0:T(8,128)(2,1)} %copy-done, bf16[1024,1280]{1,0:T(8,128)(2,1)} %refs_2_.5, bf16[1024,1280]{1,0:T(8,128)(2,1)} %copy-done, bf16[1024,1280]{1,0:T(8,128)(2,1)} %refs_3_.1), custom_call_target="tpu_custom_call" | custom-call | flops 3355443200 | bytes 10485760 | tf_op jit(solution)/shard_map/pallas_call | solution.py:154
  134.5 5.7 %merge.1.low_ref = bf16[512,1280]{1,0:T(8,128)(2,1)} custom-call(s32[1]{0:T(128)} %bitcast.position_ref.s_ref.refs_0_, bf16[512,1280]{1,0:T(8,128)(2,1)} %get-tuple-element.12.own_ref, bf16[512,1408]{1,0:T(8,128)(2,1)} %collective-permute-done.2.far_ref.far_log, f32[512,128]{1,0:T(8,128)} %get-tuple-element.14.own_log, ...), custom_call_target="tpu_custom_call" | custom-call | flops 5242880 | bytes 3932160 | tf_op jit(solution)/shard_map/merge/pallas_call | solution.py:395
  140.8 5.6 %hidden.3.rest_0_ = bf16[1024,640]{1,0:T(8,128)(2,1)} custom-call(s32[1]{0:T(128)} %bitcast.position_ref.s_ref.refs_0_, bf16[1024,1280]{1,0:T(8,128)(2,1)} %q_ref.7, bf16[480,640]{1,0:T(8,128)(2,1)} %renorm.1.own_ref.rest_1_, bf16[480,640]{1,0:T(8,128)(2,1)} %copy-done.2, bf16[480,640]{1,0:T(8,128)(2,1)} %collective-permute-done.11.over_y.rest_3_), custom_call_target="tpu_custom_call" | custom-call | flops 1258291200 | bytes 3850240 | tf_op jit(solution)/shard_map/hidden/pallas_call | solution.py:462
  146.4 7.2 %apply.2.rest_6_ = bf16[1024,1280]{1,0:T(8,128)(2,1)} custom-call(s32[1]{0:T(128)} %bitcast.position_ref.s_ref.refs_0_, bf16[1024,1280]{1,0:T(8,128)(2,1)} %q_ref.7, bf16[512,1280]{1,0:T(8,128)(2,1)} %shard_map.100.high_ref, bf16[512,1280]{1,0:T(8,128)(2,1)} %merge.1.low_ref, bf16[1024,640]{1,0:T(8,128)(2,1)} %hidden.3.rest_0_, ...), custom_call_target="tpu_custom_call" | custom-call | flops 1258291200 | bytes 7700480 | tf_op jit(solution)/shard_map/apply/pallas_call | solution.py:546
  153.6 5.7 %hidden.2.rest_0_ = bf16[1024,640]{1,0:T(8,128)(2,1)} custom-call(s32[1]{0:T(128)} %bitcast.position_ref.s_ref.refs_0_, bf16[1024,1280]{1,0:T(8,128)(2,1)} %q_ref.7, bf16[480,640]{1,0:T(8,128)(2,1)} %collective-permute-done.8.own_ref.rest_1_, bf16[480,640]{1,0:T(8,128)(2,1)} %collective-permute-done.10.over_x.rest_2_, ...), custom_call_target="tpu_custom_call" | custom-call | flops 1258291200 | bytes 3850240 | tf_op jit(solution)/shard_map/hidden/pallas_call | solution.py:462
  159.2 0.7 copy-done.7
  160.7 7.1 %apply.3 = bf16[1024,1280]{1,0:T(8,128)(2,1)} custom-call(s32[1]{0:T(128)} %bitcast.position_ref.s_ref.refs_0_, bf16[1024,1280]{1,0:T(8,128)(2,1)} %q_ref.7, bf16[512,1280]{1,0:T(8,128)(2,1)} %shard_map.100.high_ref, bf16[512,1280]{1,0:T(8,128)(2,1)} %merge.1.low_ref, bf16[1024,640]{1,0:T(8,128)(2,1)} %hidden.2.rest_0_, ...), custom_call_target="tpu_custom_call", output_to_operand_aliasing={{}: (10, {})} | custom-call | flops 1258291200 | bytes 7700480 | tf_op jit(solution)/shard_map/apply/pallas_call | solution.py:546
  (41 shorter events, 3.0 us)
Async XLA Ops:
  0.0 12.2 %copy-start.1 = (bf16[1024,1280]{1,0:T(8,128)(2,1)S(1)}, bf16[1024,1280]{1,0:T(8,128)(2,1)}, u32[]{:S(2)}) copy-start(bf16[1024,1280]{1,0:T(8,128)(2,1)} %refs_1_.3) | copy-start | bytes 7864324
  11.7 8.2 %collective-permute-start.3 = (bf16[1920,640]{1,0:T(8,128)(2,1)}, bf16[1920,640]{1,0:T(8,128)(2,1)}, u32[]{:S(2)}, u32[]{:S(2)}) collective-permute-start(bf16[1920,640]{1,0:T(8,128)(2,1)} %grads.2), channel_id=1, source_target_pairs={{0,4},{4,0},{8,12},{12,8},{16,20},{20,16},{24,28},{28,24},{1,5},{5... | collective-permute-start | bytes 7372808 | tf_op jit(solution)/shard_map/ppermute | solution.py:571
  13.3 1.6 slice-start
  13.3 1.7 %slice-start.1 = ((bf16[1024,1280]{1,0:T(8,128)(2,1)}), bf16[512,1280]{1,0:T(8,128)(2,1)S(1)}, s32[]{:S(2)}) async-start(bf16[1024,1280]{1,0:T(8,128)(2,1)} %refs_2_.5), calls=%async_computation.1 | async-start | bytes 2621440 | tf_op jit(solution)/shard_map/slice | solution.py:634
  13.3 24.1 %collective-permute-start.1 = (bf16[512,1280]{1,0:T(8,128)(2,1)}, bf16[512,1280]{1,0:T(8,128)(2,1)}, u32[]{:S(2)}, u32[]{:S(2)}) collective-permute-start(bf16[512,1280]{1,0:T(8,128)(2,1)} %slice.17), channel_id=1, source_target_pairs={{4,0},{8,4},{12,8},{16,12},{20,16},{24,20},{28,24},{5,1},{9,5},{13... | collective-permute-start | bytes 3932168 | tf_op jit(solution)/shard_map/ppermute | solution.py:576
  16.7 103.4 %collective-permute-start = (bf16[1024,1280]{1,0:T(8,128)(2,1)}, bf16[1024,1280]{1,0:T(8,128)(2,1)S(1)}, u32[]{:S(2)}, u32[]{:S(2)}) collective-permute-start(bf16[1024,1280]{1,0:T(8,128)(2,1)} %pad_maximum_fusion), channel_id=1, source_target_pairs={{0,4},{4,8},{8,12},{12,16},{16,20},{20,24},{24,28},{1,5},{5,9},{9,... | collective-permute-start | bytes 7864328 | tf_op jit(solution)/shard_map/ppermute | solution.py:576
  32.5 26.3 %collective-permute-start.4 = (bf16[480,640]{1,0:T(8,128)(2,1)}, bf16[480,640]{1,0:T(8,128)(2,1)}, u32[]{:S(2)}, u32[]{:S(2)}) collective-permute-start(bf16[480,640]{1,0:T(8,128)(2,1)} %get-tuple-element.16), channel_id=1, source_target_pairs={{0,8},{4,12},{8,0},{12,4},{16,24},{20,28},{24,16},{28,20},{1,9},{5... | collective-permute-start | bytes 1843208 | tf_op jit(solution)/shard_map/ppermute | solution.py:571
  34.8 23.9 %copy-start.3 = (bf16[480,640]{1,0:T(8,128)(2,1)S(1)}, bf16[480,640]{1,0:T(8,128)(2,1)}, u32[]{:S(2)}) copy-start(bf16[480,640]{1,0:T(8,128)(2,1)} %get-tuple-element.15.refs_0_) | copy-start | bytes 1843204
  34.8 37.8 %collective-permute-start.6 = (bf16[480,640]{1,0:T(8,128)(2,1)}, bf16[480,640]{1,0:T(8,128)(2,1)}, u32[]{:S(2)}, u32[]{:S(2)}) collective-permute-start(bf16[480,640]{1,0:T(8,128)(2,1)} %get-tuple-element.18), channel_id=1, source_target_pairs={{0,16},{4,20},{8,24},{12,28},{16,0},{20,4},{24,8},{28,12},{1,17},{... | collective-permute-start | bytes 1843208 | tf_op jit(solution)/shard_map/ppermute | solution.py:571
  51.1 69.2 %collective-permute-start.2 = (bf16[512,1408]{1,0:T(8,128)(2,1)}, bf16[512,1408]{1,0:T(8,128)(2,1)}, u32[]{:S(2)}, u32[]{:S(2)}) collective-permute-start(bf16[512,1408]{1,0:T(8,128)(2,1)} %get-tuple-element.13), channel_id=1, source_target_pairs={{0,4},{4,8},{8,12},{12,16},{16,20},{20,24},{24,28},{1,5},{5,9},{9,... | collective-permute-start | bytes 4325384 | tf_op jit(solution)/shard_map/ppermute | solution.py:576
  59.8 23.5 %collective-permute-start.5 = (bf16[240,640]{1,0:T(8,128)(2,1)S(1)}, bf16[240,640]{1,0:T(8,128)(2,1)S(1)}, u32[]{:S(2)}, u32[]{:S(2)}) collective-permute-start(bf16[240,640]{1,0:T(8,128)(2,1)S(1)} %add_convert_fusion.1), channel_id=1, source_target_pairs={{0,16},{4,20},{8,24},{12,28},{16,0},{20,4},{24,8},{28,12},{1,17},{... | collective-permute-start | bytes 921608 | tf_op jit(solution)/shard_map/ppermute | solution.py:571
  74.5 10.4 %collective-permute-start.7 = (bf16[240,640]{1,0:T(8,128)(2,1)}, bf16[240,640]{1,0:T(8,128)(2,1)S(1)}, u32[]{:S(2)}, u32[]{:S(2)}) collective-permute-start(bf16[240,640]{1,0:T(8,128)(2,1)} %add_convert_fusion), channel_id=1, source_target_pairs={{0,8},{4,12},{8,0},{12,4},{16,24},{20,28},{24,16},{28,20},{1,9},{5... | collective-permute-start | bytes 921608 | tf_op jit(solution)/shard_map/ppermute | solution.py:571
  83.3 1.5 copy-start.5
  84.8 0.7 copy-start.6
  88.8 20.9 %collective-permute-start.9 = (bf16[480,640]{1,0:T(8,128)(2,1)}, bf16[480,640]{1,0:T(8,128)(2,1)S(1)}, u32[]{:S(2)}, u32[]{:S(2)}) collective-permute-start(bf16[480,640]{1,0:T(8,128)(2,1)} %renorm.1.own_ref.rest_1_), channel_id=1, source_target_pairs={{0,8},{4,12},{8,0},{12,4},{16,24},{20,28},{24,16},{28,20},{1,9},{5... | collective-permute-start | bytes 1843208 | tf_op jit(solution)/shard_map/ppermute | solution.py:571
  88.8 26.2 %collective-permute-start.11 = (bf16[480,640]{1,0:T(8,128)(2,1)}, bf16[480,640]{1,0:T(8,128)(2,1)}, u32[]{:S(2)}, u32[]{:S(2)}) collective-permute-start(bf16[480,640]{1,0:T(8,128)(2,1)} %renorm.1.own_ref.rest_1_), channel_id=1, source_target_pairs={{0,16},{4,20},{8,24},{12,28},{16,0},{20,4},{24,8},{28,12},{1,17},{... | collective-permute-start | bytes 1843208 | tf_op jit(solution)/shard_map/ppermute | solution.py:571
  91.2 62.3 %collective-permute-start.8 = (bf16[480,640]{1,0:T(8,128)(2,1)}, bf16[480,640]{1,0:T(8,128)(2,1)}, u32[]{:S(2)}, u32[]{:S(2)}) collective-permute-start(bf16[480,640]{1,0:T(8,128)(2,1)} %renorm.1.own_ref.rest_1_), channel_id=1, source_target_pairs={{0,4},{4,0},{8,12},{12,8},{16,20},{20,16},{24,28},{28,24},{1,5},{5... | collective-permute-start | bytes 1843208 | tf_op jit(solution)/shard_map/ppermute | solution.py:571
  109.7 24.8 %copy-start.2 = (bf16[480,640]{1,0:T(8,128)(2,1)}, bf16[480,640]{1,0:T(8,128)(2,1)S(1)}, u32[]{:S(2)}) copy-start(bf16[480,640]{1,0:T(8,128)(2,1)S(1)} %collective-permute-done.9.over_x.rest_2_) | copy-start | bytes 1843204
  109.7 43.8 %collective-permute-start.10 = (bf16[480,640]{1,0:T(8,128)(2,1)S(1)}, bf16[480,640]{1,0:T(8,128)(2,1)}, u32[]{:S(2)}, u32[]{:S(2)}) collective-permute-start(bf16[480,640]{1,0:T(8,128)(2,1)S(1)} %collective-permute-done.9.over_x.rest_2_), channel_id=1, source_target_pairs={{0,4},{4,0},{8,12},{12,8},{16,20},{20,16},{24,28},{28,24},{1,5},{5... | collective-permute-start | bytes 1843208 | tf_op jit(solution)/shard_map/ppermute | solution.py:571
  115.0 38.6 %collective-permute-start.12 = (bf16[480,640]{1,0:T(8,128)(2,1)}, bf16[480,640]{1,0:T(8,128)(2,1)}, u32[]{:S(2)}, u32[]{:S(2)}) collective-permute-start(bf16[480,640]{1,0:T(8,128)(2,1)} %collective-permute-done.11.over_y.rest_3_), channel_id=1, source_target_pairs={{0,4},{4,0},{8,12},{12,8},{16,20},{20,16},{24,28},{28,24},{1,5},{5... | collective-permute-start | bytes 1843208 | tf_op jit(solution)/shard_map/ppermute | solution.py:571
  120.1 2.0 %copy-start = (bf16[1024,1280]{1,0:T(8,128)(2,1)}, bf16[1024,1280]{1,0:T(8,128)(2,1)S(1)}, u32[]{:S(2)}) copy-start(bf16[1024,1280]{1,0:T(8,128)(2,1)S(1)} %collective-permute-done.refs_1_.refs_3_) | copy-start | bytes 7864324
  120.1 20.1 %collective-permute-start.13 = (bf16[240,640]{1,0:T(8,128)(2,1)}, bf16[240,640]{1,0:T(8,128)(2,1)S(1)}, u32[]{:S(2)}, u32[]{:S(2)}) collective-permute-start(bf16[240,640]{1,0:T(8,128)(2,1)} %slice.20), channel_id=1, source_target_pairs={{0,8},{4,12},{8,0},{12,4},{16,24},{20,28},{24,16},{28,20},{1,9},{5... | collective-permute-start | bytes 921608 | tf_op jit(solution)/shard_map/ppermute | solution.py:571
  120.4 19.9 %collective-permute-start.15 = (bf16[240,640]{1,0:T(8,128)(2,1)}, bf16[240,640]{1,0:T(8,128)(2,1)}, u32[]{:S(2)}, u32[]{:S(2)}) collective-permute-start(bf16[240,640]{1,0:T(8,128)(2,1)} %slice.21), channel_id=1, source_target_pairs={{0,16},{4,20},{8,24},{12,28},{16,0},{20,4},{24,8},{28,12},{1,17},{... | collective-permute-start | bytes 921608 | tf_op jit(solution)/shard_map/ppermute | solution.py:571
  140.2 6.2 %copy-start.4 = (bf16[240,640]{1,0:T(8,128)(2,1)}, bf16[240,640]{1,0:T(8,128)(2,1)S(1)}, u32[]{:S(2)}) copy-start(bf16[240,640]{1,0:T(8,128)(2,1)S(1)} %collective-permute-done.13.rest_4_) | copy-start | bytes 921604
  140.2 19.0 %collective-permute-start.14 = (bf16[240,640]{1,0:T(8,128)(2,1)S(1)}, bf16[240,640]{1,0:T(8,128)(2,1)S(1)}, u32[]{:S(2)}, u32[]{:S(2)}) collective-permute-start(bf16[240,640]{1,0:T(8,128)(2,1)S(1)} %collective-permute-done.13.rest_4_), channel_id=1, source_target_pairs={{0,4},{4,0},{8,12},{12,8},{16,20},{20,16},{24,28},{28,24},{1,5},{5... | collective-permute-start | bytes 921608 | tf_op jit(solution)/shard_map/ppermute | solution.py:571
  140.3 18.9 %collective-permute-start.16 = (bf16[240,640]{1,0:T(8,128)(2,1)}, bf16[240,640]{1,0:T(8,128)(2,1)S(1)}, u32[]{:S(2)}, u32[]{:S(2)}) collective-permute-start(bf16[240,640]{1,0:T(8,128)(2,1)} %collective-permute-done.15.rest_5_), channel_id=1, source_target_pairs={{0,4},{4,0},{8,12},{12,8},{16,20},{20,16},{24,28},{28,24},{1,5},{5... | collective-permute-start | bytes 921608 | tf_op jit(solution)/shard_map/ppermute | solution.py:571
  159.2 0.7 copy-start.7
  160.0 0.7 copy-start.8

commit v3 on v2

--- a/solution.py
+++ b/solution.py
@@ -14,6 +14,10 @@
 NN = (((1,), (0,)), ((), ()))
 NT = (((1,), (1,)), ((), ()))
 TN = (((0,), (0,)), ((), ()))
+
+
+def room(mib):
+    return pltpu.CompilerParams(vmem_limit_bytes=mib << 20)
 
 
 def mm(a, b, dims=NN):
@@ -164,6 +168,7 @@
         cost_estimate=pl.CostEstimate(
             flops=4 * pairs * HD, bytes_accessed=8 * bq * cols * len(ranges), transcendentals=pairs
         ),
+        compiler_params=room(14),
     )(position, *[job[0] for job in jobs], *[x[0] for x in sources], *[x[2] for x in sources])
 
 
@@ -297,6 +302,7 @@
             flops=12 * rows * F * F, bytes_accessed=rows * F * 4 + F * F * 18, transcendentals=rows * F
         ),
         name="grads",
+        compiler_params=room(40),
     )(*args)
 
 
@@ -328,6 +334,7 @@
         out_shape=jax.ShapeDtypeStruct(shape, jnp.float32),
         cost_estimate=pl.CostEstimate(flops=3 * F * F, bytes_accessed=24 * F * F, transcendentals=0),
         name="turned",
+        compiler_params=room(20),
     )(position, w1, w3, w2)
 
 
@@ -365,6 +372,7 @@
         out_shape=jax.ShapeDtypeStruct((rows, F), jnp.bfloat16),
         cost_estimate=pl.CostEstimate(flops=10 * rows * F, bytes_accessed=12 * rows * F, transcendentals=0),
         name="renorm",
+        compiler_params=room(12),
     )(position, old, *[array for array, _ in upper + lower])
 
 
@@ -405,6 +413,7 @@
             flops=8 * rows * cols, bytes_accessed=6 * rows * cols, transcendentals=rows * cols // HD
         ),
         name="merge",
+        compiler_params=room(8),
     )(position, own, far, own_log, far)
 
 
@@ -473,6 +482,7 @@
             flops=3 * rows * F * F, bytes_accessed=rows * F * 4 + F * F * 3, transcendentals=rows * F
         ),
         name="hidden",
+        compiler_params=room(14),
     )(position, fq, *pieces[:3])
 
 
@@ -563,6 +573,7 @@
             flops=3 * rows * F * F, bytes_accessed=rows * F * 8 + F * F * 6, transcendentals=rows * F
         ),
         name="apply",
+        compiler_params=room(14),
     )(*args)
 
 

time: 168 us -> 156 us (0.929)
  Pallas kernels: 90 us -> 68.3 us
  starting transfers between devices: 51.6 us -> 30.6 us
  waiting for transfers between devices: 15.7 us -> 31.5 us
  local copies, waits for them, and re-layouts: 5.97 us -> 21.2 us
    ppermute x14, starting transfers between devices: 39.2 us -> 19.7 us  [exchange(): return lax.ppermute(block, 'seq', [(i, i ^ 1 << bit) for i in range(size)])]
    unnamed x18 -> x48, local copies, waits for them, and re-layouts: 2.2 us -> 19.8 us
    ppermute x14, waiting for transfers between devices: 15.7 us -> 31.5 us  [exchange(): return lax.ppermute(block, 'seq', [(i, i ^ 1 << bit) for i in range(size)])]
    pallas_call x2, Pallas kernels: 24.2 us -> 19.3 us  [gradients(): pl.pallas_call(body, grid_spec=pltpu.PrefetchScalarGridSpec(num_scalar_pr...]
    pallas_call x2, Pallas kernels: 11.2 us -> 6.46 us  [hidden_part(): pl.pallas_call(functools.partial(hidden_kernel, tm=min(256, half)), grid_...]
    pallas_call x2, Pallas kernels: 14.3 us -> 10.1 us  [apply_head(): pl.pallas_call(functools.partial(apply_kernel, tm=min(256, half), split=s...]
    pallas_call x1, Pallas kernels: 5.1 us -> 1.58 us  [turned(): pl.pallas_call(functools.partial(turn_kernel, parts=parts), grid_spec=plt...]
    slice x2, local copies, waits for them, and re-layouts: 2.48 us -> 0.06 us  [synced_square(): top2, bottom2 = (exchange(over_y[:n], 1), exchange(over_x[n:], 2))]
  transfers between devices with their start and end apart: 17 -> 17, of which waited for: 3 -> 3; matrix products, arithmetic and copies ran while one was open for 5% -> 3% of each run, Pallas kernels for 42% -> 35%
where the time goes in v3:
time: 156 us
  Pallas kernels  68.3 us (44%)
  waiting for transfers between devices  31.5 us (20%)
  starting transfers between devices  30.6 us (20%)
  local copies, waits for them, and re-layouts  21.2 us (14%)
  other arithmetic  3.84 us (2%)
    ppermute x14, waiting for transfers between devices, exchange(): return lax.ppermute(block, 'seq', [(i, i ^ 1 << bit) for i in range(size)])  31.5 us
    pallas_call x2, Pallas kernels, attention(): pl.pallas_call(kernel, grid_spec=pltpu.PrefetchScalarGridSpec(num_scalar_...  24.5 us
    unnamed x48, local copies, waits for them, and re-layouts  19.8 us
    ppermute x14, starting transfers between devices, exchange(): return lax.ppermute(block, 'seq', [(i, i ^ 1 << bit) for i in range(size)])  19.7 us
    pallas_call x2, Pallas kernels, gradients(): pl.pallas_call(body, grid_spec=pltpu.PrefetchScalarGridSpec(num_scalar_pr...  19.3 us
    ppermute x3, starting transfers between devices, shifted(): lax.ppermute(block, 'seq', [(i, i + by) for i in range(size) if 0 <= i +...  10.9 us
    pallas_call x2, Pallas kernels, apply_head(): pl.pallas_call(functools.partial(apply_kernel, tm=min(256, half), split=s...  10.1 us
    pallas_call x2, Pallas kernels, hidden_part(): pl.pallas_call(functools.partial(hidden_kernel, tm=min(256, half)), grid_...  6.46 us
  transfers between devices with their start and end apart: 17, of which 3 were waited for; matrix products, arithmetic and copies ran while one was open for 3% of the time, Pallas kernels for 35%

profile of v3, /device:TPU:0, one launch (start us, length us, event | category | flops | bytes accessed | tf_op | source)
XLA Modules:
  0.0 155.7 jit_solution(16478310348493620446)
XLA Ops:
  0.0 1.9 %copy-done.7 = f32[2,640,640]{2,1,0:T(8,128)S(1)} copy-done((f32[2,640,640]{2,1,0:T(8,128)S(1)}, f32[2,640,640]{2,1,0:T(8,128)}, u32[]{:S(2)}) %copy-start.7) | copy-done | bytes 3276824
  1.9 1.9 %copy-done.9 = f32[2,640,640]{2,1,0:T(8,128)S(1)} copy-done((f32[2,640,640]{2,1,0:T(8,128)S(1)}, f32[2,640,640]{2,1,0:T(8,128)}, u32[]{:S(2)}) %copy-start.9) | copy-done | bytes 3276824
  3.9 1.7 %copy-done.16 = bf16[1024,1280]{1,0:T(8,128)(2,1)S(1)} copy-done((bf16[1024,1280]{1,0:T(8,128)(2,1)S(1)}, bf16[1024,1280]{1,0:T(8,128)(2,1)}, u32[]{:S(2)}) %copy-start.16) | copy-done | bytes 2621464
  5.6 1.7 %copy-done.18 = bf16[1024,1280]{1,0:T(8,128)(2,1)S(1)} copy-done((bf16[1024,1280]{1,0:T(8,128)(2,1)S(1)}, bf16[1024,1280]{1,0:T(8,128)(2,1)}, u32[]{:S(2)}) %copy-start.18) | copy-done | bytes 2621464
  8.0 8.7 %grads.2 = bf16[1920,640]{1,0:T(8,128)(2,1)S(1)} custom-call(s32[1]{0:T(128)} %bitcast.position_ref.s_ref.refs_0_, bf16[1024,1280]{1,0:T(8,128)(2,1)S(1)} %copy-done.16, bf16[1024,1280]{1,0:T(8,128)(2,1)S(1)} %copy-done.18, f32[2,1024]{1,0:T(2,128)S(1)} %bitcast.2, f32[2,640,640]{2,1,0:T(8,128)S(1)} %copy-done.7, f32[2,640,640]{2,1,0:T(8,128)S(1)} %copy-done.9, ...), custom_call_target="tpu_custom_call" | custom-call | flops 5033164800 | bytes 9994240 | tf_op jit(solution)/shard_map/grads/pallas_call | solution.py:291
  20.2 1.7 %pad_maximum_fusion = bf16[1024,1280]{1,0:T(8,128)(2,1)} fusion(bf16[512,1280]{1,0:T(8,128)(2,1)S(1)} %slice-done, bf16[512,1280]{1,0:T(8,128)(2,1)S(1)} %slice-done.1), kind=kLoop, calls=%fused_computation | loop fusion | flops 5242880 | bytes 5242880 | tf_op jit(solution)/shard_map/concatenate | solution.py:645
  21.9 3.5 %collective-permute-start = (bf16[1024,1280]{1,0:T(8,128)(2,1)}, bf16[1024,1280]{1,0:T(8,128)(2,1)S(1)}, u32[]{:S(2)}, u32[]{:S(2)}) collective-permute-start(bf16[1024,1280]{1,0:T(8,128)(2,1)} %pad_maximum_fusion), channel_id=1, source_target_pairs={{0,4},{4,8},{8,12},{12,16},{16,20},{20,24},{24,28},{1,5},{5,9},{9,... | collective-permute-start | bytes 7864328 | tf_op jit(solution)/shard_map/ppermute | solution.py:587
  26.9 1.7 %copy-done.21 = bf16[1920,640]{1,0:T(8,128)(2,1)S(1)} copy-done((bf16[1920,640]{1,0:T(8,128)(2,1)S(1)}, bf16[1920,640]{1,0:T(8,128)(2,1)}, u32[]{:S(2)}) %copy-start.21) | copy-done | bytes 2457624
  28.6 10.6 %grads.3 = (bf16[480,640]{1,0:T(8,128)(2,1)S(1)}, bf16[480,640]{1,0:T(8,128)(2,1)}, bf16[480,640]{1,0:T(8,128)(2,1)S(1)}, bf16[480,640]{1,0:T(8,128)(2,1)}) custom-call(s32[1]{0:T(128)} %bitcast.position_ref.s_ref.refs_0_, bf16[1024,1280]{1,0:T(8,128)(2,1)S(1)} %copy-done.17, bf16[1024,1280]{1,0:T(8,128)(2,1)S(1)} %copy-done.19, f32[2,1024]{1,0:T(2,128)S(1)} %bitcast.3, ...), custom_call_target="tpu_custom_call" | custom-call | flops 5033164800 | bytes 9994240 | tf_op jit(solution)/shard_map/grads/pallas_call | solution.py:291
  39.2 2.3 %collective-permute-start.4 = (bf16[480,640]{1,0:T(8,128)(2,1)}, bf16[480,640]{1,0:T(8,128)(2,1)}, u32[]{:S(2)}, u32[]{:S(2)}) collective-permute-start(bf16[480,640]{1,0:T(8,128)(2,1)} %get-tuple-element.16), channel_id=1, source_target_pairs={{0,8},{4,12},{8,0},{12,4},{16,24},{20,28},{24,16},{28,20},{1,9},{5... | collective-permute-start | bytes 1843208 | tf_op jit(solution)/shard_map/ppermute | solution.py:582
  41.5 2.6 %collective-permute-start.6 = (bf16[480,640]{1,0:T(8,128)(2,1)}, bf16[480,640]{1,0:T(8,128)(2,1)}, u32[]{:S(2)}, u32[]{:S(2)}) collective-permute-start(bf16[480,640]{1,0:T(8,128)(2,1)} %get-tuple-element.18), channel_id=1, source_target_pairs={{0,16},{4,20},{8,24},{12,28},{16,0},{20,4},{24,8},{28,12},{1,17},{... | collective-permute-start | bytes 1843208 | tf_op jit(solution)/shard_map/ppermute | solution.py:582
  44.1 1.7 %copy-done.5 = bf16[1024,1280]{1,0:T(8,128)(2,1)S(1)} copy-done((bf16[1024,1280]{1,0:T(8,128)(2,1)S(1)}, bf16[1024,1280]{1,0:T(8,128)(2,1)}, u32[]{:S(2)}) %copy-start.5) | copy-done | bytes 2621464
  45.8 13.5 %shard_map.101 = (bf16[512,1408]{1,0:T(8,128)(2,1)}, bf16[512,1280]{1,0:T(8,128)(2,1)S(1)}, f32[512,128]{1,0:T(8,128)S(1)}) custom-call(s32[1]{0:T(128)} %bitcast.position_ref.s_ref.refs_0_, bf16[512,1280]{1,0:T(8,128)(2,1)} %collective-permute-done.1.refs_0_, bf16[1024,1280]{1,0:T(8,128)(2,1)S(1)} %copy-done.1, bf16[1024,1280]{1,0:T(8,128)(2,1)S(1)} %copy-done.5, ...), custom_call_target="tpu_custom_call" | custom-call | flops 3355443200 | bytes 10485760 | tf_op jit(solution)/shard_map/pallas_call | solution.py:158
  60.4 5.8 %collective-permute-start.2 = (bf16[512,1408]{1,0:T(8,128)(2,1)}, bf16[512,1408]{1,0:T(8,128)(2,1)}, u32[]{:S(2)}, u32[]{:S(2)}) collective-permute-start(bf16[512,1408]{1,0:T(8,128)(2,1)} %get-tuple-element.13), channel_id=1, source_target_pairs={{0,4},{4,8},{8,12},{12,16},{16,20},{20,24},{24,28},{1,5},{5,9},{9,... | collective-permute-start | bytes 4325384 | tf_op jit(solution)/shard_map/ppermute | solution.py:587
  67.3 2.4 %collective-permute-start.5 = (bf16[240,640]{1,0:T(8,128)(2,1)S(1)}, bf16[240,640]{1,0:T(8,128)(2,1)S(1)}, u32[]{:S(2)}, u32[]{:S(2)}) collective-permute-start(bf16[240,640]{1,0:T(8,128)(2,1)S(1)} %add_convert_fusion.1), channel_id=1, source_target_pairs={{0,16},{4,20},{8,24},{12,28},{16,0},{20,4},{24,8},{28,12},{1,17},{... | collective-permute-start | bytes 921608 | tf_op jit(solution)/shard_map/ppermute | solution.py:582
  69.7 9.0 %collective-permute-done.6.refs_4_ = bf16[480,640]{1,0:T(8,128)(2,1)} collective-permute-done((bf16[480,640]{1,0:T(8,128)(2,1)}, bf16[480,640]{1,0:T(8,128)(2,1)}, u32[]{:S(2)}, u32[]{:S(2)}) %collective-permute-start.6) | collective-permute-done | bytes 614432 | tf_op jit(solution)/shard_map/ppermute | solution.py:582
  79.9 1.9 %copy-done.8 = f32[2,640,640]{2,1,0:T(8,128)S(1)} copy-done((f32[2,640,640]{2,1,0:T(8,128)S(1)}, f32[2,640,640]{2,1,0:T(8,128)}, u32[]{:S(2)}) %copy-start.8) | copy-done | bytes 3276824
  81.8 1.9 %copy-done.10 = f32[2,640,640]{2,1,0:T(8,128)S(1)} copy-done((f32[2,640,640]{2,1,0:T(8,128)S(1)}, f32[2,640,640]{2,1,0:T(8,128)}, u32[]{:S(2)}) %copy-start.10) | copy-done | bytes 3276824
  83.8 1.9 %copy-done.11 = f32[2,640,640]{2,1,0:T(8,128)S(1)} copy-done((f32[2,640,640]{2,1,0:T(8,128)S(1)}, f32[2,640,640]{2,1,0:T(8,128)}, u32[]{:S(2)}) %copy-start.11) | copy-done | bytes 3276824
  87.3 12.4 %collective-permute-done.5.refs_2_ = bf16[240,640]{1,0:T(8,128)(2,1)S(1)} collective-permute-done((bf16[240,640]{1,0:T(8,128)(2,1)S(1)}, bf16[240,640]{1,0:T(8,128)(2,1)S(1)}, u32[]{:S(2)}, u32[]{:S(2)}) %collective-permute-start.5) | collective-permute-done | bytes 307232 | tf_op jit(solution)/shard_map/ppermute | solution.py:582
  99.8 1.7 %renorm.1.own_ref.rest_1_ = bf16[480,640]{1,0:T(8,128)(2,1)S(1)} custom-call(s32[1]{0:T(128)} %bitcast.position_ref.s_ref.refs_0_, f32[480,640]{1,0:T(8,128)S(1)} %turned.1.old_ref, bf16[480,640]{1,0:T(8,128)(2,1)S(1)} %get-tuple-element.15.refs_0_, bf16[480,640]{1,0:T(8,128)(2,1)} %collective-permute-done.4.refs_1_, ...), custom_call_target="tpu_custom_call" | custom-call | flops 3072000 | bytes 3686400 | tf_op jit(solution)/shard_map/renorm/pallas_call | solution.py:364
  101.5 2.5 %collective-permute-start.11 = (bf16[480,640]{1,0:T(8,128)(2,1)S(1)}, bf16[480,640]{1,0:T(8,128)(2,1)S(1)}, u32[]{:S(2)}, u32[]{:S(2)}) collective-permute-start(bf16[480,640]{1,0:T(8,128)(2,1)S(1)} %renorm.1.own_ref.rest_1_), channel_id=1, source_target_pairs={{0,16},{4,20},{8,24},{12,28},{16,0},{20,4},{24,8},{28,12},{1,17},{... | collective-permute-start | bytes 1843208 | tf_op jit(solution)/shard_map/ppermute | solution.py:582
  104.1 2.8 %collective-permute-start.8 = (bf16[480,640]{1,0:T(8,128)(2,1)S(1)}, bf16[480,640]{1,0:T(8,128)(2,1)S(1)}, u32[]{:S(2)}, u32[]{:S(2)}) collective-permute-start(bf16[480,640]{1,0:T(8,128)(2,1)S(1)} %renorm.1.own_ref.rest_1_), channel_id=1, source_target_pairs={{0,4},{4,0},{8,12},{12,8},{16,20},{20,16},{24,28},{28,24},{1,5},{5... | collective-permute-start | bytes 1843208 | tf_op jit(solution)/shard_map/ppermute | solution.py:582
  106.9 10.0 %collective-permute-done.9.over_x.rest_2_ = bf16[480,640]{1,0:T(8,128)(2,1)S(1)} collective-permute-done((bf16[480,640]{1,0:T(8,128)(2,1)S(1)}, bf16[480,640]{1,0:T(8,128)(2,1)S(1)}, u32[]{:S(2)}, u32[]{:S(2)}) %collective-permute-start.9) | collective-permute-done | bytes 614432 | tf_op jit(solution)/shard_map/ppermute | solution.py:582
  118.7 2.0 %collective-permute-start.13 = (bf16[240,640]{1,0:T(8,128)(2,1)S(1)}, bf16[240,640]{1,0:T(8,128)(2,1)S(1)}, u32[]{:S(2)}, u32[]{:S(2)}) collective-permute-start(bf16[240,640]{1,0:T(8,128)(2,1)S(1)} %slice.20), channel_id=1, source_target_pairs={{0,8},{4,12},{8,0},{12,4},{16,24},{20,28},{24,16},{28,20},{1,9},{5... | collective-permute-start | bytes 921608 | tf_op jit(solution)/shard_map/ppermute | solution.py:582
  120.7 2.0 %collective-permute-start.15 = (bf16[240,640]{1,0:T(8,128)(2,1)S(1)}, bf16[240,640]{1,0:T(8,128)(2,1)S(1)}, u32[]{:S(2)}, u32[]{:S(2)}) collective-permute-start(bf16[240,640]{1,0:T(8,128)(2,1)S(1)} %slice.21), channel_id=1, source_target_pairs={{0,16},{4,20},{8,24},{12,28},{16,0},{20,4},{24,8},{28,12},{1,17},{... | collective-permute-start | bytes 921608 | tf_op jit(solution)/shard_map/ppermute | solution.py:582
  122.8 11.0 %shard_map.100.high_ref = bf16[512,1280]{1,0:T(8,128)(2,1)S(1)} custom-call(s32[1]{0:T(128)} %bitcast.position_ref.s_ref.refs_0_, bf16[1024,1280]{1,0:T(8,128)(2,1)S(1)} %copy-done.2, bf16[1024,1280]{1,0:T(8,128)(2,1)S(1)} %collective-permute-done.refs_1_.refs_3_, bf16[1024,1280]{1,0:T(8,128)(2,1)S(1)} %copy-done.6, ...), custom_call_target="tpu_custom_call" | custom-call | flops 3355443200 | bytes 10485760 | tf_op jit(solution)/shard_map/pallas_call | solution.py:158
  133.8 4.7 %merge.1.low_ref = bf16[512,1280]{1,0:T(8,128)(2,1)S(1)} custom-call(s32[1]{0:T(128)} %bitcast.position_ref.s_ref.refs_0_, bf16[512,1280]{1,0:T(8,128)(2,1)S(1)} %copy-done.15, bf16[512,1408]{1,0:T(8,128)(2,1)} %collective-permute-done.2.far_ref.far_log, f32[512,128]{1,0:T(8,128)S(1)} %get-tuple-element.14.own_log, ...), custom_call_target="tpu_custom_call" | custom-call | flops 5242880 | bytes 3932160 | tf_op jit(solution)/shard_map/merge/pallas_call | solution.py:403
  139.1 3.2 %hidden.3.rest_0_ = bf16[1024,640]{1,0:T(8,128)(2,1)S(1)} custom-call(s32[1]{0:T(128)} %bitcast.position_ref.s_ref.refs_0_, bf16[1024,1280]{1,0:T(8,128)(2,1)S(1)} %copy-done, bf16[480,640]{1,0:T(8,128)(2,1)S(1)} %renorm.1.own_ref.rest_1_, bf16[480,640]{1,0:T(8,128)(2,1)S(1)} %collective-permute-done.9.over_x.rest_2_, ...), custom_call_target="tpu_custom_call" | custom-call | flops 1258291200 | bytes 3850240 | tf_op jit(solution)/shard_map/hidden/pallas_call | solution.py:471
  142.3 5.0 %apply.2.rest_6_ = bf16[1024,1280]{1,0:T(8,128)(2,1)} custom-call(s32[1]{0:T(128)} %bitcast.position_ref.s_ref.refs_0_, bf16[1024,1280]{1,0:T(8,128)(2,1)S(1)} %copy-done, bf16[512,1280]{1,0:T(8,128)(2,1)S(1)} %shard_map.100.high_ref, bf16[512,1280]{1,0:T(8,128)(2,1)S(1)} %merge.1.low_ref, bf16[1024,640]{1,0:T(8,128)(2,1)S(1)} %hidden.3.rest_0_, ...), custom_call_target="tpu_custom_call" | custom-call | flops 1258291200 | bytes 7700480 | tf_op jit(solution)/shard_map/apply/pallas_call | solution.py:556
  147.4 3.2 %hidden.2.rest_0_ = bf16[1024,640]{1,0:T(8,128)(2,1)S(1)} custom-call(s32[1]{0:T(128)} %bitcast.position_ref.s_ref.refs_0_, bf16[1024,1280]{1,0:T(8,128)(2,1)S(1)} %copy-done, bf16[480,640]{1,0:T(8,128)(2,1)S(1)} %collective-permute-done.8.own_ref.rest_1_, bf16[480,640]{1,0:T(8,128)(2,1)S(1)} %collective-permute-done.10.over_x.rest_2_, ...), custom_call_target="tpu_custom_call" | custom-call | flops 1258291200 | bytes 3850240 | tf_op jit(solution)/shard_map/hidden/pallas_call | solution.py:471
  150.6 5.0 %apply.3 = bf16[1024,1280]{1,0:T(8,128)(2,1)} custom-call(s32[1]{0:T(128)} %bitcast.position_ref.s_ref.refs_0_, bf16[1024,1280]{1,0:T(8,128)(2,1)S(1)} %copy-done, bf16[512,1280]{1,0:T(8,128)(2,1)S(1)} %shard_map.100.high_ref, bf16[512,1280]{1,0:T(8,128)(2,1)S(1)} %merge.1.low_ref, ...), custom_call_target="tpu_custom_call", output_to_operand_aliasing={{}: (10, {})} | custom-call | flops 1258291200 | bytes 7700480 | tf_op jit(solution)/shard_map/apply/pallas_call | solution.py:556
  (71 shorter events, 13.1 us)
Async XLA Ops:
  0.0 1.9 %copy-start.7 = (f32[2,640,640]{2,1,0:T(8,128)S(1)}, f32[2,640,640]{2,1,0:T(8,128)}, u32[]{:S(2)}) copy-start(f32[2,640,640]{2,1,0:T(8,128)} %refs_4_.5) | copy-start | bytes 9830404
  1.9 1.9 %copy-start.9 = (f32[2,640,640]{2,1,0:T(8,128)S(1)}, f32[2,640,640]{2,1,0:T(8,128)}, u32[]{:S(2)}) copy-start(f32[2,640,640]{2,1,0:T(8,128)} %refs_5_.3) | copy-start | bytes 9830404
  8.0 9.3 %copy-start.1 = (bf16[1024,1280]{1,0:T(8,128)(2,1)S(1)}, bf16[1024,1280]{1,0:T(8,128)(2,1)}, u32[]{:S(2)}) copy-start(bf16[1024,1280]{1,0:T(8,128)(2,1)} %refs_1_.3) | copy-start | bytes 7864324
  16.8 8.7 %collective-permute-start.3 = (bf16[1920,640]{1,0:T(8,128)(2,1)S(1)}, bf16[1920,640]{1,0:T(8,128)(2,1)S(1)}, u32[]{:S(2)}, u32[]{:S(2)}) collective-permute-start(bf16[1920,640]{1,0:T(8,128)(2,1)S(1)} %grads.2), channel_id=1, source_target_pairs={{0,4},{4,0},{8,12},{12,8},{16,20},{20,16},{24,28},{28,24},{1,5},{5... | collective-permute-start | bytes 7372808 | tf_op jit(solution)/shard_map/ppermute | solution.py:582
  18.5 25.6 %collective-permute-start.1 = (bf16[512,1280]{1,0:T(8,128)(2,1)}, bf16[512,1280]{1,0:T(8,128)(2,1)}, u32[]{:S(2)}, u32[]{:S(2)}) collective-permute-start(bf16[512,1280]{1,0:T(8,128)(2,1)} %slice.17), channel_id=1, source_target_pairs={{4,0},{8,4},{12,8},{16,12},{20,16},{24,20},{28,24},{5,1},{9,5},{13... | collective-permute-start | bytes 3932168 | tf_op jit(solution)/shard_map/ppermute | solution.py:587
  20.1 6.8 %copy-start.23 = (f32[1024,2]{0,1:T(2,128)S(1)}, f32[1024,2]{0,1:T(2,128)}, u32[]{:S(2)}) copy-start(f32[1024,2]{0,1:T(2,128)} %param.16) | copy-start | bytes 24580
  20.2 6.6 %copy-start.17 = (bf16[1024,1280]{1,0:T(8,128)(2,1)S(1)}, bf16[1024,1280]{1,0:T(8,128)(2,1)}, u32[]{:S(2)}) copy-start(bf16[1024,1280]{1,0:T(8,128)(2,1)} %refs_1_.5) | copy-start | bytes 7864324
  20.2 6.6 %copy-start.19 = (bf16[1024,1280]{1,0:T(8,128)(2,1)S(1)}, bf16[1024,1280]{1,0:T(8,128)(2,1)}, u32[]{:S(2)}) copy-start(bf16[1024,1280]{1,0:T(8,128)(2,1)} %refs_2_.7) | copy-start | bytes 7864324
  21.9 22.2 %copy-start.3 = (bf16[1024,1280]{1,0:T(8,128)(2,1)S(1)}, bf16[1024,1280]{1,0:T(8,128)(2,1)}, u32[]{:S(2)}) copy-start(bf16[1024,1280]{1,0:T(8,128)(2,1)} %refs_3_.1) | copy-start | bytes 7864324
  21.9 96.8 %collective-permute-start = (bf16[1024,1280]{1,0:T(8,128)(2,1)}, bf16[1024,1280]{1,0:T(8,128)(2,1)S(1)}, u32[]{:S(2)}, u32[]{:S(2)}) collective-permute-start(bf16[1024,1280]{1,0:T(8,128)(2,1)} %pad_maximum_fusion), channel_id=1, source_target_pairs={{0,4},{4,8},{8,12},{12,16},{16,20},{20,24},{24,28},{1,5},{5,9},{9,... | collective-permute-start | bytes 7864328 | tf_op jit(solution)/shard_map/ppermute | solution.py:587
  39.2 20.2 %copy-start.12 = (bf16[480,640]{1,0:T(8,128)(2,1)}, bf16[480,640]{1,0:T(8,128)(2,1)S(1)}, u32[]{:S(2)}) copy-start(bf16[480,640]{1,0:T(8,128)(2,1)S(1)} %get-tuple-element.17.refs_3_) | copy-start | bytes 1843204
  39.2 27.1 %collective-permute-start.4 = (bf16[480,640]{1,0:T(8,128)(2,1)}, bf16[480,640]{1,0:T(8,128)(2,1)}, u32[]{:S(2)}, u32[]{:S(2)}) collective-permute-start(bf16[480,640]{1,0:T(8,128)(2,1)} %get-tuple-element.16), channel_id=1, source_target_pairs={{0,8},{4,12},{8,0},{12,4},{16,24},{20,28},{24,16},{28,20},{1,9},{5... | collective-permute-start | bytes 1843208 | tf_op jit(solution)/shard_map/ppermute | solution.py:582
  41.5 37.2 %collective-permute-start.6 = (bf16[480,640]{1,0:T(8,128)(2,1)}, bf16[480,640]{1,0:T(8,128)(2,1)}, u32[]{:S(2)}, u32[]{:S(2)}) collective-permute-start(bf16[480,640]{1,0:T(8,128)(2,1)} %get-tuple-element.18), channel_id=1, source_target_pairs={{0,16},{4,20},{8,24},{12,28},{16,0},{20,4},{24,8},{28,12},{1,17},{... | collective-permute-start | bytes 1843208 | tf_op jit(solution)/shard_map/ppermute | solution.py:582
  60.4 60.3 %collective-permute-start.2 = (bf16[512,1408]{1,0:T(8,128)(2,1)}, bf16[512,1408]{1,0:T(8,128)(2,1)}, u32[]{:S(2)}, u32[]{:S(2)}) collective-permute-start(bf16[512,1408]{1,0:T(8,128)(2,1)} %get-tuple-element.13), channel_id=1, source_target_pairs={{0,4},{4,8},{8,12},{12,16},{16,20},{20,24},{24,28},{1,5},{5,9},{9,... | collective-permute-start | bytes 4325384 | tf_op jit(solution)/shard_map/ppermute | solution.py:587
  67.3 32.5 %collective-permute-start.5 = (bf16[240,640]{1,0:T(8,128)(2,1)S(1)}, bf16[240,640]{1,0:T(8,128)(2,1)S(1)}, u32[]{:S(2)}, u32[]{:S(2)}) collective-permute-start(bf16[240,640]{1,0:T(8,128)(2,1)S(1)} %add_convert_fusion.1), channel_id=1, source_target_pairs={{0,16},{4,20},{8,24},{12,28},{16,0},{20,4},{24,8},{28,12},{1,17},{... | collective-permute-start | bytes 921608 | tf_op jit(solution)/shard_map/ppermute | solution.py:582
  79.8 19.9 %collective-permute-start.7 = (bf16[240,640]{1,0:T(8,128)(2,1)S(1)}, bf16[240,640]{1,0:T(8,128)(2,1)S(1)}, u32[]{:S(2)}, u32[]{:S(2)}) collective-permute-start(bf16[240,640]{1,0:T(8,128)(2,1)S(1)} %add_convert_fusion), channel_id=1, source_target_pairs={{0,8},{4,12},{8,0},{12,4},{16,24},{20,28},{24,16},{28,20},{1,9},{5... | collective-permute-start | bytes 921608 | tf_op jit(solution)/shard_map/ppermute | solution.py:582
  79.9 1.9 %copy-start.8 = (f32[2,640,640]{2,1,0:T(8,128)S(1)}, f32[2,640,640]{2,1,0:T(8,128)}, u32[]{:S(2)}) copy-start(f32[2,640,640]{2,1,0:T(8,128)} %refs_4_.5) | copy-start | bytes 9830404
  85.7 14.1 %copy-start.13 = (bf16[480,640]{1,0:T(8,128)(2,1)S(1)}, bf16[480,640]{1,0:T(8,128)(2,1)}, u32[]{:S(2)}) copy-start(bf16[480,640]{1,0:T(8,128)(2,1)} %copy-done.12) | copy-start | bytes 1843204
  85.7 37.0 %copy-start.6 = (bf16[1024,1280]{1,0:T(8,128)(2,1)S(1)}, bf16[1024,1280]{1,0:T(8,128)(2,1)}, u32[]{:S(2)}) copy-start(bf16[1024,1280]{1,0:T(8,128)(2,1)} %refs_2_.5) | copy-start | bytes 7864324
  87.3 35.5 %copy-start.2 = (bf16[1024,1280]{1,0:T(8,128)(2,1)S(1)}, bf16[1024,1280]{1,0:T(8,128)(2,1)}, u32[]{:S(2)}) copy-start(bf16[1024,1280]{1,0:T(8,128)(2,1)} %refs_1_.3) | copy-start | bytes 7864324
  87.3 35.4 %copy-start.4 = (bf16[1024,1280]{1,0:T(8,128)(2,1)S(1)}, bf16[1024,1280]{1,0:T(8,128)(2,1)}, u32[]{:S(2)}) copy-start(bf16[1024,1280]{1,0:T(8,128)(2,1)} %refs_3_.1) | copy-start | bytes 7864324
  101.5 15.4 %collective-permute-start.9 = (bf16[480,640]{1,0:T(8,128)(2,1)S(1)}, bf16[480,640]{1,0:T(8,128)(2,1)S(1)}, u32[]{:S(2)}, u32[]{:S(2)}) collective-permute-start(bf16[480,640]{1,0:T(8,128)(2,1)S(1)} %renorm.1.own_ref.rest_1_), channel_id=1, source_target_pairs={{0,8},{4,12},{8,0},{12,4},{16,24},{20,28},{24,16},{28,20},{1,9},{5... | collective-permute-start | bytes 1843208 | tf_op jit(solution)/shard_map/ppermute | solution.py:582
  101.5 16.5 %collective-permute-start.11 = (bf16[480,640]{1,0:T(8,128)(2,1)S(1)}, bf16[480,640]{1,0:T(8,128)(2,1)S(1)}, u32[]{:S(2)}, u32[]{:S(2)}) collective-permute-start(bf16[480,640]{1,0:T(8,128)(2,1)S(1)} %renorm.1.own_ref.rest_1_), channel_id=1, source_target_pairs={{0,16},{4,20},{8,24},{12,28},{16,0},{20,4},{24,8},{28,12},{1,17},{... | collective-permute-start | bytes 1843208 | tf_op jit(solution)/shard_map/ppermute | solution.py:582
  104.1 43.3 %collective-permute-start.8 = (bf16[480,640]{1,0:T(8,128)(2,1)S(1)}, bf16[480,640]{1,0:T(8,128)(2,1)S(1)}, u32[]{:S(2)}, u32[]{:S(2)}) collective-permute-start(bf16[480,640]{1,0:T(8,128)(2,1)S(1)} %renorm.1.own_ref.rest_1_), channel_id=1, source_target_pairs={{0,4},{4,0},{8,12},{12,8},{16,20},{20,16},{24,28},{28,24},{1,5},{5... | collective-permute-start | bytes 1843208 | tf_op jit(solution)/shard_map/ppermute | solution.py:582
  116.8 30.5 %collective-permute-start.10 = (bf16[480,640]{1,0:T(8,128)(2,1)S(1)}, bf16[480,640]{1,0:T(8,128)(2,1)S(1)}, u32[]{:S(2)}, u32[]{:S(2)}) collective-permute-start(bf16[480,640]{1,0:T(8,128)(2,1)S(1)} %collective-permute-done.9.over_x.rest_2_), channel_id=1, source_target_pairs={{0,4},{4,0},{8,12},{12,8},{16,20},{20,16},{24,28},{28,24},{1,5},{5... | collective-permute-start | bytes 1843208 | tf_op jit(solution)/shard_map/ppermute | solution.py:582
  118.1 29.3 %collective-permute-start.12 = (bf16[480,640]{1,0:T(8,128)(2,1)S(1)}, bf16[480,640]{1,0:T(8,128)(2,1)S(1)}, u32[]{:S(2)}, u32[]{:S(2)}) collective-permute-start(bf16[480,640]{1,0:T(8,128)(2,1)S(1)} %collective-permute-done.11.over_y.rest_3_), channel_id=1, source_target_pairs={{0,4},{4,0},{8,12},{12,8},{16,20},{20,16},{24,28},{28,24},{1,5},{5... | collective-permute-start | bytes 1843208 | tf_op jit(solution)/shard_map/ppermute | solution.py:582
  118.7 15.1 %copy-start.15 = (bf16[512,1280]{1,0:T(8,128)(2,1)S(1)}, bf16[512,1280]{1,0:T(8,128)(2,1)}, u32[]{:S(2)}) copy-start(bf16[512,1280]{1,0:T(8,128)(2,1)} %copy-done.14) | copy-start | bytes 3932164
  118.7 19.8 %collective-permute-start.13 = (bf16[240,640]{1,0:T(8,128)(2,1)S(1)}, bf16[240,640]{1,0:T(8,128)(2,1)S(1)}, u32[]{:S(2)}, u32[]{:S(2)}) collective-permute-start(bf16[240,640]{1,0:T(8,128)(2,1)S(1)} %slice.20), channel_id=1, source_target_pairs={{0,8},{4,12},{8,0},{12,4},{16,24},{20,28},{24,16},{28,20},{1,9},{5... | collective-permute-start | bytes 921608 | tf_op jit(solution)/shard_map/ppermute | solution.py:582
  120.7 17.9 %collective-permute-start.15 = (bf16[240,640]{1,0:T(8,128)(2,1)S(1)}, bf16[240,640]{1,0:T(8,128)(2,1)S(1)}, u32[]{:S(2)}, u32[]{:S(2)}) collective-permute-start(bf16[240,640]{1,0:T(8,128)(2,1)S(1)} %slice.21), channel_id=1, source_target_pairs={{0,16},{4,20},{8,24},{12,28},{16,0},{20,4},{24,8},{28,12},{1,17},{... | collective-permute-start | bytes 921608 | tf_op jit(solution)/shard_map/ppermute | solution.py:582
  133.8 5.3 %copy-start = (bf16[1024,1280]{1,0:T(8,128)(2,1)S(1)}, bf16[1024,1280]{1,0:T(8,128)(2,1)}, u32[]{:S(2)}) copy-start(bf16[1024,1280]{1,0:T(8,128)(2,1)} %q_ref.7) | copy-start | bytes 7864324
  138.5 12.1 %collective-permute-start.14 = (bf16[240,640]{1,0:T(8,128)(2,1)S(1)}, bf16[240,640]{1,0:T(8,128)(2,1)S(1)}, u32[]{:S(2)}, u32[]{:S(2)}) collective-permute-start(bf16[240,640]{1,0:T(8,128)(2,1)S(1)} %collective-permute-done.13.rest_4_), channel_id=1, source_target_pairs={{0,4},{4,0},{8,12},{12,8},{16,20},{20,16},{24,28},{28,24},{1,5},{5... | collective-permute-start | bytes 921608 | tf_op jit(solution)/shard_map/ppermute | solution.py:582
  138.6 12.0 %collective-permute-start.16 = (bf16[240,640]{1,0:T(8,128)(2,1)S(1)}, bf16[240,640]{1,0:T(8,128)(2,1)S(1)}, u32[]{:S(2)}, u32[]{:S(2)}) collective-permute-start(bf16[240,640]{1,0:T(8,128)(2,1)S(1)} %collective-permute-done.15.rest_5_), channel_id=1, source_target_pairs={{0,4},{4,0},{8,12},{12,8},{16,20},{20,16},{24,28},{28,24},{1,5},{5... | collective-permute-start | bytes 921608 | tf_op jit(solution)/shard_map/ppermute | solution.py:582
  (11 other events, 17.3 us)

commit v4 on v3

--- a/solution.py
+++ b/solution.py
@@ -260,9 +260,10 @@
     F = w1.shape[1]
     tm = min(256, rows)
     tn = 256 if 2 * F % 256 == 0 else HD
-    col = pl.BlockSpec((rows, F), lambda i, s: (0, head(s)))
-    weight = pl.BlockSpec((1, F, F), lambda i, s: (head(s), 0, 0))
-    whole = lambda *shape: pl.BlockSpec(shape, lambda i, s: (0,) * len(shape))
+    once = dict(pipeline_mode=pl.Buffered(1))
+    col = pl.BlockSpec((rows, F), lambda i, s: (0, head(s)), **once)
+    weight = pl.BlockSpec((1, F, F), lambda i, s: (head(s), 0, 0), **once)
+    whole = lambda *shape: pl.BlockSpec(shape, lambda i, s: (0,) * len(shape), **once)
     bf = jnp.bfloat16
     args = [position, fk, fv, rates_t, w1, w3, w2]
     specs = [col, col, whole(*rates_t.shape), weight, weight, weight]
@@ -302,7 +303,7 @@
             flops=12 * rows * F * F, bytes_accessed=rows * F * 4 + F * F * 18, transcendentals=rows * F
         ),
         name="grads",
-        compiler_params=room(40),
+        compiler_params=room(40 if received is None else 36),
     )(*args)
 
 
@@ -645,7 +646,10 @@
     prev = shifted(jnp.concatenate([attn_k[half:], attn_v[half:]], axis=0), 1)
     guests = shifted(attn_q[:half], -1)
     rates_t = rates.T
-    weights = (fast_gate, fast_up, fast_down)
+    stay = lambda a: pltpu.with_memory_space_constraint(a, pltpu.HBM)
+    attn_q, attn_k, attn_v = stay(attn_q), stay(attn_k), stay(attn_v)
+    fast_k, fast_v = stay(fast_k), stay(fast_v)
+    weights = (stay(fast_gate), stay(fast_up), stay(fast_down))
 
     def grads(head, received=None):
         return gradients(position, head, fast_k, fast_v, rates_t, *weights, received)

time: 156 us -> 150 us (0.962)
  starting transfers between devices: 30.6 us -> 53.4 us
  local copies, waits for them, and re-layouts: 21.2 us -> 2.18 us
  waiting for transfers between devices: 31.5 us -> 15.7 us
  Pallas kernels: 68.3 us -> 74 us
    ppermute x14, starting transfers between devices: 19.7 us -> 39.9 us  [exchange(): return lax.ppermute(block, 'seq', [(i, i ^ 1 << bit) for i in range(size)])]
    unnamed x48 -> x16, local copies, waits for them, and re-layouts: 19.8 us -> 1.78 us
    ppermute x14, waiting for transfers between devices: 31.5 us -> 15.7 us  [exchange(): return lax.ppermute(block, 'seq', [(i, i ^ 1 << bit) for i in range(size)])]
    ppermute x3, starting transfers between devices: 10.9 us -> 13.5 us  [shifted(): lax.ppermute(block, 'seq', [(i, i + by) for i in range(size) if 0 <= i +...]
    pallas_call x2, Pallas kernels: 19.3 us -> 21.9 us  [gradients(): pl.pallas_call(body, grid_spec=pltpu.PrefetchScalarGridSpec(num_scalar_pr...]
    pallas_call x1, Pallas kernels: 1.58 us -> 4.05 us  [turned(): pl.pallas_call(functools.partial(turn_kernel, parts=parts), grid_spec=plt...]
  transfers between devices with their start and end apart: 17 -> 17, of which waited for: 3 -> 3; matrix products, arithmetic and copies ran while one was open for 3% -> 3% of each run, Pallas kernels for 35% -> 39%
where the time goes in v4:
time: 150 us; the launch traced here: 149 us
  Pallas kernels  74 us (49%)
  starting transfers between devices  53.4 us (36%)
  waiting for transfers between devices  15.7 us (10%)
  other arithmetic  3.84 us (3%)
  local copies, waits for them, and re-layouts  2.18 us (1%)
    ppermute x14, starting transfers between devices, exchange(): return lax.ppermute(block, 'seq', [(i, i ^ 1 << bit) for i in range(size)])  39.9 us
    pallas_call x2, Pallas kernels, attention(): pl.pallas_call(kernel, grid_spec=pltpu.PrefetchScalarGridSpec(num_scalar_...  25.3 us
    pallas_call x2, Pallas kernels, gradients(): pl.pallas_call(body, grid_spec=pltpu.PrefetchScalarGridSpec(num_scalar_pr...  21.9 us
    ppermute x14, waiting for transfers between devices, exchange(): return lax.ppermute(block, 'seq', [(i, i ^ 1 << bit) for i in range(size)])  15.7 us
    ppermute x3, starting transfers between devices, shifted(): lax.ppermute(block, 'seq', [(i, i + by) for i in range(size) if 0 <= i +...  13.5 us
    pallas_call x2, Pallas kernels, apply_head(): pl.pallas_call(functools.partial(apply_kernel, tm=min(256, half), split=s...  10 us
    pallas_call x2, Pallas kernels, hidden_part(): pl.pallas_call(functools.partial(hidden_kernel, tm=min(256, half)), grid_...  6.46 us
    pallas_call x1, Pallas kernels, merged(): pl.pallas_call(functools.partial(merge_kernel, stride=log_stride_of(cols)...  4.7 us
  transfers between devices with their start and end apart: 17, of which 3 were waited for; matrix products, arithmetic and copies ran while one was open for 3% of the time, Pallas kernels for 39%

profile of v4, /device:TPU:0, one launch (start us, length us, event | category | flops | bytes accessed | tf_op | source)
XLA Modules:
  0.0 149.5 jit_solution(14798085279717968729)
XLA Ops:
  0.0 0.7 copy-done.5
  0.7 10.2 %grads.2 = bf16[1920,640]{1,0:T(8,128)(2,1)S(1)} custom-call(s32[1]{0:T(128)} %bitcast.position_ref.s_ref.refs_0_, bf16[1024,1280]{1,0:T(8,128)(2,1)} %refs_1_.5, bf16[1024,1280]{1,0:T(8,128)(2,1)} %refs_2_.7, f32[2,1024]{1,0:T(2,128)S(1)} %bitcast.2, f32[2,640,640]{2,1,0:T(8,128)} %refs_4_.5, f32[2,640,640]{2,1,0:T(8,128)} %refs_5_.3, f32[2,640,640]{2,1,0:T(8,128)} %refs_6_.3), custom_call_target="tpu_custom_call" | custom-call | flops 5033164800 | bytes 9994240 | tf_op jit(solution)/shard_map/grads/pallas_call | solution.py:292
  10.9 0.6 collective-permute-start.3
  11.6 1.4 collective-permute-start.1
  13.3 1.7 %pad_maximum_fusion = bf16[1024,1280]{1,0:T(8,128)(2,1)} fusion(bf16[512,1280]{1,0:T(8,128)(2,1)S(1)} %slice-done, bf16[512,1280]{1,0:T(8,128)(2,1)S(1)} %slice-done.1), kind=kLoop, calls=%fused_computation | loop fusion | flops 5242880 | bytes 5242880 | tf_op jit(solution)/shard_map/concatenate | solution.py:646
  15.0 3.1 %collective-permute-start = (bf16[1024,1280]{1,0:T(8,128)(2,1)}, bf16[1024,1280]{1,0:T(8,128)(2,1)S(1)}, u32[]{:S(2)}, u32[]{:S(2)}) collective-permute-start(bf16[1024,1280]{1,0:T(8,128)(2,1)} %pad_maximum_fusion), channel_id=1, source_target_pairs={{0,4},{4,8},{8,12},{12,16},{16,20},{20,24},{24,28},{1,5},{5,9},{9,... | collective-permute-start | bytes 7864328 | tf_op jit(solution)/shard_map/ppermute | solution.py:588
  18.1 11.7 %grads.3 = (bf16[480,640]{1,0:T(8,128)(2,1)S(1)}, bf16[480,640]{1,0:T(8,128)(2,1)}, bf16[480,640]{1,0:T(8,128)(2,1)S(1)}, bf16[480,640]{1,0:T(8,128)(2,1)}) custom-call(s32[1]{0:T(128)} %bitcast.position_ref.s_ref.refs_0_, bf16[1024,1280]{1,0:T(8,128)(2,1)} %refs_1_.5, bf16[1024,1280]{1,0:T(8,128)(2,1)} %refs_2_.7, f32[2,1024]{1,0:T(2,128)S(1)} %bitcast.3, ...), custom_call_target="tpu_custom_call" | custom-call | flops 5033164800 | bytes 9994240 | tf_op jit(solution)/shard_map/grads/pallas_call | solution.py:292
  29.8 2.3 %collective-permute-start.4 = (bf16[480,640]{1,0:T(8,128)(2,1)}, bf16[480,640]{1,0:T(8,128)(2,1)}, u32[]{:S(2)}, u32[]{:S(2)}) collective-permute-start(bf16[480,640]{1,0:T(8,128)(2,1)} %get-tuple-element.16), channel_id=1, source_target_pairs={{0,8},{4,12},{8,0},{12,4},{16,24},{20,28},{24,16},{28,20},{1,9},{5... | collective-permute-start | bytes 1843208 | tf_op jit(solution)/shard_map/ppermute | solution.py:583
  32.1 1.7 %collective-permute-start.6 = (bf16[480,640]{1,0:T(8,128)(2,1)}, bf16[480,640]{1,0:T(8,128)(2,1)}, u32[]{:S(2)}, u32[]{:S(2)}) collective-permute-start(bf16[480,640]{1,0:T(8,128)(2,1)} %get-tuple-element.18), channel_id=1, source_target_pairs={{0,16},{4,20},{8,24},{12,28},{16,0},{20,4},{24,8},{28,12},{1,17},{... | collective-permute-start | bytes 1843208 | tf_op jit(solution)/shard_map/ppermute | solution.py:583
  33.8 13.6 %shard_map.101 = (bf16[512,1408]{1,0:T(8,128)(2,1)}, bf16[512,1280]{1,0:T(8,128)(2,1)S(1)}, f32[512,128]{1,0:T(8,128)S(1)}) custom-call(s32[1]{0:T(128)} %bitcast.position_ref.s_ref.refs_0_, bf16[512,1280]{1,0:T(8,128)(2,1)S(1)} %collective-permute-done.1.refs_0_, bf16[1024,1280]{1,0:T(8,128)(2,1)} %refs_1_.3, bf16[1024,1280]{1,0:T(8,128)(2,1)} %refs_2_.5, ...), custom_call_target="tpu_custom_call" | custom-call | flops 3355443200 | bytes 10485760 | tf_op jit(solution)/shard_map/pallas_call | solution.py:158
  47.4 1.1 copy-done.3
  48.5 9.0 %collective-permute-start.2 = (bf16[512,1408]{1,0:T(8,128)(2,1)}, bf16[512,1408]{1,0:T(8,128)(2,1)}, u32[]{:S(2)}, u32[]{:S(2)}) collective-permute-start(bf16[512,1408]{1,0:T(8,128)(2,1)} %get-tuple-element.13), channel_id=1, source_target_pairs={{0,4},{4,8},{8,12},{12,16},{16,20},{20,24},{24,28},{1,5},{5,9},{9,... | collective-permute-start | bytes 4325384 | tf_op jit(solution)/shard_map/ppermute | solution.py:588
  57.4 1.0 add_convert_fusion.1
  58.5 2.3 %collective-permute-start.5 = (bf16[240,640]{1,0:T(8,128)(2,1)S(1)}, bf16[240,640]{1,0:T(8,128)(2,1)S(1)}, u32[]{:S(2)}, u32[]{:S(2)}) collective-permute-start(bf16[240,640]{1,0:T(8,128)(2,1)S(1)} %add_convert_fusion.1), channel_id=1, source_target_pairs={{0,16},{4,20},{8,24},{12,28},{16,0},{20,4},{24,8},{28,12},{1,17},{... | collective-permute-start | bytes 921608 | tf_op jit(solution)/shard_map/ppermute | solution.py:583
  60.7 9.6 %collective-permute-done.6.refs_4_ = bf16[480,640]{1,0:T(8,128)(2,1)} collective-permute-done((bf16[480,640]{1,0:T(8,128)(2,1)}, bf16[480,640]{1,0:T(8,128)(2,1)}, u32[]{:S(2)}, u32[]{:S(2)}) %collective-permute-start.6) | collective-permute-done | bytes 614432 | tf_op jit(solution)/shard_map/ppermute | solution.py:583
  70.3 1.1 add_convert_fusion
  71.6 4.0 %turned.1.old_ref = f32[480,640]{1,0:T(8,128)S(1)} custom-call(s32[1]{0:T(128)} %bitcast.position_ref.s_ref.refs_0_, f32[2,640,640]{2,1,0:T(8,128)} %refs_4_.5, f32[2,640,640]{2,1,0:T(8,128)} %refs_5_.3, f32[2,640,640]{2,1,0:T(8,128)} %refs_6_.3), custom_call_target="tpu_custom_call" | custom-call | flops 1228800 | bytes 9830400 | tf_op jit(solution)/shard_map/turned/pallas_call | solution.py:326
  75.6 2.5 %collective-permute-done.5.refs_2_ = bf16[240,640]{1,0:T(8,128)(2,1)S(1)} collective-permute-done((bf16[240,640]{1,0:T(8,128)(2,1)S(1)}, bf16[240,640]{1,0:T(8,128)(2,1)S(1)}, u32[]{:S(2)}, u32[]{:S(2)}) %collective-permute-start.5) | collective-permute-done | bytes 307232 | tf_op jit(solution)/shard_map/ppermute | solution.py:583
  78.1 3.6 %collective-permute-done.7.refs_5_ = bf16[240,640]{1,0:T(8,128)(2,1)S(1)} collective-permute-done((bf16[240,640]{1,0:T(8,128)(2,1)S(1)}, bf16[240,640]{1,0:T(8,128)(2,1)S(1)}, u32[]{:S(2)}, u32[]{:S(2)}) %collective-permute-start.7) | collective-permute-done | bytes 307232 | tf_op jit(solution)/shard_map/ppermute | solution.py:583
  81.7 1.7 %renorm.1.own_ref.rest_1_ = bf16[480,640]{1,0:T(8,128)(2,1)S(1)} custom-call(s32[1]{0:T(128)} %bitcast.position_ref.s_ref.refs_0_, f32[480,640]{1,0:T(8,128)S(1)} %turned.1.old_ref, bf16[480,640]{1,0:T(8,128)(2,1)S(1)} %get-tuple-element.15.refs_0_, bf16[480,640]{1,0:T(8,128)(2,1)} %collective-permute-done.4.refs_1_, ...), custom_call_target="tpu_custom_call" | custom-call | flops 3072000 | bytes 3686400 | tf_op jit(solution)/shard_map/renorm/pallas_call | solution.py:365
  83.4 2.5 %collective-permute-start.11 = (bf16[480,640]{1,0:T(8,128)(2,1)S(1)}, bf16[480,640]{1,0:T(8,128)(2,1)S(1)}, u32[]{:S(2)}, u32[]{:S(2)}) collective-permute-start(bf16[480,640]{1,0:T(8,128)(2,1)S(1)} %renorm.1.own_ref.rest_1_), channel_id=1, source_target_pairs={{0,16},{4,20},{8,24},{12,28},{16,0},{20,4},{24,8},{28,12},{1,17},{... | collective-permute-start | bytes 1843208 | tf_op jit(solution)/shard_map/ppermute | solution.py:583
  85.9 20.2 %collective-permute-start.8 = (bf16[480,640]{1,0:T(8,128)(2,1)S(1)}, bf16[480,640]{1,0:T(8,128)(2,1)S(1)}, u32[]{:S(2)}, u32[]{:S(2)}) collective-permute-start(bf16[480,640]{1,0:T(8,128)(2,1)S(1)} %renorm.1.own_ref.rest_1_), channel_id=1, source_target_pairs={{0,4},{4,0},{8,12},{12,8},{16,20},{20,16},{24,28},{28,24},{1,5},{5... | collective-permute-start | bytes 1843208 | tf_op jit(solution)/shard_map/ppermute | solution.py:583
  106.2 6.1 %collective-permute-start.10 = (bf16[480,640]{1,0:T(8,128)(2,1)S(1)}, bf16[480,640]{1,0:T(8,128)(2,1)S(1)}, u32[]{:S(2)}, u32[]{:S(2)}) collective-permute-start(bf16[480,640]{1,0:T(8,128)(2,1)S(1)} %collective-permute-done.9.over_x.rest_2_), channel_id=1, source_target_pairs={{0,4},{4,0},{8,12},{12,8},{16,20},{20,16},{24,28},{28,24},{1,5},{5... | collective-permute-start | bytes 1843208 | tf_op jit(solution)/shard_map/ppermute | solution.py:583
  112.2 1.4 collective-permute-start.12
  114.2 1.7 %collective-permute-start.15 = (bf16[240,640]{1,0:T(8,128)(2,1)S(1)}, bf16[240,640]{1,0:T(8,128)(2,1)S(1)}, u32[]{:S(2)}, u32[]{:S(2)}) collective-permute-start(bf16[240,640]{1,0:T(8,128)(2,1)S(1)} %slice.21), channel_id=1, source_target_pairs={{0,16},{4,20},{8,24},{12,28},{16,0},{20,4},{24,8},{28,12},{1,17},{... | collective-permute-start | bytes 921608 | tf_op jit(solution)/shard_map/ppermute | solution.py:583
  115.9 11.6 %shard_map.100.high_ref = bf16[512,1280]{1,0:T(8,128)(2,1)S(1)} custom-call(s32[1]{0:T(128)} %bitcast.position_ref.s_ref.refs_0_, bf16[1024,1280]{1,0:T(8,128)(2,1)} %refs_1_.3, bf16[1024,1280]{1,0:T(8,128)(2,1)S(1)} %collective-permute-done.refs_1_.refs_3_, bf16[1024,1280]{1,0:T(8,128)(2,1)} %refs_2_.5, ...), custom_call_target="tpu_custom_call" | custom-call | flops 3355443200 | bytes 10485760 | tf_op jit(solution)/shard_map/pallas_call | solution.py:158
  127.6 4.7 %merge.1.low_ref = bf16[512,1280]{1,0:T(8,128)(2,1)S(1)} custom-call(s32[1]{0:T(128)} %bitcast.position_ref.s_ref.refs_0_, bf16[512,1280]{1,0:T(8,128)(2,1)S(1)} %copy-done.4, bf16[512,1408]{1,0:T(8,128)(2,1)} %collective-permute-done.2.far_ref.far_log, f32[512,128]{1,0:T(8,128)S(1)} %get-tuple-element.14.own_log, ...), custom_call_target="tpu_custom_call" | custom-call | flops 5242880 | bytes 3932160 | tf_op jit(solution)/shard_map/merge/pallas_call | solution.py:404
  132.4 0.5 collective-permute-start.16
  132.9 3.2 %hidden.3.rest_0_ = bf16[1024,640]{1,0:T(8,128)(2,1)S(1)} custom-call(s32[1]{0:T(128)} %bitcast.position_ref.s_ref.refs_0_, bf16[1024,1280]{1,0:T(8,128)(2,1)S(1)} %copy-done, bf16[480,640]{1,0:T(8,128)(2,1)S(1)} %renorm.1.own_ref.rest_1_, bf16[480,640]{1,0:T(8,128)(2,1)S(1)} %collective-permute-done.9.over_x.rest_2_, ...), custom_call_target="tpu_custom_call" | custom-call | flops 1258291200 | bytes 3850240 | tf_op jit(solution)/shard_map/hidden/pallas_call | solution.py:472
  136.2 5.0 %apply.2.rest_6_ = bf16[1024,1280]{1,0:T(8,128)(2,1)} custom-call(s32[1]{0:T(128)} %bitcast.position_ref.s_ref.refs_0_, bf16[1024,1280]{1,0:T(8,128)(2,1)S(1)} %copy-done, bf16[512,1280]{1,0:T(8,128)(2,1)S(1)} %shard_map.100.high_ref, bf16[512,1280]{1,0:T(8,128)(2,1)S(1)} %merge.1.low_ref, bf16[1024,640]{1,0:T(8,128)(2,1)S(1)} %hidden.3.rest_0_, ...), custom_call_target="tpu_custom_call" | custom-call | flops 1258291200 | bytes 7700480 | tf_op jit(solution)/shard_map/apply/pallas_call | solution.py:557
  141.2 3.2 %hidden.2.rest_0_ = bf16[1024,640]{1,0:T(8,128)(2,1)S(1)} custom-call(s32[1]{0:T(128)} %bitcast.position_ref.s_ref.refs_0_, bf16[1024,1280]{1,0:T(8,128)(2,1)S(1)} %copy-done, bf16[480,640]{1,0:T(8,128)(2,1)S(1)} %collective-permute-done.8.own_ref.rest_1_, bf16[480,640]{1,0:T(8,128)(2,1)S(1)} %collective-permute-done.10.over_x.rest_2_, ...), custom_call_target="tpu_custom_call" | custom-call | flops 1258291200 | bytes 3850240 | tf_op jit(solution)/shard_map/hidden/pallas_call | solution.py:472
  144.5 5.0 %apply.3 = bf16[1024,1280]{1,0:T(8,128)(2,1)} custom-call(s32[1]{0:T(128)} %bitcast.position_ref.s_ref.refs_0_, bf16[1024,1280]{1,0:T(8,128)(2,1)S(1)} %copy-done, bf16[512,1280]{1,0:T(8,128)(2,1)S(1)} %shard_map.100.high_ref, bf16[512,1280]{1,0:T(8,128)(2,1)S(1)} %merge.1.low_ref, ...), custom_call_target="tpu_custom_call", output_to_operand_aliasing={{}: (10, {})} | custom-call | flops 1258291200 | bytes 7700480 | tf_op jit(solution)/shard_map/apply/pallas_call | solution.py:557
  (39 shorter events, 1.1 us)
Async XLA Ops:
  0.0 0.7 copy-start.5
  0.7 10.8 %copy-start.7 = (bf16[1024,1280]{1,0:T(8,128)(2,1)S(1)}, bf16[1024,1280]{1,0:T(8,128)(2,1)}, u32[]{:S(2)}) copy-start(bf16[1024,1280]{1,0:T(8,128)(2,1)} %refs_1_.3) | copy-start | bytes 7864324
  10.9 7.2 %collective-permute-start.3 = (bf16[1920,640]{1,0:T(8,128)(2,1)S(1)}, bf16[1920,640]{1,0:T(8,128)(2,1)S(1)}, u32[]{:S(2)}, u32[]{:S(2)}) collective-permute-start(bf16[1920,640]{1,0:T(8,128)(2,1)S(1)} %grads.2), channel_id=1, source_target_pairs={{0,4},{4,0},{8,12},{12,8},{16,20},{20,16},{24,28},{28,24},{1,5},{5... | collective-permute-start | bytes 7372808 | tf_op jit(solution)/shard_map/ppermute | solution.py:583
  11.6 1.5 slice-start
  11.6 1.7 %slice-start.1 = ((bf16[1024,1280]{1,0:T(8,128)(2,1)}), bf16[512,1280]{1,0:T(8,128)(2,1)S(1)}, s32[]{:S(2)}) async-start(bf16[1024,1280]{1,0:T(8,128)(2,1)} %refs_2_.5), calls=%async_computation.1 | async-start | bytes 2621440 | tf_op jit(solution)/shard_map/slice | solution.py:646
  11.6 22.2 %collective-permute-start.1 = (bf16[512,1280]{1,0:T(8,128)(2,1)S(1)}, bf16[512,1280]{1,0:T(8,128)(2,1)S(1)}, u32[]{:S(2)}, u32[]{:S(2)}) collective-permute-start(bf16[512,1280]{1,0:T(8,128)(2,1)S(1)} %slice.17), channel_id=1, source_target_pairs={{4,0},{8,4},{12,8},{16,12},{20,16},{24,20},{28,24},{5,1},{9,5},{13... | collective-permute-start | bytes 3932168 | tf_op jit(solution)/shard_map/ppermute | solution.py:588
  13.3 4.8 %copy-start.6 = (f32[1024,2]{0,1:T(2,128)S(1)}, f32[1024,2]{0,1:T(2,128)}, u32[]{:S(2)}) copy-start(f32[1024,2]{0,1:T(2,128)} %param.16) | copy-start | bytes 24580
  15.0 98.8 %collective-permute-start = (bf16[1024,1280]{1,0:T(8,128)(2,1)}, bf16[1024,1280]{1,0:T(8,128)(2,1)S(1)}, u32[]{:S(2)}, u32[]{:S(2)}) collective-permute-start(bf16[1024,1280]{1,0:T(8,128)(2,1)} %pad_maximum_fusion), channel_id=1, source_target_pairs={{0,4},{4,8},{8,12},{12,16},{16,20},{20,24},{24,28},{1,5},{5,9},{9,... | collective-permute-start | bytes 7864328 | tf_op jit(solution)/shard_map/ppermute | solution.py:588
  29.8 17.6 %copy-start.1 = (bf16[480,640]{1,0:T(8,128)(2,1)}, bf16[480,640]{1,0:T(8,128)(2,1)S(1)}, u32[]{:S(2)}) copy-start(bf16[480,640]{1,0:T(8,128)(2,1)S(1)} %get-tuple-element.17.refs_3_) | copy-start | bytes 1843204
  29.8 27.6 %collective-permute-start.4 = (bf16[480,640]{1,0:T(8,128)(2,1)}, bf16[480,640]{1,0:T(8,128)(2,1)}, u32[]{:S(2)}, u32[]{:S(2)}) collective-permute-start(bf16[480,640]{1,0:T(8,128)(2,1)} %get-tuple-element.16), channel_id=1, source_target_pairs={{0,8},{4,12},{8,0},{12,4},{16,24},{20,28},{24,16},{28,20},{1,9},{5... | collective-permute-start | bytes 1843208 | tf_op jit(solution)/shard_map/ppermute | solution.py:583
  32.1 38.2 %collective-permute-start.6 = (bf16[480,640]{1,0:T(8,128)(2,1)}, bf16[480,640]{1,0:T(8,128)(2,1)}, u32[]{:S(2)}, u32[]{:S(2)}) collective-permute-start(bf16[480,640]{1,0:T(8,128)(2,1)} %get-tuple-element.18), channel_id=1, source_target_pairs={{0,16},{4,20},{8,24},{12,28},{16,0},{20,4},{24,8},{28,12},{1,17},{... | collective-permute-start | bytes 1843208 | tf_op jit(solution)/shard_map/ppermute | solution.py:583
  47.4 1.1 copy-start.3
  48.5 65.7 %collective-permute-start.2 = (bf16[512,1408]{1,0:T(8,128)(2,1)}, bf16[512,1408]{1,0:T(8,128)(2,1)}, u32[]{:S(2)}, u32[]{:S(2)}) collective-permute-start(bf16[512,1408]{1,0:T(8,128)(2,1)} %get-tuple-element.13), channel_id=1, source_target_pairs={{0,4},{4,8},{8,12},{12,16},{16,20},{20,24},{24,28},{1,5},{5,9},{9,... | collective-permute-start | bytes 4325384 | tf_op jit(solution)/shard_map/ppermute | solution.py:588
  58.5 19.7 %collective-permute-start.5 = (bf16[240,640]{1,0:T(8,128)(2,1)S(1)}, bf16[240,640]{1,0:T(8,128)(2,1)S(1)}, u32[]{:S(2)}, u32[]{:S(2)}) collective-permute-start(bf16[240,640]{1,0:T(8,128)(2,1)S(1)} %add_convert_fusion.1), channel_id=1, source_target_pairs={{0,16},{4,20},{8,24},{12,28},{16,0},{20,4},{24,8},{28,12},{1,17},{... | collective-permute-start | bytes 921608 | tf_op jit(solution)/shard_map/ppermute | solution.py:583
  71.5 10.2 %copy-start.2 = (bf16[480,640]{1,0:T(8,128)(2,1)S(1)}, bf16[480,640]{1,0:T(8,128)(2,1)}, u32[]{:S(2)}) copy-start(bf16[480,640]{1,0:T(8,128)(2,1)} %copy-done.1) | copy-start | bytes 1843204
  71.5 10.2 %collective-permute-start.7 = (bf16[240,640]{1,0:T(8,128)(2,1)S(1)}, bf16[240,640]{1,0:T(8,128)(2,1)S(1)}, u32[]{:S(2)}, u32[]{:S(2)}) collective-permute-start(bf16[240,640]{1,0:T(8,128)(2,1)S(1)} %add_convert_fusion), channel_id=1, source_target_pairs={{0,8},{4,12},{8,0},{12,4},{16,24},{20,28},{24,16},{28,20},{1,9},{5... | collective-permute-start | bytes 921608 | tf_op jit(solution)/shard_map/ppermute | solution.py:583
  83.4 22.8 %collective-permute-start.9 = (bf16[480,640]{1,0:T(8,128)(2,1)S(1)}, bf16[480,640]{1,0:T(8,128)(2,1)S(1)}, u32[]{:S(2)}, u32[]{:S(2)}) collective-permute-start(bf16[480,640]{1,0:T(8,128)(2,1)S(1)} %renorm.1.own_ref.rest_1_), channel_id=1, source_target_pairs={{0,8},{4,12},{8,0},{12,4},{16,24},{20,28},{24,16},{28,20},{1,9},{5... | collective-permute-start | bytes 1843208 | tf_op jit(solution)/shard_map/ppermute | solution.py:583
  83.4 28.8 %collective-permute-start.11 = (bf16[480,640]{1,0:T(8,128)(2,1)S(1)}, bf16[480,640]{1,0:T(8,128)(2,1)S(1)}, u32[]{:S(2)}, u32[]{:S(2)}) collective-permute-start(bf16[480,640]{1,0:T(8,128)(2,1)S(1)} %renorm.1.own_ref.rest_1_), channel_id=1, source_target_pairs={{0,16},{4,20},{8,24},{12,28},{16,0},{20,4},{24,8},{28,12},{1,17},{... | collective-permute-start | bytes 1843208 | tf_op jit(solution)/shard_map/ppermute | solution.py:583
  85.9 55.3 %collective-permute-start.8 = (bf16[480,640]{1,0:T(8,128)(2,1)S(1)}, bf16[480,640]{1,0:T(8,128)(2,1)S(1)}, u32[]{:S(2)}, u32[]{:S(2)}) collective-permute-start(bf16[480,640]{1,0:T(8,128)(2,1)S(1)} %renorm.1.own_ref.rest_1_), channel_id=1, source_target_pairs={{0,4},{4,0},{8,12},{12,8},{16,20},{20,16},{24,28},{28,24},{1,5},{5... | collective-permute-start | bytes 1843208 | tf_op jit(solution)/shard_map/ppermute | solution.py:583
  106.2 35.0 %collective-permute-start.10 = (bf16[480,640]{1,0:T(8,128)(2,1)S(1)}, bf16[480,640]{1,0:T(8,128)(2,1)S(1)}, u32[]{:S(2)}, u32[]{:S(2)}) collective-permute-start(bf16[480,640]{1,0:T(8,128)(2,1)S(1)} %collective-permute-done.9.over_x.rest_2_), channel_id=1, source_target_pairs={{0,4},{4,0},{8,12},{12,8},{16,20},{20,16},{24,28},{28,24},{1,5},{5... | collective-permute-start | bytes 1843208 | tf_op jit(solution)/shard_map/ppermute | solution.py:583
  112.2 28.9 %collective-permute-start.12 = (bf16[480,640]{1,0:T(8,128)(2,1)S(1)}, bf16[480,640]{1,0:T(8,128)(2,1)S(1)}, u32[]{:S(2)}, u32[]{:S(2)}) collective-permute-start(bf16[480,640]{1,0:T(8,128)(2,1)S(1)} %collective-permute-done.11.over_y.rest_3_), channel_id=1, source_target_pairs={{0,4},{4,0},{8,12},{12,8},{16,20},{20,16},{24,28},{28,24},{1,5},{5... | collective-permute-start | bytes 1843208 | tf_op jit(solution)/shard_map/ppermute | solution.py:583
  113.8 13.8 %copy-start.4 = (bf16[512,1280]{1,0:T(8,128)(2,1)S(1)}, bf16[512,1280]{1,0:T(8,128)(2,1)}, u32[]{:S(2)}) copy-start(bf16[512,1280]{1,0:T(8,128)(2,1)} %copy-done.3) | copy-start | bytes 3932164
  113.8 18.6 %collective-permute-start.13 = (bf16[240,640]{1,0:T(8,128)(2,1)S(1)}, bf16[240,640]{1,0:T(8,128)(2,1)S(1)}, u32[]{:S(2)}, u32[]{:S(2)}) collective-permute-start(bf16[240,640]{1,0:T(8,128)(2,1)S(1)} %slice.20), channel_id=1, source_target_pairs={{0,8},{4,12},{8,0},{12,4},{16,24},{20,28},{24,16},{28,20},{1,9},{5... | collective-permute-start | bytes 921608 | tf_op jit(solution)/shard_map/ppermute | solution.py:583
  114.2 18.2 %collective-permute-start.15 = (bf16[240,640]{1,0:T(8,128)(2,1)S(1)}, bf16[240,640]{1,0:T(8,128)(2,1)S(1)}, u32[]{:S(2)}, u32[]{:S(2)}) collective-permute-start(bf16[240,640]{1,0:T(8,128)(2,1)S(1)} %slice.21), channel_id=1, source_target_pairs={{0,16},{4,20},{8,24},{12,28},{16,0},{20,4},{24,8},{28,12},{1,17},{... | collective-permute-start | bytes 921608 | tf_op jit(solution)/shard_map/ppermute | solution.py:583
  127.6 5.3 %copy-start = (bf16[1024,1280]{1,0:T(8,128)(2,1)S(1)}, bf16[1024,1280]{1,0:T(8,128)(2,1)}, u32[]{:S(2)}) copy-start(bf16[1024,1280]{1,0:T(8,128)(2,1)} %q_ref.7) | copy-start | bytes 7864324
  132.3 12.1 %collective-permute-start.14 = (bf16[240,640]{1,0:T(8,128)(2,1)S(1)}, bf16[240,640]{1,0:T(8,128)(2,1)S(1)}, u32[]{:S(2)}, u32[]{:S(2)}) collective-permute-start(bf16[240,640]{1,0:T(8,128)(2,1)S(1)} %collective-permute-done.13.rest_4_), channel_id=1, source_target_pairs={{0,4},{4,0},{8,12},{12,8},{16,20},{20,16},{24,28},{28,24},{1,5},{5... | collective-permute-start | bytes 921608 | tf_op jit(solution)/shard_map/ppermute | solution.py:583
  132.4 12.0 %collective-permute-start.16 = (bf16[240,640]{1,0:T(8,128)(2,1)S(1)}, bf16[240,640]{1,0:T(8,128)(2,1)S(1)}, u32[]{:S(2)}, u32[]{:S(2)}) collective-permute-start(bf16[240,640]{1,0:T(8,128)(2,1)S(1)} %collective-permute-done.15.rest_5_), channel_id=1, source_target_pairs={{0,4},{4,0},{8,12},{12,8},{16,20},{20,16},{24,28},{28,24},{1,5},{5... | collective-permute-start | bytes 921608 | tf_op jit(solution)/shard_map/ppermute | solution.py:583

commit v5 on v4

--- a/solution.py
+++ b/solution.py
@@ -431,150 +431,136 @@
         cur = nxt
 
 
-def put_quarter(s_ref, ref, rows, values, flip_x, flip_y):
-    n = ref.shape[1] // 4
-    chip = 2 * (at_x(s_ref) ^ flip_x) + (at_y(s_ref) ^ flip_y)
+def for_each_chip(s_ref, body):
+    chip = 2 * at_x(s_ref) + at_y(s_ref)
     for k in range(4):
-
-        @pl.when(chip == k)
-        def _():
-            ref[rows, k * n : (k + 1) * n] = values
-
-
-def hidden_kernel(s_ref, q_ref, own_ref, over_x, over_y, o_ref, w_ref, v_ref, *, tm):
-    F = q_ref.shape[1]
+        pl.when(chip == k)(functools.partial(body, k))
+
+
+NEIGHBOURS = (0, 2, 1, 3)
+
+
+def hidden_kernel(s_ref, q_ref, own_ref, over_x, over_y, o_ref, w_ref, *, tm, head):
+    F = own_ref.shape[1]
     n = F // 4
-
-    @pl.when(pl.program_id(0) == 0)
-    def _():
-        for i, ref in enumerate((own_ref, over_x, over_y)):
-            w_ref[i * n : (i + 1) * n, :] = ref[:n, :]
-            w_ref[(3 + i) * n : (4 + i) * n, :] = ref[n : 2 * n, :]
+    for i, ref in enumerate((own_ref, over_x, over_y)):
+        w_ref[i * n : (i + 1) * n, :] = ref[:n, :]
+        w_ref[(3 + i) * n : (4 + i) * n, :] = ref[n : 2 * n, :]
+    cols = pl.ds(pl.multiple_of(head(s_ref) * F, HD), F)
 
     def first(i):
-        return mm(q_ref[i * tm : (i + 1) * tm, :], w_ref[...], NT)
+        return mm(q_ref[i * tm : (i + 1) * tm, cols], w_ref[...], NT)
 
     def second(i, h):
-        v_ref[i * tm : (i + 1) * tm, : 3 * n] = gated(h, 3 * n)
+        o_ref[i * tm : (i + 1) * tm, : 3 * n] = gated(h, 3 * n)
 
     staggered(q_ref.shape[0] // tm, first, second)
-    every = slice(0, q_ref.shape[0])
-    for i, flips in enumerate(((0, 0), (1, 0), (0, 1))):
-        put_quarter(s_ref, o_ref, every, v_ref[:, i * n : (i + 1) * n], *flips)
+
+
+VMEM = pl.BlockSpec(memory_space=pltpu.VMEM)
+SMEM = pl.BlockSpec(memory_space=pltpu.SMEM)
+ANY = pl.BlockSpec(memory_space=pl.ANY)
 
 
 def hidden_part(position, head, fq, pieces):
     rows = fq.shape[0]
     F = pieces[0].shape[1]
-    half = rows // 2
-    whole = pl.BlockSpec(pieces[0].shape, lambda i, s: (0, 0))
     bf = jnp.bfloat16
     return pl.pallas_call(
-        functools.partial(hidden_kernel, tm=min(256, half)),
-        grid_spec=pltpu.PrefetchScalarGridSpec(
-            num_scalar_prefetch=1,
-            grid=(2,),
-            in_specs=[pl.BlockSpec((half, F), lambda i, s: (i, head(s)))] + [whole] * 3,
-            out_specs=pl.BlockSpec((half, F), lambda i, s: (i, 0)),
-            scratch_shapes=[pltpu.VMEM((3 * F // 2, F), bf), pltpu.VMEM((half, F), bf)],
-        ),
+        functools.partial(hidden_kernel, tm=min(256, rows), head=head),
+        in_specs=[SMEM] + [VMEM] * 4,
+        out_specs=VMEM,
+        scratch_shapes=[pltpu.VMEM((3 * F // 2, F), bf)],
         out_shape=jax.ShapeDtypeStruct((rows, F), bf),
         cost_estimate=pl.CostEstimate(
             flops=3 * rows * F * F, bytes_accessed=rows * F * 4 + F * F * 3, transcendentals=rows * F
         ),
         name="hidden",
-        compiler_params=room(14),
+        compiler_params=room(24),
     )(position, fq, *pieces[:3])
 
 
-def apply_kernel(s_ref, q_ref, high_ref, low_ref, *rest, tm, split):
-    n_ref, w_ref, h_ref, a_ref = rest[-4:]
-    o_ref = rest[-5]
-    F = q_ref.shape[1]
+def apply_kernel(s_ref, q_ref, high_ref, low_ref, *rest, tm, head, split):
+    o_ref, n_ref, w_ref, h_ref, r_ref, sems = rest[-6:]
+    rows = q_ref.shape[0]
+    half = rows // 2
+    F = n_ref.shape[1]
     n, m = F // 4, F // 8
-    step = pl.program_id(0)
-
-    @pl.when(step == 0)
-    def _():
-        if split:
-            own, over_x, over_y, upper, lower = rest[1:6]
-            for ref, row, flips in (
-                (own, 2 * n, (0, 0)),
-                (over_x, 2 * n, (1, 0)),
-                (over_y, 2 * n, (0, 1)),
-                (lower, m, (1, 1)),
-            ):
-                to = pl.multiple_of(quarter(F, *flips)(s_ref), 16)
-                n_ref[pl.ds(to, n), :] = ref[row : row + n, :]
-            w_ref[: n + m, :] = upper[...]
-            w_ref[n + m :, :] = lower[:m, :]
-        else:
-            w_ref[...] = rest[0][: 2 * F, :]
-            n_ref[...] = rest[0][2 * F :, :]
-        a_ref[...] = low_ref[...]
-
-    @pl.when(step == 1)
-    def _():
-        a_ref[...] = high_ref[...]
+    cols = pl.ds(pl.multiple_of(head(s_ref) * F, HD), F)
+    if split:
+        own, over_x, over_y, upper, lower = rest[1:6]
+        w_ref[: n + m, :] = upper[...]
+        w_ref[n + m :, :] = lower[:m, :]
+    else:
+        w_ref[...] = rest[0][: 2 * F, :]
+        n_ref[...] = rest[0][2 * F :, :]
+
+    def copy_out(i):
+        r = pl.ds(i * tm, tm)
+        return pltpu.make_async_copy(r_ref.at[r, :], o_ref.at[r, cols], sems.at[i])
+
+    def place(k):
+        rows_of = ((own, 2 * n), (over_x, 2 * n), (over_y, 2 * n), (lower, m))
+        for flip, (ref, row) in zip(NEIGHBOURS, rows_of):
+            for j, from_flip in enumerate(NEIGHBOURS):
+                to, at = (k ^ flip) * n, (k ^ from_flip) * n
+                n_ref[to : to + n, j * n : (j + 1) * n] = ref[row : row + n, at : at + n]
+
+    if split:
+        for_each_chip(s_ref, place)
 
     def first(i):
-        return mm(q_ref[i * tm : (i + 1) * tm, :], w_ref[...], NT)
+        return mm(q_ref[i * tm : (i + 1) * tm, cols], w_ref[...], NT)
 
     def second(i, h):
         r = slice(i * tm, (i + 1) * tm)
         if split:
-            h_ref[r, :] = rest[0][r, :]
-            put_quarter(s_ref, h_ref, r, gated(h, n), 1, 1)
+            h_ref[r, : 3 * n] = rest[0][r, : 3 * n]
+            h_ref[r, 3 * n :] = gated(h, n)
             hid = h_ref[r, :]
         else:
             hid = gated(h, F)
-        o_ref[r, :] = (a_ref[r, :].astype(jnp.float32) + mm(hid, n_ref[...], NT)).astype(o_ref.dtype)
-
-    staggered(q_ref.shape[0] // tm, first, second)
+        source, at = (low_ref, i * tm) if i * tm < half else (high_ref, i * tm - half)
+        a = source[at : at + tm, cols].astype(jnp.float32)
+        r_ref[r, :] = (a + mm(hid, n_ref[...], NT)).astype(r_ref.dtype)
+        copy_out(i).start()
+
+    staggered(rows // tm, first, second)
+    for i in range(rows // tm):
+        copy_out(i).wait()
 
 
 def apply_head(position, head, fq, hidden, pieces, high, low, into=None):
     rows, cols = fq.shape
     F = pieces[0].shape[1]
-    half = rows // 2
     split = hidden is not None
-    col = pl.BlockSpec((half, F), lambda i, s: (i, head(s)))
-    part = pl.BlockSpec((half, F), lambda i, s: (0, head(s)))
-    whole = lambda a: pl.BlockSpec(a.shape, lambda i, s: (0, 0))
-    args = [position, fq, high, low]
-    specs = [col, part, part]
-    if split:
-        args.append(hidden)
-        specs.append(pl.BlockSpec((half, F), lambda i, s: (i, 0)))
-    args += pieces
-    specs += [whole(p) for p in pieces]
+    tm = min(256, rows // 2)
+    args = [position, fq, high, low] + ([hidden] if split else []) + list(pieces)
+    specs = [SMEM] + [VMEM] * (len(args) - 1)
     aliases = {}
     if into is not None:
         aliases = {len(args): 0}
         args.append(into)
-        specs.append(pl.BlockSpec(memory_space=pl.ANY))
+        specs.append(ANY)
     bf = jnp.bfloat16
     return pl.pallas_call(
-        functools.partial(apply_kernel, tm=min(256, half), split=split),
-        grid_spec=pltpu.PrefetchScalarGridSpec(
-            num_scalar_prefetch=1,
-            grid=(2,),
-            in_specs=specs,
-            out_specs=col,
-            scratch_shapes=[
-                pltpu.VMEM((F, F), bf),
-                pltpu.VMEM((F // 2 if split else 2 * F, F), bf),
-                pltpu.VMEM((half, F), bf),
-                pltpu.VMEM((half, F), bf),
-            ],
-        ),
+        functools.partial(apply_kernel, tm=tm, head=head, split=split),
+        in_specs=specs,
+        out_specs=ANY,
+        scratch_shapes=[
+            pltpu.VMEM((F, F), bf),
+            pltpu.VMEM((F // 2 if split else 2 * F, F), bf),
+            pltpu.VMEM((rows, F), bf),
+            pltpu.VMEM((rows, F), bf),
+            pltpu.SemaphoreType.DMA((rows // tm,)),
+        ],
         out_shape=jax.ShapeDtypeStruct((rows, cols), bf),
         input_output_aliases=aliases,
         cost_estimate=pl.CostEstimate(
             flops=3 * rows * F * F, bytes_accessed=rows * F * 8 + F * F * 6, transcendentals=rows * F
         ),
         name="apply",
-        compiler_params=room(14),
+        compiler_params=room(24),
     )(*args)
 
 

time: 150 us -> 144 us (0.960)
  Pallas kernels: 74 us -> 68.4 us
    pallas_call x4, Pallas kernels: 16.5 us -> 10.8 us  [the longest x2 6.8 us: apply_head(): pl.pallas_call(functools.partial(apply_kernel, tm=tm, head=head, split=sp...]
  transfers between devices with their start and end apart: 17 -> 17, of which waited for: 3 -> 3; matrix products, arithmetic and copies ran while one was open for 3% -> 3% of each run, Pallas kernels for 39% -> 38%
where the time goes in v5:
time: 144 us
  Pallas kernels  68.4 us (48%)
  starting transfers between devices  53.7 us (37%)
  waiting for transfers between devices  15.5 us (11%)
  other arithmetic  3.84 us (3%)
  local copies, waits for them, and re-layouts  2.18 us (2%)
    ppermute x14, starting transfers between devices, exchange(): return lax.ppermute(block, 'seq', [(i, i ^ 1 << bit) for i in range(size)])  40.2 us
    pallas_call x2, Pallas kernels, attention(): pl.pallas_call(kernel, grid_spec=pltpu.PrefetchScalarGridSpec(num_scalar_...  25.3 us
    pallas_call x2, Pallas kernels, gradients(): pl.pallas_call(body, grid_spec=pltpu.PrefetchScalarGridSpec(num_scalar_pr...  21.9 us
    ppermute x14, waiting for transfers between devices, exchange(): return lax.ppermute(block, 'seq', [(i, i ^ 1 << bit) for i in range(size)])  15.5 us
    ppermute x3, starting transfers between devices, shifted(): lax.ppermute(block, 'seq', [(i, i + by) for i in range(size) if 0 <= i +...  13.5 us
    pallas_call x2, Pallas kernels, apply_head(): pl.pallas_call(functools.partial(apply_kernel, tm=tm, head=head, split=sp...  6.8 us
    pallas_call x1, Pallas kernels, merged(): pl.pallas_call(functools.partial(merge_kernel, stride=log_stride_of(cols)...  4.7 us
    pallas_call x1, Pallas kernels, turned(): pl.pallas_call(functools.partial(turn_kernel, parts=parts), grid_spec=plt...  4.05 us
  transfers between devices with their start and end apart: 17, of which 3 were waited for; matrix products, arithmetic and copies ran while one was open for 3% of the time, Pallas kernels for 38%

profile of v5, /device:TPU:0, one launch (start us, length us, event | category | flops | bytes accessed | tf_op | source)
XLA Modules:
  0.0 144.0 jit_solution(15010023940809240233)
XLA Ops:
  0.0 0.7 copy-done.5
  0.7 10.2 %grads.2 = bf16[1920,640]{1,0:T(8,128)(2,1)S(1)} custom-call(s32[1]{0:T(128)} %bitcast.position_ref.s_ref.refs_0_, bf16[1024,1280]{1,0:T(8,128)(2,1)} %refs_1_.5, bf16[1024,1280]{1,0:T(8,128)(2,1)} %refs_2_.7, f32[2,1024]{1,0:T(2,128)S(1)} %bitcast.2, f32[2,640,640]{2,1,0:T(8,128)} %refs_4_.5, f32[2,640,640]{2,1,0:T(8,128)} %refs_5_.3, f32[2,640,640]{2,1,0:T(8,128)} %refs_6_.3), custom_call_target="tpu_custom_call" | custom-call | flops 5033164800 | bytes 9994240 | tf_op jit(solution)/shard_map/grads/pallas_call | solution.py:292
  10.9 0.6 collective-permute-start.3
  11.6 1.4 collective-permute-start.1
  13.3 1.7 %pad_maximum_fusion = bf16[1024,1280]{1,0:T(8,128)(2,1)} fusion(bf16[512,1280]{1,0:T(8,128)(2,1)S(1)} %slice-done, bf16[512,1280]{1,0:T(8,128)(2,1)S(1)} %slice-done.1), kind=kLoop, calls=%fused_computation | loop fusion | flops 5242880 | bytes 5242880 | tf_op jit(solution)/shard_map/concatenate | solution.py:632
  15.0 3.1 %collective-permute-start = (bf16[1024,1280]{1,0:T(8,128)(2,1)}, bf16[1024,1280]{1,0:T(8,128)(2,1)S(1)}, u32[]{:S(2)}, u32[]{:S(2)}) collective-permute-start(bf16[1024,1280]{1,0:T(8,128)(2,1)} %pad_maximum_fusion), channel_id=1, source_target_pairs={{0,4},{4,8},{8,12},{12,16},{16,20},{20,24},{24,28},{1,5},{5,9},{9,... | collective-permute-start | bytes 7864328 | tf_op jit(solution)/shard_map/ppermute | solution.py:574
  18.1 11.7 %grads.3 = (bf16[480,640]{1,0:T(8,128)(2,1)S(1)}, bf16[480,640]{1,0:T(8,128)(2,1)}, bf16[480,640]{1,0:T(8,128)(2,1)S(1)}, bf16[480,640]{1,0:T(8,128)(2,1)}) custom-call(s32[1]{0:T(128)} %bitcast.position_ref.s_ref.refs_0_, bf16[1024,1280]{1,0:T(8,128)(2,1)} %refs_1_.5, bf16[1024,1280]{1,0:T(8,128)(2,1)} %refs_2_.7, f32[2,1024]{1,0:T(2,128)S(1)} %bitcast.3, ...), custom_call_target="tpu_custom_call" | custom-call | flops 5033164800 | bytes 9994240 | tf_op jit(solution)/shard_map/grads/pallas_call | solution.py:292
  29.8 2.3 %collective-permute-start.4 = (bf16[480,640]{1,0:T(8,128)(2,1)}, bf16[480,640]{1,0:T(8,128)(2,1)}, u32[]{:S(2)}, u32[]{:S(2)}) collective-permute-start(bf16[480,640]{1,0:T(8,128)(2,1)} %get-tuple-element.16), channel_id=1, source_target_pairs={{0,8},{4,12},{8,0},{12,4},{16,24},{20,28},{24,16},{28,20},{1,9},{5... | collective-permute-start | bytes 1843208 | tf_op jit(solution)/shard_map/ppermute | solution.py:569
  32.1 1.7 %collective-permute-start.6 = (bf16[480,640]{1,0:T(8,128)(2,1)}, bf16[480,640]{1,0:T(8,128)(2,1)}, u32[]{:S(2)}, u32[]{:S(2)}) collective-permute-start(bf16[480,640]{1,0:T(8,128)(2,1)} %get-tuple-element.18), channel_id=1, source_target_pairs={{0,16},{4,20},{8,24},{12,28},{16,0},{20,4},{24,8},{28,12},{1,17},{... | collective-permute-start | bytes 1843208 | tf_op jit(solution)/shard_map/ppermute | solution.py:569
  33.8 13.6 %shard_map.101 = (bf16[512,1408]{1,0:T(8,128)(2,1)}, bf16[512,1280]{1,0:T(8,128)(2,1)S(1)}, f32[512,128]{1,0:T(8,128)S(1)}) custom-call(s32[1]{0:T(128)} %bitcast.position_ref.s_ref.refs_0_, bf16[512,1280]{1,0:T(8,128)(2,1)S(1)} %collective-permute-done.1.refs_0_, bf16[1024,1280]{1,0:T(8,128)(2,1)} %refs_1_.3, bf16[1024,1280]{1,0:T(8,128)(2,1)} %refs_2_.5, ...), custom_call_target="tpu_custom_call" | custom-call | flops 3355443200 | bytes 10485760 | tf_op jit(solution)/shard_map/pallas_call | solution.py:158
  47.4 1.1 copy-done.3
  48.5 9.0 %collective-permute-start.2 = (bf16[512,1408]{1,0:T(8,128)(2,1)}, bf16[512,1408]{1,0:T(8,128)(2,1)}, u32[]{:S(2)}, u32[]{:S(2)}) collective-permute-start(bf16[512,1408]{1,0:T(8,128)(2,1)} %get-tuple-element.13), channel_id=1, source_target_pairs={{0,4},{4,8},{8,12},{12,16},{16,20},{20,24},{24,28},{1,5},{5,9},{9,... | collective-permute-start | bytes 4325384 | tf_op jit(solution)/shard_map/ppermute | solution.py:574
  57.4 1.0 add_convert_fusion.1
  58.5 2.5 %collective-permute-start.5 = (bf16[240,640]{1,0:T(8,128)(2,1)S(1)}, bf16[240,640]{1,0:T(8,128)(2,1)S(1)}, u32[]{:S(2)}, u32[]{:S(2)}) collective-permute-start(bf16[240,640]{1,0:T(8,128)(2,1)S(1)} %add_convert_fusion.1), channel_id=1, source_target_pairs={{0,16},{4,20},{8,24},{12,28},{16,0},{20,4},{24,8},{28,12},{1,17},{... | collective-permute-start | bytes 921608 | tf_op jit(solution)/shard_map/ppermute | solution.py:569
  60.9 9.4 %collective-permute-done.6.refs_4_ = bf16[480,640]{1,0:T(8,128)(2,1)} collective-permute-done((bf16[480,640]{1,0:T(8,128)(2,1)}, bf16[480,640]{1,0:T(8,128)(2,1)}, u32[]{:S(2)}, u32[]{:S(2)}) %collective-permute-start.6) | collective-permute-done | bytes 614432 | tf_op jit(solution)/shard_map/ppermute | solution.py:569
  70.3 1.1 add_convert_fusion
  71.6 4.0 %turned.1.old_ref = f32[480,640]{1,0:T(8,128)S(1)} custom-call(s32[1]{0:T(128)} %bitcast.position_ref.s_ref.refs_0_, f32[2,640,640]{2,1,0:T(8,128)} %refs_4_.5, f32[2,640,640]{2,1,0:T(8,128)} %refs_5_.3, f32[2,640,640]{2,1,0:T(8,128)} %refs_6_.3), custom_call_target="tpu_custom_call" | custom-call | flops 1228800 | bytes 9830400 | tf_op jit(solution)/shard_map/turned/pallas_call | solution.py:326
  75.6 2.5 %collective-permute-done.5.refs_2_ = bf16[240,640]{1,0:T(8,128)(2,1)S(1)} collective-permute-done((bf16[240,640]{1,0:T(8,128)(2,1)S(1)}, bf16[240,640]{1,0:T(8,128)(2,1)S(1)}, u32[]{:S(2)}, u32[]{:S(2)}) %collective-permute-start.5) | collective-permute-done | bytes 307232 | tf_op jit(solution)/shard_map/ppermute | solution.py:569
  78.1 3.6 %collective-permute-done.7.refs_5_ = bf16[240,640]{1,0:T(8,128)(2,1)S(1)} collective-permute-done((bf16[240,640]{1,0:T(8,128)(2,1)S(1)}, bf16[240,640]{1,0:T(8,128)(2,1)S(1)}, u32[]{:S(2)}, u32[]{:S(2)}) %collective-permute-start.7) | collective-permute-done | bytes 307232 | tf_op jit(solution)/shard_map/ppermute | solution.py:569
  81.7 1.7 %renorm.1.own_ref.rest_1_ = bf16[480,640]{1,0:T(8,128)(2,1)S(1)} custom-call(s32[1]{0:T(128)} %bitcast.position_ref.s_ref.refs_0_, f32[480,640]{1,0:T(8,128)S(1)} %turned.1.old_ref, bf16[480,640]{1,0:T(8,128)(2,1)S(1)} %get-tuple-element.15.refs_0_, bf16[480,640]{1,0:T(8,128)(2,1)} %collective-permute-done.4.refs_1_, ...), custom_call_target="tpu_custom_call" | custom-call | flops 3072000 | bytes 3686400 | tf_op jit(solution)/shard_map/renorm/pallas_call | solution.py:365
  83.4 2.5 %collective-permute-start.11 = (bf16[480,640]{1,0:T(8,128)(2,1)S(1)}, bf16[480,640]{1,0:T(8,128)(2,1)S(1)}, u32[]{:S(2)}, u32[]{:S(2)}) collective-permute-start(bf16[480,640]{1,0:T(8,128)(2,1)S(1)} %renorm.1.own_ref.rest_1_), channel_id=1, source_target_pairs={{0,16},{4,20},{8,24},{12,28},{16,0},{20,4},{24,8},{28,12},{1,17},{... | collective-permute-start | bytes 1843208 | tf_op jit(solution)/shard_map/ppermute | solution.py:569
  85.9 20.2 %collective-permute-start.8 = (bf16[480,640]{1,0:T(8,128)(2,1)S(1)}, bf16[480,640]{1,0:T(8,128)(2,1)S(1)}, u32[]{:S(2)}, u32[]{:S(2)}) collective-permute-start(bf16[480,640]{1,0:T(8,128)(2,1)S(1)} %renorm.1.own_ref.rest_1_), channel_id=1, source_target_pairs={{0,4},{4,0},{8,12},{12,8},{16,20},{20,16},{24,28},{28,24},{1,5},{5... | collective-permute-start | bytes 1843208 | tf_op jit(solution)/shard_map/ppermute | solution.py:569
  106.2 6.1 %collective-permute-start.10 = (bf16[480,640]{1,0:T(8,128)(2,1)S(1)}, bf16[480,640]{1,0:T(8,128)(2,1)S(1)}, u32[]{:S(2)}, u32[]{:S(2)}) collective-permute-start(bf16[480,640]{1,0:T(8,128)(2,1)S(1)} %collective-permute-done.9.over_x.rest_2_), channel_id=1, source_target_pairs={{0,4},{4,0},{8,12},{12,8},{16,20},{20,16},{24,28},{28,24},{1,5},{5... | collective-permute-start | bytes 1843208 | tf_op jit(solution)/shard_map/ppermute | solution.py:569
  112.2 1.5 %collective-permute-start.12 = (bf16[480,640]{1,0:T(8,128)(2,1)S(1)}, bf16[480,640]{1,0:T(8,128)(2,1)S(1)}, u32[]{:S(2)}, u32[]{:S(2)}) collective-permute-start(bf16[480,640]{1,0:T(8,128)(2,1)S(1)} %collective-permute-done.11.over_y.rest_3_), channel_id=1, source_target_pairs={{0,4},{4,0},{8,12},{12,8},{16,20},{20,16},{24,28},{28,24},{1,5},{5... | collective-permute-start | bytes 1843208 | tf_op jit(solution)/shard_map/ppermute | solution.py:569
  114.2 1.7 %collective-permute-start.15 = (bf16[240,640]{1,0:T(8,128)(2,1)S(1)}, bf16[240,640]{1,0:T(8,128)(2,1)S(1)}, u32[]{:S(2)}, u32[]{:S(2)}) collective-permute-start(bf16[240,640]{1,0:T(8,128)(2,1)S(1)} %slice.21), channel_id=1, source_target_pairs={{0,16},{4,20},{8,24},{12,28},{16,0},{20,4},{24,8},{28,12},{1,17},{... | collective-permute-start | bytes 921608 | tf_op jit(solution)/shard_map/ppermute | solution.py:569
  116.0 11.6 %shard_map.100.high_ref = bf16[512,1280]{1,0:T(8,128)(2,1)S(1)} custom-call(s32[1]{0:T(128)} %bitcast.position_ref.s_ref.refs_0_, bf16[1024,1280]{1,0:T(8,128)(2,1)} %refs_1_.3, bf16[1024,1280]{1,0:T(8,128)(2,1)S(1)} %collective-permute-done.refs_1_.refs_3_, bf16[1024,1280]{1,0:T(8,128)(2,1)} %refs_2_.5, ...), custom_call_target="tpu_custom_call" | custom-call | flops 3355443200 | bytes 10485760 | tf_op jit(solution)/shard_map/pallas_call | solution.py:158
  127.6 4.7 %merge.1.low_ref = bf16[512,1280]{1,0:T(8,128)(2,1)S(1)} custom-call(s32[1]{0:T(128)} %bitcast.position_ref.s_ref.refs_0_, bf16[512,1280]{1,0:T(8,128)(2,1)S(1)} %copy-done.4, bf16[512,1408]{1,0:T(8,128)(2,1)} %collective-permute-done.2.far_ref.far_log, f32[512,128]{1,0:T(8,128)S(1)} %get-tuple-element.14.own_log, ...), custom_call_target="tpu_custom_call" | custom-call | flops 5242880 | bytes 3932160 | tf_op jit(solution)/shard_map/merge/pallas_call | solution.py:404
  132.4 0.5 collective-permute-start.16
  132.9 2.0 %hidden.3.rest_0_ = bf16[1024,640]{1,0:T(8,128)(2,1)S(1)} custom-call(s32[1]{0:T(128)} %bitcast.position_ref.s_ref.refs_0_, bf16[1024,1280]{1,0:T(8,128)(2,1)S(1)} %copy-done, bf16[480,640]{1,0:T(8,128)(2,1)S(1)} %renorm.1.own_ref.rest_1_, bf16[480,640]{1,0:T(8,128)(2,1)S(1)} %collective-permute-done.9.over_x.rest_2_, ...), custom_call_target="tpu_custom_call" | custom-call | flops 1258291200 | bytes 3850240 | tf_op jit(solution)/shard_map/hidden/pallas_call | solution.py:469
  134.9 3.3 %apply.2.rest_6_ = bf16[1024,1280]{1,0:T(8,128)(2,1)} custom-call(s32[1]{0:T(128)} %bitcast.position_ref.s_ref.refs_0_, bf16[1024,1280]{1,0:T(8,128)(2,1)S(1)} %copy-done, bf16[512,1280]{1,0:T(8,128)(2,1)S(1)} %shard_map.100.high_ref, bf16[512,1280]{1,0:T(8,128)(2,1)S(1)} %merge.1.low_ref, bf16[1024,640]{1,0:T(8,128)(2,1)S(1)} %hidden.3.rest_0_, ...), custom_call_target="tpu_custom_call" | custom-call | flops 1258291200 | bytes 7700480 | tf_op jit(solution)/shard_map/apply/pallas_call | solution.py:546
  138.2 2.0 %hidden.2.rest_0_ = bf16[1024,640]{1,0:T(8,128)(2,1)S(1)} custom-call(s32[1]{0:T(128)} %bitcast.position_ref.s_ref.refs_0_, bf16[1024,1280]{1,0:T(8,128)(2,1)S(1)} %copy-done, bf16[480,640]{1,0:T(8,128)(2,1)S(1)} %collective-permute-done.8.own_ref.rest_1_, bf16[480,640]{1,0:T(8,128)(2,1)S(1)} %collective-permute-done.10.over_x.rest_2_, ...), custom_call_target="tpu_custom_call" | custom-call | flops 1258291200 | bytes 3850240 | tf_op jit(solution)/shard_map/hidden/pallas_call | solution.py:469
  140.3 3.6 %apply.3 = bf16[1024,1280]{1,0:T(8,128)(2,1)} custom-call(s32[1]{0:T(128)} %bitcast.position_ref.s_ref.refs_0_, bf16[1024,1280]{1,0:T(8,128)(2,1)S(1)} %copy-done, bf16[512,1280]{1,0:T(8,128)(2,1)S(1)} %shard_map.100.high_ref, bf16[512,1280]{1,0:T(8,128)(2,1)S(1)} %merge.1.low_ref, ...), custom_call_target="tpu_custom_call", output_to_operand_aliasing={{}: (10, {})} | custom-call | flops 1258291200 | bytes 7700480 | tf_op jit(solution)/shard_map/apply/pallas_call | solution.py:546
  (39 shorter events, 1.1 us)
Async XLA Ops:
  0.0 0.7 copy-start.5
  0.7 10.8 %copy-start.7 = (bf16[1024,1280]{1,0:T(8,128)(2,1)S(1)}, bf16[1024,1280]{1,0:T(8,128)(2,1)}, u32[]{:S(2)}) copy-start(bf16[1024,1280]{1,0:T(8,128)(2,1)} %refs_1_.3) | copy-start | bytes 7864324
  10.9 7.2 %collective-permute-start.3 = (bf16[1920,640]{1,0:T(8,128)(2,1)S(1)}, bf16[1920,640]{1,0:T(8,128)(2,1)S(1)}, u32[]{:S(2)}, u32[]{:S(2)}) collective-permute-start(bf16[1920,640]{1,0:T(8,128)(2,1)S(1)} %grads.2), channel_id=1, source_target_pairs={{0,4},{4,0},{8,12},{12,8},{16,20},{20,16},{24,28},{28,24},{1,5},{5... | collective-permute-start | bytes 7372808 | tf_op jit(solution)/shard_map/ppermute | solution.py:569
  11.6 1.5 %slice-start = ((bf16[1024,1280]{1,0:T(8,128)(2,1)}), bf16[512,1280]{1,0:T(8,128)(2,1)S(1)}, s32[]{:S(2)}) async-start(bf16[1024,1280]{1,0:T(8,128)(2,1)} %refs_3_.1), calls=%async_computation | async-start | bytes 2621440 | tf_op jit(solution)/shard_map/slice | solution.py:632
  11.6 1.7 %slice-start.1 = ((bf16[1024,1280]{1,0:T(8,128)(2,1)}), bf16[512,1280]{1,0:T(8,128)(2,1)S(1)}, s32[]{:S(2)}) async-start(bf16[1024,1280]{1,0:T(8,128)(2,1)} %refs_2_.5), calls=%async_computation.1 | async-start | bytes 2621440 | tf_op jit(solution)/shard_map/slice | solution.py:632
  11.6 22.2 %collective-permute-start.1 = (bf16[512,1280]{1,0:T(8,128)(2,1)S(1)}, bf16[512,1280]{1,0:T(8,128)(2,1)S(1)}, u32[]{:S(2)}, u32[]{:S(2)}) collective-permute-start(bf16[512,1280]{1,0:T(8,128)(2,1)S(1)} %slice.17), channel_id=1, source_target_pairs={{4,0},{8,4},{12,8},{16,12},{20,16},{24,20},{28,24},{5,1},{9,5},{13... | collective-permute-start | bytes 3932168 | tf_op jit(solution)/shard_map/ppermute | solution.py:574
  13.3 4.8 %copy-start.6 = (f32[1024,2]{0,1:T(2,128)S(1)}, f32[1024,2]{0,1:T(2,128)}, u32[]{:S(2)}) copy-start(f32[1024,2]{0,1:T(2,128)} %param.16) | copy-start | bytes 24580
  15.0 98.8 %collective-permute-start = (bf16[1024,1280]{1,0:T(8,128)(2,1)}, bf16[1024,1280]{1,0:T(8,128)(2,1)S(1)}, u32[]{:S(2)}, u32[]{:S(2)}) collective-permute-start(bf16[1024,1280]{1,0:T(8,128)(2,1)} %pad_maximum_fusion), channel_id=1, source_target_pairs={{0,4},{4,8},{8,12},{12,16},{16,20},{20,24},{24,28},{1,5},{5,9},{9,... | collective-permute-start | bytes 7864328 | tf_op jit(solution)/shard_map/ppermute | solution.py:574
  29.8 17.6 %copy-start.1 = (bf16[480,640]{1,0:T(8,128)(2,1)}, bf16[480,640]{1,0:T(8,128)(2,1)S(1)}, u32[]{:S(2)}) copy-start(bf16[480,640]{1,0:T(8,128)(2,1)S(1)} %get-tuple-element.17.refs_3_) | copy-start | bytes 1843204
  29.8 27.6 %collective-permute-start.4 = (bf16[480,640]{1,0:T(8,128)(2,1)}, bf16[480,640]{1,0:T(8,128)(2,1)}, u32[]{:S(2)}, u32[]{:S(2)}) collective-permute-start(bf16[480,640]{1,0:T(8,128)(2,1)} %get-tuple-element.16), channel_id=1, source_target_pairs={{0,8},{4,12},{8,0},{12,4},{16,24},{20,28},{24,16},{28,20},{1,9},{5... | collective-permute-start | bytes 1843208 | tf_op jit(solution)/shard_map/ppermute | solution.py:569
  32.1 38.2 %collective-permute-start.6 = (bf16[480,640]{1,0:T(8,128)(2,1)}, bf16[480,640]{1,0:T(8,128)(2,1)}, u32[]{:S(2)}, u32[]{:S(2)}) collective-permute-start(bf16[480,640]{1,0:T(8,128)(2,1)} %get-tuple-element.18), channel_id=1, source_target_pairs={{0,16},{4,20},{8,24},{12,28},{16,0},{20,4},{24,8},{28,12},{1,17},{... | collective-permute-start | bytes 1843208 | tf_op jit(solution)/shard_map/ppermute | solution.py:569
  47.4 1.1 copy-start.3
  48.5 65.8 %collective-permute-start.2 = (bf16[512,1408]{1,0:T(8,128)(2,1)}, bf16[512,1408]{1,0:T(8,128)(2,1)}, u32[]{:S(2)}, u32[]{:S(2)}) collective-permute-start(bf16[512,1408]{1,0:T(8,128)(2,1)} %get-tuple-element.13), channel_id=1, source_target_pairs={{0,4},{4,8},{8,12},{12,16},{16,20},{20,24},{24,28},{1,5},{5,9},{9,... | collective-permute-start | bytes 4325384 | tf_op jit(solution)/shard_map/ppermute | solution.py:574
  58.5 19.7 %collective-permute-start.5 = (bf16[240,640]{1,0:T(8,128)(2,1)S(1)}, bf16[240,640]{1,0:T(8,128)(2,1)S(1)}, u32[]{:S(2)}, u32[]{:S(2)}) collective-permute-start(bf16[240,640]{1,0:T(8,128)(2,1)S(1)} %add_convert_fusion.1), channel_id=1, source_target_pairs={{0,16},{4,20},{8,24},{12,28},{16,0},{20,4},{24,8},{28,12},{1,17},{... | collective-permute-start | bytes 921608 | tf_op jit(solution)/shard_map/ppermute | solution.py:569
  71.5 10.2 %copy-start.2 = (bf16[480,640]{1,0:T(8,128)(2,1)S(1)}, bf16[480,640]{1,0:T(8,128)(2,1)}, u32[]{:S(2)}) copy-start(bf16[480,640]{1,0:T(8,128)(2,1)} %copy-done.1) | copy-start | bytes 1843204
  71.5 10.2 %collective-permute-start.7 = (bf16[240,640]{1,0:T(8,128)(2,1)S(1)}, bf16[240,640]{1,0:T(8,128)(2,1)S(1)}, u32[]{:S(2)}, u32[]{:S(2)}) collective-permute-start(bf16[240,640]{1,0:T(8,128)(2,1)S(1)} %add_convert_fusion), channel_id=1, source_target_pairs={{0,8},{4,12},{8,0},{12,4},{16,24},{20,28},{24,16},{28,20},{1,9},{5... | collective-permute-start | bytes 921608 | tf_op jit(solution)/shard_map/ppermute | solution.py:569
  83.4 22.8 %collective-permute-start.9 = (bf16[480,640]{1,0:T(8,128)(2,1)S(1)}, bf16[480,640]{1,0:T(8,128)(2,1)S(1)}, u32[]{:S(2)}, u32[]{:S(2)}) collective-permute-start(bf16[480,640]{1,0:T(8,128)(2,1)S(1)} %renorm.1.own_ref.rest_1_), channel_id=1, source_target_pairs={{0,8},{4,12},{8,0},{12,4},{16,24},{20,28},{24,16},{28,20},{1,9},{5... | collective-permute-start | bytes 1843208 | tf_op jit(solution)/shard_map/ppermute | solution.py:569
  83.4 28.8 %collective-permute-start.11 = (bf16[480,640]{1,0:T(8,128)(2,1)S(1)}, bf16[480,640]{1,0:T(8,128)(2,1)S(1)}, u32[]{:S(2)}, u32[]{:S(2)}) collective-permute-start(bf16[480,640]{1,0:T(8,128)(2,1)S(1)} %renorm.1.own_ref.rest_1_), channel_id=1, source_target_pairs={{0,16},{4,20},{8,24},{12,28},{16,0},{20,4},{24,8},{28,12},{1,17},{... | collective-permute-start | bytes 1843208 | tf_op jit(solution)/shard_map/ppermute | solution.py:569
  85.9 52.3 %collective-permute-start.8 = (bf16[480,640]{1,0:T(8,128)(2,1)S(1)}, bf16[480,640]{1,0:T(8,128)(2,1)S(1)}, u32[]{:S(2)}, u32[]{:S(2)}) collective-permute-start(bf16[480,640]{1,0:T(8,128)(2,1)S(1)} %renorm.1.own_ref.rest_1_), channel_id=1, source_target_pairs={{0,4},{4,0},{8,12},{12,8},{16,20},{20,16},{24,28},{28,24},{1,5},{5... | collective-permute-start | bytes 1843208 | tf_op jit(solution)/shard_map/ppermute | solution.py:569
  106.2 32.0 %collective-permute-start.10 = (bf16[480,640]{1,0:T(8,128)(2,1)S(1)}, bf16[480,640]{1,0:T(8,128)(2,1)S(1)}, u32[]{:S(2)}, u32[]{:S(2)}) collective-permute-start(bf16[480,640]{1,0:T(8,128)(2,1)S(1)} %collective-permute-done.9.over_x.rest_2_), channel_id=1, source_target_pairs={{0,4},{4,0},{8,12},{12,8},{16,20},{20,16},{24,28},{28,24},{1,5},{5... | collective-permute-start | bytes 1843208 | tf_op jit(solution)/shard_map/ppermute | solution.py:569
  112.2 26.0 %collective-permute-start.12 = (bf16[480,640]{1,0:T(8,128)(2,1)S(1)}, bf16[480,640]{1,0:T(8,128)(2,1)S(1)}, u32[]{:S(2)}, u32[]{:S(2)}) collective-permute-start(bf16[480,640]{1,0:T(8,128)(2,1)S(1)} %collective-permute-done.11.over_y.rest_3_), channel_id=1, source_target_pairs={{0,4},{4,0},{8,12},{12,8},{16,20},{20,16},{24,28},{28,24},{1,5},{5... | collective-permute-start | bytes 1843208 | tf_op jit(solution)/shard_map/ppermute | solution.py:569
  113.8 13.8 %copy-start.4 = (bf16[512,1280]{1,0:T(8,128)(2,1)S(1)}, bf16[512,1280]{1,0:T(8,128)(2,1)}, u32[]{:S(2)}) copy-start(bf16[512,1280]{1,0:T(8,128)(2,1)} %copy-done.3) | copy-start | bytes 3932164
  113.8 18.6 %collective-permute-start.13 = (bf16[240,640]{1,0:T(8,128)(2,1)S(1)}, bf16[240,640]{1,0:T(8,128)(2,1)S(1)}, u32[]{:S(2)}, u32[]{:S(2)}) collective-permute-start(bf16[240,640]{1,0:T(8,128)(2,1)S(1)} %slice.20), channel_id=1, source_target_pairs={{0,8},{4,12},{8,0},{12,4},{16,24},{20,28},{24,16},{28,20},{1,9},{5... | collective-permute-start | bytes 921608 | tf_op jit(solution)/shard_map/ppermute | solution.py:569
  114.2 18.2 %collective-permute-start.15 = (bf16[240,640]{1,0:T(8,128)(2,1)S(1)}, bf16[240,640]{1,0:T(8,128)(2,1)S(1)}, u32[]{:S(2)}, u32[]{:S(2)}) collective-permute-start(bf16[240,640]{1,0:T(8,128)(2,1)S(1)} %slice.21), channel_id=1, source_target_pairs={{0,16},{4,20},{8,24},{12,28},{16,0},{20,4},{24,8},{28,12},{1,17},{... | collective-permute-start | bytes 921608 | tf_op jit(solution)/shard_map/ppermute | solution.py:569
  127.6 5.3 %copy-start = (bf16[1024,1280]{1,0:T(8,128)(2,1)S(1)}, bf16[1024,1280]{1,0:T(8,128)(2,1)}, u32[]{:S(2)}) copy-start(bf16[1024,1280]{1,0:T(8,128)(2,1)} %q_ref.7) | copy-start | bytes 7864324
  132.4 7.9 %collective-permute-start.14 = (bf16[240,640]{1,0:T(8,128)(2,1)S(1)}, bf16[240,640]{1,0:T(8,128)(2,1)S(1)}, u32[]{:S(2)}, u32[]{:S(2)}) collective-permute-start(bf16[240,640]{1,0:T(8,128)(2,1)S(1)} %collective-permute-done.13.rest_4_), channel_id=1, source_target_pairs={{0,4},{4,0},{8,12},{12,8},{16,20},{20,16},{24,28},{28,24},{1,5},{5... | collective-permute-start | bytes 921608 | tf_op jit(solution)/shard_map/ppermute | solution.py:569
  132.4 7.8 %collective-permute-start.16 = (bf16[240,640]{1,0:T(8,128)(2,1)S(1)}, bf16[240,640]{1,0:T(8,128)(2,1)S(1)}, u32[]{:S(2)}, u32[]{:S(2)}) collective-permute-start(bf16[240,640]{1,0:T(8,128)(2,1)S(1)} %collective-permute-done.15.rest_5_), channel_id=1, source_target_pairs={{0,4},{4,0},{8,12},{12,8},{16,20},{20,16},{24,28},{28,24},{1,5},{5... | collective-permute-start | bytes 921608 | tf_op jit(solution)/shard_map/ppermute | solution.py:569

commit v6 on v5

--- a/solution.py
+++ b/solution.py
@@ -24,7 +24,13 @@
     return lax.dot_general(a, b, dims, preferred_element_type=jnp.float32)
 
 
-def attn_kernel(position_ref, *refs, bq, jobs, sources, log_stride):
+def attn_kernel(position_ref, *refs, only, **sizes):
+    if only is None:
+        return attend(position_ref, *refs, **sizes)
+    pl.when(position_ref[0] == only)(functools.partial(attend, position_ref, *refs, **sizes))
+
+
+def attend(position_ref, *refs, bq, jobs, sources, log_stride):
     queries = refs[: len(jobs)]
     keys = refs[len(jobs) : len(jobs) + sources]
     values = refs[len(jobs) + sources : len(jobs) + 2 * sources]
@@ -124,7 +130,7 @@
     return 16 * pl.cdiv(cols // HD, 16)
 
 
-def attention(position, jobs, sources, bq, width):
+def attention(position, jobs, sources, bq, width, only=None):
     cols = jobs[0][0].shape[1]
     w = width * HD
     ranges = [r for _, _, plan, _ in jobs for tile in plan for r in tile]
@@ -150,6 +156,7 @@
     specs += [block(n, at) for _, at, _, _, n in sources] + [block(n, at) for _, _, _, at, n in sources]
     kernel = functools.partial(
         attn_kernel,
+        only=only,
         bq=bq,
         jobs=[(plan, sums) for _, _, plan, sums in jobs],
         sources=len(sources),
@@ -377,9 +384,11 @@
     )(position, old, *[array for array, _ in upper + lower])
 
 
-def merge_kernel(s_ref, own_ref, far_ref, own_log, far_log, o_ref, *, stride):
+def merge_kernel(s_ref, own_ref, far_ref, own_log, far_log, *rest, stride, local):
+    o_ref = rest[-1]
     lane = lax.broadcasted_iota(jnp.int32, own_log.shape, 1)
     heads = o_ref.shape[1] // HD
+    here = s_ref[0] == local
     for j in range(heads):
         cs = slice(j * HD, (j + 1) * HD)
         at = pl.program_id(0) * heads + j
@@ -388,25 +397,32 @@
         )
         own = pick(own_log, lane == at)
         far = pick(far_log, (lane == at) | (lane == at + stride) | (lane == at + 2 * stride))
+        b = far_ref[:, cs]
+        if local is not None:
+            far = jnp.where(here, pick(rest[1], lane == at), far)
+            b = jnp.where(here, rest[0][:, cs], b)
         far = jnp.where(s_ref[0] == 0, -jnp.inf, far)
         top = jnp.maximum(own, far)
         own, far = jnp.exp2(own - top), jnp.exp2(far - top)
         share = own / (own + far)
-        a, b = own_ref[:, cs].astype(jnp.float32), far_ref[:, cs].astype(jnp.float32)
-        o_ref[:, cs] = (a * share + b * (1.0 - share)).astype(o_ref.dtype)
-
-
-def merged(position, own, far, own_log, width):
+        a = own_ref[:, cs].astype(jnp.float32)
+        o_ref[:, cs] = (a * share + b.astype(jnp.float32) * (1.0 - share)).astype(o_ref.dtype)
+
+
+def merged(position, own, far, own_log, width, local=None, local_parts=()):
     rows, cols = own.shape
     w = width * HD
     col = pl.BlockSpec((rows, w), lambda g, s: (0, g))
     log = lambda at: pl.BlockSpec((rows, HD), lambda g, s: (0, at))
+    specs = [col, col, log(0), log(cols // HD)]
+    if local is not None:
+        specs += [col, log(0)]
     return pl.pallas_call(
-        functools.partial(merge_kernel, stride=log_stride_of(cols)),
+        functools.partial(merge_kernel, stride=log_stride_of(cols), local=local),
         grid_spec=pltpu.PrefetchScalarGridSpec(
             num_scalar_prefetch=1,
             grid=(cols // w,),
-            in_specs=[col, col, log(0), log(cols // HD)],
+            in_specs=specs,
             out_specs=col,
         ),
         out_shape=jax.ShapeDtypeStruct((rows, cols), jnp.bfloat16),
@@ -414,8 +430,8 @@
             flops=8 * rows * cols, bytes_accessed=6 * rows * cols, transcendentals=rows * cols // HD
         ),
         name="merge",
-        compiler_params=room(8),
-    )(position, own, far, own_log, far)
+        compiler_params=room(10),
+    )(position, own, far, own_log, far, *local_parts)
 
 
 def gated(h, n):
@@ -569,9 +585,16 @@
     return lax.ppermute(block, "seq", [(i, i ^ (1 << bit)) for i in range(size)])
 
 
-def shifted(block, by):
+def shifted(block, by, skip=None):
     size = lax.axis_size("seq")
-    return lax.ppermute(block, "seq", [(i, i + by) for i in range(size) if 0 <= i + by < size])
+    route = [(i, i + by) for i in range(size) if 0 <= i + by < size and (i, i + by) != skip]
+    return lax.ppermute(block, "seq", route)
+
+
+def sent(block, source, target):
+    size = lax.axis_size("seq")
+    route = [(source, target)] + [(i, i) for i in range(size) if i not in (source, target)]
+    return lax.ppermute(block, "seq", route)
 
 
 def synced(total, old, bits, position):
@@ -629,8 +652,11 @@
     rows = attn_q.shape[0]
     half = rows // 2
     width = 2 if attn_q.shape[1] // HD % 2 == 0 else 1
-    prev = shifted(jnp.concatenate([attn_k[half:], attn_v[half:]], axis=0), 1)
-    guests = shifted(attn_q[:half], -1)
+    square = heads == 2 and count == 8
+    pack = lambda lo, hi: jnp.concatenate([attn_k[lo:hi], attn_v[lo:hi]], axis=0)
+    guests = shifted(attn_q[:half], -1, (4, 3) if square else None)
+    prev = shifted(pack(half, rows), 1)
+    all_k, all_v = attn_k, attn_v
     rates_t = rates.T
     stay = lambda a: pltpu.with_memory_space_constraint(a, pltpu.HBM)
     attn_q, attn_k, attn_v = stay(attn_q), stay(attn_k), stay(attn_v)
@@ -640,9 +666,10 @@
     def grads(head, received=None):
         return gradients(position, head, fast_k, fast_v, rates_t, *weights, received)
 
-    if heads == 2 and count == 8:
+    if square:
         near, far = (lambda s: s[0] & 1), (lambda s: 1 - (s[0] & 1))
-        received = exchange(grads(far)[0], 0)
+        theirs = grads(far)[0]
+        received = exchange(theirs, 0)
         F = fast_gate.shape[1]
         mine = quarter(F)
         starts = [(F // 4, lambda s, at=i * F: at + mine(s)) for i in range(3)]
@@ -670,9 +697,20 @@
     guest = [[(0, t * bq, rows, 1)] for t in range(tiles)]
     here = (attn_k, 0, attn_v, 0, rows)
     returned, own_out, own_log = attention(position, [(guests, 0, guest, 2), (attn_q, 0, early, 1)], [here], bq, width)
-    far_out = shifted(returned, 1)
+    far_out = shifted(returned, 1, (3, 4) if square else None)
     (high,) = attention(position, [(attn_q, 1, late, 0)], [(prev, 0, prev, 1, half), here], bq, width)
-    low = merged(position, own_out, far_out, own_log, width)
+    local, local_parts = None, ()
+    if square:
+        local = 4
+        all_k, all_v, _ = lax.optimization_barrier((all_k, all_v, theirs))
+        first = jnp.concatenate([all_k[:half], all_v[:half]], axis=0)
+        first = sent(first, 3, 7)
+        first = sent(first, 7, local)
+        both = [[(0, t * bq, half, 1), (1, 0, half, 0)] for t in range(tiles)]
+        local_parts = attention(
+            position, [(attn_q, 0, both, 1)], [(first, 0, first, 1, half), (prev, 0, prev, 1, half)], bq, width, local
+        )
+    low = merged(position, own_out, far_out, own_log, width, local, local_parts)
     mixed = None
     for head, hidden, new in news:
         mixed = apply_head(position, head, fast_q, hidden, new, high, low, mixed)

time: 144 us -> 184 us (1.28)
  the two profiles are of different devices: /device:TPU:0 before, /device:TPU:20 now
where the time goes in v6:
time: 184 us; the launch traced here: 182 us
  Pallas kernels  75.7 us (41%)
  starting transfers between devices  71.5 us (39%)
  waiting for transfers between devices  25.7 us (14%)
  local copies, waits for them, and re-layouts  4.41 us (2%)
  other arithmetic  4.01 us (2%)
    ppermute x14, starting transfers between devices, exchange(): return lax.ppermute(block, 'seq', [(i, i ^ 1 << bit) for i in range(size)])  62.1 us
    pallas_call x3, Pallas kernels, attention(): pl.pallas_call(kernel, grid_spec=pltpu.PrefetchScalarGridSpec(num_scalar_...  33.2 us
    ppermute x14, waiting for transfers between devices, exchange(): return lax.ppermute(block, 'seq', [(i, i ^ 1 << bit) for i in range(size)])  25.7 us
    pallas_call x2, Pallas kernels, gradients(): pl.pallas_call(body, grid_spec=pltpu.PrefetchScalarGridSpec(num_scalar_pr...  21.8 us
    pallas_call x2, Pallas kernels, apply_head(): pl.pallas_call(functools.partial(apply_kernel, tm=tm, head=head, split=sp...  7.12 us
    ppermute x3, starting transfers between devices, shifted(): return lax.ppermute(block, 'seq', route)  5.88 us
    pallas_call x1, Pallas kernels, turned(): pl.pallas_call(functools.partial(turn_kernel, parts=parts), grid_spec=plt...  4.05 us
    pallas_call x2, Pallas kernels, hidden_part(): pl.pallas_call(functools.partial(hidden_kernel, tm=min(256, rows), head=h...  4.04 us
  transfers between devices with their start and end apart: 19, of which 4 were waited for; matrix products, arithmetic and copies ran while one was open for 3% of the time, Pallas kernels for 34%

profile of v6, /device:TPU:20, one launch (start us, length us, event | category | flops | bytes accessed | tf_op | source)
XLA Modules:
  0.0 181.8 jit_solution(15342912181586659758)
XLA Ops:
  0.7 10.1 %grads.2 = bf16[1920,640]{1,0:T(8,128)(2,1)S(1)} custom-call(s32[1]{0:T(128)} %bitcast.position_ref.refs_0_.s_ref, bf16[1024,1280]{1,0:T(8,128)(2,1)} %refs_1_.5, bf16[1024,1280]{1,0:T(8,128)(2,1)} %refs_2_.7, f32[2,1024]{1,0:T(2,128)S(1)} %bitcast.2, f32[2,640,640]{2,1,0:T(8,128)} %refs_4_.5, f32[2,640,640]{2,1,0:T(8,128)} %refs_5_.3, f32[2,640,640]{2,1,0:T(8,128)} %refs_6_.3), custom_call_target="tpu_custom_call" | custom-call | flops 5033164800 | bytes 9994240 | tf_op jit(solution)/shard_map/grads/pallas_call | solution.py:299
  10.9 1.2 slice-done
  12.7 2.3 %collective-permute-start.3 = (bf16[1024,1280]{1,0:T(8,128)(2,1)S(1)}, bf16[1024,1280]{1,0:T(8,128)(2,1)}, u32[]{:S(2)}, u32[]{:S(2)}) collective-permute-start(bf16[1024,1280]{1,0:T(8,128)(2,1)S(1)} %pad_maximum_fusion.1), channel_id=1, source_target_pairs={{12,28},{0,0},{4,4},{8,8},{16,16},{20,20},{24,24},{13,29},{1,1},{5... | collective-permute-start | bytes 7864328 | tf_op jit(solution)/shard_map/ppermute | solution.py:597
  15.0 1.7 pad_maximum_fusion
  16.7 2.4 %collective-permute-start = (bf16[1024,1280]{1,0:T(8,128)(2,1)}, bf16[1024,1280]{1,0:T(8,128)(2,1)S(1)}, u32[]{:S(2)}, u32[]{:S(2)}) collective-permute-start(bf16[1024,1280]{1,0:T(8,128)(2,1)} %pad_maximum_fusion), channel_id=1, source_target_pairs={{0,4},{4,8},{8,12},{12,16},{16,20},{20,24},{24,28},{1,5},{5,9},{9,... | collective-permute-start | bytes 7864328 | tf_op jit(solution)/shard_map/ppermute | solution.py:591
  19.0 11.7 %grads.3 = (bf16[480,640]{1,0:T(8,128)(2,1)S(1)}, bf16[480,640]{1,0:T(8,128)(2,1)}, bf16[480,640]{1,0:T(8,128)(2,1)S(1)}, bf16[480,640]{1,0:T(8,128)(2,1)}) custom-call(s32[1]{0:T(128)} %bitcast.position_ref.refs_0_.s_ref, bf16[1024,1280]{1,0:T(8,128)(2,1)} %refs_1_.5, bf16[1024,1280]{1,0:T(8,128)(2,1)} %refs_2_.7, f32[2,1024]{1,0:T(2,128)S(1)} %bitcast.3, ...), custom_call_target="tpu_custom_call" | custom-call | flops 5033164800 | bytes 9994240 | tf_op jit(solution)/shard_map/grads/pallas_call | solution.py:299
  31.6 1.5 collective-permute-start.6
  33.1 2.8 %collective-permute-start.8 = (bf16[480,640]{1,0:T(8,128)(2,1)}, bf16[480,640]{1,0:T(8,128)(2,1)}, u32[]{:S(2)}, u32[]{:S(2)}) collective-permute-start(bf16[480,640]{1,0:T(8,128)(2,1)} %get-tuple-element.26), channel_id=1, source_target_pairs={{0,16},{4,20},{8,24},{12,28},{16,0},{20,4},{24,8},{28,12},{1,17},{... | collective-permute-start | bytes 1843208 | tf_op jit(solution)/shard_map/ppermute | solution.py:585
  35.9 1.1 slice.23
  37.0 1.3 collective-permute-start.1
  38.3 1.3 collective-permute-start.4
  39.6 8.3 %collective-permute-done.6.refs_1_ = bf16[480,640]{1,0:T(8,128)(2,1)} collective-permute-done((bf16[480,640]{1,0:T(8,128)(2,1)}, bf16[480,640]{1,0:T(8,128)(2,1)}, u32[]{:S(2)}, u32[]{:S(2)}) %collective-permute-start.6) | collective-permute-done | bytes 614432 | tf_op jit(solution)/shard_map/ppermute | solution.py:585
  49.0 11.6 %collective-permute-start.7 = (bf16[240,640]{1,0:T(8,128)(2,1)S(1)}, bf16[240,640]{1,0:T(8,128)(2,1)S(1)}, u32[]{:S(2)}, u32[]{:S(2)}) collective-permute-start(bf16[240,640]{1,0:T(8,128)(2,1)S(1)} %add_convert_fusion.1), channel_id=1, source_target_pairs={{0,16},{4,20},{8,24},{12,28},{16,0},{20,4},{24,8},{28,12},{1,17},{... | collective-permute-start | bytes 921608 | tf_op jit(solution)/shard_map/ppermute | solution.py:585
  60.6 2.9 %collective-permute-done.8.refs_4_ = bf16[480,640]{1,0:T(8,128)(2,1)} collective-permute-done((bf16[480,640]{1,0:T(8,128)(2,1)}, bf16[480,640]{1,0:T(8,128)(2,1)}, u32[]{:S(2)}, u32[]{:S(2)}) %collective-permute-start.8) | collective-permute-done | bytes 614432 | tf_op jit(solution)/shard_map/ppermute | solution.py:585
  64.7 4.0 %turned.1.old_ref = f32[480,640]{1,0:T(8,128)S(1)} custom-call(s32[1]{0:T(128)} %bitcast.position_ref.refs_0_.s_ref, f32[2,640,640]{2,1,0:T(8,128)} %refs_4_.5, f32[2,640,640]{2,1,0:T(8,128)} %refs_5_.3, f32[2,640,640]{2,1,0:T(8,128)} %refs_6_.3), custom_call_target="tpu_custom_call" | custom-call | flops 1228800 | bytes 9830400 | tf_op jit(solution)/shard_map/turned/pallas_call | solution.py:333
  68.8 7.1 %collective-permute-done.9.refs_5_ = bf16[240,640]{1,0:T(8,128)(2,1)S(1)} collective-permute-done((bf16[240,640]{1,0:T(8,128)(2,1)S(1)}, bf16[240,640]{1,0:T(8,128)(2,1)S(1)}, u32[]{:S(2)}, u32[]{:S(2)}) %collective-permute-start.9) | collective-permute-done | bytes 307232 | tf_op jit(solution)/shard_map/ppermute | solution.py:585
  75.9 1.7 renorm.1.own_ref.rest_1_
  77.6 6.9 %collective-permute-start.13 = (bf16[480,640]{1,0:T(8,128)(2,1)S(1)}, bf16[480,640]{1,0:T(8,128)(2,1)S(1)}, u32[]{:S(2)}, u32[]{:S(2)}) collective-permute-start(bf16[480,640]{1,0:T(8,128)(2,1)S(1)} %renorm.1.own_ref.rest_1_), channel_id=1, source_target_pairs={{0,16},{4,20},{8,24},{12,28},{16,0},{20,4},{24,8},{28,12},{1,17},{... | collective-permute-start | bytes 1843208 | tf_op jit(solution)/shard_map/ppermute | solution.py:585
  84.5 21.0 %collective-permute-start.10 = (bf16[480,640]{1,0:T(8,128)(2,1)S(1)}, bf16[480,640]{1,0:T(8,128)(2,1)S(1)}, u32[]{:S(2)}, u32[]{:S(2)}) collective-permute-start(bf16[480,640]{1,0:T(8,128)(2,1)S(1)} %renorm.1.own_ref.rest_1_), channel_id=1, source_target_pairs={{0,4},{4,0},{8,12},{12,8},{16,20},{20,16},{24,28},{28,24},{1,5},{5... | collective-permute-start | bytes 1843208 | tf_op jit(solution)/shard_map/ppermute | solution.py:585
  105.5 12.5 %shard_map.101 = (bf16[512,1408]{1,0:T(8,128)(2,1)S(1)}, bf16[512,1280]{1,0:T(8,128)(2,1)S(1)}, f32[512,128]{1,0:T(8,128)S(1)}) custom-call(s32[1]{0:T(128)} %bitcast.position_ref.refs_0_.s_ref, bf16[512,1280]{1,0:T(8,128)(2,1)} %collective-permute-done.1.refs_0_, bf16[1024,1280]{1,0:T(8,128)(2,1)} %refs_0_.3, bf16[1024,1280]{1,0:T(8,128)(2,1)} %refs_2_.5, ...), custom_call_target="tpu_custom_call" | custom-call | flops 3355443200 | bytes 10485760 | tf_op jit(solution)/shard_map/pallas_call | solution.py:165
  118.1 2.2 %collective-permute-start.2 = (bf16[512,1408]{1,0:T(8,128)(2,1)S(1)}, bf16[512,1408]{1,0:T(8,128)(2,1)S(1)}, u32[]{:S(2)}, u32[]{:S(2)}) collective-permute-start(bf16[512,1408]{1,0:T(8,128)(2,1)S(1)} %get-tuple-element.17), channel_id=1, source_target_pairs={{0,4},{4,8},{8,12},{16,20},{20,24},{24,28},{1,5},{5,9},{9,13},{17,... | collective-permute-start | bytes 4325384 | tf_op jit(solution)/shard_map/ppermute | solution.py:591
  120.4 1.6 collective-permute-start.15
  122.6 7.3 %collective-permute-done.15.rest_4_ = bf16[240,640]{1,0:T(8,128)(2,1)S(1)} collective-permute-done((bf16[240,640]{1,0:T(8,128)(2,1)S(1)}, bf16[240,640]{1,0:T(8,128)(2,1)S(1)}, u32[]{:S(2)}, u32[]{:S(2)}) %collective-permute-start.15) | collective-permute-done | bytes 307232 | tf_op jit(solution)/shard_map/ppermute | solution.py:585
  129.9 1.5 collective-permute-start.17
  131.4 11.6 %shard_map.100.high_ref = bf16[512,1280]{1,0:T(8,128)(2,1)S(1)} custom-call(s32[1]{0:T(128)} %bitcast.position_ref.refs_0_.s_ref, bf16[1024,1280]{1,0:T(8,128)(2,1)} %refs_0_.3, bf16[1024,1280]{1,0:T(8,128)(2,1)S(1)} %collective-permute-done.refs_1_.refs_3_.refs_2_.refs_4_, bf16[1024,1280]{1,0:T(8,128)(2,1)} %refs_2_.5, ...), custom_call_target="tpu_custom_call" | custom-call | flops 3355443200 | bytes 10485760 | tf_op jit(solution)/shard_map/pallas_call | solution.py:165
  143.1 2.0 %hidden.3.rest_0_ = bf16[1024,640]{1,0:T(8,128)(2,1)S(1)} custom-call(s32[1]{0:T(128)} %bitcast.position_ref.refs_0_.s_ref, bf16[1024,1280]{1,0:T(8,128)(2,1)S(1)} %copy-done, bf16[480,640]{1,0:T(8,128)(2,1)S(1)} %renorm.1.own_ref.rest_1_, bf16[480,640]{1,0:T(8,128)(2,1)S(1)} %collective-permute-done.11.over_x.rest_2_, ...), custom_call_target="tpu_custom_call" | custom-call | flops 1258291200 | bytes 3850240 | tf_op jit(solution)/shard_map/hidden/pallas_call | solution.py:485
  145.1 14.4 %collective-permute-start.16 = (bf16[240,640]{1,0:T(8,128)(2,1)S(1)}, bf16[240,640]{1,0:T(8,128)(2,1)S(1)}, u32[]{:S(2)}, u32[]{:S(2)}) collective-permute-start(bf16[240,640]{1,0:T(8,128)(2,1)S(1)} %collective-permute-done.15.rest_4_), channel_id=1, source_target_pairs={{0,4},{4,0},{8,12},{12,8},{16,20},{20,16},{24,28},{28,24},{1,5},{5... | collective-permute-start | bytes 921608 | tf_op jit(solution)/shard_map/ppermute | solution.py:585
  159.6 2.0 %hidden.2.rest_0_ = bf16[1024,640]{1,0:T(8,128)(2,1)S(1)} custom-call(s32[1]{0:T(128)} %bitcast.position_ref.refs_0_.s_ref, bf16[1024,1280]{1,0:T(8,128)(2,1)S(1)} %copy-done, bf16[480,640]{1,0:T(8,128)(2,1)S(1)} %collective-permute-done.10.own_ref.rest_1_, bf16[480,640]{1,0:T(8,128)(2,1)S(1)} %collective-permute-done.12.over_x.rest_2_, ...), custom_call_target="tpu_custom_call" | custom-call | flops 1258291200 | bytes 3850240 | tf_op jit(solution)/shard_map/hidden/pallas_call | solution.py:485
  161.6 9.0 %shard_map.102 = (bf16[512,1280]{1,0:T(8,128)(2,1)S(1)}, f32[512,128]{1,0:T(8,128)S(1)}) custom-call(s32[1]{0:T(128)} %bitcast.position_ref.refs_0_.s_ref, bf16[1024,1280]{1,0:T(8,128)(2,1)} %refs_0_.3, bf16[1024,1280]{1,0:T(8,128)(2,1)} %collective-permute-done.4.refs_1_.refs_3_, ...), custom_call_target="tpu_custom_call" | custom-call | flops 2348810240 | bytes 10485760 | tf_op jit(solution)/shard_map/pallas_call | solution.py:165
  170.6 3.9 %merge.1.low_ref = bf16[512,1280]{1,0:T(8,128)(2,1)S(1)} custom-call(s32[1]{0:T(128)} %bitcast.position_ref.refs_0_.s_ref, bf16[512,1280]{1,0:T(8,128)(2,1)S(1)} %get-tuple-element.16.own_ref, bf16[512,1408]{1,0:T(8,128)(2,1)S(1)} %collective-permute-done.2.far_ref.far_log, f32[512,128]{1,0:T(8,128)S(1)} %get-tuple-element.18.own_log, ...), custom_call_target="tpu_custom_call" | custom-call | flops 5242880 | bytes 3932160 | tf_op jit(solution)/shard_map/merge/pallas_call | solution.py:420
  174.5 3.4 %apply.2.rest_6_ = bf16[1024,1280]{1,0:T(8,128)(2,1)} custom-call(s32[1]{0:T(128)} %bitcast.position_ref.refs_0_.s_ref, bf16[1024,1280]{1,0:T(8,128)(2,1)S(1)} %copy-done, bf16[512,1280]{1,0:T(8,128)(2,1)S(1)} %shard_map.100.high_ref, bf16[512,1280]{1,0:T(8,128)(2,1)S(1)} %merge.1.low_ref, bf16[1024,640]{1,0:T(8,128)(2,1)S(1)} %hidden.3.rest_0_, ...), custom_call_target="tpu_custom_call" | custom-call | flops 1258291200 | bytes 7700480 | tf_op jit(solution)/shard_map/apply/pallas_call | solution.py:562
  177.9 3.7 %apply.3 = bf16[1024,1280]{1,0:T(8,128)(2,1)} custom-call(s32[1]{0:T(128)} %bitcast.position_ref.refs_0_.s_ref, bf16[1024,1280]{1,0:T(8,128)(2,1)S(1)} %copy-done, bf16[512,1280]{1,0:T(8,128)(2,1)S(1)} %shard_map.100.high_ref, bf16[512,1280]{1,0:T(8,128)(2,1)S(1)} %merge.1.low_ref, ...), custom_call_target="tpu_custom_call", output_to_operand_aliasing={{}: (10, {})} | custom-call | flops 1258291200 | bytes 7700480 | tf_op jit(solution)/shard_map/apply/pallas_call | solution.py:562
  (45 shorter events, 5.2 us)
Async XLA Ops:
  0.0 0.7 copy-start.3
  10.8 1.3 slice-start
  10.8 1.7 slice-start.2
  10.8 8.2 %collective-permute-start.5 = (bf16[1920,640]{1,0:T(8,128)(2,1)S(1)}, bf16[1920,640]{1,0:T(8,128)(2,1)S(1)}, u32[]{:S(2)}, u32[]{:S(2)}) collective-permute-start(bf16[1920,640]{1,0:T(8,128)(2,1)S(1)} %grads.2), channel_id=1, source_target_pairs={{0,4},{4,0},{8,12},{12,8},{16,20},{20,16},{24,28},{28,24},{1,5},{5... | collective-permute-start | bytes 7372808 | tf_op jit(solution)/shard_map/ppermute | solution.py:585
  12.7 2.3 %slice-start.1 = ((bf16[1024,1280]{1,0:T(8,128)(2,1)}), bf16[512,1280]{1,0:T(8,128)(2,1)S(1)}, s32[]{:S(2)}) async-start(bf16[1024,1280]{1,0:T(8,128)(2,1)} %refs_3_.1), calls=%async_computation.1 | async-start | bytes 2621440 | tf_op jit(solution)/shard_map/slice | solution.py:656
  12.7 2.3 %slice-start.3 = ((bf16[1024,1280]{1,0:T(8,128)(2,1)}), bf16[512,1280]{1,0:T(8,128)(2,1)S(1)}, s32[]{:S(2)}) async-start(bf16[1024,1280]{1,0:T(8,128)(2,1)} %refs_2_.5), calls=%async_computation.3 | async-start | bytes 2621440 | tf_op jit(solution)/shard_map/slice | solution.py:656
  12.7 25.6 %collective-permute-start.3 = (bf16[1024,1280]{1,0:T(8,128)(2,1)S(1)}, bf16[1024,1280]{1,0:T(8,128)(2,1)}, u32[]{:S(2)}, u32[]{:S(2)}) collective-permute-start(bf16[1024,1280]{1,0:T(8,128)(2,1)S(1)} %pad_maximum_fusion.1), channel_id=1, source_target_pairs={{12,28},{0,0},{4,4},{8,8},{16,16},{20,20},{24,24},{13,29},{1,1},{5... | collective-permute-start | bytes 7864328 | tf_op jit(solution)/shard_map/ppermute | solution.py:597
  15.0 4.0 %copy-start.4 = (f32[1024,2]{0,1:T(2,128)S(1)}, f32[1024,2]{0,1:T(2,128)}, u32[]{:S(2)}) copy-start(f32[1024,2]{0,1:T(2,128)} %param.16) | copy-start | bytes 24580
  16.6 19.2 %copy-start.5 = (bf16[1024,1280]{1,0:T(8,128)(2,1)S(1)}, bf16[1024,1280]{1,0:T(8,128)(2,1)}, u32[]{:S(2)}) copy-start(bf16[1024,1280]{1,0:T(8,128)(2,1)} %refs_0_.3) | copy-start | bytes 7864324
  16.7 103.7 %collective-permute-start = (bf16[1024,1280]{1,0:T(8,128)(2,1)}, bf16[1024,1280]{1,0:T(8,128)(2,1)S(1)}, u32[]{:S(2)}, u32[]{:S(2)}) collective-permute-start(bf16[1024,1280]{1,0:T(8,128)(2,1)} %pad_maximum_fusion), channel_id=1, source_target_pairs={{0,4},{4,8},{8,12},{12,16},{16,20},{20,24},{24,28},{1,5},{5,9},{9,... | collective-permute-start | bytes 7864328 | tf_op jit(solution)/shard_map/ppermute | solution.py:591
  30.7 0.9 copy-start.1
  31.6 16.4 %collective-permute-start.6 = (bf16[480,640]{1,0:T(8,128)(2,1)}, bf16[480,640]{1,0:T(8,128)(2,1)}, u32[]{:S(2)}, u32[]{:S(2)}) collective-permute-start(bf16[480,640]{1,0:T(8,128)(2,1)} %get-tuple-element.24), channel_id=1, source_target_pairs={{0,8},{4,12},{8,0},{12,4},{16,24},{20,28},{24,16},{28,20},{1,9},{5... | collective-permute-start | bytes 1843208 | tf_op jit(solution)/shard_map/ppermute | solution.py:585
  33.1 30.4 %collective-permute-start.8 = (bf16[480,640]{1,0:T(8,128)(2,1)}, bf16[480,640]{1,0:T(8,128)(2,1)}, u32[]{:S(2)}, u32[]{:S(2)}) collective-permute-start(bf16[480,640]{1,0:T(8,128)(2,1)} %get-tuple-element.26), channel_id=1, source_target_pairs={{0,16},{4,20},{8,24},{12,28},{16,0},{20,4},{24,8},{28,12},{1,17},{... | collective-permute-start | bytes 1843208 | tf_op jit(solution)/shard_map/ppermute | solution.py:585
  37.0 47.5 %collective-permute-start.1 = (bf16[512,1280]{1,0:T(8,128)(2,1)}, bf16[512,1280]{1,0:T(8,128)(2,1)}, u32[]{:S(2)}, u32[]{:S(2)}) collective-permute-start(bf16[512,1280]{1,0:T(8,128)(2,1)} %slice.23), channel_id=1, source_target_pairs={{4,0},{8,4},{12,8},{20,16},{24,20},{28,24},{5,1},{9,5},{13,9},{21,... | collective-permute-start | bytes 3932168 | tf_op jit(solution)/shard_map/ppermute | solution.py:591
  38.3 123.3 %collective-permute-start.4 = (bf16[1024,1280]{1,0:T(8,128)(2,1)}, bf16[1024,1280]{1,0:T(8,128)(2,1)}, u32[]{:S(2)}, u32[]{:S(2)}) collective-permute-start(bf16[1024,1280]{1,0:T(8,128)(2,1)} %collective-permute-done.3), channel_id=1, source_target_pairs={{28,16},{0,0},{4,4},{8,8},{12,12},{20,20},{24,24},{29,17},{1,1},{5... | collective-permute-start | bytes 7864328 | tf_op jit(solution)/shard_map/ppermute | solution.py:597
  49.0 19.8 %collective-permute-start.7 = (bf16[240,640]{1,0:T(8,128)(2,1)S(1)}, bf16[240,640]{1,0:T(8,128)(2,1)S(1)}, u32[]{:S(2)}, u32[]{:S(2)}) collective-permute-start(bf16[240,640]{1,0:T(8,128)(2,1)S(1)} %add_convert_fusion.1), channel_id=1, source_target_pairs={{0,16},{4,20},{8,24},{12,28},{16,0},{20,4},{24,8},{28,12},{1,17},{... | collective-permute-start | bytes 921608 | tf_op jit(solution)/shard_map/ppermute | solution.py:585
  64.6 11.3 %copy-start.2 = (bf16[480,640]{1,0:T(8,128)(2,1)S(1)}, bf16[480,640]{1,0:T(8,128)(2,1)}, u32[]{:S(2)}) copy-start(bf16[480,640]{1,0:T(8,128)(2,1)} %copy-done.1) | copy-start | bytes 1843204
  64.6 11.3 %collective-permute-start.9 = (bf16[240,640]{1,0:T(8,128)(2,1)S(1)}, bf16[240,640]{1,0:T(8,128)(2,1)S(1)}, u32[]{:S(2)}, u32[]{:S(2)}) collective-permute-start(bf16[240,640]{1,0:T(8,128)(2,1)S(1)} %add_convert_fusion), channel_id=1, source_target_pairs={{0,8},{4,12},{8,0},{12,4},{16,24},{20,28},{24,16},{28,20},{1,9},{5... | collective-permute-start | bytes 921608 | tf_op jit(solution)/shard_map/ppermute | solution.py:585
  77.6 40.5 %collective-permute-start.13 = (bf16[480,640]{1,0:T(8,128)(2,1)S(1)}, bf16[480,640]{1,0:T(8,128)(2,1)S(1)}, u32[]{:S(2)}, u32[]{:S(2)}) collective-permute-start(bf16[480,640]{1,0:T(8,128)(2,1)S(1)} %renorm.1.own_ref.rest_1_), channel_id=1, source_target_pairs={{0,16},{4,20},{8,24},{12,28},{16,0},{20,4},{24,8},{28,12},{1,17},{... | collective-permute-start | bytes 1843208 | tf_op jit(solution)/shard_map/ppermute | solution.py:585
  84.5 37.5 %collective-permute-start.11 = (bf16[480,640]{1,0:T(8,128)(2,1)S(1)}, bf16[480,640]{1,0:T(8,128)(2,1)S(1)}, u32[]{:S(2)}, u32[]{:S(2)}) collective-permute-start(bf16[480,640]{1,0:T(8,128)(2,1)S(1)} %renorm.1.own_ref.rest_1_), channel_id=1, source_target_pairs={{0,8},{4,12},{8,0},{12,4},{16,24},{20,28},{24,16},{28,20},{1,9},{5... | collective-permute-start | bytes 1843208 | tf_op jit(solution)/shard_map/ppermute | solution.py:585
  84.5 37.7 %collective-permute-start.10 = (bf16[480,640]{1,0:T(8,128)(2,1)S(1)}, bf16[480,640]{1,0:T(8,128)(2,1)S(1)}, u32[]{:S(2)}, u32[]{:S(2)}) collective-permute-start(bf16[480,640]{1,0:T(8,128)(2,1)S(1)} %renorm.1.own_ref.rest_1_), channel_id=1, source_target_pairs={{0,4},{4,0},{8,12},{12,8},{16,20},{20,16},{24,28},{28,24},{1,5},{5... | collective-permute-start | bytes 1843208 | tf_op jit(solution)/shard_map/ppermute | solution.py:585
  118.1 52.5 %collective-permute-start.2 = (bf16[512,1408]{1,0:T(8,128)(2,1)S(1)}, bf16[512,1408]{1,0:T(8,128)(2,1)S(1)}, u32[]{:S(2)}, u32[]{:S(2)}) collective-permute-start(bf16[512,1408]{1,0:T(8,128)(2,1)S(1)} %get-tuple-element.17), channel_id=1, source_target_pairs={{0,4},{4,8},{8,12},{16,20},{20,24},{24,28},{1,5},{5,9},{9,13},{17,... | collective-permute-start | bytes 4325384 | tf_op jit(solution)/shard_map/ppermute | solution.py:591
  120.4 9.5 %collective-permute-start.15 = (bf16[240,640]{1,0:T(8,128)(2,1)S(1)}, bf16[240,640]{1,0:T(8,128)(2,1)S(1)}, u32[]{:S(2)}, u32[]{:S(2)}) collective-permute-start(bf16[240,640]{1,0:T(8,128)(2,1)S(1)} %slice.28), channel_id=1, source_target_pairs={{0,8},{4,12},{8,0},{12,4},{16,24},{20,28},{24,16},{28,20},{1,9},{5... | collective-permute-start | bytes 921608 | tf_op jit(solution)/shard_map/ppermute | solution.py:585
  122.0 37.5 %collective-permute-start.12 = (bf16[480,640]{1,0:T(8,128)(2,1)S(1)}, bf16[480,640]{1,0:T(8,128)(2,1)S(1)}, u32[]{:S(2)}, u32[]{:S(2)}) collective-permute-start(bf16[480,640]{1,0:T(8,128)(2,1)S(1)} %collective-permute-done.11.over_x.rest_2_), channel_id=1, source_target_pairs={{0,4},{4,0},{8,12},{12,8},{16,20},{20,16},{24,28},{28,24},{1,5},{5... | collective-permute-start | bytes 1843208 | tf_op jit(solution)/shard_map/ppermute | solution.py:585
  122.2 37.4 %collective-permute-start.14 = (bf16[480,640]{1,0:T(8,128)(2,1)S(1)}, bf16[480,640]{1,0:T(8,128)(2,1)S(1)}, u32[]{:S(2)}, u32[]{:S(2)}) collective-permute-start(bf16[480,640]{1,0:T(8,128)(2,1)S(1)} %collective-permute-done.13.over_y.rest_3_), channel_id=1, source_target_pairs={{0,4},{4,0},{8,12},{12,8},{16,20},{20,16},{24,28},{28,24},{1,5},{5... | collective-permute-start | bytes 1843208 | tf_op jit(solution)/shard_map/ppermute | solution.py:585
  122.6 20.5 %copy-start = (bf16[1024,1280]{1,0:T(8,128)(2,1)S(1)}, bf16[1024,1280]{1,0:T(8,128)(2,1)}, u32[]{:S(2)}) copy-start(bf16[1024,1280]{1,0:T(8,128)(2,1)} %q_ref.7) | copy-start | bytes 7864324
  129.9 15.2 %collective-permute-start.17 = (bf16[240,640]{1,0:T(8,128)(2,1)S(1)}, bf16[240,640]{1,0:T(8,128)(2,1)S(1)}, u32[]{:S(2)}, u32[]{:S(2)}) collective-permute-start(bf16[240,640]{1,0:T(8,128)(2,1)S(1)} %slice.29), channel_id=1, source_target_pairs={{0,16},{4,20},{8,24},{12,28},{16,0},{20,4},{24,8},{28,12},{1,17},{... | collective-permute-start | bytes 921608 | tf_op jit(solution)/shard_map/ppermute | solution.py:585
  145.1 32.8 %collective-permute-start.16 = (bf16[240,640]{1,0:T(8,128)(2,1)S(1)}, bf16[240,640]{1,0:T(8,128)(2,1)S(1)}, u32[]{:S(2)}, u32[]{:S(2)}) collective-permute-start(bf16[240,640]{1,0:T(8,128)(2,1)S(1)} %collective-permute-done.15.rest_4_), channel_id=1, source_target_pairs={{0,4},{4,0},{8,12},{12,8},{16,20},{20,16},{24,28},{28,24},{1,5},{5... | collective-permute-start | bytes 921608 | tf_op jit(solution)/shard_map/ppermute | solution.py:585
  159.5 18.4 %collective-permute-start.18 = (bf16[240,640]{1,0:T(8,128)(2,1)S(1)}, bf16[240,640]{1,0:T(8,128)(2,1)S(1)}, u32[]{:S(2)}, u32[]{:S(2)}) collective-permute-start(bf16[240,640]{1,0:T(8,128)(2,1)S(1)} %collective-permute-done.17.rest_5_), channel_id=1, source_target_pairs={{0,4},{4,0},{8,12},{12,8},{16,20},{20,16},{24,28},{28,24},{1,5},{5... | collective-permute-start | bytes 921608 | tf_op jit(solution)/shard_map/ppermute | solution.py:585

commit v7 on v6

--- a/solution.py
+++ b/solution.py
@@ -136,7 +136,8 @@
     ranges = [r for _, _, plan, _ in jobs for tile in plan for r in tile]
     span = max(sum(hi - lo for _, lo, hi, _ in tile) for _, _, plan, _ in jobs for tile in plan)
     pairs = bq * sum(hi - lo for _, lo, hi, _ in ranges) * cols // HD
-    block = lambda n, at: pl.BlockSpec((n, w), lambda g, f: (at, g))
+    moving = (lambda g, f: g) if only is None else (lambda g, f: jnp.where(f[0] == only, g, 0))
+    block = lambda n, at: pl.BlockSpec((n, w), lambda g, f: (at, moving(g, f)))
     whole = lambda *shape: pl.BlockSpec(shape, lambda g, f: (0, 0))
     outs, out_specs, logs = [], [], []
     for _, _, plan, sums in jobs:
@@ -592,9 +593,7 @@
 
 
 def sent(block, source, target):
-    size = lax.axis_size("seq")
-    route = [(source, target)] + [(i, i) for i in range(size) if i not in (source, target)]
-    return lax.ppermute(block, "seq", route)
+    return lax.ppermute(block, "seq", [(source, target)])
 
 
 def synced(total, old, bits, position):

time: 184 us -> 183 us (level)
  the two profiles are of different devices: /device:TPU:20 before, /device:TPU:28 now
where the time goes in v7:
time: 183 us; the launch traced here: 182 us
  Pallas kernels  75.9 us (41%)
  starting transfers between devices  62.9 us (34%)
  waiting for transfers between devices  34.4 us (19%)
  local copies, waits for them, and re-layouts  4.41 us (2%)
  other arithmetic  4.01 us (2%)
    ppermute x14, starting transfers between devices, exchange(): return lax.ppermute(block, 'seq', [(i, i ^ 1 << bit) for i in range(size)])  53.4 us
    ppermute x14, waiting for transfers between devices, exchange(): return lax.ppermute(block, 'seq', [(i, i ^ 1 << bit) for i in range(size)])  34.4 us
    pallas_call x3, Pallas kernels, attention(): pl.pallas_call(kernel, grid_spec=pltpu.PrefetchScalarGridSpec(num_scalar_...  33.4 us
    pallas_call x2, Pallas kernels, gradients(): pl.pallas_call(body, grid_spec=pltpu.PrefetchScalarGridSpec(num_scalar_pr...  21.8 us
    pallas_call x2, Pallas kernels, apply_head(): pl.pallas_call(functools.partial(apply_kernel, tm=tm, head=head, split=sp...  7.12 us
    ppermute x3, starting transfers between devices, shifted(): return lax.ppermute(block, 'seq', route)  5.88 us
    pallas_call x1, Pallas kernels, turned(): pl.pallas_call(functools.partial(turn_kernel, parts=parts), grid_spec=plt...  4.05 us
    pallas_call x2, Pallas kernels, hidden_part(): pl.pallas_call(functools.partial(hidden_kernel, tm=min(256, rows), head=h...  4.03 us
  transfers between devices with their start and end apart: 19, of which 4 were waited for; matrix products, arithmetic and copies ran while one was open for 3% of the time, Pallas kernels for 34%

profile of v7, /device:TPU:28, one launch (start us, length us, event | category | flops | bytes accessed | tf_op | source)
XLA Modules:
  0.0 182.1 jit_solution(8729892431793544080)
XLA Ops:
  0.7 10.1 %grads.2 = bf16[1920,640]{1,0:T(8,128)(2,1)S(1)} custom-call(s32[1]{0:T(128)} %bitcast.position_ref.refs_0_.s_ref, bf16[1024,1280]{1,0:T(8,128)(2,1)} %refs_1_.5, bf16[1024,1280]{1,0:T(8,128)(2,1)} %refs_2_.7, f32[2,1024]{1,0:T(2,128)S(1)} %bitcast.2, f32[2,640,640]{2,1,0:T(8,128)} %refs_4_.5, f32[2,640,640]{2,1,0:T(8,128)} %refs_5_.3, f32[2,640,640]{2,1,0:T(8,128)} %refs_6_.3), custom_call_target="tpu_custom_call" | custom-call | flops 5033164800 | bytes 9994240 | tf_op jit(solution)/shard_map/grads/pallas_call | solution.py:300
  10.9 1.2 slice-done
  12.7 2.3 %collective-permute-start.3 = (bf16[1024,1280]{1,0:T(8,128)(2,1)S(1)}, bf16[1024,1280]{1,0:T(8,128)(2,1)}, u32[]{:S(2)}, u32[]{:S(2)}) collective-permute-start(bf16[1024,1280]{1,0:T(8,128)(2,1)S(1)} %pad_maximum_fusion.1), channel_id=1, source_target_pairs={{12,28},{13,29},{14,30},{15,31}} | collective-permute-start | bytes 7864328 | tf_op jit(solution)/shard_map/ppermute | solution.py:596
  15.0 1.7 pad_maximum_fusion
  16.7 2.4 %collective-permute-start = (bf16[1024,1280]{1,0:T(8,128)(2,1)}, bf16[1024,1280]{1,0:T(8,128)(2,1)S(1)}, u32[]{:S(2)}, u32[]{:S(2)}) collective-permute-start(bf16[1024,1280]{1,0:T(8,128)(2,1)} %pad_maximum_fusion), channel_id=1, source_target_pairs={{0,4},{4,8},{8,12},{12,16},{16,20},{20,24},{24,28},{1,5},{5,9},{9,... | collective-permute-start | bytes 7864328 | tf_op jit(solution)/shard_map/ppermute | solution.py:592
  19.0 11.7 %grads.3 = (bf16[480,640]{1,0:T(8,128)(2,1)S(1)}, bf16[480,640]{1,0:T(8,128)(2,1)}, bf16[480,640]{1,0:T(8,128)(2,1)S(1)}, bf16[480,640]{1,0:T(8,128)(2,1)}) custom-call(s32[1]{0:T(128)} %bitcast.position_ref.refs_0_.s_ref, bf16[1024,1280]{1,0:T(8,128)(2,1)} %refs_1_.5, bf16[1024,1280]{1,0:T(8,128)(2,1)} %refs_2_.7, f32[2,1024]{1,0:T(2,128)S(1)} %bitcast.3, ...), custom_call_target="tpu_custom_call" | custom-call | flops 5033164800 | bytes 9994240 | tf_op jit(solution)/shard_map/grads/pallas_call | solution.py:300
  31.6 1.5 collective-permute-start.6
  33.1 2.8 %collective-permute-start.8 = (bf16[480,640]{1,0:T(8,128)(2,1)}, bf16[480,640]{1,0:T(8,128)(2,1)}, u32[]{:S(2)}, u32[]{:S(2)}) collective-permute-start(bf16[480,640]{1,0:T(8,128)(2,1)} %get-tuple-element.26), channel_id=1, source_target_pairs={{0,16},{4,20},{8,24},{12,28},{16,0},{20,4},{24,8},{28,12},{1,17},{... | collective-permute-start | bytes 1843208 | tf_op jit(solution)/shard_map/ppermute | solution.py:586
  35.9 1.1 slice.23
  37.0 1.3 collective-permute-start.1
  38.3 1.3 collective-permute-start.4
  39.6 8.4 %collective-permute-done.6.refs_1_ = bf16[480,640]{1,0:T(8,128)(2,1)} collective-permute-done((bf16[480,640]{1,0:T(8,128)(2,1)}, bf16[480,640]{1,0:T(8,128)(2,1)}, u32[]{:S(2)}, u32[]{:S(2)}) %collective-permute-start.6) | collective-permute-done | bytes 614432 | tf_op jit(solution)/shard_map/ppermute | solution.py:586
  49.1 2.9 %collective-permute-start.7 = (bf16[240,640]{1,0:T(8,128)(2,1)S(1)}, bf16[240,640]{1,0:T(8,128)(2,1)S(1)}, u32[]{:S(2)}, u32[]{:S(2)}) collective-permute-start(bf16[240,640]{1,0:T(8,128)(2,1)S(1)} %add_convert_fusion.1), channel_id=1, source_target_pairs={{0,16},{4,20},{8,24},{12,28},{16,0},{20,4},{24,8},{28,12},{1,17},{... | collective-permute-start | bytes 921608 | tf_op jit(solution)/shard_map/ppermute | solution.py:586
  52.0 11.5 %collective-permute-done.8.refs_4_ = bf16[480,640]{1,0:T(8,128)(2,1)} collective-permute-done((bf16[480,640]{1,0:T(8,128)(2,1)}, bf16[480,640]{1,0:T(8,128)(2,1)}, u32[]{:S(2)}, u32[]{:S(2)}) %collective-permute-start.8) | collective-permute-done | bytes 614432 | tf_op jit(solution)/shard_map/ppermute | solution.py:586
  64.7 4.0 %turned.1.old_ref = f32[480,640]{1,0:T(8,128)S(1)} custom-call(s32[1]{0:T(128)} %bitcast.position_ref.refs_0_.s_ref, f32[2,640,640]{2,1,0:T(8,128)} %refs_4_.5, f32[2,640,640]{2,1,0:T(8,128)} %refs_5_.3, f32[2,640,640]{2,1,0:T(8,128)} %refs_6_.3), custom_call_target="tpu_custom_call" | custom-call | flops 1228800 | bytes 9830400 | tf_op jit(solution)/shard_map/turned/pallas_call | solution.py:334
  68.8 7.2 %collective-permute-done.9.refs_5_ = bf16[240,640]{1,0:T(8,128)(2,1)S(1)} collective-permute-done((bf16[240,640]{1,0:T(8,128)(2,1)S(1)}, bf16[240,640]{1,0:T(8,128)(2,1)S(1)}, u32[]{:S(2)}, u32[]{:S(2)}) %collective-permute-start.9) | collective-permute-done | bytes 307232 | tf_op jit(solution)/shard_map/ppermute | solution.py:586
  75.9 1.7 renorm.1.own_ref.rest_1_
  77.6 6.9 %collective-permute-start.13 = (bf16[480,640]{1,0:T(8,128)(2,1)S(1)}, bf16[480,640]{1,0:T(8,128)(2,1)S(1)}, u32[]{:S(2)}, u32[]{:S(2)}) collective-permute-start(bf16[480,640]{1,0:T(8,128)(2,1)S(1)} %renorm.1.own_ref.rest_1_), channel_id=1, source_target_pairs={{0,16},{4,20},{8,24},{12,28},{16,0},{20,4},{24,8},{28,12},{1,17},{... | collective-permute-start | bytes 1843208 | tf_op jit(solution)/shard_map/ppermute | solution.py:586
  84.5 21.0 %collective-permute-start.10 = (bf16[480,640]{1,0:T(8,128)(2,1)S(1)}, bf16[480,640]{1,0:T(8,128)(2,1)S(1)}, u32[]{:S(2)}, u32[]{:S(2)}) collective-permute-start(bf16[480,640]{1,0:T(8,128)(2,1)S(1)} %renorm.1.own_ref.rest_1_), channel_id=1, source_target_pairs={{0,4},{4,0},{8,12},{12,8},{16,20},{20,16},{24,28},{28,24},{1,5},{5... | collective-permute-start | bytes 1843208 | tf_op jit(solution)/shard_map/ppermute | solution.py:586
  105.6 12.5 %shard_map.101 = (bf16[512,1408]{1,0:T(8,128)(2,1)S(1)}, bf16[512,1280]{1,0:T(8,128)(2,1)S(1)}, f32[512,128]{1,0:T(8,128)S(1)}) custom-call(s32[1]{0:T(128)} %bitcast.position_ref.refs_0_.s_ref, bf16[512,1280]{1,0:T(8,128)(2,1)} %collective-permute-done.1.refs_0_, bf16[1024,1280]{1,0:T(8,128)(2,1)} %refs_0_.3, bf16[1024,1280]{1,0:T(8,128)(2,1)} %refs_2_.5, ...), custom_call_target="tpu_custom_call" | custom-call | flops 3355443200 | bytes 10485760 | tf_op jit(solution)/shard_map/pallas_call | solution.py:166
  118.1 2.2 %collective-permute-start.2 = (bf16[512,1408]{1,0:T(8,128)(2,1)S(1)}, bf16[512,1408]{1,0:T(8,128)(2,1)S(1)}, u32[]{:S(2)}, u32[]{:S(2)}) collective-permute-start(bf16[512,1408]{1,0:T(8,128)(2,1)S(1)} %get-tuple-element.17), channel_id=1, source_target_pairs={{0,4},{4,8},{8,12},{16,20},{20,24},{24,28},{1,5},{5,9},{9,13},{17,... | collective-permute-start | bytes 4325384 | tf_op jit(solution)/shard_map/ppermute | solution.py:592
  120.4 1.6 collective-permute-start.15
  122.6 7.3 %collective-permute-done.15.rest_4_ = bf16[240,640]{1,0:T(8,128)(2,1)S(1)} collective-permute-done((bf16[240,640]{1,0:T(8,128)(2,1)S(1)}, bf16[240,640]{1,0:T(8,128)(2,1)S(1)}, u32[]{:S(2)}, u32[]{:S(2)}) %collective-permute-start.15) | collective-permute-done | bytes 307232 | tf_op jit(solution)/shard_map/ppermute | solution.py:586
  129.9 1.5 collective-permute-start.17
  131.4 11.6 %shard_map.100.high_ref = bf16[512,1280]{1,0:T(8,128)(2,1)S(1)} custom-call(s32[1]{0:T(128)} %bitcast.position_ref.refs_0_.s_ref, bf16[1024,1280]{1,0:T(8,128)(2,1)} %refs_0_.3, bf16[1024,1280]{1,0:T(8,128)(2,1)S(1)} %collective-permute-done.refs_1_.refs_3_.refs_2_.refs_4_, bf16[1024,1280]{1,0:T(8,128)(2,1)} %refs_2_.5, ...), custom_call_target="tpu_custom_call" | custom-call | flops 3355443200 | bytes 10485760 | tf_op jit(solution)/shard_map/pallas_call | solution.py:166
  143.1 2.0 %hidden.3.rest_0_ = bf16[1024,640]{1,0:T(8,128)(2,1)S(1)} custom-call(s32[1]{0:T(128)} %bitcast.position_ref.refs_0_.s_ref, bf16[1024,1280]{1,0:T(8,128)(2,1)S(1)} %copy-done, bf16[480,640]{1,0:T(8,128)(2,1)S(1)} %renorm.1.own_ref.rest_1_, bf16[480,640]{1,0:T(8,128)(2,1)S(1)} %collective-permute-done.11.over_x.rest_2_, ...), custom_call_target="tpu_custom_call" | custom-call | flops 1258291200 | bytes 3850240 | tf_op jit(solution)/shard_map/hidden/pallas_call | solution.py:486
  145.1 14.4 %collective-permute-start.16 = (bf16[240,640]{1,0:T(8,128)(2,1)S(1)}, bf16[240,640]{1,0:T(8,128)(2,1)S(1)}, u32[]{:S(2)}, u32[]{:S(2)}) collective-permute-start(bf16[240,640]{1,0:T(8,128)(2,1)S(1)} %collective-permute-done.15.rest_4_), channel_id=1, source_target_pairs={{0,4},{4,0},{8,12},{12,8},{16,20},{20,16},{24,28},{28,24},{1,5},{5... | collective-permute-start | bytes 921608 | tf_op jit(solution)/shard_map/ppermute | solution.py:586
  159.6 2.0 %hidden.2.rest_0_ = bf16[1024,640]{1,0:T(8,128)(2,1)S(1)} custom-call(s32[1]{0:T(128)} %bitcast.position_ref.refs_0_.s_ref, bf16[1024,1280]{1,0:T(8,128)(2,1)S(1)} %copy-done, bf16[480,640]{1,0:T(8,128)(2,1)S(1)} %collective-permute-done.10.own_ref.rest_1_, bf16[480,640]{1,0:T(8,128)(2,1)S(1)} %collective-permute-done.12.over_x.rest_2_, ...), custom_call_target="tpu_custom_call" | custom-call | flops 1258291200 | bytes 3850240 | tf_op jit(solution)/shard_map/hidden/pallas_call | solution.py:486
  161.6 9.2 %shard_map.102 = (bf16[512,1280]{1,0:T(8,128)(2,1)S(1)}, f32[512,128]{1,0:T(8,128)S(1)}) custom-call(s32[1]{0:T(128)} %bitcast.position_ref.refs_0_.s_ref, bf16[1024,1280]{1,0:T(8,128)(2,1)} %refs_0_.3, bf16[1024,1280]{1,0:T(8,128)(2,1)} %collective-permute-done.4.refs_1_.refs_3_, ...), custom_call_target="tpu_custom_call" | custom-call | flops 2348810240 | bytes 10485760 | tf_op jit(solution)/shard_map/pallas_call | solution.py:166
  170.9 3.9 %merge.1.low_ref = bf16[512,1280]{1,0:T(8,128)(2,1)S(1)} custom-call(s32[1]{0:T(128)} %bitcast.position_ref.refs_0_.s_ref, bf16[512,1280]{1,0:T(8,128)(2,1)S(1)} %get-tuple-element.16.own_ref, bf16[512,1408]{1,0:T(8,128)(2,1)S(1)} %collective-permute-done.2.far_ref.far_log, f32[512,128]{1,0:T(8,128)S(1)} %get-tuple-element.18.own_log, ...), custom_call_target="tpu_custom_call" | custom-call | flops 5242880 | bytes 3932160 | tf_op jit(solution)/shard_map/merge/pallas_call | solution.py:421
  174.8 3.4 %apply.2.rest_6_ = bf16[1024,1280]{1,0:T(8,128)(2,1)} custom-call(s32[1]{0:T(128)} %bitcast.position_ref.refs_0_.s_ref, bf16[1024,1280]{1,0:T(8,128)(2,1)S(1)} %copy-done, bf16[512,1280]{1,0:T(8,128)(2,1)S(1)} %shard_map.100.high_ref, bf16[512,1280]{1,0:T(8,128)(2,1)S(1)} %merge.1.low_ref, bf16[1024,640]{1,0:T(8,128)(2,1)S(1)} %hidden.3.rest_0_, ...), custom_call_target="tpu_custom_call" | custom-call | flops 1258291200 | bytes 7700480 | tf_op jit(solution)/shard_map/apply/pallas_call | solution.py:563
  178.2 3.7 %apply.3 = bf16[1024,1280]{1,0:T(8,128)(2,1)} custom-call(s32[1]{0:T(128)} %bitcast.position_ref.refs_0_.s_ref, bf16[1024,1280]{1,0:T(8,128)(2,1)S(1)} %copy-done, bf16[512,1280]{1,0:T(8,128)(2,1)S(1)} %shard_map.100.high_ref, bf16[512,1280]{1,0:T(8,128)(2,1)S(1)} %merge.1.low_ref, ...), custom_call_target="tpu_custom_call", output_to_operand_aliasing={{}: (10, {})} | custom-call | flops 1258291200 | bytes 7700480 | tf_op jit(solution)/shard_map/apply/pallas_call | solution.py:563
  (45 shorter events, 5.2 us)
Async XLA Ops:
  0.0 0.7 copy-start.3
  10.8 1.3 slice-start
  10.8 1.7 slice-start.2
  10.8 8.2 %collective-permute-start.5 = (bf16[1920,640]{1,0:T(8,128)(2,1)S(1)}, bf16[1920,640]{1,0:T(8,128)(2,1)S(1)}, u32[]{:S(2)}, u32[]{:S(2)}) collective-permute-start(bf16[1920,640]{1,0:T(8,128)(2,1)S(1)} %grads.2), channel_id=1, source_target_pairs={{0,4},{4,0},{8,12},{12,8},{16,20},{20,16},{24,28},{28,24},{1,5},{5... | collective-permute-start | bytes 7372808 | tf_op jit(solution)/shard_map/ppermute | solution.py:586
  12.7 2.3 %slice-start.1 = ((bf16[1024,1280]{1,0:T(8,128)(2,1)}), bf16[512,1280]{1,0:T(8,128)(2,1)S(1)}, s32[]{:S(2)}) async-start(bf16[1024,1280]{1,0:T(8,128)(2,1)} %refs_3_.1), calls=%async_computation.1 | async-start | bytes 2621440 | tf_op jit(solution)/shard_map/slice | solution.py:655
  12.7 2.3 %slice-start.3 = ((bf16[1024,1280]{1,0:T(8,128)(2,1)}), bf16[512,1280]{1,0:T(8,128)(2,1)S(1)}, s32[]{:S(2)}) async-start(bf16[1024,1280]{1,0:T(8,128)(2,1)} %refs_2_.5), calls=%async_computation.3 | async-start | bytes 2621440 | tf_op jit(solution)/shard_map/slice | solution.py:655
  12.7 25.6 %collective-permute-start.3 = (bf16[1024,1280]{1,0:T(8,128)(2,1)S(1)}, bf16[1024,1280]{1,0:T(8,128)(2,1)}, u32[]{:S(2)}, u32[]{:S(2)}) collective-permute-start(bf16[1024,1280]{1,0:T(8,128)(2,1)S(1)} %pad_maximum_fusion.1), channel_id=1, source_target_pairs={{12,28},{13,29},{14,30},{15,31}} | collective-permute-start | bytes 7864328 | tf_op jit(solution)/shard_map/ppermute | solution.py:596
  15.0 4.0 %copy-start.4 = (f32[1024,2]{0,1:T(2,128)S(1)}, f32[1024,2]{0,1:T(2,128)}, u32[]{:S(2)}) copy-start(f32[1024,2]{0,1:T(2,128)} %param.16) | copy-start | bytes 24580
  16.7 19.2 %copy-start.5 = (bf16[1024,1280]{1,0:T(8,128)(2,1)S(1)}, bf16[1024,1280]{1,0:T(8,128)(2,1)}, u32[]{:S(2)}) copy-start(bf16[1024,1280]{1,0:T(8,128)(2,1)} %refs_0_.3) | copy-start | bytes 7864324
  16.7 103.7 %collective-permute-start = (bf16[1024,1280]{1,0:T(8,128)(2,1)}, bf16[1024,1280]{1,0:T(8,128)(2,1)S(1)}, u32[]{:S(2)}, u32[]{:S(2)}) collective-permute-start(bf16[1024,1280]{1,0:T(8,128)(2,1)} %pad_maximum_fusion), channel_id=1, source_target_pairs={{0,4},{4,8},{8,12},{12,16},{16,20},{20,24},{24,28},{1,5},{5,9},{9,... | collective-permute-start | bytes 7864328 | tf_op jit(solution)/shard_map/ppermute | solution.py:592
  30.7 0.9 copy-start.1
  31.6 16.4 %collective-permute-start.6 = (bf16[480,640]{1,0:T(8,128)(2,1)}, bf16[480,640]{1,0:T(8,128)(2,1)}, u32[]{:S(2)}, u32[]{:S(2)}) collective-permute-start(bf16[480,640]{1,0:T(8,128)(2,1)} %get-tuple-element.24), channel_id=1, source_target_pairs={{0,8},{4,12},{8,0},{12,4},{16,24},{20,28},{24,16},{28,20},{1,9},{5... | collective-permute-start | bytes 1843208 | tf_op jit(solution)/shard_map/ppermute | solution.py:586
  33.1 30.4 %collective-permute-start.8 = (bf16[480,640]{1,0:T(8,128)(2,1)}, bf16[480,640]{1,0:T(8,128)(2,1)}, u32[]{:S(2)}, u32[]{:S(2)}) collective-permute-start(bf16[480,640]{1,0:T(8,128)(2,1)} %get-tuple-element.26), channel_id=1, source_target_pairs={{0,16},{4,20},{8,24},{12,28},{16,0},{20,4},{24,8},{28,12},{1,17},{... | collective-permute-start | bytes 1843208 | tf_op jit(solution)/shard_map/ppermute | solution.py:586
  37.0 47.5 %collective-permute-start.1 = (bf16[512,1280]{1,0:T(8,128)(2,1)}, bf16[512,1280]{1,0:T(8,128)(2,1)}, u32[]{:S(2)}, u32[]{:S(2)}) collective-permute-start(bf16[512,1280]{1,0:T(8,128)(2,1)} %slice.23), channel_id=1, source_target_pairs={{4,0},{8,4},{12,8},{20,16},{24,20},{28,24},{5,1},{9,5},{13,9},{21,... | collective-permute-start | bytes 3932168 | tf_op jit(solution)/shard_map/ppermute | solution.py:592
  38.3 123.3 %collective-permute-start.4 = (bf16[1024,1280]{1,0:T(8,128)(2,1)}, bf16[1024,1280]{1,0:T(8,128)(2,1)}, u32[]{:S(2)}, u32[]{:S(2)}) collective-permute-start(bf16[1024,1280]{1,0:T(8,128)(2,1)} %collective-permute-done.3), channel_id=1, source_target_pairs={{28,16},{29,17},{30,18},{31,19}} | collective-permute-start | bytes 7864328 | tf_op jit(solution)/shard_map/ppermute | solution.py:596
  49.1 19.7 %collective-permute-start.7 = (bf16[240,640]{1,0:T(8,128)(2,1)S(1)}, bf16[240,640]{1,0:T(8,128)(2,1)S(1)}, u32[]{:S(2)}, u32[]{:S(2)}) collective-permute-start(bf16[240,640]{1,0:T(8,128)(2,1)S(1)} %add_convert_fusion.1), channel_id=1, source_target_pairs={{0,16},{4,20},{8,24},{12,28},{16,0},{20,4},{24,8},{28,12},{1,17},{... | collective-permute-start | bytes 921608 | tf_op jit(solution)/shard_map/ppermute | solution.py:586
  64.6 11.3 %copy-start.2 = (bf16[480,640]{1,0:T(8,128)(2,1)S(1)}, bf16[480,640]{1,0:T(8,128)(2,1)}, u32[]{:S(2)}) copy-start(bf16[480,640]{1,0:T(8,128)(2,1)} %copy-done.1) | copy-start | bytes 1843204
  64.6 11.3 %collective-permute-start.9 = (bf16[240,640]{1,0:T(8,128)(2,1)S(1)}, bf16[240,640]{1,0:T(8,128)(2,1)S(1)}, u32[]{:S(2)}, u32[]{:S(2)}) collective-permute-start(bf16[240,640]{1,0:T(8,128)(2,1)S(1)} %add_convert_fusion), channel_id=1, source_target_pairs={{0,8},{4,12},{8,0},{12,4},{16,24},{20,28},{24,16},{28,20},{1,9},{5... | collective-permute-start | bytes 921608 | tf_op jit(solution)/shard_map/ppermute | solution.py:586
  77.6 40.5 %collective-permute-start.13 = (bf16[480,640]{1,0:T(8,128)(2,1)S(1)}, bf16[480,640]{1,0:T(8,128)(2,1)S(1)}, u32[]{:S(2)}, u32[]{:S(2)}) collective-permute-start(bf16[480,640]{1,0:T(8,128)(2,1)S(1)} %renorm.1.own_ref.rest_1_), channel_id=1, source_target_pairs={{0,16},{4,20},{8,24},{12,28},{16,0},{20,4},{24,8},{28,12},{1,17},{... | collective-permute-start | bytes 1843208 | tf_op jit(solution)/shard_map/ppermute | solution.py:586
  84.5 37.5 %collective-permute-start.11 = (bf16[480,640]{1,0:T(8,128)(2,1)S(1)}, bf16[480,640]{1,0:T(8,128)(2,1)S(1)}, u32[]{:S(2)}, u32[]{:S(2)}) collective-permute-start(bf16[480,640]{1,0:T(8,128)(2,1)S(1)} %renorm.1.own_ref.rest_1_), channel_id=1, source_target_pairs={{0,8},{4,12},{8,0},{12,4},{16,24},{20,28},{24,16},{28,20},{1,9},{5... | collective-permute-start | bytes 1843208 | tf_op jit(solution)/shard_map/ppermute | solution.py:586
  84.5 37.7 %collective-permute-start.10 = (bf16[480,640]{1,0:T(8,128)(2,1)S(1)}, bf16[480,640]{1,0:T(8,128)(2,1)S(1)}, u32[]{:S(2)}, u32[]{:S(2)}) collective-permute-start(bf16[480,640]{1,0:T(8,128)(2,1)S(1)} %renorm.1.own_ref.rest_1_), channel_id=1, source_target_pairs={{0,4},{4,0},{8,12},{12,8},{16,20},{20,16},{24,28},{28,24},{1,5},{5... | collective-permute-start | bytes 1843208 | tf_op jit(solution)/shard_map/ppermute | solution.py:586
  118.1 52.8 %collective-permute-start.2 = (bf16[512,1408]{1,0:T(8,128)(2,1)S(1)}, bf16[512,1408]{1,0:T(8,128)(2,1)S(1)}, u32[]{:S(2)}, u32[]{:S(2)}) collective-permute-start(bf16[512,1408]{1,0:T(8,128)(2,1)S(1)} %get-tuple-element.17), channel_id=1, source_target_pairs={{0,4},{4,8},{8,12},{16,20},{20,24},{24,28},{1,5},{5,9},{9,13},{17,... | collective-permute-start | bytes 4325384 | tf_op jit(solution)/shard_map/ppermute | solution.py:592
  120.4 9.5 %collective-permute-start.15 = (bf16[240,640]{1,0:T(8,128)(2,1)S(1)}, bf16[240,640]{1,0:T(8,128)(2,1)S(1)}, u32[]{:S(2)}, u32[]{:S(2)}) collective-permute-start(bf16[240,640]{1,0:T(8,128)(2,1)S(1)} %slice.28), channel_id=1, source_target_pairs={{0,8},{4,12},{8,0},{12,4},{16,24},{20,28},{24,16},{28,20},{1,9},{5... | collective-permute-start | bytes 921608 | tf_op jit(solution)/shard_map/ppermute | solution.py:586
  122.0 37.5 %collective-permute-start.12 = (bf16[480,640]{1,0:T(8,128)(2,1)S(1)}, bf16[480,640]{1,0:T(8,128)(2,1)S(1)}, u32[]{:S(2)}, u32[]{:S(2)}) collective-permute-start(bf16[480,640]{1,0:T(8,128)(2,1)S(1)} %collective-permute-done.11.over_x.rest_2_), channel_id=1, source_target_pairs={{0,4},{4,0},{8,12},{12,8},{16,20},{20,16},{24,28},{28,24},{1,5},{5... | collective-permute-start | bytes 1843208 | tf_op jit(solution)/shard_map/ppermute | solution.py:586
  122.2 37.3 %collective-permute-start.14 = (bf16[480,640]{1,0:T(8,128)(2,1)S(1)}, bf16[480,640]{1,0:T(8,128)(2,1)S(1)}, u32[]{:S(2)}, u32[]{:S(2)}) collective-permute-start(bf16[480,640]{1,0:T(8,128)(2,1)S(1)} %collective-permute-done.13.over_y.rest_3_), channel_id=1, source_target_pairs={{0,4},{4,0},{8,12},{12,8},{16,20},{20,16},{24,28},{28,24},{1,5},{5... | collective-permute-start | bytes 1843208 | tf_op jit(solution)/shard_map/ppermute | solution.py:586
  122.6 20.5 %copy-start = (bf16[1024,1280]{1,0:T(8,128)(2,1)S(1)}, bf16[1024,1280]{1,0:T(8,128)(2,1)}, u32[]{:S(2)}) copy-start(bf16[1024,1280]{1,0:T(8,128)(2,1)} %q_ref.7) | copy-start | bytes 7864324
  129.9 15.2 %collective-permute-start.17 = (bf16[240,640]{1,0:T(8,128)(2,1)S(1)}, bf16[240,640]{1,0:T(8,128)(2,1)S(1)}, u32[]{:S(2)}, u32[]{:S(2)}) collective-permute-start(bf16[240,640]{1,0:T(8,128)(2,1)S(1)} %slice.29), channel_id=1, source_target_pairs={{0,16},{4,20},{8,24},{12,28},{16,0},{20,4},{24,8},{28,12},{1,17},{... | collective-permute-start | bytes 921608 | tf_op jit(solution)/shard_map/ppermute | solution.py:586
  145.1 33.1 %collective-permute-start.16 = (bf16[240,640]{1,0:T(8,128)(2,1)S(1)}, bf16[240,640]{1,0:T(8,128)(2,1)S(1)}, u32[]{:S(2)}, u32[]{:S(2)}) collective-permute-start(bf16[240,640]{1,0:T(8,128)(2,1)S(1)} %collective-permute-done.15.rest_4_), channel_id=1, source_target_pairs={{0,4},{4,0},{8,12},{12,8},{16,20},{20,16},{24,28},{28,24},{1,5},{5... | collective-permute-start | bytes 921608 | tf_op jit(solution)/shard_map/ppermute | solution.py:586
  159.5 18.7 %collective-permute-start.18 = (bf16[240,640]{1,0:T(8,128)(2,1)S(1)}, bf16[240,640]{1,0:T(8,128)(2,1)S(1)}, u32[]{:S(2)}, u32[]{:S(2)}) collective-permute-start(bf16[240,640]{1,0:T(8,128)(2,1)S(1)} %collective-permute-done.17.rest_5_), channel_id=1, source_target_pairs={{0,4},{4,0},{8,12},{12,8},{16,20},{20,16},{24,28},{28,24},{1,5},{5... | collective-permute-start | bytes 921608 | tf_op jit(solution)/shard_map/ppermute | solution.py:586

commit v8 on v5

--- a/solution.py
+++ b/solution.py
@@ -396,17 +396,19 @@
         o_ref[:, cs] = (a * share + b * (1.0 - share)).astype(o_ref.dtype)
 
 
-def merged(position, own, far, own_log, width):
-    rows, cols = own.shape
+def merged(position, own, far, own_log, width, tile):
+    rows, cols = far.shape[0], own.shape[1]
     w = width * HD
+    mine = pl.BlockSpec((rows, w), lambda g, s: (tile, g))
     col = pl.BlockSpec((rows, w), lambda g, s: (0, g))
-    log = lambda at: pl.BlockSpec((rows, HD), lambda g, s: (0, at))
+    own_logs = pl.BlockSpec((rows, HD), lambda g, s: (tile, 0))
+    far_logs = pl.BlockSpec((rows, HD), lambda g, s: (0, cols // HD))
     return pl.pallas_call(
         functools.partial(merge_kernel, stride=log_stride_of(cols)),
         grid_spec=pltpu.PrefetchScalarGridSpec(
             num_scalar_prefetch=1,
             grid=(cols // w,),
-            in_specs=[col, col, log(0), log(cols // HD)],
+            in_specs=[mine, col, own_logs, far_logs],
             out_specs=col,
         ),
         out_shape=jax.ShapeDtypeStruct((rows, cols), jnp.bfloat16),
@@ -480,10 +482,9 @@
     )(position, fq, *pieces[:3])
 
 
-def apply_kernel(s_ref, q_ref, high_ref, low_ref, *rest, tm, head, split):
+def apply_kernel(s_ref, q_ref, *rest, tm, head, split, tiles, sources):
+    attended, rest = rest[:sources], rest[sources:]
     o_ref, n_ref, w_ref, h_ref, r_ref, sems = rest[-6:]
-    rows = q_ref.shape[0]
-    half = rows // 2
     F = n_ref.shape[1]
     n, m = F // 4, F // 8
     cols = pl.ds(pl.multiple_of(head(s_ref) * F, HD), F)
@@ -496,8 +497,8 @@
         n_ref[...] = rest[0][2 * F :, :]
 
     def copy_out(i):
-        r = pl.ds(i * tm, tm)
-        return pltpu.make_async_copy(r_ref.at[r, :], o_ref.at[r, cols], sems.at[i])
+        to = pl.ds(tiles[i][0] * tm, tm)
+        return pltpu.make_async_copy(r_ref.at[pl.ds(i * tm, tm), :], o_ref.at[to, cols], sems.at[i])
 
     def place(k):
         rows_of = ((own, 2 * n), (over_x, 2 * n), (over_y, 2 * n), (lower, m))
@@ -510,32 +511,32 @@
         for_each_chip(s_ref, place)
 
     def first(i):
-        return mm(q_ref[i * tm : (i + 1) * tm, cols], w_ref[...], NT)
+        at = tiles[i][0] * tm
+        return mm(q_ref[at : at + tm, cols], w_ref[...], NT)
 
     def second(i, h):
+        tile, source, at = tiles[i]
         r = slice(i * tm, (i + 1) * tm)
         if split:
-            h_ref[r, : 3 * n] = rest[0][r, : 3 * n]
+            h_ref[r, : 3 * n] = rest[0][tile * tm : (tile + 1) * tm, : 3 * n]
             h_ref[r, 3 * n :] = gated(h, n)
             hid = h_ref[r, :]
         else:
             hid = gated(h, F)
-        source, at = (low_ref, i * tm) if i * tm < half else (high_ref, i * tm - half)
-        a = source[at : at + tm, cols].astype(jnp.float32)
+        a = attended[source][at : at + tm, cols].astype(jnp.float32)
         r_ref[r, :] = (a + mm(hid, n_ref[...], NT)).astype(r_ref.dtype)
         copy_out(i).start()
 
-    staggered(rows // tm, first, second)
-    for i in range(rows // tm):
+    staggered(len(tiles), first, second)
+    for i in range(len(tiles)):
         copy_out(i).wait()
 
 
-def apply_head(position, head, fq, hidden, pieces, high, low, into=None):
+def apply_head(position, head, fq, hidden, pieces, attended, tiles, tm, into=None):
     rows, cols = fq.shape
     F = pieces[0].shape[1]
     split = hidden is not None
-    tm = min(256, rows // 2)
-    args = [position, fq, high, low] + ([hidden] if split else []) + list(pieces)
+    args = [position, fq, *attended] + ([hidden] if split else []) + list(pieces)
     specs = [SMEM] + [VMEM] * (len(args) - 1)
     aliases = {}
     if into is not None:
@@ -543,21 +544,24 @@
         args.append(into)
         specs.append(ANY)
     bf = jnp.bfloat16
+    mine = len(tiles) * tm
     return pl.pallas_call(
-        functools.partial(apply_kernel, tm=tm, head=head, split=split),
+        functools.partial(
+            apply_kernel, tm=tm, head=head, split=split, tiles=tiles, sources=len(attended)
+        ),
         in_specs=specs,
         out_specs=ANY,
         scratch_shapes=[
             pltpu.VMEM((F, F), bf),
             pltpu.VMEM((F // 2 if split else 2 * F, F), bf),
-            pltpu.VMEM((rows, F), bf),
-            pltpu.VMEM((rows, F), bf),
-            pltpu.SemaphoreType.DMA((rows // tm,)),
+            pltpu.VMEM((mine, F), bf),
+            pltpu.VMEM((mine, F), bf),
+            pltpu.SemaphoreType.DMA((len(tiles),)),
         ],
         out_shape=jax.ShapeDtypeStruct((rows, cols), bf),
         input_output_aliases=aliases,
         cost_estimate=pl.CostEstimate(
-            flops=3 * rows * F * F, bytes_accessed=rows * F * 8 + F * F * 6, transcendentals=rows * F
+            flops=3 * mine * F * F, bytes_accessed=mine * F * 8 + F * F * 6, transcendentals=mine * F
         ),
         name="apply",
         compiler_params=room(24),
@@ -669,13 +673,18 @@
     early = [[(0, 0, (t + 1) * bq, -1)] for t in range(tiles)]
     guest = [[(0, t * bq, rows, 1)] for t in range(tiles)]
     here = (attn_k, 0, attn_v, 0, rows)
-    returned, own_out, own_log = attention(position, [(guests, 0, guest, 2), (attn_q, 0, early, 1)], [here], bq, width)
-    far_out = shifted(returned, 1)
+    jobs = [(guests, t, guest[t : t + 1], 2) for t in range(tiles)] + [(attn_q, 0, early, 1)]
+    *returned, own_out, own_log = attention(position, jobs, [here], bq, width)
+    far_outs = [shifted(part, 1) for part in returned]
     (high,) = attention(position, [(attn_q, 1, late, 0)], [(prev, 0, prev, 1, half), here], bq, width)
-    low = merged(position, own_out, far_out, own_log, width)
+    lows = []
+    for t, part in enumerate(far_outs):
+        lows.append(merged(position, own_out, part, own_log, width, t))
+    soon = [(t, t, 0) for t in range(tiles - 1)] + [(tiles + t, tiles - 1, t * bq) for t in range(tiles)]
     mixed = None
-    for head, hidden, new in news:
-        mixed = apply_head(position, head, fast_q, hidden, new, high, low, mixed)
+    for attended, rows_of in (([*lows[:-1], high], soon), (lows[-1:], [(tiles - 1, 0, 0)])):
+        for head, hidden, new in news:
+            mixed = apply_head(position, head, fast_q, hidden, new, attended, rows_of, bq, mixed)
     return mixed
 
 

time: 144 us -> 161 us (1.12)
  waiting for transfers between devices: 15.5 us -> 47.5 us
  starting transfers between devices: 53.7 us -> 35.8 us
  local copies, waits for them, and re-layouts: 2.18 us -> 3.9 us
    ppermute x14, waiting for transfers between devices: 15.5 us -> 47.5 us  [exchange(): return lax.ppermute(block, 'seq', [(i, i ^ 1 << bit) for i in range(size)])]
    ppermute x14, starting transfers between devices: 40.2 us -> 15.6 us  [exchange(): return lax.ppermute(block, 'seq', [(i, i ^ 1 << bit) for i in range(size)])]
    ppermute x3 -> x4, starting transfers between devices: 13.5 us -> 20.3 us  [shifted(): lax.ppermute(block, 'seq', [(i, i + by) for i in range(size) if 0 <= i +...]
    pallas_call x2 -> x4, Pallas kernels: 6.8 us -> 9.88 us  [apply_head(): pl.pallas_call(functools.partial(apply_kernel, tm=tm, head=head, split=sp...]
    pallas_call x1 -> x2, Pallas kernels: 4.7 us -> 3.35 us  [merged(): pl.pallas_call(functools.partial(merge_kernel, stride=log_stride_of(cols)...]
  transfers between devices with their start and end apart: 17 -> 18, of which waited for: 3 -> 2; matrix products, arithmetic and copies ran while one was open for 3% -> 3% of each run, Pallas kernels for 38% -> 32%
where the time goes in v8:
time: 161 us
  Pallas kernels  69.1 us (43%)
  waiting for transfers between devices  47.5 us (30%)
  starting transfers between devices  35.8 us (22%)
  local copies, waits for them, and re-layouts  3.9 us (2%)
  other arithmetic  3.84 us (2%)
    ppermute x14, waiting for transfers between devices, exchange(): return lax.ppermute(block, 'seq', [(i, i ^ 1 << bit) for i in range(size)])  47.5 us
    pallas_call x2, Pallas kernels, attention(): pl.pallas_call(kernel, grid_spec=pltpu.PrefetchScalarGridSpec(num_scalar_...  24.4 us
    pallas_call x2, Pallas kernels, gradients(): pl.pallas_call(body, grid_spec=pltpu.PrefetchScalarGridSpec(num_scalar_pr...  21.7 us
    ppermute x4, starting transfers between devices, shifted(): lax.ppermute(block, 'seq', [(i, i + by) for i in range(size) if 0 <= i +...  20.3 us
    ppermute x14, starting transfers between devices, exchange(): return lax.ppermute(block, 'seq', [(i, i ^ 1 << bit) for i in range(size)])  15.6 us
    pallas_call x4, Pallas kernels, apply_head(): pl.pallas_call(functools.partial(apply_kernel, tm=tm, head=head, split=sp...  9.88 us
    pallas_call x2, Pallas kernels, hidden_part(): pl.pallas_call(functools.partial(hidden_kernel, tm=min(256, rows), head=h...  4.03 us
    pallas_call x1, Pallas kernels, turned(): pl.pallas_call(functools.partial(turn_kernel, parts=parts), grid_spec=plt...  4 us
  transfers between devices with their start and end apart: 18, of which 2 were waited for; matrix products, arithmetic and copies ran while one was open for 3% of the time, Pallas kernels for 32%

profile of v8, /device:TPU:0, one launch (start us, length us, event | category | flops | bytes accessed | tf_op | source)
XLA Modules:
  0.0 160.7 jit_solution(7891490086636963916)
XLA Ops:
  0.0 0.7 copy-done.3
  0.7 10.1 %grads.2 = bf16[1920,640]{1,0:T(8,128)(2,1)S(1)} custom-call(s32[1]{0:T(128)} %bitcast.position_ref.s_ref.refs_0_, bf16[1024,1280]{1,0:T(8,128)(2,1)} %refs_1_.3, bf16[1024,1280]{1,0:T(8,128)(2,1)} %refs_2_.6, f32[2,1024]{1,0:T(2,128)S(1)} %bitcast.2, f32[2,640,640]{2,1,0:T(8,128)} %refs_4_.6, f32[2,640,640]{2,1,0:T(8,128)} %refs_5_.3, f32[2,640,640]{2,1,0:T(8,128)} %refs_6_.3), custom_call_target="tpu_custom_call" | custom-call | flops 5033164800 | bytes 9994240 | tf_op jit(solution)/shard_map/grads/pallas_call | solution.py:292
  11.4 0.7 slice-done
  12.5 1.7 %pad_maximum_fusion = bf16[1024,1280]{1,0:T(8,128)(2,1)} fusion(bf16[512,1280]{1,0:T(8,128)(2,1)S(1)} %slice-done.1, bf16[512,1280]{1,0:T(8,128)(2,1)S(1)} %slice-done), kind=kLoop, calls=%fused_computation | loop fusion | flops 5242880 | bytes 5242880 | tf_op jit(solution)/shard_map/concatenate | solution.py:636
  14.2 2.7 %collective-permute-start.17 = (bf16[1024,1280]{1,0:T(8,128)(2,1)}, bf16[1024,1280]{1,0:T(8,128)(2,1)S(1)}, u32[]{:S(2)}, u32[]{:S(2)}) collective-permute-start(bf16[1024,1280]{1,0:T(8,128)(2,1)} %pad_maximum_fusion), channel_id=1, source_target_pairs={{0,4},{4,8},{8,12},{12,16},{16,20},{20,24},{24,28},{1,5},{5,9},{9,... | collective-permute-start | bytes 7864328 | tf_op jit(solution)/shard_map/ppermute | solution.py:578
  16.9 1.2 slice.15
  18.0 1.5 collective-permute-start
  19.5 11.6 %grads.3 = (bf16[480,640]{1,0:T(8,128)(2,1)S(1)}, bf16[480,640]{1,0:T(8,128)(2,1)}, bf16[480,640]{1,0:T(8,128)(2,1)S(1)}, bf16[480,640]{1,0:T(8,128)(2,1)}) custom-call(s32[1]{0:T(128)} %bitcast.position_ref.s_ref.refs_0_, bf16[1024,1280]{1,0:T(8,128)(2,1)} %refs_1_.3, bf16[1024,1280]{1,0:T(8,128)(2,1)} %refs_2_.6, f32[2,1024]{1,0:T(2,128)S(1)} %bitcast.3, ...), custom_call_target="tpu_custom_call" | custom-call | flops 5033164800 | bytes 9994240 | tf_op jit(solution)/shard_map/grads/pallas_call | solution.py:292
  31.2 0.8 copy-done.1
  32.0 4.7 %collective-permute-start.3 = (bf16[480,640]{1,0:T(8,128)(2,1)}, bf16[480,640]{1,0:T(8,128)(2,1)}, u32[]{:S(2)}, u32[]{:S(2)}) collective-permute-start(bf16[480,640]{1,0:T(8,128)(2,1)} %get-tuple-element.17), channel_id=1, source_target_pairs={{0,8},{4,12},{8,0},{12,4},{16,24},{20,28},{24,16},{28,20},{1,9},{5... | collective-permute-start | bytes 1843208 | tf_op jit(solution)/shard_map/ppermute | solution.py:573
  36.7 1.5 collective-permute-start.5
  38.2 28.9 %collective-permute-done.3.refs_1_ = bf16[480,640]{1,0:T(8,128)(2,1)} collective-permute-done((bf16[480,640]{1,0:T(8,128)(2,1)}, bf16[480,640]{1,0:T(8,128)(2,1)}, u32[]{:S(2)}, u32[]{:S(2)}) %collective-permute-start.3) | collective-permute-done | bytes 614432 | tf_op jit(solution)/shard_map/ppermute | solution.py:573
  67.1 1.0 add_convert_fusion.1
  68.7 1.1 add_convert_fusion
  69.8 2.5 %collective-permute-start.6 = (bf16[240,640]{1,0:T(8,128)(2,1)S(1)}, bf16[240,640]{1,0:T(8,128)(2,1)S(1)}, u32[]{:S(2)}, u32[]{:S(2)}) collective-permute-start(bf16[240,640]{1,0:T(8,128)(2,1)S(1)} %add_convert_fusion), channel_id=1, source_target_pairs={{0,8},{4,12},{8,0},{12,4},{16,24},{20,28},{24,16},{28,20},{1,9},{5... | collective-permute-start | bytes 921608 | tf_op jit(solution)/shard_map/ppermute | solution.py:573
  72.4 12.6 %shard_map.100 = (bf16[256,1408]{1,0:T(8,128)(2,1)S(1)}, bf16[256,1408]{1,0:T(8,128)(2,1)S(1)}, bf16[512,1280]{1,0:T(8,128)(2,1)S(1)}, f32[512,128]{1,0:T(8,128)S(1)}) custom-call(s32[1]{0:T(128)} %bitcast.position_ref.s_ref.refs_0_, bf16[512,1280]{1,0:T(8,128)(2,1)} %collective-permute-done.refs_0_.refs_1_, ...), custom_call_target="tpu_custom_call" | custom-call | flops 3355443200 | bytes 10485760 | tf_op jit(solution)/shard_map/pallas_call | solution.py:158
  84.9 13.8 %collective-permute-start.1 = (bf16[256,1408]{1,0:T(8,128)(2,1)S(1)}, bf16[256,1408]{1,0:T(8,128)(2,1)S(1)}, u32[]{:S(2)}, u32[]{:S(2)}) collective-permute-start(bf16[256,1408]{1,0:T(8,128)(2,1)S(1)} %get-tuple-element.14), channel_id=1, source_target_pairs={{0,4},{4,8},{8,12},{12,16},{16,20},{20,24},{24,28},{1,5},{5,9},{9,... | collective-permute-start | bytes 2162696 | tf_op jit(solution)/shard_map/ppermute | solution.py:578
  98.8 2.3 %collective-permute-start.16 = (bf16[256,1408]{1,0:T(8,128)(2,1)S(1)}, bf16[256,1408]{1,0:T(8,128)(2,1)S(1)}, u32[]{:S(2)}, u32[]{:S(2)}) collective-permute-start(bf16[256,1408]{1,0:T(8,128)(2,1)S(1)} %get-tuple-element.20), channel_id=1, source_target_pairs={{0,4},{4,8},{8,12},{12,16},{16,20},{20,24},{24,28},{1,5},{5,9},{9,... | collective-permute-start | bytes 2162696 | tf_op jit(solution)/shard_map/ppermute | solution.py:578
  101.1 4.0 %turned.1.old_ref = f32[480,640]{1,0:T(8,128)S(1)} custom-call(s32[1]{0:T(128)} %bitcast.position_ref.s_ref.refs_0_, f32[2,640,640]{2,1,0:T(8,128)} %refs_4_.6, f32[2,640,640]{2,1,0:T(8,128)} %refs_5_.3, f32[2,640,640]{2,1,0:T(8,128)} %refs_6_.3), custom_call_target="tpu_custom_call" | custom-call | flops 1228800 | bytes 9830400 | tf_op jit(solution)/shard_map/turned/pallas_call | solution.py:326
  105.1 1.7 %renorm.1.own_ref.rest_3_.rest_2_ = bf16[480,640]{1,0:T(8,128)(2,1)S(1)} custom-call(s32[1]{0:T(128)} %bitcast.position_ref.s_ref.refs_0_, f32[480,640]{1,0:T(8,128)S(1)} %turned.1.old_ref, bf16[480,640]{1,0:T(8,128)(2,1)S(1)} %get-tuple-element.16.refs_0_, bf16[480,640]{1,0:T(8,128)(2,1)} %collective-permute-done.3.refs_1_, ...), custom_call_target="tpu_custom_call" | custom-call | flops 3072000 | bytes 3686400 | tf_op jit(solution)/shard_map/renorm/pallas_call | solution.py:365
  107.2 1.7 %collective-permute-start.8 = (bf16[480,640]{1,0:T(8,128)(2,1)S(1)}, bf16[480,640]{1,0:T(8,128)(2,1)S(1)}, u32[]{:S(2)}, u32[]{:S(2)}) collective-permute-start(bf16[480,640]{1,0:T(8,128)(2,1)S(1)} %renorm.1.own_ref.rest_3_.rest_2_), channel_id=1, source_target_pairs={{0,8},{4,12},{8,0},{12,4},{16,24},{20,28},{24,16},{28,20},{1,9},{5... | collective-permute-start | bytes 1843208 | tf_op jit(solution)/shard_map/ppermute | solution.py:573
  108.9 18.6 %collective-permute-done.10.over_y.rest_5_.rest_4_ = bf16[480,640]{1,0:T(8,128)(2,1)S(1)} collective-permute-done((bf16[480,640]{1,0:T(8,128)(2,1)S(1)}, bf16[480,640]{1,0:T(8,128)(2,1)S(1)}, u32[]{:S(2)}, u32[]{:S(2)}) %collective-permute-start.10) | collective-permute-done | bytes 614432 | tf_op jit(solution)/shard_map/ppermute | solution.py:573
  128.3 1.7 %merge.2.rest_0_ = bf16[256,1280]{1,0:T(8,128)(2,1)S(1)} custom-call(s32[1]{0:T(128)} %bitcast.position_ref.s_ref.refs_0_, bf16[512,1280]{1,0:T(8,128)(2,1)S(1)} %get-tuple-element.13.own_ref, bf16[256,1408]{1,0:T(8,128)(2,1)S(1)} %collective-permute-done.1.far_ref.far_log, f32[512,128]{1,0:T(8,128)S(1)} %get-tuple-element.15.own_log, ...), custom_call_target="tpu_custom_call" | custom-call | flops 2621440 | bytes 1966080 | tf_op jit(solution)/shard_map/merge/pallas_call | solution.py:406
  130.0 1.7 %merge.3.rest_0_ = bf16[256,1280]{1,0:T(8,128)(2,1)S(1)} custom-call(s32[1]{0:T(128)} %bitcast.position_ref.s_ref.refs_0_, bf16[512,1280]{1,0:T(8,128)(2,1)S(1)} %get-tuple-element.13.own_ref, bf16[256,1408]{1,0:T(8,128)(2,1)S(1)} %collective-permute-done.16.far_ref.far_log, f32[512,128]{1,0:T(8,128)S(1)} %get-tuple-element.15.own_log, ...), custom_call_target="tpu_custom_call" | custom-call | flops 2621440 | bytes 1966080 | tf_op jit(solution)/shard_map/merge/pallas_call | solution.py:406
  131.8 1.8 %collective-permute-start.12 = (bf16[240,640]{1,0:T(8,128)(2,1)S(1)}, bf16[240,640]{1,0:T(8,128)(2,1)S(1)}, u32[]{:S(2)}, u32[]{:S(2)}) collective-permute-start(bf16[240,640]{1,0:T(8,128)(2,1)S(1)} %slice.20), channel_id=1, source_target_pairs={{0,8},{4,12},{8,0},{12,4},{16,24},{20,28},{24,16},{28,20},{1,9},{5... | collective-permute-start | bytes 921608 | tf_op jit(solution)/shard_map/ppermute | solution.py:573
  134.0 11.9 %shard_map.101.rest_1_ = bf16[512,1280]{1,0:T(8,128)(2,1)S(1)} custom-call(s32[1]{0:T(128)} %bitcast.position_ref.s_ref.refs_0_, bf16[1024,1280]{1,0:T(8,128)(2,1)} %refs_0_.1, bf16[1024,1280]{1,0:T(8,128)(2,1)S(1)} %collective-permute-done.17.refs_1_.refs_3_, bf16[1024,1280]{1,0:T(8,128)(2,1)} %refs_2_.7, ...), custom_call_target="tpu_custom_call" | custom-call | flops 3355443200 | bytes 10485760 | tf_op jit(solution)/shard_map/pallas_call | solution.py:158
  146.5 2.0 %hidden.3.rest_2_.rest_1_ = bf16[1024,640]{1,0:T(8,128)(2,1)S(1)} custom-call(s32[1]{0:T(128)} %bitcast.position_ref.s_ref.refs_0_, bf16[1024,1280]{1,0:T(8,128)(2,1)S(1)} %copy-done, bf16[480,640]{1,0:T(8,128)(2,1)S(1)} %renorm.1.own_ref.rest_3_.rest_2_, bf16[480,640]{1,0:T(8,128)(2,1)S(1)} %collective-permute-done.8.over_x.rest_4_.rest_3_, ...), custom_call_target="tpu_custom_call" | custom-call | flops 1258291200 | bytes 3850240 | tf_op jit(solution)/shard_map/hidden/pallas_call | solution.py:471
  148.5 2.9 %apply.4.rest_8_ = bf16[1024,1280]{1,0:T(8,128)(2,1)} custom-call(s32[1]{0:T(128)} %bitcast.position_ref.s_ref.refs_0_, bf16[1024,1280]{1,0:T(8,128)(2,1)S(1)} %copy-done, bf16[256,1280]{1,0:T(8,128)(2,1)S(1)} %merge.3.rest_0_, bf16[512,1280]{1,0:T(8,128)(2,1)S(1)} %shard_map.101.rest_1_, bf16[1024,640]{1,0:T(8,128)(2,1)S(1)} %hidden.3.rest_2_.rest_1_, ...), custom_call_target="tpu_custom_call" | custom-call | flops 943718400 | bytes 6389760 | tf_op jit(solution)/shard_map/apply/pallas_call | solution.py:548
  151.4 2.0 %hidden.2.rest_2_.rest_1_ = bf16[1024,640]{1,0:T(8,128)(2,1)S(1)} custom-call(s32[1]{0:T(128)} %bitcast.position_ref.s_ref.refs_0_, bf16[1024,1280]{1,0:T(8,128)(2,1)S(1)} %copy-done, bf16[480,640]{1,0:T(8,128)(2,1)S(1)} %collective-permute-done.7.own_ref.rest_3_.rest_2_, bf16[480,640]{1,0:T(8,128)(2,1)S(1)} %collective-permute-done.9.over_x.rest_4_.rest_3_, ...), custom_call_target="tpu_custom_call" | custom-call | flops 1258291200 | bytes 3850240 | tf_op jit(solution)/shard_map/hidden/pallas_call | solution.py:471
  153.5 3.1 %apply.5.rest_7_ = bf16[1024,1280]{1,0:T(8,128)(2,1)} custom-call(s32[1]{0:T(128)} %bitcast.position_ref.s_ref.refs_0_, bf16[1024,1280]{1,0:T(8,128)(2,1)S(1)} %copy-done, bf16[256,1280]{1,0:T(8,128)(2,1)S(1)} %merge.3.rest_0_, bf16[512,1280]{1,0:T(8,128)(2,1)S(1)} %shard_map.101.rest_1_, ...), custom_call_target="tpu_custom_call", output_to_operand_aliasing={{}: (10, {})} | custom-call | flops 943718400 | bytes 6389760 | tf_op jit(solution)/shard_map/apply/pallas_call | solution.py:548
  156.6 1.9 %apply.6.rest_7_ = bf16[1024,1280]{1,0:T(8,128)(2,1)} custom-call(s32[1]{0:T(128)} %bitcast.position_ref.s_ref.refs_0_, bf16[1024,1280]{1,0:T(8,128)(2,1)S(1)} %copy-done, bf16[256,1280]{1,0:T(8,128)(2,1)S(1)} %merge.2.rest_0_, bf16[1024,640]{1,0:T(8,128)(2,1)S(1)} %hidden.3.rest_2_.rest_1_, ...), custom_call_target="tpu_custom_call", output_to_operand_aliasing={{}: (9, {})} | custom-call | flops 314572800 | bytes 3768320 | tf_op jit(solution)/shard_map/apply/pallas_call | solution.py:548
  158.5 1.9 %apply.7 = bf16[1024,1280]{1,0:T(8,128)(2,1)} custom-call(s32[1]{0:T(128)} %bitcast.position_ref.s_ref.refs_0_, bf16[1024,1280]{1,0:T(8,128)(2,1)S(1)} %copy-done, bf16[256,1280]{1,0:T(8,128)(2,1)S(1)} %merge.2.rest_0_, bf16[1024,640]{1,0:T(8,128)(2,1)S(1)} %hidden.2.rest_2_.rest_1_, ...), custom_call_target="tpu_custom_call", output_to_operand_aliasing={{}: (9, {})} | custom-call | flops 314572800 | bytes 3768320 | tf_op jit(solution)/shard_map/apply/pallas_call | solution.py:548
  (40 shorter events, 3.9 us)
Async XLA Ops:
  0.0 0.7 copy-start.3
  10.8 1.3 slice-start
  10.8 1.7 %slice-start.1 = ((bf16[1024,1280]{1,0:T(8,128)(2,1)}), bf16[512,1280]{1,0:T(8,128)(2,1)S(1)}, s32[]{:S(2)}) async-start(bf16[1024,1280]{1,0:T(8,128)(2,1)} %refs_4_.7), calls=%async_computation.1 | async-start | bytes 2621440 | tf_op jit(solution)/shard_map/slice | solution.py:636
  10.8 8.7 %collective-permute-start.2 = (bf16[1920,640]{1,0:T(8,128)(2,1)S(1)}, bf16[1920,640]{1,0:T(8,128)(2,1)S(1)}, u32[]{:S(2)}, u32[]{:S(2)}) collective-permute-start(bf16[1920,640]{1,0:T(8,128)(2,1)S(1)} %grads.2), channel_id=1, source_target_pairs={{0,4},{4,0},{8,12},{12,8},{16,20},{20,16},{24,28},{28,24},{1,5},{5... | collective-permute-start | bytes 7372808 | tf_op jit(solution)/shard_map/ppermute | solution.py:573
  12.5 4.4 %copy-start.5 = (bf16[1024,1280]{1,0:T(8,128)(2,1)S(1)}, bf16[1024,1280]{1,0:T(8,128)(2,1)}, u32[]{:S(2)}) copy-start(bf16[1024,1280]{1,0:T(8,128)(2,1)} %refs_0_.1) | copy-start | bytes 7864324
  14.2 5.3 %copy-start.4 = (f32[1024,2]{0,1:T(2,128)S(1)}, f32[1024,2]{0,1:T(2,128)}, u32[]{:S(2)}) copy-start(f32[1024,2]{0,1:T(2,128)} %param.16) | copy-start | bytes 24580
  14.2 119.4 %collective-permute-start.17 = (bf16[1024,1280]{1,0:T(8,128)(2,1)}, bf16[1024,1280]{1,0:T(8,128)(2,1)S(1)}, u32[]{:S(2)}, u32[]{:S(2)}) collective-permute-start(bf16[1024,1280]{1,0:T(8,128)(2,1)} %pad_maximum_fusion), channel_id=1, source_target_pairs={{0,4},{4,8},{8,12},{12,16},{16,20},{20,24},{24,28},{1,5},{5,9},{9,... | collective-permute-start | bytes 7864328 | tf_op jit(solution)/shard_map/ppermute | solution.py:578
  18.0 54.3 %collective-permute-start = (bf16[512,1280]{1,0:T(8,128)(2,1)}, bf16[512,1280]{1,0:T(8,128)(2,1)}, u32[]{:S(2)}, u32[]{:S(2)}) collective-permute-start(bf16[512,1280]{1,0:T(8,128)(2,1)} %slice.15), channel_id=1, source_target_pairs={{4,0},{8,4},{12,8},{16,12},{20,16},{24,20},{28,24},{5,1},{9,5},{13... | collective-permute-start | bytes 3932168 | tf_op jit(solution)/shard_map/ppermute | solution.py:578
  31.2 0.8 copy-start.1
  32.0 35.1 %collective-permute-start.3 = (bf16[480,640]{1,0:T(8,128)(2,1)}, bf16[480,640]{1,0:T(8,128)(2,1)}, u32[]{:S(2)}, u32[]{:S(2)}) collective-permute-start(bf16[480,640]{1,0:T(8,128)(2,1)} %get-tuple-element.17), channel_id=1, source_target_pairs={{0,8},{4,12},{8,0},{12,4},{16,24},{20,28},{24,16},{28,20},{1,9},{5... | collective-permute-start | bytes 1843208 | tf_op jit(solution)/shard_map/ppermute | solution.py:573
  36.7 32.0 %collective-permute-start.5 = (bf16[480,640]{1,0:T(8,128)(2,1)}, bf16[480,640]{1,0:T(8,128)(2,1)}, u32[]{:S(2)}, u32[]{:S(2)}) collective-permute-start(bf16[480,640]{1,0:T(8,128)(2,1)} %get-tuple-element.19), channel_id=1, source_target_pairs={{0,16},{4,20},{8,24},{12,28},{16,0},{20,4},{24,8},{28,12},{1,17},{... | collective-permute-start | bytes 1843208 | tf_op jit(solution)/shard_map/ppermute | solution.py:573
  68.1 37.0 %collective-permute-start.4 = (bf16[240,640]{1,0:T(8,128)(2,1)S(1)}, bf16[240,640]{1,0:T(8,128)(2,1)S(1)}, u32[]{:S(2)}, u32[]{:S(2)}) collective-permute-start(bf16[240,640]{1,0:T(8,128)(2,1)S(1)} %add_convert_fusion.1), channel_id=1, source_target_pairs={{0,16},{4,20},{8,24},{12,28},{16,0},{20,4},{24,8},{28,12},{1,17},{... | collective-permute-start | bytes 921608 | tf_op jit(solution)/shard_map/ppermute | solution.py:573
  69.8 35.3 %collective-permute-start.6 = (bf16[240,640]{1,0:T(8,128)(2,1)S(1)}, bf16[240,640]{1,0:T(8,128)(2,1)S(1)}, u32[]{:S(2)}, u32[]{:S(2)}) collective-permute-start(bf16[240,640]{1,0:T(8,128)(2,1)S(1)} %add_convert_fusion), channel_id=1, source_target_pairs={{0,8},{4,12},{8,0},{12,4},{16,24},{20,28},{24,16},{28,20},{1,9},{5... | collective-permute-start | bytes 921608 | tf_op jit(solution)/shard_map/ppermute | solution.py:573
  84.9 23.9 %collective-permute-start.1 = (bf16[256,1408]{1,0:T(8,128)(2,1)S(1)}, bf16[256,1408]{1,0:T(8,128)(2,1)S(1)}, u32[]{:S(2)}, u32[]{:S(2)}) collective-permute-start(bf16[256,1408]{1,0:T(8,128)(2,1)S(1)} %get-tuple-element.14), channel_id=1, source_target_pairs={{0,4},{4,8},{8,12},{12,16},{16,20},{20,24},{24,28},{1,5},{5,9},{9,... | collective-permute-start | bytes 2162696 | tf_op jit(solution)/shard_map/ppermute | solution.py:578
  98.8 6.3 %copy-start.2 = (bf16[480,640]{1,0:T(8,128)(2,1)S(1)}, bf16[480,640]{1,0:T(8,128)(2,1)}, u32[]{:S(2)}) copy-start(bf16[480,640]{1,0:T(8,128)(2,1)} %copy-done.1) | copy-start | bytes 1843204
  98.8 31.2 %collective-permute-start.16 = (bf16[256,1408]{1,0:T(8,128)(2,1)S(1)}, bf16[256,1408]{1,0:T(8,128)(2,1)S(1)}, u32[]{:S(2)}, u32[]{:S(2)}) collective-permute-start(bf16[256,1408]{1,0:T(8,128)(2,1)S(1)} %get-tuple-element.20), channel_id=1, source_target_pairs={{0,4},{4,8},{8,12},{12,16},{16,20},{20,24},{24,28},{1,5},{5,9},{9,... | collective-permute-start | bytes 2162696 | tf_op jit(solution)/shard_map/ppermute | solution.py:578
  106.8 20.6 %collective-permute-start.10 = (bf16[480,640]{1,0:T(8,128)(2,1)S(1)}, bf16[480,640]{1,0:T(8,128)(2,1)S(1)}, u32[]{:S(2)}, u32[]{:S(2)}) collective-permute-start(bf16[480,640]{1,0:T(8,128)(2,1)S(1)} %renorm.1.own_ref.rest_3_.rest_2_), channel_id=1, source_target_pairs={{0,16},{4,20},{8,24},{12,28},{16,0},{20,4},{24,8},{28,12},{1,17},{... | collective-permute-start | bytes 1843208 | tf_op jit(solution)/shard_map/ppermute | solution.py:573
  107.2 20.5 %collective-permute-start.8 = (bf16[480,640]{1,0:T(8,128)(2,1)S(1)}, bf16[480,640]{1,0:T(8,128)(2,1)S(1)}, u32[]{:S(2)}, u32[]{:S(2)}) collective-permute-start(bf16[480,640]{1,0:T(8,128)(2,1)S(1)} %renorm.1.own_ref.rest_3_.rest_2_), channel_id=1, source_target_pairs={{0,8},{4,12},{8,0},{12,4},{16,24},{20,28},{24,16},{28,20},{1,9},{5... | collective-permute-start | bytes 1843208 | tf_op jit(solution)/shard_map/ppermute | solution.py:573
  108.9 42.5 %collective-permute-start.7 = (bf16[480,640]{1,0:T(8,128)(2,1)S(1)}, bf16[480,640]{1,0:T(8,128)(2,1)S(1)}, u32[]{:S(2)}, u32[]{:S(2)}) collective-permute-start(bf16[480,640]{1,0:T(8,128)(2,1)S(1)} %renorm.1.own_ref.rest_3_.rest_2_), channel_id=1, source_target_pairs={{0,4},{4,0},{8,12},{12,8},{16,20},{20,16},{24,28},{28,24},{1,5},{5... | collective-permute-start | bytes 1843208 | tf_op jit(solution)/shard_map/ppermute | solution.py:573
  127.4 24.0 %collective-permute-start.11 = (bf16[480,640]{1,0:T(8,128)(2,1)S(1)}, bf16[480,640]{1,0:T(8,128)(2,1)S(1)}, u32[]{:S(2)}, u32[]{:S(2)}) collective-permute-start(bf16[480,640]{1,0:T(8,128)(2,1)S(1)} %collective-permute-done.10.over_y.rest_5_.rest_4_), channel_id=1, source_target_pairs={{0,4},{4,0},{8,12},{12,8},{16,20},{20,16},{24,28},{28,24},{1,5},{5... | collective-permute-start | bytes 1843208 | tf_op jit(solution)/shard_map/ppermute | solution.py:573
  127.7 23.7 %collective-permute-start.9 = (bf16[480,640]{1,0:T(8,128)(2,1)S(1)}, bf16[480,640]{1,0:T(8,128)(2,1)S(1)}, u32[]{:S(2)}, u32[]{:S(2)}) collective-permute-start(bf16[480,640]{1,0:T(8,128)(2,1)S(1)} %collective-permute-done.8.over_x.rest_4_.rest_3_), channel_id=1, source_target_pairs={{0,4},{4,0},{8,12},{12,8},{16,20},{20,16},{24,28},{28,24},{1,5},{5... | collective-permute-start | bytes 1843208 | tf_op jit(solution)/shard_map/ppermute | solution.py:573
  131.8 14.2 %collective-permute-start.12 = (bf16[240,640]{1,0:T(8,128)(2,1)S(1)}, bf16[240,640]{1,0:T(8,128)(2,1)S(1)}, u32[]{:S(2)}, u32[]{:S(2)}) collective-permute-start(bf16[240,640]{1,0:T(8,128)(2,1)S(1)} %slice.20), channel_id=1, source_target_pairs={{0,8},{4,12},{8,0},{12,4},{16,24},{20,28},{24,16},{28,20},{1,9},{5... | collective-permute-start | bytes 921608 | tf_op jit(solution)/shard_map/ppermute | solution.py:573
  133.6 12.9 %copy-start = (bf16[1024,1280]{1,0:T(8,128)(2,1)S(1)}, bf16[1024,1280]{1,0:T(8,128)(2,1)}, u32[]{:S(2)}) copy-start(bf16[1024,1280]{1,0:T(8,128)(2,1)} %q_ref.11) | copy-start | bytes 7864324
  133.6 12.4 %collective-permute-start.14 = (bf16[240,640]{1,0:T(8,128)(2,1)S(1)}, bf16[240,640]{1,0:T(8,128)(2,1)S(1)}, u32[]{:S(2)}, u32[]{:S(2)}) collective-permute-start(bf16[240,640]{1,0:T(8,128)(2,1)S(1)} %slice.21), channel_id=1, source_target_pairs={{0,16},{4,20},{8,24},{12,28},{16,0},{20,4},{24,8},{28,12},{1,17},{... | collective-permute-start | bytes 921608 | tf_op jit(solution)/shard_map/ppermute | solution.py:573
  145.9 7.5 %collective-permute-start.13 = (bf16[240,640]{1,0:T(8,128)(2,1)S(1)}, bf16[240,640]{1,0:T(8,128)(2,1)S(1)}, u32[]{:S(2)}, u32[]{:S(2)}) collective-permute-start(bf16[240,640]{1,0:T(8,128)(2,1)S(1)} %collective-permute-done.12.rest_6_.rest_5_), channel_id=1, source_target_pairs={{0,4},{4,0},{8,12},{12,8},{16,20},{20,16},{24,28},{28,24},{1,5},{5... | collective-permute-start | bytes 921608 | tf_op jit(solution)/shard_map/ppermute | solution.py:573
  146.0 7.4 %collective-permute-start.15 = (bf16[240,640]{1,0:T(8,128)(2,1)S(1)}, bf16[240,640]{1,0:T(8,128)(2,1)S(1)}, u32[]{:S(2)}, u32[]{:S(2)}) collective-permute-start(bf16[240,640]{1,0:T(8,128)(2,1)S(1)} %collective-permute-done.14.rest_7_.rest_6_), channel_id=1, source_target_pairs={{0,4},{4,0},{8,12},{12,8},{16,20},{20,16},{24,28},{28,24},{1,5},{5... | collective-permute-start | bytes 921608 | tf_op jit(solution)/shard_map/ppermute | solution.py:573

commit v9 on v8

--- a/solution.py
+++ b/solution.py
@@ -377,7 +377,8 @@
     )(position, old, *[array for array, _ in upper + lower])
 
 
-def merge_kernel(s_ref, own_ref, far_ref, own_log, far_log, o_ref, *, stride):
+def merge_kernel(s_ref, own_ref, far_ref, own_log, far_log, *rest, stride, head_of):
+    o_ref = rest[-1]
     lane = lax.broadcasted_iota(jnp.int32, own_log.shape, 1)
     heads = o_ref.shape[1] // HD
     for j in range(heads):
@@ -393,31 +394,48 @@
         own, far = jnp.exp2(own - top), jnp.exp2(far - top)
         share = own / (own + far)
         a, b = own_ref[:, cs].astype(jnp.float32), far_ref[:, cs].astype(jnp.float32)
-        o_ref[:, cs] = (a * share + b * (1.0 - share)).astype(o_ref.dtype)
-
-
-def merged(position, own, far, own_log, width, tile):
+        out = a * share + b * (1.0 - share)
+        if head_of:
+            per = rest[0].shape[1] // HD
+            cols = pl.ds(pl.multiple_of(lax.rem(at, per) * HD, HD), HD)
+            added = rest[0][:, cols]
+            for ref, head in zip(rest[1 : len(head_of)], head_of[1:]):
+                added = jnp.where(head(s_ref) == lax.div(at, per), ref[:, cols], added)
+            out = out + added
+        o_ref[:, cs] = out.astype(o_ref.dtype)
+
+
+def merged(position, own, far, own_log, width, tile, head_of=(), added=(), into=None):
     rows, cols = far.shape[0], own.shape[1]
     w = width * HD
     mine = pl.BlockSpec((rows, w), lambda g, s: (tile, g))
     col = pl.BlockSpec((rows, w), lambda g, s: (0, g))
     own_logs = pl.BlockSpec((rows, HD), lambda g, s: (tile, 0))
     far_logs = pl.BlockSpec((rows, HD), lambda g, s: (0, cols // HD))
+    args = [position, own, far, own_log, far, *added]
+    specs = [mine, col, own_logs, far_logs] + [pl.BlockSpec(a.shape, lambda g, s: (0, 0)) for a in added]
+    shape, aliases = (rows, cols), {}
+    if into is not None:
+        shape, aliases = into.shape, {len(args): 0}
+        args.append(into)
+        specs.append(ANY)
+    kernel = functools.partial(merge_kernel, stride=log_stride_of(cols), head_of=head_of)
     return pl.pallas_call(
-        functools.partial(merge_kernel, stride=log_stride_of(cols)),
+        kernel,
         grid_spec=pltpu.PrefetchScalarGridSpec(
             num_scalar_prefetch=1,
             grid=(cols // w,),
-            in_specs=[mine, col, own_logs, far_logs],
-            out_specs=col,
-        ),
-        out_shape=jax.ShapeDtypeStruct((rows, cols), jnp.bfloat16),
+            in_specs=specs,
+            out_specs=mine if into is not None else col,
+        ),
+        out_shape=jax.ShapeDtypeStruct(shape, jnp.bfloat16),
+        input_output_aliases=aliases,
         cost_estimate=pl.CostEstimate(
             flops=8 * rows * cols, bytes_accessed=6 * rows * cols, transcendentals=rows * cols // HD
         ),
         name="merge",
-        compiler_params=room(8),
-    )(position, own, far, own_log, far)
+        compiler_params=room(10),
+    )(*args)
 
 
 def gated(h, n):
@@ -484,7 +502,7 @@
 
 def apply_kernel(s_ref, q_ref, *rest, tm, head, split, tiles, sources):
     attended, rest = rest[:sources], rest[sources:]
-    o_ref, n_ref, w_ref, h_ref, r_ref, sems = rest[-6:]
+    o_ref, x_ref, n_ref, w_ref, h_ref, r_ref, sems = rest[-7:]
     F = n_ref.shape[1]
     n, m = F // 4, F // 8
     cols = pl.ds(pl.multiple_of(head(s_ref) * F, HD), F)
@@ -523,13 +541,18 @@
             hid = h_ref[r, :]
         else:
             hid = gated(h, F)
-        a = attended[source][at : at + tm, cols].astype(jnp.float32)
-        r_ref[r, :] = (a + mm(hid, n_ref[...], NT)).astype(r_ref.dtype)
-        copy_out(i).start()
+        out = mm(hid, n_ref[...], NT)
+        if source is None:
+            x_ref[...] = out
+        else:
+            a = attended[source][at : at + tm, cols].astype(jnp.float32)
+            r_ref[r, :] = (a + out).astype(r_ref.dtype)
+            copy_out(i).start()
 
     staggered(len(tiles), first, second)
     for i in range(len(tiles)):
-        copy_out(i).wait()
+        if tiles[i][1] is not None:
+            copy_out(i).wait()
 
 
 def apply_head(position, head, fq, hidden, pieces, attended, tiles, tm, into=None):
@@ -550,7 +573,7 @@
             apply_kernel, tm=tm, head=head, split=split, tiles=tiles, sources=len(attended)
         ),
         in_specs=specs,
-        out_specs=ANY,
+        out_specs=[ANY, VMEM],
         scratch_shapes=[
             pltpu.VMEM((F, F), bf),
             pltpu.VMEM((F // 2 if split else 2 * F, F), bf),
@@ -558,7 +581,7 @@
             pltpu.VMEM((mine, F), bf),
             pltpu.SemaphoreType.DMA((len(tiles),)),
         ],
-        out_shape=jax.ShapeDtypeStruct((rows, cols), bf),
+        out_shape=[jax.ShapeDtypeStruct((rows, cols), bf), jax.ShapeDtypeStruct((tm, F), jnp.float32)],
         input_output_aliases=aliases,
         cost_estimate=pl.CostEstimate(
             flops=3 * mine * F * F, bytes_accessed=mine * F * 8 + F * F * 6, transcendentals=mine * F
@@ -678,14 +701,18 @@
     far_outs = [shifted(part, 1) for part in returned]
     (high,) = attention(position, [(attn_q, 1, late, 0)], [(prev, 0, prev, 1, half), here], bq, width)
     lows = []
-    for t, part in enumerate(far_outs):
+    for t, part in enumerate(far_outs[:-1]):
         lows.append(merged(position, own_out, part, own_log, width, t))
-    soon = [(t, t, 0) for t in range(tiles - 1)] + [(tiles + t, tiles - 1, t * bq) for t in range(tiles)]
-    mixed = None
-    for attended, rows_of in (([*lows[:-1], high], soon), (lows[-1:], [(tiles - 1, 0, 0)])):
-        for head, hidden, new in news:
-            mixed = apply_head(position, head, fast_q, hidden, new, attended, rows_of, bq, mixed)
-    return mixed
+    rows_of = [(t, t, 0) for t in range(tiles - 1)] + [(tiles + t, tiles - 1, t * bq) for t in range(tiles)]
+    rows_of.append((tiles - 1, None, 0))
+    mixed, added = None, []
+    for head, hidden, new in news:
+        mixed, extra = apply_head(
+            position, head, fast_q, hidden, new, [*lows, high], rows_of, bq, mixed
+        )
+        added.append(extra)
+    head_of = [head for head, _, _ in news]
+    return merged(position, own_out, far_outs[-1], own_log, width, tiles - 1, head_of, added, mixed)
 
 
 def solution(mesh):

time: 161 us -> 155 us (0.963)
  waiting for transfers between devices: 47.5 us -> 43.2 us
  Pallas kernels: 69.1 us -> 66.7 us
    ppermute x14, waiting for transfers between devices: 47.5 us -> 43.2 us  [exchange(): return lax.ppermute(block, 'seq', [(i, i ^ 1 << bit) for i in range(size)])]
    pallas_call x4 -> x2, Pallas kernels: 9.88 us -> 6.34 us  [apply_head(): pl.pallas_call(functools.partial(apply_kernel, tm=tm, head=head, split=sp...]
  transfers between devices with their start and end apart: 18 -> 18, of which waited for: 2 -> 2; matrix products, arithmetic and copies ran while one was open for 3% -> 3% of each run, Pallas kernels for 32% -> 35%
where the time goes in v9:
time: 155 us; the launch traced here: 154 us
  Pallas kernels  66.7 us (43%)
  waiting for transfers between devices  43.2 us (28%)
  starting transfers between devices  36.5 us (24%)
  local copies, waits for them, and re-layouts  3.92 us (3%)
  other arithmetic  3.84 us (2%)
    ppermute x14, waiting for transfers between devices, exchange(): return lax.ppermute(block, 'seq', [(i, i ^ 1 << bit) for i in range(size)])  43.2 us
    pallas_call x2, Pallas kernels, attention(): pl.pallas_call(kernel, grid_spec=pltpu.PrefetchScalarGridSpec(num_scalar_...  24.2 us
    pallas_call x2, Pallas kernels, gradients(): pl.pallas_call(body, grid_spec=pltpu.PrefetchScalarGridSpec(num_scalar_pr...  21.7 us
    ppermute x4, starting transfers between devices, shifted(): lax.ppermute(block, 'seq', [(i, i + by) for i in range(size) if 0 <= i +...  20.3 us
    ppermute x14, starting transfers between devices, exchange(): return lax.ppermute(block, 'seq', [(i, i ^ 1 << bit) for i in range(size)])  16.2 us
    pallas_call x2, Pallas kernels, apply_head(): pl.pallas_call(functools.partial(apply_kernel, tm=tm, head=head, split=sp...  6.34 us
    pallas_call x2, Pallas kernels, merged(): pl.pallas_call(kernel, grid_spec=pltpu.PrefetchScalarGridSpec(num_scalar_...  4.67 us
    pallas_call x2, Pallas kernels, hidden_part(): pl.pallas_call(functools.partial(hidden_kernel, tm=min(256, rows), head=h...  4.04 us
  transfers between devices with their start and end apart: 18, of which 2 were waited for; matrix products, arithmetic and copies ran while one was open for 3% of the time, Pallas kernels for 35%

profile of v9, /device:TPU:0, one launch (start us, length us, event | category | flops | bytes accessed | tf_op | source)
XLA Modules:
  0.0 154.3 jit_solution(14328323924299056728)
XLA Ops:
  0.0 0.7 copy-done.3
  0.7 10.1 %grads.2 = bf16[1920,640]{1,0:T(8,128)(2,1)S(1)} custom-call(s32[1]{0:T(128)} %bitcast.position_ref.s_ref.refs_0_, bf16[1024,1280]{1,0:T(8,128)(2,1)} %refs_1_.3, bf16[1024,1280]{1,0:T(8,128)(2,1)} %refs_2_.7, f32[2,1024]{1,0:T(2,128)S(1)} %bitcast.2, f32[2,640,640]{2,1,0:T(8,128)} %refs_4_.7, f32[2,640,640]{2,1,0:T(8,128)} %refs_5_.3, f32[2,640,640]{2,1,0:T(8,128)} %refs_6_.3), custom_call_target="tpu_custom_call" | custom-call | flops 5033164800 | bytes 9994240 | tf_op jit(solution)/shard_map/grads/pallas_call | solution.py:292
  10.8 0.6 collective-permute-start.4
  11.4 0.7 slice-done
  12.5 1.7 %pad_maximum_fusion = bf16[1024,1280]{1,0:T(8,128)(2,1)} fusion(bf16[512,1280]{1,0:T(8,128)(2,1)S(1)} %slice-done.1, bf16[512,1280]{1,0:T(8,128)(2,1)S(1)} %slice-done), kind=kLoop, calls=%fused_computation | loop fusion | flops 5242880 | bytes 5242880 | tf_op jit(solution)/shard_map/concatenate | solution.py:659
  14.2 2.7 %collective-permute-start.3 = (bf16[1024,1280]{1,0:T(8,128)(2,1)}, bf16[1024,1280]{1,0:T(8,128)(2,1)S(1)}, u32[]{:S(2)}, u32[]{:S(2)}) collective-permute-start(bf16[1024,1280]{1,0:T(8,128)(2,1)} %pad_maximum_fusion), channel_id=1, source_target_pairs={{0,4},{4,8},{8,12},{12,16},{16,20},{20,24},{24,28},{1,5},{5,9},{9,... | collective-permute-start | bytes 7864328 | tf_op jit(solution)/shard_map/ppermute | solution.py:601
  16.9 1.2 slice.15
  18.0 1.5 collective-permute-start
  19.5 11.6 %grads.3 = (bf16[480,640]{1,0:T(8,128)(2,1)S(1)}, bf16[480,640]{1,0:T(8,128)(2,1)}, bf16[480,640]{1,0:T(8,128)(2,1)S(1)}, bf16[480,640]{1,0:T(8,128)(2,1)}) custom-call(s32[1]{0:T(128)} %bitcast.position_ref.s_ref.refs_0_, bf16[1024,1280]{1,0:T(8,128)(2,1)} %refs_1_.3, bf16[1024,1280]{1,0:T(8,128)(2,1)} %refs_2_.7, f32[2,1024]{1,0:T(2,128)S(1)} %bitcast.3, ...), custom_call_target="tpu_custom_call" | custom-call | flops 5033164800 | bytes 9994240 | tf_op jit(solution)/shard_map/grads/pallas_call | solution.py:292
  31.2 0.8 copy-done.1
  32.0 4.7 %collective-permute-start.5 = (bf16[480,640]{1,0:T(8,128)(2,1)}, bf16[480,640]{1,0:T(8,128)(2,1)}, u32[]{:S(2)}, u32[]{:S(2)}) collective-permute-start(bf16[480,640]{1,0:T(8,128)(2,1)} %get-tuple-element.22), channel_id=1, source_target_pairs={{0,8},{4,12},{8,0},{12,4},{16,24},{20,28},{24,16},{28,20},{1,9},{5... | collective-permute-start | bytes 1843208 | tf_op jit(solution)/shard_map/ppermute | solution.py:596
  36.7 1.5 collective-permute-start.7
  38.2 28.9 %collective-permute-done.5.refs_1_ = bf16[480,640]{1,0:T(8,128)(2,1)} collective-permute-done((bf16[480,640]{1,0:T(8,128)(2,1)}, bf16[480,640]{1,0:T(8,128)(2,1)}, u32[]{:S(2)}, u32[]{:S(2)}) %collective-permute-start.5) | collective-permute-done | bytes 614432 | tf_op jit(solution)/shard_map/ppermute | solution.py:596
  67.1 1.0 add_convert_fusion.1
  68.7 1.1 add_convert_fusion
  69.8 2.5 %collective-permute-start.8 = (bf16[240,640]{1,0:T(8,128)(2,1)S(1)}, bf16[240,640]{1,0:T(8,128)(2,1)S(1)}, u32[]{:S(2)}, u32[]{:S(2)}) collective-permute-start(bf16[240,640]{1,0:T(8,128)(2,1)S(1)} %add_convert_fusion), channel_id=1, source_target_pairs={{0,8},{4,12},{8,0},{12,4},{16,24},{20,28},{24,16},{28,20},{1,9},{5... | collective-permute-start | bytes 921608 | tf_op jit(solution)/shard_map/ppermute | solution.py:596
  72.4 12.6 %shard_map.100 = (bf16[256,1408]{1,0:T(8,128)(2,1)S(1)}, bf16[256,1408]{1,0:T(8,128)(2,1)S(1)}, bf16[512,1280]{1,0:T(8,128)(2,1)S(1)}, f32[512,128]{1,0:T(8,128)S(1)}) custom-call(s32[1]{0:T(128)} %bitcast.position_ref.s_ref.refs_0_, bf16[512,1280]{1,0:T(8,128)(2,1)} %collective-permute-done.refs_0_.refs_1_, ...), custom_call_target="tpu_custom_call" | custom-call | flops 3355443200 | bytes 10485760 | tf_op jit(solution)/shard_map/pallas_call | solution.py:158
  85.0 14.0 %collective-permute-start.2 = (bf16[256,1408]{1,0:T(8,128)(2,1)S(1)}, bf16[256,1408]{1,0:T(8,128)(2,1)S(1)}, u32[]{:S(2)}, u32[]{:S(2)}) collective-permute-start(bf16[256,1408]{1,0:T(8,128)(2,1)S(1)} %get-tuple-element.20), channel_id=1, source_target_pairs={{0,4},{4,8},{8,12},{12,16},{16,20},{20,24},{24,28},{1,5},{5,9},{9,... | collective-permute-start | bytes 2162696 | tf_op jit(solution)/shard_map/ppermute | solution.py:601
  98.9 4.0 %turned.1.old_ref = f32[480,640]{1,0:T(8,128)S(1)} custom-call(s32[1]{0:T(128)} %bitcast.position_ref.s_ref.refs_0_, f32[2,640,640]{2,1,0:T(8,128)} %refs_4_.7, f32[2,640,640]{2,1,0:T(8,128)} %refs_5_.3, f32[2,640,640]{2,1,0:T(8,128)} %refs_6_.3), custom_call_target="tpu_custom_call" | custom-call | flops 1228800 | bytes 9830400 | tf_op jit(solution)/shard_map/turned/pallas_call | solution.py:326
  103.0 1.7 %renorm.1.own_ref.rest_3_ = bf16[480,640]{1,0:T(8,128)(2,1)S(1)} custom-call(s32[1]{0:T(128)} %bitcast.position_ref.s_ref.refs_0_, f32[480,640]{1,0:T(8,128)S(1)} %turned.1.old_ref, bf16[480,640]{1,0:T(8,128)(2,1)S(1)} %get-tuple-element.21.refs_0_, bf16[480,640]{1,0:T(8,128)(2,1)} %collective-permute-done.5.refs_1_, ...), custom_call_target="tpu_custom_call" | custom-call | flops 3072000 | bytes 3686400 | tf_op jit(solution)/shard_map/renorm/pallas_call | solution.py:365
  105.0 1.7 %collective-permute-start.10 = (bf16[480,640]{1,0:T(8,128)(2,1)S(1)}, bf16[480,640]{1,0:T(8,128)(2,1)S(1)}, u32[]{:S(2)}, u32[]{:S(2)}) collective-permute-start(bf16[480,640]{1,0:T(8,128)(2,1)S(1)} %renorm.1.own_ref.rest_3_), channel_id=1, source_target_pairs={{0,16},{4,20},{8,24},{12,28},{16,0},{20,4},{24,8},{28,12},{1,17},{... | collective-permute-start | bytes 1843208 | tf_op jit(solution)/shard_map/ppermute | solution.py:596
  106.7 14.2 %collective-permute-done.9.over_x.rest_4_ = bf16[480,640]{1,0:T(8,128)(2,1)S(1)} collective-permute-done((bf16[480,640]{1,0:T(8,128)(2,1)S(1)}, bf16[480,640]{1,0:T(8,128)(2,1)S(1)}, u32[]{:S(2)}, u32[]{:S(2)}) %collective-permute-start.9) | collective-permute-done | bytes 614432 | tf_op jit(solution)/shard_map/ppermute | solution.py:596
  121.5 2.2 %collective-permute-start.1 = (bf16[256,1408]{1,0:T(8,128)(2,1)S(1)}, bf16[256,1408]{1,0:T(8,128)(2,1)S(1)}, u32[]{:S(2)}, u32[]{:S(2)}) collective-permute-start(bf16[256,1408]{1,0:T(8,128)(2,1)S(1)} %get-tuple-element.18), channel_id=1, source_target_pairs={{0,4},{4,8},{8,12},{12,16},{16,20},{20,24},{24,28},{1,5},{5,9},{9,... | collective-permute-start | bytes 2162696 | tf_op jit(solution)/shard_map/ppermute | solution.py:601
  123.6 1.7 %merge.2.rest_0_ = bf16[256,1280]{1,0:T(8,128)(2,1)S(1)} custom-call(s32[1]{0:T(128)} %bitcast.position_ref.s_ref.refs_0_, bf16[512,1280]{1,0:T(8,128)(2,1)S(1)} %get-tuple-element.17.own_ref, bf16[256,1408]{1,0:T(8,128)(2,1)S(1)} %collective-permute-done.2.far_ref.far_log, f32[512,128]{1,0:T(8,128)S(1)} %get-tuple-element.19.own_log, ...), custom_call_target="tpu_custom_call" | custom-call | flops 2621440 | bytes 1966080 | tf_op jit(solution)/shard_map/merge/pallas_call | solution.py:423
  125.4 1.5 collective-permute-start.11
  127.5 11.6 %shard_map.101.rest_1_ = bf16[512,1280]{1,0:T(8,128)(2,1)S(1)} custom-call(s32[1]{0:T(128)} %bitcast.position_ref.s_ref.refs_0_, bf16[1024,1280]{1,0:T(8,128)(2,1)} %refs_0_.1, bf16[1024,1280]{1,0:T(8,128)(2,1)S(1)} %collective-permute-done.3.refs_1_.refs_3_, bf16[1024,1280]{1,0:T(8,128)(2,1)} %refs_2_.5, ...), custom_call_target="tpu_custom_call" | custom-call | flops 3355443200 | bytes 10485760 | tf_op jit(solution)/shard_map/pallas_call | solution.py:158
  139.1 1.8 %collective-permute-start.16 = (bf16[240,640]{1,0:T(8,128)(2,1)S(1)}, bf16[240,640]{1,0:T(8,128)(2,1)S(1)}, u32[]{:S(2)}, u32[]{:S(2)}) collective-permute-start(bf16[240,640]{1,0:T(8,128)(2,1)S(1)} %collective-permute-done.11.rest_6_), channel_id=1, source_target_pairs={{0,4},{4,0},{8,12},{12,8},{16,20},{20,16},{24,28},{28,24},{1,5},{5... | collective-permute-start | bytes 921608 | tf_op jit(solution)/shard_map/ppermute | solution.py:596
  140.9 2.0 %hidden.2.rest_2_ = bf16[1024,640]{1,0:T(8,128)(2,1)S(1)} custom-call(s32[1]{0:T(128)} %bitcast.position_ref.s_ref.refs_0_, bf16[1024,1280]{1,0:T(8,128)(2,1)S(1)} %copy-done, bf16[480,640]{1,0:T(8,128)(2,1)S(1)} %renorm.1.own_ref.rest_3_, bf16[480,640]{1,0:T(8,128)(2,1)S(1)} %collective-permute-done.9.over_x.rest_4_, ...), custom_call_target="tpu_custom_call" | custom-call | flops 1258291200 | bytes 3850240 | tf_op jit(solution)/shard_map/hidden/pallas_call | solution.py:489
  142.9 3.0 %apply.2 = (bf16[1024,1280]{1,0:T(8,128)(2,1)}, f32[256,640]{1,0:T(8,128)S(1)}) custom-call(s32[1]{0:T(128)} %bitcast.position_ref.s_ref.refs_0_, bf16[1024,1280]{1,0:T(8,128)(2,1)S(1)} %copy-done, bf16[256,1280]{1,0:T(8,128)(2,1)S(1)} %merge.2.rest_0_, bf16[512,1280]{1,0:T(8,128)(2,1)S(1)} %shard_map.101.rest_1_, bf16[1024,640]{1,0:T(8,128)(2,1)S(1)} %hidden.2.rest_2_, ...), custom_call_target="tpu_custom_call" | custom-call | flops 1258291200 | bytes 7700480 | tf_op jit(solution)/shard_map/apply/pallas_call | solution.py:571
  146.0 2.0 %hidden.3.rest_2_ = bf16[1024,640]{1,0:T(8,128)(2,1)S(1)} custom-call(s32[1]{0:T(128)} %bitcast.position_ref.s_ref.refs_0_, bf16[1024,1280]{1,0:T(8,128)(2,1)S(1)} %copy-done, bf16[480,640]{1,0:T(8,128)(2,1)S(1)} %collective-permute-done.13.own_ref.rest_3_, bf16[480,640]{1,0:T(8,128)(2,1)S(1)} %collective-permute-done.14.over_x.rest_4_, ...), custom_call_target="tpu_custom_call" | custom-call | flops 1258291200 | bytes 3850240 | tf_op jit(solution)/shard_map/hidden/pallas_call | solution.py:489
  148.0 3.3 %apply.3 = (bf16[1024,1280]{1,0:T(8,128)(2,1)}, f32[256,640]{1,0:T(8,128)S(1)}) custom-call(s32[1]{0:T(128)} %bitcast.position_ref.s_ref.refs_0_, bf16[1024,1280]{1,0:T(8,128)(2,1)S(1)} %copy-done, bf16[256,1280]{1,0:T(8,128)(2,1)S(1)} %merge.2.rest_0_, bf16[512,1280]{1,0:T(8,128)(2,1)S(1)} %shard_map.101.rest_1_, ...), custom_call_target="tpu_custom_call", output_to_operand_aliasing={{0}: (10, {})} | custom-call | flops 1258291200 | bytes 7700480 | tf_op jit(solution)/shard_map/apply/pallas_call | solution.py:571
  151.4 3.0 %merge.3 = bf16[1024,1280]{1,0:T(8,128)(2,1)} custom-call(s32[1]{0:T(128)} %bitcast.position_ref.s_ref.refs_0_, bf16[512,1280]{1,0:T(8,128)(2,1)S(1)} %get-tuple-element.17.own_ref, bf16[256,1408]{1,0:T(8,128)(2,1)S(1)} %collective-permute-done.1.far_ref.far_log, f32[512,128]{1,0:T(8,128)S(1)} %get-tuple-element.19.own_log, ...), custom_call_target="tpu_custom_call", output_to_operand_aliasing={{}: (7, {})} | custom-call | flops 2621440 | bytes 1966080 | tf_op jit(solution)/shard_map/merge/pallas_call | solution.py:423
  (38 shorter events, 2.4 us)
Async XLA Ops:
  0.0 0.7 copy-start.3
  10.8 1.3 slice-start
  10.8 1.7 %slice-start.1 = ((bf16[1024,1280]{1,0:T(8,128)(2,1)}), bf16[512,1280]{1,0:T(8,128)(2,1)S(1)}, s32[]{:S(2)}) async-start(bf16[1024,1280]{1,0:T(8,128)(2,1)} %refs_4_.5), calls=%async_computation.1 | async-start | bytes 2621440 | tf_op jit(solution)/shard_map/slice | solution.py:659
  10.8 8.7 %collective-permute-start.4 = (bf16[1920,640]{1,0:T(8,128)(2,1)S(1)}, bf16[1920,640]{1,0:T(8,128)(2,1)S(1)}, u32[]{:S(2)}, u32[]{:S(2)}) collective-permute-start(bf16[1920,640]{1,0:T(8,128)(2,1)S(1)} %grads.2), channel_id=1, source_target_pairs={{0,4},{4,0},{8,12},{12,8},{16,20},{20,16},{24,28},{28,24},{1,5},{5... | collective-permute-start | bytes 7372808 | tf_op jit(solution)/shard_map/ppermute | solution.py:596
  12.5 4.4 %copy-start.5 = (bf16[1024,1280]{1,0:T(8,128)(2,1)S(1)}, bf16[1024,1280]{1,0:T(8,128)(2,1)}, u32[]{:S(2)}) copy-start(bf16[1024,1280]{1,0:T(8,128)(2,1)} %refs_0_.1) | copy-start | bytes 7864324
  14.2 5.4 %copy-start.4 = (f32[1024,2]{0,1:T(2,128)S(1)}, f32[1024,2]{0,1:T(2,128)}, u32[]{:S(2)}) copy-start(f32[1024,2]{0,1:T(2,128)} %param.16) | copy-start | bytes 24580
  14.2 111.2 %collective-permute-start.3 = (bf16[1024,1280]{1,0:T(8,128)(2,1)}, bf16[1024,1280]{1,0:T(8,128)(2,1)S(1)}, u32[]{:S(2)}, u32[]{:S(2)}) collective-permute-start(bf16[1024,1280]{1,0:T(8,128)(2,1)} %pad_maximum_fusion), channel_id=1, source_target_pairs={{0,4},{4,8},{8,12},{12,16},{16,20},{20,24},{24,28},{1,5},{5,9},{9,... | collective-permute-start | bytes 7864328 | tf_op jit(solution)/shard_map/ppermute | solution.py:601
  18.0 54.3 %collective-permute-start = (bf16[512,1280]{1,0:T(8,128)(2,1)}, bf16[512,1280]{1,0:T(8,128)(2,1)}, u32[]{:S(2)}, u32[]{:S(2)}) collective-permute-start(bf16[512,1280]{1,0:T(8,128)(2,1)} %slice.15), channel_id=1, source_target_pairs={{4,0},{8,4},{12,8},{16,12},{20,16},{24,20},{28,24},{5,1},{9,5},{13... | collective-permute-start | bytes 3932168 | tf_op jit(solution)/shard_map/ppermute | solution.py:601
  31.2 0.8 copy-start.1
  32.0 35.1 %collective-permute-start.5 = (bf16[480,640]{1,0:T(8,128)(2,1)}, bf16[480,640]{1,0:T(8,128)(2,1)}, u32[]{:S(2)}, u32[]{:S(2)}) collective-permute-start(bf16[480,640]{1,0:T(8,128)(2,1)} %get-tuple-element.22), channel_id=1, source_target_pairs={{0,8},{4,12},{8,0},{12,4},{16,24},{20,28},{24,16},{28,20},{1,9},{5... | collective-permute-start | bytes 1843208 | tf_op jit(solution)/shard_map/ppermute | solution.py:596
  36.7 32.0 %collective-permute-start.7 = (bf16[480,640]{1,0:T(8,128)(2,1)}, bf16[480,640]{1,0:T(8,128)(2,1)}, u32[]{:S(2)}, u32[]{:S(2)}) collective-permute-start(bf16[480,640]{1,0:T(8,128)(2,1)} %get-tuple-element.24), channel_id=1, source_target_pairs={{0,16},{4,20},{8,24},{12,28},{16,0},{20,4},{24,8},{28,12},{1,17},{... | collective-permute-start | bytes 1843208 | tf_op jit(solution)/shard_map/ppermute | solution.py:596
  68.1 34.8 %collective-permute-start.6 = (bf16[240,640]{1,0:T(8,128)(2,1)S(1)}, bf16[240,640]{1,0:T(8,128)(2,1)S(1)}, u32[]{:S(2)}, u32[]{:S(2)}) collective-permute-start(bf16[240,640]{1,0:T(8,128)(2,1)S(1)} %add_convert_fusion.1), channel_id=1, source_target_pairs={{0,16},{4,20},{8,24},{12,28},{16,0},{20,4},{24,8},{28,12},{1,17},{... | collective-permute-start | bytes 921608 | tf_op jit(solution)/shard_map/ppermute | solution.py:596
  69.8 33.1 %collective-permute-start.8 = (bf16[240,640]{1,0:T(8,128)(2,1)S(1)}, bf16[240,640]{1,0:T(8,128)(2,1)S(1)}, u32[]{:S(2)}, u32[]{:S(2)}) collective-permute-start(bf16[240,640]{1,0:T(8,128)(2,1)S(1)} %add_convert_fusion), channel_id=1, source_target_pairs={{0,8},{4,12},{8,0},{12,4},{16,24},{20,28},{24,16},{28,20},{1,9},{5... | collective-permute-start | bytes 921608 | tf_op jit(solution)/shard_map/ppermute | solution.py:596
  84.9 18.0 %copy-start.2 = (bf16[480,640]{1,0:T(8,128)(2,1)S(1)}, bf16[480,640]{1,0:T(8,128)(2,1)}, u32[]{:S(2)}) copy-start(bf16[480,640]{1,0:T(8,128)(2,1)} %copy-done.1) | copy-start | bytes 1843204
  85.0 36.5 %collective-permute-start.2 = (bf16[256,1408]{1,0:T(8,128)(2,1)S(1)}, bf16[256,1408]{1,0:T(8,128)(2,1)S(1)}, u32[]{:S(2)}, u32[]{:S(2)}) collective-permute-start(bf16[256,1408]{1,0:T(8,128)(2,1)S(1)} %get-tuple-element.20), channel_id=1, source_target_pairs={{0,4},{4,8},{8,12},{12,16},{16,20},{20,24},{24,28},{1,5},{5,9},{9,... | collective-permute-start | bytes 2162696 | tf_op jit(solution)/shard_map/ppermute | solution.py:601
  104.7 16.3 %collective-permute-start.9 = (bf16[480,640]{1,0:T(8,128)(2,1)S(1)}, bf16[480,640]{1,0:T(8,128)(2,1)S(1)}, u32[]{:S(2)}, u32[]{:S(2)}) collective-permute-start(bf16[480,640]{1,0:T(8,128)(2,1)S(1)} %renorm.1.own_ref.rest_3_), channel_id=1, source_target_pairs={{0,8},{4,12},{8,0},{12,4},{16,24},{20,28},{24,16},{28,20},{1,9},{5... | collective-permute-start | bytes 1843208 | tf_op jit(solution)/shard_map/ppermute | solution.py:596
  105.0 15.9 %collective-permute-start.10 = (bf16[480,640]{1,0:T(8,128)(2,1)S(1)}, bf16[480,640]{1,0:T(8,128)(2,1)S(1)}, u32[]{:S(2)}, u32[]{:S(2)}) collective-permute-start(bf16[480,640]{1,0:T(8,128)(2,1)S(1)} %renorm.1.own_ref.rest_3_), channel_id=1, source_target_pairs={{0,16},{4,20},{8,24},{12,28},{16,0},{20,4},{24,8},{28,12},{1,17},{... | collective-permute-start | bytes 1843208 | tf_op jit(solution)/shard_map/ppermute | solution.py:596
  106.7 20.3 %collective-permute-start.13 = (bf16[480,640]{1,0:T(8,128)(2,1)S(1)}, bf16[480,640]{1,0:T(8,128)(2,1)S(1)}, u32[]{:S(2)}, u32[]{:S(2)}) collective-permute-start(bf16[480,640]{1,0:T(8,128)(2,1)S(1)} %renorm.1.own_ref.rest_3_), channel_id=1, source_target_pairs={{0,4},{4,0},{8,12},{12,8},{16,20},{20,16},{24,28},{28,24},{1,5},{5... | collective-permute-start | bytes 1843208 | tf_op jit(solution)/shard_map/ppermute | solution.py:596
  120.9 25.0 %collective-permute-start.14 = (bf16[480,640]{1,0:T(8,128)(2,1)S(1)}, bf16[480,640]{1,0:T(8,128)(2,1)S(1)}, u32[]{:S(2)}, u32[]{:S(2)}) collective-permute-start(bf16[480,640]{1,0:T(8,128)(2,1)S(1)} %collective-permute-done.9.over_x.rest_4_), channel_id=1, source_target_pairs={{0,4},{4,0},{8,12},{12,8},{16,20},{20,16},{24,28},{28,24},{1,5},{5... | collective-permute-start | bytes 1843208 | tf_op jit(solution)/shard_map/ppermute | solution.py:596
  120.9 25.0 %collective-permute-start.15 = (bf16[480,640]{1,0:T(8,128)(2,1)S(1)}, bf16[480,640]{1,0:T(8,128)(2,1)S(1)}, u32[]{:S(2)}, u32[]{:S(2)}) collective-permute-start(bf16[480,640]{1,0:T(8,128)(2,1)S(1)} %collective-permute-done.10.over_y.rest_5_), channel_id=1, source_target_pairs={{0,4},{4,0},{8,12},{12,8},{16,20},{20,16},{24,28},{28,24},{1,5},{5... | collective-permute-start | bytes 1843208 | tf_op jit(solution)/shard_map/ppermute | solution.py:596
  121.5 29.9 %collective-permute-start.1 = (bf16[256,1408]{1,0:T(8,128)(2,1)S(1)}, bf16[256,1408]{1,0:T(8,128)(2,1)S(1)}, u32[]{:S(2)}, u32[]{:S(2)}) collective-permute-start(bf16[256,1408]{1,0:T(8,128)(2,1)S(1)} %get-tuple-element.18), channel_id=1, source_target_pairs={{0,4},{4,8},{8,12},{12,16},{16,20},{20,24},{24,28},{1,5},{5,9},{9,... | collective-permute-start | bytes 2162696 | tf_op jit(solution)/shard_map/ppermute | solution.py:601
  125.4 15.5 %copy-start = (bf16[1024,1280]{1,0:T(8,128)(2,1)S(1)}, bf16[1024,1280]{1,0:T(8,128)(2,1)}, u32[]{:S(2)}) copy-start(bf16[1024,1280]{1,0:T(8,128)(2,1)} %q_ref.7) | copy-start | bytes 7864324
  125.4 13.7 %collective-permute-start.11 = (bf16[240,640]{1,0:T(8,128)(2,1)S(1)}, bf16[240,640]{1,0:T(8,128)(2,1)S(1)}, u32[]{:S(2)}, u32[]{:S(2)}) collective-permute-start(bf16[240,640]{1,0:T(8,128)(2,1)S(1)} %slice.20), channel_id=1, source_target_pairs={{0,8},{4,12},{8,0},{12,4},{16,24},{20,28},{24,16},{28,20},{1,9},{5... | collective-permute-start | bytes 921608 | tf_op jit(solution)/shard_map/ppermute | solution.py:596
  127.0 13.9 %collective-permute-start.12 = (bf16[240,640]{1,0:T(8,128)(2,1)S(1)}, bf16[240,640]{1,0:T(8,128)(2,1)S(1)}, u32[]{:S(2)}, u32[]{:S(2)}) collective-permute-start(bf16[240,640]{1,0:T(8,128)(2,1)S(1)} %slice.21), channel_id=1, source_target_pairs={{0,16},{4,20},{8,24},{12,28},{16,0},{20,4},{24,8},{28,12},{1,17},{... | collective-permute-start | bytes 921608 | tf_op jit(solution)/shard_map/ppermute | solution.py:596
  139.1 8.9 %collective-permute-start.16 = (bf16[240,640]{1,0:T(8,128)(2,1)S(1)}, bf16[240,640]{1,0:T(8,128)(2,1)S(1)}, u32[]{:S(2)}, u32[]{:S(2)}) collective-permute-start(bf16[240,640]{1,0:T(8,128)(2,1)S(1)} %collective-permute-done.11.rest_6_), channel_id=1, source_target_pairs={{0,4},{4,0},{8,12},{12,8},{16,20},{20,16},{24,28},{28,24},{1,5},{5... | collective-permute-start | bytes 921608 | tf_op jit(solution)/shard_map/ppermute | solution.py:596
  140.9 7.1 %collective-permute-start.17 = (bf16[240,640]{1,0:T(8,128)(2,1)S(1)}, bf16[240,640]{1,0:T(8,128)(2,1)S(1)}, u32[]{:S(2)}, u32[]{:S(2)}) collective-permute-start(bf16[240,640]{1,0:T(8,128)(2,1)S(1)} %collective-permute-done.12.rest_7_), channel_id=1, source_target_pairs={{0,4},{4,0},{8,12},{12,8},{16,20},{20,16},{24,28},{28,24},{1,5},{5... | collective-permute-start | bytes 921608 | tf_op jit(solution)/shard_map/ppermute | solution.py:596

commit v10 on v9

--- a/solution.py
+++ b/solution.py
@@ -434,7 +434,7 @@
             flops=8 * rows * cols, bytes_accessed=6 * rows * cols, transcendentals=rows * cols // HD
         ),
         name="merge",
-        compiler_params=room(10),
+        compiler_params=room(12),
     )(*args)
 
 
@@ -712,7 +712,9 @@
         )
         added.append(extra)
     head_of = [head for head, _, _ in news]
-    return merged(position, own_out, far_outs[-1], own_log, width, tiles - 1, head_of, added, mixed)
+    span = attn_q.shape[1] // HD
+    wide = span // 2 if span % 2 == 0 else 1
+    return merged(position, own_out, far_outs[-1], own_log, wide, tiles - 1, head_of, added, mixed)
 
 
 def solution(mesh):

time: 155 us -> 154 us (level)
  no operation moved by 1% of the time
where the time goes in v10:
time: 154 us; the launch traced here: 153 us
  Pallas kernels  65.8 us (43%)
  waiting for transfers between devices  43.2 us (28%)
  starting transfers between devices  36.5 us (24%)
  local copies, waits for them, and re-layouts  3.92 us (3%)
  other arithmetic  3.84 us (2%)
    ppermute x14, waiting for transfers between devices, exchange(): return lax.ppermute(block, 'seq', [(i, i ^ 1 << bit) for i in range(size)])  43.2 us
    pallas_call x2, Pallas kernels, attention(): pl.pallas_call(kernel, grid_spec=pltpu.PrefetchScalarGridSpec(num_scalar_...  24.2 us
    pallas_call x2, Pallas kernels, gradients(): pl.pallas_call(body, grid_spec=pltpu.PrefetchScalarGridSpec(num_scalar_pr...  21.7 us
    ppermute x4, starting transfers between devices, shifted(): lax.ppermute(block, 'seq', [(i, i + by) for i in range(size) if 0 <= i +...  20.3 us
    ppermute x14, starting transfers between devices, exchange(): return lax.ppermute(block, 'seq', [(i, i ^ 1 << bit) for i in range(size)])  16.2 us
    pallas_call x2, Pallas kernels, apply_head(): pl.pallas_call(functools.partial(apply_kernel, tm=tm, head=head, split=sp...  6.34 us
    pallas_call x2, Pallas kernels, hidden_part(): pl.pallas_call(functools.partial(hidden_kernel, tm=min(256, rows), head=h...  4.04 us
    pallas_call x1, Pallas kernels, turned(): pl.pallas_call(functools.partial(turn_kernel, parts=parts), grid_spec=plt...  4 us
  transfers between devices with their start and end apart: 18, of which 2 were waited for; matrix products, arithmetic and copies ran while one was open for 3% of the time, Pallas kernels for 35%

profile of v10, /device:TPU:0, one launch (start us, length us, event | category | flops | bytes accessed | tf_op | source)
XLA Modules:
  0.0 153.5 jit_solution(15083273444032210393)
XLA Ops:
  0.0 0.7 copy-done.3
  0.7 10.1 %grads.2 = bf16[1920,640]{1,0:T(8,128)(2,1)S(1)} custom-call(s32[1]{0:T(128)} %bitcast.position_ref.s_ref.refs_0_, bf16[1024,1280]{1,0:T(8,128)(2,1)} %refs_1_.3, bf16[1024,1280]{1,0:T(8,128)(2,1)} %refs_2_.7, f32[2,1024]{1,0:T(2,128)S(1)} %bitcast.2, f32[2,640,640]{2,1,0:T(8,128)} %refs_4_.7, f32[2,640,640]{2,1,0:T(8,128)} %refs_5_.3, f32[2,640,640]{2,1,0:T(8,128)} %refs_6_.3), custom_call_target="tpu_custom_call" | custom-call | flops 5033164800 | bytes 9994240 | tf_op jit(solution)/shard_map/grads/pallas_call | solution.py:292
  10.8 0.6 collective-permute-start.4
  11.4 0.7 slice-done
  12.5 1.7 %pad_maximum_fusion = bf16[1024,1280]{1,0:T(8,128)(2,1)} fusion(bf16[512,1280]{1,0:T(8,128)(2,1)S(1)} %slice-done.1, bf16[512,1280]{1,0:T(8,128)(2,1)S(1)} %slice-done), kind=kLoop, calls=%fused_computation | loop fusion | flops 5242880 | bytes 5242880 | tf_op jit(solution)/shard_map/concatenate | solution.py:659
  14.2 2.7 %collective-permute-start.3 = (bf16[1024,1280]{1,0:T(8,128)(2,1)}, bf16[1024,1280]{1,0:T(8,128)(2,1)S(1)}, u32[]{:S(2)}, u32[]{:S(2)}) collective-permute-start(bf16[1024,1280]{1,0:T(8,128)(2,1)} %pad_maximum_fusion), channel_id=1, source_target_pairs={{0,4},{4,8},{8,12},{12,16},{16,20},{20,24},{24,28},{1,5},{5,9},{9,... | collective-permute-start | bytes 7864328 | tf_op jit(solution)/shard_map/ppermute | solution.py:601
  16.9 1.2 slice.15
  18.0 1.5 collective-permute-start
  19.5 11.6 %grads.3 = (bf16[480,640]{1,0:T(8,128)(2,1)S(1)}, bf16[480,640]{1,0:T(8,128)(2,1)}, bf16[480,640]{1,0:T(8,128)(2,1)S(1)}, bf16[480,640]{1,0:T(8,128)(2,1)}) custom-call(s32[1]{0:T(128)} %bitcast.position_ref.s_ref.refs_0_, bf16[1024,1280]{1,0:T(8,128)(2,1)} %refs_1_.3, bf16[1024,1280]{1,0:T(8,128)(2,1)} %refs_2_.7, f32[2,1024]{1,0:T(2,128)S(1)} %bitcast.3, ...), custom_call_target="tpu_custom_call" | custom-call | flops 5033164800 | bytes 9994240 | tf_op jit(solution)/shard_map/grads/pallas_call | solution.py:292
  31.2 0.8 copy-done.1
  32.0 4.7 %collective-permute-start.5 = (bf16[480,640]{1,0:T(8,128)(2,1)}, bf16[480,640]{1,0:T(8,128)(2,1)}, u32[]{:S(2)}, u32[]{:S(2)}) collective-permute-start(bf16[480,640]{1,0:T(8,128)(2,1)} %get-tuple-element.22), channel_id=1, source_target_pairs={{0,8},{4,12},{8,0},{12,4},{16,24},{20,28},{24,16},{28,20},{1,9},{5... | collective-permute-start | bytes 1843208 | tf_op jit(solution)/shard_map/ppermute | solution.py:596
  36.7 1.5 collective-permute-start.7
  38.2 28.9 %collective-permute-done.5.refs_1_ = bf16[480,640]{1,0:T(8,128)(2,1)} collective-permute-done((bf16[480,640]{1,0:T(8,128)(2,1)}, bf16[480,640]{1,0:T(8,128)(2,1)}, u32[]{:S(2)}, u32[]{:S(2)}) %collective-permute-start.5) | collective-permute-done | bytes 614432 | tf_op jit(solution)/shard_map/ppermute | solution.py:596
  67.1 1.0 add_convert_fusion.1
  68.7 1.1 add_convert_fusion
  69.8 2.5 %collective-permute-start.8 = (bf16[240,640]{1,0:T(8,128)(2,1)S(1)}, bf16[240,640]{1,0:T(8,128)(2,1)S(1)}, u32[]{:S(2)}, u32[]{:S(2)}) collective-permute-start(bf16[240,640]{1,0:T(8,128)(2,1)S(1)} %add_convert_fusion), channel_id=1, source_target_pairs={{0,8},{4,12},{8,0},{12,4},{16,24},{20,28},{24,16},{28,20},{1,9},{5... | collective-permute-start | bytes 921608 | tf_op jit(solution)/shard_map/ppermute | solution.py:596
  72.4 12.6 %shard_map.100 = (bf16[256,1408]{1,0:T(8,128)(2,1)S(1)}, bf16[256,1408]{1,0:T(8,128)(2,1)S(1)}, bf16[512,1280]{1,0:T(8,128)(2,1)S(1)}, f32[512,128]{1,0:T(8,128)S(1)}) custom-call(s32[1]{0:T(128)} %bitcast.position_ref.s_ref.refs_0_, bf16[512,1280]{1,0:T(8,128)(2,1)} %collective-permute-done.refs_0_.refs_1_, ...), custom_call_target="tpu_custom_call" | custom-call | flops 3355443200 | bytes 10485760 | tf_op jit(solution)/shard_map/pallas_call | solution.py:158
  85.0 14.0 %collective-permute-start.2 = (bf16[256,1408]{1,0:T(8,128)(2,1)S(1)}, bf16[256,1408]{1,0:T(8,128)(2,1)S(1)}, u32[]{:S(2)}, u32[]{:S(2)}) collective-permute-start(bf16[256,1408]{1,0:T(8,128)(2,1)S(1)} %get-tuple-element.20), channel_id=1, source_target_pairs={{0,4},{4,8},{8,12},{12,16},{16,20},{20,24},{24,28},{1,5},{5,9},{9,... | collective-permute-start | bytes 2162696 | tf_op jit(solution)/shard_map/ppermute | solution.py:601
  98.9 4.0 %turned.1.old_ref = f32[480,640]{1,0:T(8,128)S(1)} custom-call(s32[1]{0:T(128)} %bitcast.position_ref.s_ref.refs_0_, f32[2,640,640]{2,1,0:T(8,128)} %refs_4_.7, f32[2,640,640]{2,1,0:T(8,128)} %refs_5_.3, f32[2,640,640]{2,1,0:T(8,128)} %refs_6_.3), custom_call_target="tpu_custom_call" | custom-call | flops 1228800 | bytes 9830400 | tf_op jit(solution)/shard_map/turned/pallas_call | solution.py:326
  103.0 1.7 %renorm.1.own_ref.rest_3_ = bf16[480,640]{1,0:T(8,128)(2,1)S(1)} custom-call(s32[1]{0:T(128)} %bitcast.position_ref.s_ref.refs_0_, f32[480,640]{1,0:T(8,128)S(1)} %turned.1.old_ref, bf16[480,640]{1,0:T(8,128)(2,1)S(1)} %get-tuple-element.21.refs_0_, bf16[480,640]{1,0:T(8,128)(2,1)} %collective-permute-done.5.refs_1_, ...), custom_call_target="tpu_custom_call" | custom-call | flops 3072000 | bytes 3686400 | tf_op jit(solution)/shard_map/renorm/pallas_call | solution.py:365
  105.0 1.7 %collective-permute-start.10 = (bf16[480,640]{1,0:T(8,128)(2,1)S(1)}, bf16[480,640]{1,0:T(8,128)(2,1)S(1)}, u32[]{:S(2)}, u32[]{:S(2)}) collective-permute-start(bf16[480,640]{1,0:T(8,128)(2,1)S(1)} %renorm.1.own_ref.rest_3_), channel_id=1, source_target_pairs={{0,16},{4,20},{8,24},{12,28},{16,0},{20,4},{24,8},{28,12},{1,17},{... | collective-permute-start | bytes 1843208 | tf_op jit(solution)/shard_map/ppermute | solution.py:596
  106.7 14.2 %collective-permute-done.9.over_x.rest_4_ = bf16[480,640]{1,0:T(8,128)(2,1)S(1)} collective-permute-done((bf16[480,640]{1,0:T(8,128)(2,1)S(1)}, bf16[480,640]{1,0:T(8,128)(2,1)S(1)}, u32[]{:S(2)}, u32[]{:S(2)}) %collective-permute-start.9) | collective-permute-done | bytes 614432 | tf_op jit(solution)/shard_map/ppermute | solution.py:596
  121.5 2.2 %collective-permute-start.1 = (bf16[256,1408]{1,0:T(8,128)(2,1)S(1)}, bf16[256,1408]{1,0:T(8,128)(2,1)S(1)}, u32[]{:S(2)}, u32[]{:S(2)}) collective-permute-start(bf16[256,1408]{1,0:T(8,128)(2,1)S(1)} %get-tuple-element.18), channel_id=1, source_target_pairs={{0,4},{4,8},{8,12},{12,16},{16,20},{20,24},{24,28},{1,5},{5,9},{9,... | collective-permute-start | bytes 2162696 | tf_op jit(solution)/shard_map/ppermute | solution.py:601
  123.6 1.7 %merge.2.rest_0_ = bf16[256,1280]{1,0:T(8,128)(2,1)S(1)} custom-call(s32[1]{0:T(128)} %bitcast.position_ref.s_ref.refs_0_, bf16[512,1280]{1,0:T(8,128)(2,1)S(1)} %get-tuple-element.17.own_ref, bf16[256,1408]{1,0:T(8,128)(2,1)S(1)} %collective-permute-done.2.far_ref.far_log, f32[512,128]{1,0:T(8,128)S(1)} %get-tuple-element.19.own_log, ...), custom_call_target="tpu_custom_call" | custom-call | flops 2621440 | bytes 1966080 | tf_op jit(solution)/shard_map/merge/pallas_call | solution.py:423
  125.4 1.5 %collective-permute-start.11 = (bf16[240,640]{1,0:T(8,128)(2,1)S(1)}, bf16[240,640]{1,0:T(8,128)(2,1)S(1)}, u32[]{:S(2)}, u32[]{:S(2)}) collective-permute-start(bf16[240,640]{1,0:T(8,128)(2,1)S(1)} %slice.20), channel_id=1, source_target_pairs={{0,8},{4,12},{8,0},{12,4},{16,24},{20,28},{24,16},{28,20},{1,9},{5... | collective-permute-start | bytes 921608 | tf_op jit(solution)/shard_map/ppermute | solution.py:596
  127.5 11.6 %shard_map.101.rest_1_ = bf16[512,1280]{1,0:T(8,128)(2,1)S(1)} custom-call(s32[1]{0:T(128)} %bitcast.position_ref.s_ref.refs_0_, bf16[1024,1280]{1,0:T(8,128)(2,1)} %refs_0_.1, bf16[1024,1280]{1,0:T(8,128)(2,1)S(1)} %collective-permute-done.3.refs_1_.refs_3_, bf16[1024,1280]{1,0:T(8,128)(2,1)} %refs_2_.5, ...), custom_call_target="tpu_custom_call" | custom-call | flops 3355443200 | bytes 10485760 | tf_op jit(solution)/shard_map/pallas_call | solution.py:158
  139.1 1.8 %collective-permute-start.16 = (bf16[240,640]{1,0:T(8,128)(2,1)S(1)}, bf16[240,640]{1,0:T(8,128)(2,1)S(1)}, u32[]{:S(2)}, u32[]{:S(2)}) collective-permute-start(bf16[240,640]{1,0:T(8,128)(2,1)S(1)} %collective-permute-done.11.rest_6_), channel_id=1, source_target_pairs={{0,4},{4,0},{8,12},{12,8},{16,20},{20,16},{24,28},{28,24},{1,5},{5... | collective-permute-start | bytes 921608 | tf_op jit(solution)/shard_map/ppermute | solution.py:596
  140.9 2.0 %hidden.2.rest_2_ = bf16[1024,640]{1,0:T(8,128)(2,1)S(1)} custom-call(s32[1]{0:T(128)} %bitcast.position_ref.s_ref.refs_0_, bf16[1024,1280]{1,0:T(8,128)(2,1)S(1)} %copy-done, bf16[480,640]{1,0:T(8,128)(2,1)S(1)} %renorm.1.own_ref.rest_3_, bf16[480,640]{1,0:T(8,128)(2,1)S(1)} %collective-permute-done.9.over_x.rest_4_, ...), custom_call_target="tpu_custom_call" | custom-call | flops 1258291200 | bytes 3850240 | tf_op jit(solution)/shard_map/hidden/pallas_call | solution.py:489
  142.9 3.0 %apply.2 = (bf16[1024,1280]{1,0:T(8,128)(2,1)}, f32[256,640]{1,0:T(8,128)S(1)}) custom-call(s32[1]{0:T(128)} %bitcast.position_ref.s_ref.refs_0_, bf16[1024,1280]{1,0:T(8,128)(2,1)S(1)} %copy-done, bf16[256,1280]{1,0:T(8,128)(2,1)S(1)} %merge.2.rest_0_, bf16[512,1280]{1,0:T(8,128)(2,1)S(1)} %shard_map.101.rest_1_, bf16[1024,640]{1,0:T(8,128)(2,1)S(1)} %hidden.2.rest_2_, ...), custom_call_target="tpu_custom_call" | custom-call | flops 1258291200 | bytes 7700480 | tf_op jit(solution)/shard_map/apply/pallas_call | solution.py:571
  146.0 2.0 %hidden.3.rest_2_ = bf16[1024,640]{1,0:T(8,128)(2,1)S(1)} custom-call(s32[1]{0:T(128)} %bitcast.position_ref.s_ref.refs_0_, bf16[1024,1280]{1,0:T(8,128)(2,1)S(1)} %copy-done, bf16[480,640]{1,0:T(8,128)(2,1)S(1)} %collective-permute-done.13.own_ref.rest_3_, bf16[480,640]{1,0:T(8,128)(2,1)S(1)} %collective-permute-done.14.over_x.rest_4_, ...), custom_call_target="tpu_custom_call" | custom-call | flops 1258291200 | bytes 3850240 | tf_op jit(solution)/shard_map/hidden/pallas_call | solution.py:489
  148.0 3.3 %apply.3 = (bf16[1024,1280]{1,0:T(8,128)(2,1)}, f32[256,640]{1,0:T(8,128)S(1)}) custom-call(s32[1]{0:T(128)} %bitcast.position_ref.s_ref.refs_0_, bf16[1024,1280]{1,0:T(8,128)(2,1)S(1)} %copy-done, bf16[256,1280]{1,0:T(8,128)(2,1)S(1)} %merge.2.rest_0_, bf16[512,1280]{1,0:T(8,128)(2,1)S(1)} %shard_map.101.rest_1_, ...), custom_call_target="tpu_custom_call", output_to_operand_aliasing={{0}: (10, {})} | custom-call | flops 1258291200 | bytes 7700480 | tf_op jit(solution)/shard_map/apply/pallas_call | solution.py:571
  151.4 2.1 %merge.3 = bf16[1024,1280]{1,0:T(8,128)(2,1)} custom-call(s32[1]{0:T(128)} %bitcast.position_ref.s_ref.refs_0_, bf16[512,1280]{1,0:T(8,128)(2,1)S(1)} %get-tuple-element.17.own_ref, bf16[256,1408]{1,0:T(8,128)(2,1)S(1)} %collective-permute-done.1.far_ref.far_log, f32[512,128]{1,0:T(8,128)S(1)} %get-tuple-element.19.own_log, ...), custom_call_target="tpu_custom_call", output_to_operand_aliasing={{}: (7, {})} | custom-call | flops 2621440 | bytes 1966080 | tf_op jit(solution)/shard_map/merge/pallas_call | solution.py:423
  (38 shorter events, 2.4 us)
Async XLA Ops:
  0.0 0.7 copy-start.3
  10.8 1.3 slice-start
  10.8 1.7 %slice-start.1 = ((bf16[1024,1280]{1,0:T(8,128)(2,1)}), bf16[512,1280]{1,0:T(8,128)(2,1)S(1)}, s32[]{:S(2)}) async-start(bf16[1024,1280]{1,0:T(8,128)(2,1)} %refs_4_.5), calls=%async_computation.1 | async-start | bytes 2621440 | tf_op jit(solution)/shard_map/slice | solution.py:659
  10.8 8.7 %collective-permute-start.4 = (bf16[1920,640]{1,0:T(8,128)(2,1)S(1)}, bf16[1920,640]{1,0:T(8,128)(2,1)S(1)}, u32[]{:S(2)}, u32[]{:S(2)}) collective-permute-start(bf16[1920,640]{1,0:T(8,128)(2,1)S(1)} %grads.2), channel_id=1, source_target_pairs={{0,4},{4,0},{8,12},{12,8},{16,20},{20,16},{24,28},{28,24},{1,5},{5... | collective-permute-start | bytes 7372808 | tf_op jit(solution)/shard_map/ppermute | solution.py:596
  12.5 4.4 %copy-start.5 = (bf16[1024,1280]{1,0:T(8,128)(2,1)S(1)}, bf16[1024,1280]{1,0:T(8,128)(2,1)}, u32[]{:S(2)}) copy-start(bf16[1024,1280]{1,0:T(8,128)(2,1)} %refs_0_.1) | copy-start | bytes 7864324
  14.2 5.4 %copy-start.4 = (f32[1024,2]{0,1:T(2,128)S(1)}, f32[1024,2]{0,1:T(2,128)}, u32[]{:S(2)}) copy-start(f32[1024,2]{0,1:T(2,128)} %param.16) | copy-start | bytes 24580
  14.2 111.2 %collective-permute-start.3 = (bf16[1024,1280]{1,0:T(8,128)(2,1)}, bf16[1024,1280]{1,0:T(8,128)(2,1)S(1)}, u32[]{:S(2)}, u32[]{:S(2)}) collective-permute-start(bf16[1024,1280]{1,0:T(8,128)(2,1)} %pad_maximum_fusion), channel_id=1, source_target_pairs={{0,4},{4,8},{8,12},{12,16},{16,20},{20,24},{24,28},{1,5},{5,9},{9,... | collective-permute-start | bytes 7864328 | tf_op jit(solution)/shard_map/ppermute | solution.py:601
  18.0 54.3 %collective-permute-start = (bf16[512,1280]{1,0:T(8,128)(2,1)}, bf16[512,1280]{1,0:T(8,128)(2,1)}, u32[]{:S(2)}, u32[]{:S(2)}) collective-permute-start(bf16[512,1280]{1,0:T(8,128)(2,1)} %slice.15), channel_id=1, source_target_pairs={{4,0},{8,4},{12,8},{16,12},{20,16},{24,20},{28,24},{5,1},{9,5},{13... | collective-permute-start | bytes 3932168 | tf_op jit(solution)/shard_map/ppermute | solution.py:601
  31.2 0.8 copy-start.1
  32.0 35.1 %collective-permute-start.5 = (bf16[480,640]{1,0:T(8,128)(2,1)}, bf16[480,640]{1,0:T(8,128)(2,1)}, u32[]{:S(2)}, u32[]{:S(2)}) collective-permute-start(bf16[480,640]{1,0:T(8,128)(2,1)} %get-tuple-element.22), channel_id=1, source_target_pairs={{0,8},{4,12},{8,0},{12,4},{16,24},{20,28},{24,16},{28,20},{1,9},{5... | collective-permute-start | bytes 1843208 | tf_op jit(solution)/shard_map/ppermute | solution.py:596
  36.7 32.0 %collective-permute-start.7 = (bf16[480,640]{1,0:T(8,128)(2,1)}, bf16[480,640]{1,0:T(8,128)(2,1)}, u32[]{:S(2)}, u32[]{:S(2)}) collective-permute-start(bf16[480,640]{1,0:T(8,128)(2,1)} %get-tuple-element.24), channel_id=1, source_target_pairs={{0,16},{4,20},{8,24},{12,28},{16,0},{20,4},{24,8},{28,12},{1,17},{... | collective-permute-start | bytes 1843208 | tf_op jit(solution)/shard_map/ppermute | solution.py:596
  68.1 34.8 %collective-permute-start.6 = (bf16[240,640]{1,0:T(8,128)(2,1)S(1)}, bf16[240,640]{1,0:T(8,128)(2,1)S(1)}, u32[]{:S(2)}, u32[]{:S(2)}) collective-permute-start(bf16[240,640]{1,0:T(8,128)(2,1)S(1)} %add_convert_fusion.1), channel_id=1, source_target_pairs={{0,16},{4,20},{8,24},{12,28},{16,0},{20,4},{24,8},{28,12},{1,17},{... | collective-permute-start | bytes 921608 | tf_op jit(solution)/shard_map/ppermute | solution.py:596
  69.8 33.1 %collective-permute-start.8 = (bf16[240,640]{1,0:T(8,128)(2,1)S(1)}, bf16[240,640]{1,0:T(8,128)(2,1)S(1)}, u32[]{:S(2)}, u32[]{:S(2)}) collective-permute-start(bf16[240,640]{1,0:T(8,128)(2,1)S(1)} %add_convert_fusion), channel_id=1, source_target_pairs={{0,8},{4,12},{8,0},{12,4},{16,24},{20,28},{24,16},{28,20},{1,9},{5... | collective-permute-start | bytes 921608 | tf_op jit(solution)/shard_map/ppermute | solution.py:596
  84.9 18.0 %copy-start.2 = (bf16[480,640]{1,0:T(8,128)(2,1)S(1)}, bf16[480,640]{1,0:T(8,128)(2,1)}, u32[]{:S(2)}) copy-start(bf16[480,640]{1,0:T(8,128)(2,1)} %copy-done.1) | copy-start | bytes 1843204
  85.0 36.5 %collective-permute-start.2 = (bf16[256,1408]{1,0:T(8,128)(2,1)S(1)}, bf16[256,1408]{1,0:T(8,128)(2,1)S(1)}, u32[]{:S(2)}, u32[]{:S(2)}) collective-permute-start(bf16[256,1408]{1,0:T(8,128)(2,1)S(1)} %get-tuple-element.20), channel_id=1, source_target_pairs={{0,4},{4,8},{8,12},{12,16},{16,20},{20,24},{24,28},{1,5},{5,9},{9,... | collective-permute-start | bytes 2162696 | tf_op jit(solution)/shard_map/ppermute | solution.py:601
  104.7 16.3 %collective-permute-start.9 = (bf16[480,640]{1,0:T(8,128)(2,1)S(1)}, bf16[480,640]{1,0:T(8,128)(2,1)S(1)}, u32[]{:S(2)}, u32[]{:S(2)}) collective-permute-start(bf16[480,640]{1,0:T(8,128)(2,1)S(1)} %renorm.1.own_ref.rest_3_), channel_id=1, source_target_pairs={{0,8},{4,12},{8,0},{12,4},{16,24},{20,28},{24,16},{28,20},{1,9},{5... | collective-permute-start | bytes 1843208 | tf_op jit(solution)/shard_map/ppermute | solution.py:596
  105.0 15.9 %collective-permute-start.10 = (bf16[480,640]{1,0:T(8,128)(2,1)S(1)}, bf16[480,640]{1,0:T(8,128)(2,1)S(1)}, u32[]{:S(2)}, u32[]{:S(2)}) collective-permute-start(bf16[480,640]{1,0:T(8,128)(2,1)S(1)} %renorm.1.own_ref.rest_3_), channel_id=1, source_target_pairs={{0,16},{4,20},{8,24},{12,28},{16,0},{20,4},{24,8},{28,12},{1,17},{... | collective-permute-start | bytes 1843208 | tf_op jit(solution)/shard_map/ppermute | solution.py:596
  106.7 20.3 %collective-permute-start.13 = (bf16[480,640]{1,0:T(8,128)(2,1)S(1)}, bf16[480,640]{1,0:T(8,128)(2,1)S(1)}, u32[]{:S(2)}, u32[]{:S(2)}) collective-permute-start(bf16[480,640]{1,0:T(8,128)(2,1)S(1)} %renorm.1.own_ref.rest_3_), channel_id=1, source_target_pairs={{0,4},{4,0},{8,12},{12,8},{16,20},{20,16},{24,28},{28,24},{1,5},{5... | collective-permute-start | bytes 1843208 | tf_op jit(solution)/shard_map/ppermute | solution.py:596
  120.9 25.0 %collective-permute-start.14 = (bf16[480,640]{1,0:T(8,128)(2,1)S(1)}, bf16[480,640]{1,0:T(8,128)(2,1)S(1)}, u32[]{:S(2)}, u32[]{:S(2)}) collective-permute-start(bf16[480,640]{1,0:T(8,128)(2,1)S(1)} %collective-permute-done.9.over_x.rest_4_), channel_id=1, source_target_pairs={{0,4},{4,0},{8,12},{12,8},{16,20},{20,16},{24,28},{28,24},{1,5},{5... | collective-permute-start | bytes 1843208 | tf_op jit(solution)/shard_map/ppermute | solution.py:596
  120.9 25.0 %collective-permute-start.15 = (bf16[480,640]{1,0:T(8,128)(2,1)S(1)}, bf16[480,640]{1,0:T(8,128)(2,1)S(1)}, u32[]{:S(2)}, u32[]{:S(2)}) collective-permute-start(bf16[480,640]{1,0:T(8,128)(2,1)S(1)} %collective-permute-done.10.over_y.rest_5_), channel_id=1, source_target_pairs={{0,4},{4,0},{8,12},{12,8},{16,20},{20,16},{24,28},{28,24},{1,5},{5... | collective-permute-start | bytes 1843208 | tf_op jit(solution)/shard_map/ppermute | solution.py:596
  121.5 29.9 %collective-permute-start.1 = (bf16[256,1408]{1,0:T(8,128)(2,1)S(1)}, bf16[256,1408]{1,0:T(8,128)(2,1)S(1)}, u32[]{:S(2)}, u32[]{:S(2)}) collective-permute-start(bf16[256,1408]{1,0:T(8,128)(2,1)S(1)} %get-tuple-element.18), channel_id=1, source_target_pairs={{0,4},{4,8},{8,12},{12,16},{16,20},{20,24},{24,28},{1,5},{5,9},{9,... | collective-permute-start | bytes 2162696 | tf_op jit(solution)/shard_map/ppermute | solution.py:601
  125.4 15.5 %copy-start = (bf16[1024,1280]{1,0:T(8,128)(2,1)S(1)}, bf16[1024,1280]{1,0:T(8,128)(2,1)}, u32[]{:S(2)}) copy-start(bf16[1024,1280]{1,0:T(8,128)(2,1)} %q_ref.7) | copy-start | bytes 7864324
  125.4 13.7 %collective-permute-start.11 = (bf16[240,640]{1,0:T(8,128)(2,1)S(1)}, bf16[240,640]{1,0:T(8,128)(2,1)S(1)}, u32[]{:S(2)}, u32[]{:S(2)}) collective-permute-start(bf16[240,640]{1,0:T(8,128)(2,1)S(1)} %slice.20), channel_id=1, source_target_pairs={{0,8},{4,12},{8,0},{12,4},{16,24},{20,28},{24,16},{28,20},{1,9},{5... | collective-permute-start | bytes 921608 | tf_op jit(solution)/shard_map/ppermute | solution.py:596
  127.0 13.9 %collective-permute-start.12 = (bf16[240,640]{1,0:T(8,128)(2,1)S(1)}, bf16[240,640]{1,0:T(8,128)(2,1)S(1)}, u32[]{:S(2)}, u32[]{:S(2)}) collective-permute-start(bf16[240,640]{1,0:T(8,128)(2,1)S(1)} %slice.21), channel_id=1, source_target_pairs={{0,16},{4,20},{8,24},{12,28},{16,0},{20,4},{24,8},{28,12},{1,17},{... | collective-permute-start | bytes 921608 | tf_op jit(solution)/shard_map/ppermute | solution.py:596
  139.1 8.9 %collective-permute-start.16 = (bf16[240,640]{1,0:T(8,128)(2,1)S(1)}, bf16[240,640]{1,0:T(8,128)(2,1)S(1)}, u32[]{:S(2)}, u32[]{:S(2)}) collective-permute-start(bf16[240,640]{1,0:T(8,128)(2,1)S(1)} %collective-permute-done.11.rest_6_), channel_id=1, source_target_pairs={{0,4},{4,0},{8,12},{12,8},{16,20},{20,16},{24,28},{28,24},{1,5},{5... | collective-permute-start | bytes 921608 | tf_op jit(solution)/shard_map/ppermute | solution.py:596
  140.9 7.1 %collective-permute-start.17 = (bf16[240,640]{1,0:T(8,128)(2,1)S(1)}, bf16[240,640]{1,0:T(8,128)(2,1)S(1)}, u32[]{:S(2)}, u32[]{:S(2)}) collective-permute-start(bf16[240,640]{1,0:T(8,128)(2,1)S(1)} %collective-permute-done.12.rest_7_), channel_id=1, source_target_pairs={{0,4},{4,0},{8,12},{12,8},{16,20},{20,16},{24,28},{28,24},{1,5},{5... | collective-permute-start | bytes 921608 | tf_op jit(solution)/shard_map/ppermute | solution.py:596

commit v11 on v10

--- a/solution.py
+++ b/solution.py
@@ -656,8 +656,10 @@
     rows = attn_q.shape[0]
     half = rows // 2
     width = 2 if attn_q.shape[1] // HD % 2 == 0 else 1
-    prev = shifted(jnp.concatenate([attn_k[half:], attn_v[half:]], axis=0), 1)
-    guests = shifted(attn_q[:half], -1)
+    asked = attn_q[:half]
+    guests = shifted(asked, -1)
+    later_k, later_v, _ = lax.optimization_barrier((attn_k, attn_v, asked))
+    prev = shifted(jnp.concatenate([later_k[half:], later_v[half:]], axis=0), 1)
     rates_t = rates.T
     stay = lambda a: pltpu.with_memory_space_constraint(a, pltpu.HBM)
     attn_q, attn_k, attn_v = stay(attn_q), stay(attn_k), stay(attn_v)

time: 154 us -> 155 us (level)
  no operation moved by 1% of the time
where the time goes in v11:
time: 155 us
  Pallas kernels  66 us (43%)
  waiting for transfers between devices  43.2 us (28%)
  starting transfers between devices  37 us (24%)
  local copies, waits for them, and re-layouts  4.48 us (3%)
  other arithmetic  3.84 us (2%)
    ppermute x14, waiting for transfers between devices, exchange(): return lax.ppermute(block, 'seq', [(i, i ^ 1 << bit) for i in range(size)])  43.1 us
    pallas_call x2, Pallas kernels, attention(): pl.pallas_call(kernel, grid_spec=pltpu.PrefetchScalarGridSpec(num_scalar_...  24.2 us
    pallas_call x2, Pallas kernels, gradients(): pl.pallas_call(body, grid_spec=pltpu.PrefetchScalarGridSpec(num_scalar_pr...  21.9 us
    ppermute x4, starting transfers between devices, shifted(): lax.ppermute(block, 'seq', [(i, i + by) for i in range(size) if 0 <= i +...  20.8 us
    ppermute x14, starting transfers between devices, exchange(): return lax.ppermute(block, 'seq', [(i, i ^ 1 << bit) for i in range(size)])  16.2 us
    pallas_call x2, Pallas kernels, apply_head(): pl.pallas_call(functools.partial(apply_kernel, tm=tm, head=head, split=sp...  6.34 us
    pallas_call x2, Pallas kernels, hidden_part(): pl.pallas_call(functools.partial(hidden_kernel, tm=min(256, rows), head=h...  4.04 us
    pallas_call x1, Pallas kernels, turned(): pl.pallas_call(functools.partial(turn_kernel, parts=parts), grid_spec=plt...  4 us
  transfers between devices with their start and end apart: 18, of which 2 were waited for; matrix products, arithmetic and copies ran while one was open for 3% of the time, Pallas kernels for 35%

profile of v11, /device:TPU:0, one launch (start us, length us, event | category | flops | bytes accessed | tf_op | source)
XLA Modules:
  0.0 154.6 jit_solution(13308792651366459000)
XLA Ops:
  0.0 0.7 copy-done.3
  0.7 10.2 %grads.2 = bf16[1920,640]{1,0:T(8,128)(2,1)S(1)} custom-call(s32[1]{0:T(128)} %bitcast.position_ref.s_ref.refs_0_, bf16[1024,1280]{1,0:T(8,128)(2,1)} %refs_1_.3, bf16[1024,1280]{1,0:T(8,128)(2,1)} %refs_2_.7, f32[2,1024]{1,0:T(2,128)S(1)} %bitcast.2, f32[2,640,640]{2,1,0:T(8,128)} %refs_4_.7, f32[2,640,640]{2,1,0:T(8,128)} %refs_5_.3, f32[2,640,640]{2,1,0:T(8,128)} %refs_6_.3), custom_call_target="tpu_custom_call" | custom-call | flops 5033164800 | bytes 9994240 | tf_op jit(solution)/shard_map/grads/pallas_call | solution.py:292
  10.9 0.6 collective-permute-start.4
  11.5 1.2 slice.15
  12.7 1.3 slice-done
  14.4 1.7 %pad_maximum_fusion = bf16[1024,1280]{1,0:T(8,128)(2,1)} fusion(bf16[512,1280]{1,0:T(8,128)(2,1)S(1)} %slice-done.1, bf16[512,1280]{1,0:T(8,128)(2,1)S(1)} %slice-done), kind=kLoop, calls=%fused_computation | loop fusion | flops 5242880 | bytes 5242880 | tf_op jit(solution)/shard_map/concatenate | solution.py:662
  16.0 2.1 %collective-permute-start.3 = (bf16[1024,1280]{1,0:T(8,128)(2,1)}, bf16[1024,1280]{1,0:T(8,128)(2,1)S(1)}, u32[]{:S(2)}, u32[]{:S(2)}) collective-permute-start(bf16[1024,1280]{1,0:T(8,128)(2,1)} %pad_maximum_fusion), channel_id=1, source_target_pairs={{0,4},{4,8},{8,12},{12,16},{16,20},{20,24},{24,28},{1,5},{5,9},{9,... | collective-permute-start | bytes 7864328 | tf_op jit(solution)/shard_map/ppermute | solution.py:601
  18.1 1.5 collective-permute-start
  19.6 11.6 %grads.3 = (bf16[480,640]{1,0:T(8,128)(2,1)S(1)}, bf16[480,640]{1,0:T(8,128)(2,1)}, bf16[480,640]{1,0:T(8,128)(2,1)S(1)}, bf16[480,640]{1,0:T(8,128)(2,1)}) custom-call(s32[1]{0:T(128)} %bitcast.position_ref.s_ref.refs_0_, bf16[1024,1280]{1,0:T(8,128)(2,1)} %refs_1_.3, bf16[1024,1280]{1,0:T(8,128)(2,1)} %refs_2_.7, f32[2,1024]{1,0:T(2,128)S(1)} %bitcast.3, ...), custom_call_target="tpu_custom_call" | custom-call | flops 5033164800 | bytes 9994240 | tf_op jit(solution)/shard_map/grads/pallas_call | solution.py:292
  31.3 0.8 copy-done.1
  32.1 4.7 %collective-permute-start.5 = (bf16[480,640]{1,0:T(8,128)(2,1)}, bf16[480,640]{1,0:T(8,128)(2,1)}, u32[]{:S(2)}, u32[]{:S(2)}) collective-permute-start(bf16[480,640]{1,0:T(8,128)(2,1)} %get-tuple-element.26), channel_id=1, source_target_pairs={{0,8},{4,12},{8,0},{12,4},{16,24},{20,28},{24,16},{28,20},{1,9},{5... | collective-permute-start | bytes 1843208 | tf_op jit(solution)/shard_map/ppermute | solution.py:596
  36.8 1.5 collective-permute-start.7
  38.3 28.9 %collective-permute-done.5.refs_1_ = bf16[480,640]{1,0:T(8,128)(2,1)} collective-permute-done((bf16[480,640]{1,0:T(8,128)(2,1)}, bf16[480,640]{1,0:T(8,128)(2,1)}, u32[]{:S(2)}, u32[]{:S(2)}) %collective-permute-start.5) | collective-permute-done | bytes 614432 | tf_op jit(solution)/shard_map/ppermute | solution.py:596
  67.2 1.0 add_convert_fusion.1
  68.8 1.1 add_convert_fusion
  69.9 2.5 %collective-permute-start.8 = (bf16[240,640]{1,0:T(8,128)(2,1)S(1)}, bf16[240,640]{1,0:T(8,128)(2,1)S(1)}, u32[]{:S(2)}, u32[]{:S(2)}) collective-permute-start(bf16[240,640]{1,0:T(8,128)(2,1)S(1)} %add_convert_fusion), channel_id=1, source_target_pairs={{0,8},{4,12},{8,0},{12,4},{16,24},{20,28},{24,16},{28,20},{1,9},{5... | collective-permute-start | bytes 921608 | tf_op jit(solution)/shard_map/ppermute | solution.py:596
  72.5 12.6 %shard_map.100 = (bf16[256,1408]{1,0:T(8,128)(2,1)S(1)}, bf16[256,1408]{1,0:T(8,128)(2,1)S(1)}, bf16[512,1280]{1,0:T(8,128)(2,1)S(1)}, f32[512,128]{1,0:T(8,128)S(1)}) custom-call(s32[1]{0:T(128)} %bitcast.position_ref.s_ref.refs_0_, bf16[512,1280]{1,0:T(8,128)(2,1)} %collective-permute-done.refs_0_.refs_1_, ...), custom_call_target="tpu_custom_call" | custom-call | flops 3355443200 | bytes 10485760 | tf_op jit(solution)/shard_map/pallas_call | solution.py:158
  85.0 15.0 %collective-permute-start.2 = (bf16[256,1408]{1,0:T(8,128)(2,1)S(1)}, bf16[256,1408]{1,0:T(8,128)(2,1)S(1)}, u32[]{:S(2)}, u32[]{:S(2)}) collective-permute-start(bf16[256,1408]{1,0:T(8,128)(2,1)S(1)} %get-tuple-element.22), channel_id=1, source_target_pairs={{0,4},{4,8},{8,12},{12,16},{16,20},{20,24},{24,28},{1,5},{5,9},{9,... | collective-permute-start | bytes 2162696 | tf_op jit(solution)/shard_map/ppermute | solution.py:601
  100.1 4.0 %turned.1.old_ref = f32[480,640]{1,0:T(8,128)S(1)} custom-call(s32[1]{0:T(128)} %bitcast.position_ref.s_ref.refs_0_, f32[2,640,640]{2,1,0:T(8,128)} %refs_4_.7, f32[2,640,640]{2,1,0:T(8,128)} %refs_5_.3, f32[2,640,640]{2,1,0:T(8,128)} %refs_6_.3), custom_call_target="tpu_custom_call" | custom-call | flops 1228800 | bytes 9830400 | tf_op jit(solution)/shard_map/turned/pallas_call | solution.py:326
  104.1 1.7 %renorm.1.own_ref.rest_3_ = bf16[480,640]{1,0:T(8,128)(2,1)S(1)} custom-call(s32[1]{0:T(128)} %bitcast.position_ref.s_ref.refs_0_, f32[480,640]{1,0:T(8,128)S(1)} %turned.1.old_ref, bf16[480,640]{1,0:T(8,128)(2,1)S(1)} %get-tuple-element.25.refs_0_, bf16[480,640]{1,0:T(8,128)(2,1)} %collective-permute-done.5.refs_1_, ...), custom_call_target="tpu_custom_call" | custom-call | flops 3072000 | bytes 3686400 | tf_op jit(solution)/shard_map/renorm/pallas_call | solution.py:365
  106.1 1.7 %collective-permute-start.10 = (bf16[480,640]{1,0:T(8,128)(2,1)S(1)}, bf16[480,640]{1,0:T(8,128)(2,1)S(1)}, u32[]{:S(2)}, u32[]{:S(2)}) collective-permute-start(bf16[480,640]{1,0:T(8,128)(2,1)S(1)} %renorm.1.own_ref.rest_3_), channel_id=1, source_target_pairs={{0,16},{4,20},{8,24},{12,28},{16,0},{20,4},{24,8},{28,12},{1,17},{... | collective-permute-start | bytes 1843208 | tf_op jit(solution)/shard_map/ppermute | solution.py:596
  107.8 14.2 %collective-permute-done.9.over_x.rest_4_ = bf16[480,640]{1,0:T(8,128)(2,1)S(1)} collective-permute-done((bf16[480,640]{1,0:T(8,128)(2,1)S(1)}, bf16[480,640]{1,0:T(8,128)(2,1)S(1)}, u32[]{:S(2)}, u32[]{:S(2)}) %collective-permute-start.9) | collective-permute-done | bytes 614432 | tf_op jit(solution)/shard_map/ppermute | solution.py:596
  122.6 2.2 %collective-permute-start.1 = (bf16[256,1408]{1,0:T(8,128)(2,1)S(1)}, bf16[256,1408]{1,0:T(8,128)(2,1)S(1)}, u32[]{:S(2)}, u32[]{:S(2)}) collective-permute-start(bf16[256,1408]{1,0:T(8,128)(2,1)S(1)} %get-tuple-element.20), channel_id=1, source_target_pairs={{0,4},{4,8},{8,12},{12,16},{16,20},{20,24},{24,28},{1,5},{5,9},{9,... | collective-permute-start | bytes 2162696 | tf_op jit(solution)/shard_map/ppermute | solution.py:601
  124.8 1.7 %merge.2.rest_0_ = bf16[256,1280]{1,0:T(8,128)(2,1)S(1)} custom-call(s32[1]{0:T(128)} %bitcast.position_ref.s_ref.refs_0_, bf16[512,1280]{1,0:T(8,128)(2,1)S(1)} %get-tuple-element.19.own_ref, bf16[256,1408]{1,0:T(8,128)(2,1)S(1)} %collective-permute-done.2.far_ref.far_log, f32[512,128]{1,0:T(8,128)S(1)} %get-tuple-element.21.own_log, ...), custom_call_target="tpu_custom_call" | custom-call | flops 2621440 | bytes 1966080 | tf_op jit(solution)/shard_map/merge/pallas_call | solution.py:423
  126.6 1.5 collective-permute-start.11
  128.6 11.6 %shard_map.101.rest_1_ = bf16[512,1280]{1,0:T(8,128)(2,1)S(1)} custom-call(s32[1]{0:T(128)} %bitcast.position_ref.s_ref.refs_0_, bf16[1024,1280]{1,0:T(8,128)(2,1)} %refs_0_.1, bf16[1024,1280]{1,0:T(8,128)(2,1)S(1)} %collective-permute-done.3.refs_1_.refs_3_, bf16[1024,1280]{1,0:T(8,128)(2,1)} %refs_2_.5, ...), custom_call_target="tpu_custom_call" | custom-call | flops 3355443200 | bytes 10485760 | tf_op jit(solution)/shard_map/pallas_call | solution.py:158
  140.3 1.7 %collective-permute-start.16 = (bf16[240,640]{1,0:T(8,128)(2,1)S(1)}, bf16[240,640]{1,0:T(8,128)(2,1)S(1)}, u32[]{:S(2)}, u32[]{:S(2)}) collective-permute-start(bf16[240,640]{1,0:T(8,128)(2,1)S(1)} %collective-permute-done.11.rest_6_), channel_id=1, source_target_pairs={{0,4},{4,0},{8,12},{12,8},{16,20},{20,16},{24,28},{28,24},{1,5},{5... | collective-permute-start | bytes 921608 | tf_op jit(solution)/shard_map/ppermute | solution.py:596
  142.0 2.0 %hidden.2.rest_2_ = bf16[1024,640]{1,0:T(8,128)(2,1)S(1)} custom-call(s32[1]{0:T(128)} %bitcast.position_ref.s_ref.refs_0_, bf16[1024,1280]{1,0:T(8,128)(2,1)S(1)} %copy-done, bf16[480,640]{1,0:T(8,128)(2,1)S(1)} %renorm.1.own_ref.rest_3_, bf16[480,640]{1,0:T(8,128)(2,1)S(1)} %collective-permute-done.9.over_x.rest_4_, ...), custom_call_target="tpu_custom_call" | custom-call | flops 1258291200 | bytes 3850240 | tf_op jit(solution)/shard_map/hidden/pallas_call | solution.py:489
  144.0 3.0 %apply.2 = (bf16[1024,1280]{1,0:T(8,128)(2,1)}, f32[256,640]{1,0:T(8,128)S(1)}) custom-call(s32[1]{0:T(128)} %bitcast.position_ref.s_ref.refs_0_, bf16[1024,1280]{1,0:T(8,128)(2,1)S(1)} %copy-done, bf16[256,1280]{1,0:T(8,128)(2,1)S(1)} %merge.2.rest_0_, bf16[512,1280]{1,0:T(8,128)(2,1)S(1)} %shard_map.101.rest_1_, bf16[1024,640]{1,0:T(8,128)(2,1)S(1)} %hidden.2.rest_2_, ...), custom_call_target="tpu_custom_call" | custom-call | flops 1258291200 | bytes 7700480 | tf_op jit(solution)/shard_map/apply/pallas_call | solution.py:571
  147.1 2.0 %hidden.3.rest_2_ = bf16[1024,640]{1,0:T(8,128)(2,1)S(1)} custom-call(s32[1]{0:T(128)} %bitcast.position_ref.s_ref.refs_0_, bf16[1024,1280]{1,0:T(8,128)(2,1)S(1)} %copy-done, bf16[480,640]{1,0:T(8,128)(2,1)S(1)} %collective-permute-done.13.own_ref.rest_3_, bf16[480,640]{1,0:T(8,128)(2,1)S(1)} %collective-permute-done.14.over_x.rest_4_, ...), custom_call_target="tpu_custom_call" | custom-call | flops 1258291200 | bytes 3850240 | tf_op jit(solution)/shard_map/hidden/pallas_call | solution.py:489
  149.2 3.3 %apply.3 = (bf16[1024,1280]{1,0:T(8,128)(2,1)}, f32[256,640]{1,0:T(8,128)S(1)}) custom-call(s32[1]{0:T(128)} %bitcast.position_ref.s_ref.refs_0_, bf16[1024,1280]{1,0:T(8,128)(2,1)S(1)} %copy-done, bf16[256,1280]{1,0:T(8,128)(2,1)S(1)} %merge.2.rest_0_, bf16[512,1280]{1,0:T(8,128)(2,1)S(1)} %shard_map.101.rest_1_, ...), custom_call_target="tpu_custom_call", output_to_operand_aliasing={{0}: (10, {})} | custom-call | flops 1258291200 | bytes 7700480 | tf_op jit(solution)/shard_map/apply/pallas_call | solution.py:571
  152.5 2.1 %merge.3 = bf16[1024,1280]{1,0:T(8,128)(2,1)} custom-call(s32[1]{0:T(128)} %bitcast.position_ref.s_ref.refs_0_, bf16[512,1280]{1,0:T(8,128)(2,1)S(1)} %get-tuple-element.19.own_ref, bf16[256,1408]{1,0:T(8,128)(2,1)S(1)} %collective-permute-done.1.far_ref.far_log, f32[512,128]{1,0:T(8,128)S(1)} %get-tuple-element.21.own_log, ...), custom_call_target="tpu_custom_call", output_to_operand_aliasing={{}: (7, {})} | custom-call | flops 2621440 | bytes 1966080 | tf_op jit(solution)/shard_map/merge/pallas_call | solution.py:423
  (38 shorter events, 2.4 us)
Async XLA Ops:
  0.0 0.7 copy-start.3
  0.7 10.8 %copy-start.5 = (bf16[1024,1280]{1,0:T(8,128)(2,1)S(1)}, bf16[1024,1280]{1,0:T(8,128)(2,1)}, u32[]{:S(2)}) copy-start(bf16[1024,1280]{1,0:T(8,128)(2,1)} %refs_0_.1) | copy-start | bytes 7864324
  10.9 8.7 %collective-permute-start.4 = (bf16[1920,640]{1,0:T(8,128)(2,1)S(1)}, bf16[1920,640]{1,0:T(8,128)(2,1)S(1)}, u32[]{:S(2)}, u32[]{:S(2)}) collective-permute-start(bf16[1920,640]{1,0:T(8,128)(2,1)S(1)} %grads.2), channel_id=1, source_target_pairs={{0,4},{4,0},{8,12},{12,8},{16,20},{20,16},{24,28},{28,24},{1,5},{5... | collective-permute-start | bytes 7372808 | tf_op jit(solution)/shard_map/ppermute | solution.py:596
  12.7 1.3 slice-start
  12.7 1.7 %slice-start.1 = ((bf16[1024,1280]{1,0:T(8,128)(2,1)}), bf16[512,1280]{1,0:T(8,128)(2,1)S(1)}, s32[]{:S(2)}) async-start(bf16[1024,1280]{1,0:T(8,128)(2,1)} %refs_4_.5), calls=%async_computation.1 | async-start | bytes 2621440 | tf_op jit(solution)/shard_map/slice | solution.py:662
  14.4 5.2 %copy-start.4 = (f32[1024,2]{0,1:T(2,128)S(1)}, f32[1024,2]{0,1:T(2,128)}, u32[]{:S(2)}) copy-start(f32[1024,2]{0,1:T(2,128)} %param.16) | copy-start | bytes 24580
  16.0 110.5 %collective-permute-start.3 = (bf16[1024,1280]{1,0:T(8,128)(2,1)}, bf16[1024,1280]{1,0:T(8,128)(2,1)S(1)}, u32[]{:S(2)}, u32[]{:S(2)}) collective-permute-start(bf16[1024,1280]{1,0:T(8,128)(2,1)} %pad_maximum_fusion), channel_id=1, source_target_pairs={{0,4},{4,8},{8,12},{12,16},{16,20},{20,24},{24,28},{1,5},{5,9},{9,... | collective-permute-start | bytes 7864328 | tf_op jit(solution)/shard_map/ppermute | solution.py:601
  18.1 54.3 %collective-permute-start = (bf16[512,1280]{1,0:T(8,128)(2,1)}, bf16[512,1280]{1,0:T(8,128)(2,1)}, u32[]{:S(2)}, u32[]{:S(2)}) collective-permute-start(bf16[512,1280]{1,0:T(8,128)(2,1)} %slice.15), channel_id=1, source_target_pairs={{4,0},{8,4},{12,8},{16,12},{20,16},{24,20},{28,24},{5,1},{9,5},{13... | collective-permute-start | bytes 3932168 | tf_op jit(solution)/shard_map/ppermute | solution.py:601
  31.3 0.8 copy-start.1
  32.1 35.1 %collective-permute-start.5 = (bf16[480,640]{1,0:T(8,128)(2,1)}, bf16[480,640]{1,0:T(8,128)(2,1)}, u32[]{:S(2)}, u32[]{:S(2)}) collective-permute-start(bf16[480,640]{1,0:T(8,128)(2,1)} %get-tuple-element.26), channel_id=1, source_target_pairs={{0,8},{4,12},{8,0},{12,4},{16,24},{20,28},{24,16},{28,20},{1,9},{5... | collective-permute-start | bytes 1843208 | tf_op jit(solution)/shard_map/ppermute | solution.py:596
  36.8 32.0 %collective-permute-start.7 = (bf16[480,640]{1,0:T(8,128)(2,1)}, bf16[480,640]{1,0:T(8,128)(2,1)}, u32[]{:S(2)}, u32[]{:S(2)}) collective-permute-start(bf16[480,640]{1,0:T(8,128)(2,1)} %get-tuple-element.28), channel_id=1, source_target_pairs={{0,16},{4,20},{8,24},{12,28},{16,0},{20,4},{24,8},{28,12},{1,17},{... | collective-permute-start | bytes 1843208 | tf_op jit(solution)/shard_map/ppermute | solution.py:596
  68.2 35.9 %collective-permute-start.6 = (bf16[240,640]{1,0:T(8,128)(2,1)S(1)}, bf16[240,640]{1,0:T(8,128)(2,1)S(1)}, u32[]{:S(2)}, u32[]{:S(2)}) collective-permute-start(bf16[240,640]{1,0:T(8,128)(2,1)S(1)} %add_convert_fusion.1), channel_id=1, source_target_pairs={{0,16},{4,20},{8,24},{12,28},{16,0},{20,4},{24,8},{28,12},{1,17},{... | collective-permute-start | bytes 921608 | tf_op jit(solution)/shard_map/ppermute | solution.py:596
  69.9 34.2 %collective-permute-start.8 = (bf16[240,640]{1,0:T(8,128)(2,1)S(1)}, bf16[240,640]{1,0:T(8,128)(2,1)S(1)}, u32[]{:S(2)}, u32[]{:S(2)}) collective-permute-start(bf16[240,640]{1,0:T(8,128)(2,1)S(1)} %add_convert_fusion), channel_id=1, source_target_pairs={{0,8},{4,12},{8,0},{12,4},{16,24},{20,28},{24,16},{28,20},{1,9},{5... | collective-permute-start | bytes 921608 | tf_op jit(solution)/shard_map/ppermute | solution.py:596
  85.0 19.1 %copy-start.2 = (bf16[480,640]{1,0:T(8,128)(2,1)S(1)}, bf16[480,640]{1,0:T(8,128)(2,1)}, u32[]{:S(2)}) copy-start(bf16[480,640]{1,0:T(8,128)(2,1)} %copy-done.1) | copy-start | bytes 1843204
  85.0 37.6 %collective-permute-start.2 = (bf16[256,1408]{1,0:T(8,128)(2,1)S(1)}, bf16[256,1408]{1,0:T(8,128)(2,1)S(1)}, u32[]{:S(2)}, u32[]{:S(2)}) collective-permute-start(bf16[256,1408]{1,0:T(8,128)(2,1)S(1)} %get-tuple-element.22), channel_id=1, source_target_pairs={{0,4},{4,8},{8,12},{12,16},{16,20},{20,24},{24,28},{1,5},{5,9},{9,... | collective-permute-start | bytes 2162696 | tf_op jit(solution)/shard_map/ppermute | solution.py:601
  105.8 16.3 %collective-permute-start.9 = (bf16[480,640]{1,0:T(8,128)(2,1)S(1)}, bf16[480,640]{1,0:T(8,128)(2,1)S(1)}, u32[]{:S(2)}, u32[]{:S(2)}) collective-permute-start(bf16[480,640]{1,0:T(8,128)(2,1)S(1)} %renorm.1.own_ref.rest_3_), channel_id=1, source_target_pairs={{0,8},{4,12},{8,0},{12,4},{16,24},{20,28},{24,16},{28,20},{1,9},{5... | collective-permute-start | bytes 1843208 | tf_op jit(solution)/shard_map/ppermute | solution.py:596
  106.1 15.9 %collective-permute-start.10 = (bf16[480,640]{1,0:T(8,128)(2,1)S(1)}, bf16[480,640]{1,0:T(8,128)(2,1)S(1)}, u32[]{:S(2)}, u32[]{:S(2)}) collective-permute-start(bf16[480,640]{1,0:T(8,128)(2,1)S(1)} %renorm.1.own_ref.rest_3_), channel_id=1, source_target_pairs={{0,16},{4,20},{8,24},{12,28},{16,0},{20,4},{24,8},{28,12},{1,17},{... | collective-permute-start | bytes 1843208 | tf_op jit(solution)/shard_map/ppermute | solution.py:596
  107.8 20.3 %collective-permute-start.13 = (bf16[480,640]{1,0:T(8,128)(2,1)S(1)}, bf16[480,640]{1,0:T(8,128)(2,1)S(1)}, u32[]{:S(2)}, u32[]{:S(2)}) collective-permute-start(bf16[480,640]{1,0:T(8,128)(2,1)S(1)} %renorm.1.own_ref.rest_3_), channel_id=1, source_target_pairs={{0,4},{4,0},{8,12},{12,8},{16,20},{20,16},{24,28},{28,24},{1,5},{5... | collective-permute-start | bytes 1843208 | tf_op jit(solution)/shard_map/ppermute | solution.py:596
  122.1 25.0 %collective-permute-start.14 = (bf16[480,640]{1,0:T(8,128)(2,1)S(1)}, bf16[480,640]{1,0:T(8,128)(2,1)S(1)}, u32[]{:S(2)}, u32[]{:S(2)}) collective-permute-start(bf16[480,640]{1,0:T(8,128)(2,1)S(1)} %collective-permute-done.9.over_x.rest_4_), channel_id=1, source_target_pairs={{0,4},{4,0},{8,12},{12,8},{16,20},{20,16},{24,28},{28,24},{1,5},{5... | collective-permute-start | bytes 1843208 | tf_op jit(solution)/shard_map/ppermute | solution.py:596
  122.1 25.0 %collective-permute-start.15 = (bf16[480,640]{1,0:T(8,128)(2,1)S(1)}, bf16[480,640]{1,0:T(8,128)(2,1)S(1)}, u32[]{:S(2)}, u32[]{:S(2)}) collective-permute-start(bf16[480,640]{1,0:T(8,128)(2,1)S(1)} %collective-permute-done.10.over_y.rest_5_), channel_id=1, source_target_pairs={{0,4},{4,0},{8,12},{12,8},{16,20},{20,16},{24,28},{28,24},{1,5},{5... | collective-permute-start | bytes 1843208 | tf_op jit(solution)/shard_map/ppermute | solution.py:596
  122.6 29.9 %collective-permute-start.1 = (bf16[256,1408]{1,0:T(8,128)(2,1)S(1)}, bf16[256,1408]{1,0:T(8,128)(2,1)S(1)}, u32[]{:S(2)}, u32[]{:S(2)}) collective-permute-start(bf16[256,1408]{1,0:T(8,128)(2,1)S(1)} %get-tuple-element.20), channel_id=1, source_target_pairs={{0,4},{4,8},{8,12},{12,16},{16,20},{20,24},{24,28},{1,5},{5,9},{9,... | collective-permute-start | bytes 2162696 | tf_op jit(solution)/shard_map/ppermute | solution.py:601
  126.6 15.5 %copy-start = (bf16[1024,1280]{1,0:T(8,128)(2,1)S(1)}, bf16[1024,1280]{1,0:T(8,128)(2,1)}, u32[]{:S(2)}) copy-start(bf16[1024,1280]{1,0:T(8,128)(2,1)} %q_ref.7) | copy-start | bytes 7864324
  126.6 13.7 %collective-permute-start.11 = (bf16[240,640]{1,0:T(8,128)(2,1)S(1)}, bf16[240,640]{1,0:T(8,128)(2,1)S(1)}, u32[]{:S(2)}, u32[]{:S(2)}) collective-permute-start(bf16[240,640]{1,0:T(8,128)(2,1)S(1)} %slice.20), channel_id=1, source_target_pairs={{0,8},{4,12},{8,0},{12,4},{16,24},{20,28},{24,16},{28,20},{1,9},{5... | collective-permute-start | bytes 921608 | tf_op jit(solution)/shard_map/ppermute | solution.py:596
  128.1 13.9 %collective-permute-start.12 = (bf16[240,640]{1,0:T(8,128)(2,1)S(1)}, bf16[240,640]{1,0:T(8,128)(2,1)S(1)}, u32[]{:S(2)}, u32[]{:S(2)}) collective-permute-start(bf16[240,640]{1,0:T(8,128)(2,1)S(1)} %slice.21), channel_id=1, source_target_pairs={{0,16},{4,20},{8,24},{12,28},{16,0},{20,4},{24,8},{28,12},{1,17},{... | collective-permute-start | bytes 921608 | tf_op jit(solution)/shard_map/ppermute | solution.py:596
  140.3 8.9 %collective-permute-start.16 = (bf16[240,640]{1,0:T(8,128)(2,1)S(1)}, bf16[240,640]{1,0:T(8,128)(2,1)S(1)}, u32[]{:S(2)}, u32[]{:S(2)}) collective-permute-start(bf16[240,640]{1,0:T(8,128)(2,1)S(1)} %collective-permute-done.11.rest_6_), channel_id=1, source_target_pairs={{0,4},{4,0},{8,12},{12,8},{16,20},{20,16},{24,28},{28,24},{1,5},{5... | collective-permute-start | bytes 921608 | tf_op jit(solution)/shard_map/ppermute | solution.py:596
  142.0 7.1 %collective-permute-start.17 = (bf16[240,640]{1,0:T(8,128)(2,1)S(1)}, bf16[240,640]{1,0:T(8,128)(2,1)S(1)}, u32[]{:S(2)}, u32[]{:S(2)}) collective-permute-start(bf16[240,640]{1,0:T(8,128)(2,1)S(1)} %collective-permute-done.12.rest_7_), channel_id=1, source_target_pairs={{0,4},{4,0},{8,12},{12,8},{16,20},{20,16},{24,28},{28,24},{1,5},{5... | collective-permute-start | bytes 921608 | tf_op jit(solution)/shard_map/ppermute | solution.py:596
